TPU v7x, 512 devices: a whole 4x8x8 slice. The times are simulated.
512 devices in a mesh: grp: 8 (over y), wide: 64 (over x, z, core).
Axes of the slice: x: 4, y: 8, z: 8, core: 2. Of those that a mesh axis runs over, the one named last changes fastest.
Arguments:
- subspace: float32 [16384, 2048], P('wide', 'grp'), may hold values from -6 to 6
- hblocks: float32 [256, 16, 64, 64], P('wide'), may hold values from -0.1875 to 0.1875
- pattern: int32 [256, 16], P('wide'), may hold values from 0 to 255, as said below
- rotation: float32 [2048, 2048], P('grp'), may hold values from -0.125 to 0.125
Outputs:
- rotated: float32 [16384, 2048], P('wide', 'grp')
- correlation: float32 [2048, 256], P(('grp', 'wide'))
Inputs may be any that keep to these rules, and one draw needn't show every extreme that they name: `pattern`: slot 0 of row block i is i itself. Every named block lies on an index of wide (counting around the axis as a loop) at most 2 from that of its row block, atom blocks with the same value of i // 4 lying on one index of wide; each row block has slots at distance 2 on both sides. Blocks may repeat within a row.
All inputs are finite; a program needn't handle non-finite values.
Results may differ from a plain program's by a relative error of at most 0.0001.
Values sent between devices are 32-bit elements; how exact they have to be, the bound alone decides.
No kernel may reach another device: no remote copies, remote signals or barrier semaphores. Data moves between devices by JAX's collectives and lax.ppermute only.
A program may use at most 64 MiB of HBM per device.

v0:
```python
import jax
import jax.numpy as jnp
from jax import lax
from jax.sharding import PartitionSpec as P

B = 64
A_DEV = 4
NB = 16
HW = 2
DEGREE = 4


cheb_center = 0.25
cheb_half = 2.0


def passed_along(value, axis, steps):
    count = lax.axis_size(axis)
    pairs = [(source, (source + steps) % count) for source in range(count)]
    return lax.ppermute(value, axis, pairs)


def build_window(field):
    below = []
    above = []
    moving = field
    for dist in range(HW):
        moving = passed_along(moving, "wide", 1)
        below.append(moving)
    moving = field
    for dist in range(HW):
        moving = passed_along(moving, "wide", -1)
        above.append(moving)
    pieces = below[::-1] + [field] + above
    return jnp.concatenate(pieces, axis=0)


def apply_ham(field, hblocks, slot_index):
    local_blocks = hblocks.shape[0]
    width = field.shape[1]
    window = build_window(field).reshape(-1, B, width)
    picked = jnp.take(window, slot_index, axis=0).reshape(local_blocks, NB, B, width)
    result = jnp.einsum("asij,asjc->aic", hblocks, picked, precision=lax.Precision.HIGHEST)
    return result.reshape(local_blocks * B, width)


def local(subspace, hblocks, pattern, rotation):
    devcount = lax.axis_size("wide")
    myself = lax.axis_index("wide")
    owner = pattern // A_DEV
    relative = (owner - myself + HW + devcount) % devcount
    slot_index = (relative * A_DEV + pattern % A_DEV).reshape(-1)
    previous = subspace
    current = (apply_ham(subspace, hblocks, slot_index) - cheb_center * subspace) / cheb_half
    for step in range(DEGREE - 1):
        nextone = (
            2.0 * (apply_ham(current, hblocks, slot_index) - cheb_center * current) / cheb_half
            - previous
        )
        previous = current
        current = nextone
    total_rows = current.shape[0] * devcount
    gram_term = lax.dot_general(
        current,
        current,
        (((0,), (0,)), ((), ())),
        precision=lax.Precision.HIGHEST,
        preferred_element_type=jnp.float32,
    )
    correlation = lax.psum_scatter(gram_term, "wide", scatter_dimension=0, tiled=True) / total_rows
    rot_term = jnp.dot(
        current, rotation, precision=lax.Precision.HIGHEST, preferred_element_type=jnp.float32
    )
    rotated = lax.psum_scatter(rot_term, "grp", scatter_dimension=1, tiled=True)
    return (rotated, correlation)


def solution(mesh):
    in_specs = (P("wide", "grp"), P("wide", None, None, None), P("wide", None), P("grp", None))
    out_specs = (P("wide", "grp"), P(("grp", "wide"), None))
    return jax.shard_map(local, mesh=mesh, in_specs=in_specs, out_specs=out_specs, check_vma=False)
```

profile of v0, /device:TPU:6, one launch (start us, length us, event | category | flops | bytes accessed | tf_op | source)
XLA Modules:
  0.0 338.5 jit_solution(3153993887702379663)
XLA Ops:
  8.0 0.0 copy-start
  8.0 0.0 all-reduce.3.cloned.1.call-start
  8.1 2.1 collective-permute-start
  10.1 10.7 %collective-permute-start.2 = (f32[256,256]{1,0:T(8,128)}, f32[256,256]{1,0:T(8,128)}, u32[]{:S(2)}, u32[]{:S(2)}) collective-permute-start(f32[256,256]{1,0:T(8,128)} %param.6), channel_id=1, source_target_pairs={{0,63},{1,0},{2,1},{3,2},{4,3},{5,4},{6,5},{7,6},{8,7},{9,8},{10,9... | collective-permute-start | bytes 786440 | tf_op jit(solution)/shard_map/ppermute | solution.py:20
  20.8 0.7 fusion.8
  21.5 0.1 reshape.49
  21.6 1.5 collective-permute-done
  23.1 1.9 collective-permute-start.1
  25.1 0.0 collective-permute-done.2
  25.1 5.8 %collective-permute-start.3 = (f32[256,256]{1,0:T(8,128)}, f32[256,256]{1,0:T(8,128)S(1)}, u32[]{:S(2)}, u32[]{:S(2)}) collective-permute-start(f32[256,256]{1,0:T(8,128)} %collective-permute-done.2), channel_id=1, source_target_pairs={{0,63},{1,0},{2,1},{3,2},{4,3},{5,4},{6,5},{7,6},{8,7},{9,8},{10,9... | collective-permute-start | bytes 786440 | tf_op jit(solution)/shard_map/ppermute | solution.py:20
  30.9 2.0 collective-permute-done.1
  32.9 1.0 constant_dynamic-update-slice_fusion.3
  33.9 1.0 constant_dynamic-update-slice_fusion.2
  34.9 1.0 constant_dynamic-update-slice_fusion.1
  35.9 2.8 gather_fusion
  38.7 2.7 broadcast_select_fusion.3
  41.3 0.2 copy-done.1
  41.5 2.7 fusion.10
  44.2 0.0 copy-start.8
  44.2 1.9 collective-permute-start.4
  46.2 5.8 %collective-permute-start.6 = (f32[256,256]{1,0:T(8,128)S(1)}, f32[256,256]{1,0:T(8,128)S(1)}, u32[]{:S(2)}, u32[]{:S(2)}) collective-permute-start(f32[256,256]{1,0:T(8,128)S(1)} %fusion.3), channel_id=1, source_target_pairs={{0,63},{1,0},{2,1},{3,2},{4,3},{5,4},{6,5},{7,6},{8,7},{9,8},{10,9... | collective-permute-start | bytes 786440 | tf_op jit(solution)/shard_map/ppermute | solution.py:20
  51.9 2.1 collective-permute-done.4
  54.0 1.9 collective-permute-start.5
  56.0 5.8 %collective-permute-start.7 = (f32[256,256]{1,0:T(8,128)S(1)}, f32[256,256]{1,0:T(8,128)S(1)}, u32[]{:S(2)}, u32[]{:S(2)}) collective-permute-start(f32[256,256]{1,0:T(8,128)S(1)} %collective-permute-done.6), channel_id=1, source_target_pairs={{0,63},{1,0},{2,1},{3,2},{4,3},{5,4},{6,5},{7,6},{8,7},{9,8},{10,9... | collective-permute-start | bytes 786440 | tf_op jit(solution)/shard_map/ppermute | solution.py:20
  61.7 2.1 collective-permute-done.5
  63.9 1.7 collective-permute-done.7
  65.6 2.8 gather_fusion.1
  68.4 2.7 broadcast_select_fusion.2
  71.1 0.2 copy-done.2
  71.3 2.7 fusion.11
  73.9 0.1 fusion.2
  74.0 0.0 copy-start.5
  74.0 1.9 collective-permute-start.8
  75.9 5.9 %collective-permute-start.10 = (f32[256,256]{1,0:T(8,128)S(1)}, f32[256,256]{1,0:T(8,128)S(1)}, u32[]{:S(2)}, u32[]{:S(2)}) collective-permute-start(f32[256,256]{1,0:T(8,128)S(1)} %fusion.2), channel_id=1, source_target_pairs={{0,63},{1,0},{2,1},{3,2},{4,3},{5,4},{6,5},{7,6},{8,7},{9,8},{10,9... | collective-permute-start | bytes 786440 | tf_op jit(solution)/shard_map/ppermute | solution.py:20
  81.9 2.1 collective-permute-done.8
  84.0 1.9 collective-permute-start.9
  85.9 5.9 %collective-permute-start.11 = (f32[256,256]{1,0:T(8,128)S(1)}, f32[256,256]{1,0:T(8,128)S(1)}, u32[]{:S(2)}, u32[]{:S(2)}) collective-permute-start(f32[256,256]{1,0:T(8,128)S(1)} %collective-permute-done.10), channel_id=1, source_target_pairs={{0,63},{1,0},{2,1},{3,2},{4,3},{5,4},{6,5},{7,6},{8,7},{9,8},{10,9... | collective-permute-start | bytes 786440 | tf_op jit(solution)/shard_map/ppermute | solution.py:20
  91.9 1.9 collective-permute-done.9
  93.9 1.7 collective-permute-done.11
  95.6 2.8 gather_fusion.2
  98.3 2.7 broadcast_select_fusion.1
  101.0 0.2 copy-done.3
  101.2 2.7 fusion.12
  103.9 0.1 fusion.1
  103.9 1.9 collective-permute-start.12
  105.9 5.9 %collective-permute-start.14 = (f32[256,256]{1,0:T(8,128)S(1)}, f32[256,256]{1,0:T(8,128)S(1)}, u32[]{:S(2)}, u32[]{:S(2)}) collective-permute-start(f32[256,256]{1,0:T(8,128)S(1)} %fusion.1), channel_id=1, source_target_pairs={{0,63},{1,0},{2,1},{3,2},{4,3},{5,4},{6,5},{7,6},{8,7},{9,8},{10,9... | collective-permute-start | bytes 786440 | tf_op jit(solution)/shard_map/ppermute | solution.py:20
  111.8 2.1 collective-permute-done.12
  113.9 1.9 collective-permute-start.13
  115.8 5.8 %collective-permute-start.15 = (f32[256,256]{1,0:T(8,128)S(1)}, f32[256,256]{1,0:T(8,128)S(1)}, u32[]{:S(2)}, u32[]{:S(2)}) collective-permute-start(f32[256,256]{1,0:T(8,128)S(1)} %collective-permute-done.14), channel_id=1, source_target_pairs={{0,63},{1,0},{2,1},{3,2},{4,3},{5,4},{6,5},{7,6},{8,7},{9,8},{10,9... | collective-permute-start | bytes 786440 | tf_op jit(solution)/shard_map/ppermute | solution.py:20
  121.6 2.1 collective-permute-done.13
  123.8 1.7 collective-permute-done.15
  125.5 2.8 gather_fusion.3
  128.3 2.7 broadcast_select_fusion
  131.0 0.2 copy-done.4
  131.1 2.7 fusion.13
  133.8 0.1 fusion
  133.9 1.3 fusion.15
  135.2 0.0 all-reduce.3.cloned.1.call-update
  135.2 0.0 reduce-scatter.2.cloned.1.call-start
  135.3 3.3 fusion.14
  138.6 0.0 reduce-scatter.2.cloned.1.call-update
  138.6 1.3 dynamic-slice
  140.5 189.3 %all-reduce.3.cloned.1.call-done = f32[256,256]{1,0:T(8,128)} async-done(((f32[256,256]{1,0:T(8,128)}), f32[256,256]{1,0:T(8,128)}) %all-reduce.3.cloned.1.call-update) | async-done | bytes 262160
  329.8 1.3 dynamic-slice_multiply_fusion
  (53 shorter events, 0.4 us)
Async XLA Ops:
  8.0 127.3 %copy-start = (f32[256,2048]{1,0:T(8,128)S(1)}, f32[256,2048]{1,0:T(8,128)}, u32[]{:S(2)}) copy-start(f32[256,2048]{1,0:T(8,128)} %param.9) | copy-start | bytes 6291460
  8.0 321.7 %all-reduce.3.cloned.1.call-start = ((), (), s32[]{:S(2)}) async-start(), calls=%async_computation.2 | async-start | bytes 524288
  8.1 15.0 %collective-permute-start = (f32[256,256]{1,0:T(8,128)}, f32[256,256]{1,0:T(8,128)S(1)}, u32[]{:S(2)}, u32[]{:S(2)}) collective-permute-start(f32[256,256]{1,0:T(8,128)} %param.6), channel_id=1, source_target_pairs={{0,1},{1,2},{2,3},{3,4},{4,5},{5,6},{6,7},{7,8},{8,9},{9,10},{10,1... | collective-permute-start | bytes 786440 | tf_op jit(solution)/shard_map/ppermute | solution.py:20
  10.1 14.9 %collective-permute-start.2 = (f32[256,256]{1,0:T(8,128)}, f32[256,256]{1,0:T(8,128)}, u32[]{:S(2)}, u32[]{:S(2)}) collective-permute-start(f32[256,256]{1,0:T(8,128)} %param.6), channel_id=1, source_target_pairs={{0,63},{1,0},{2,1},{3,2},{4,3},{5,4},{6,5},{7,6},{8,7},{9,8},{10,9... | collective-permute-start | bytes 786440 | tf_op jit(solution)/shard_map/ppermute | solution.py:20
  23.1 7.8 %copy-start.16 = (f32[256,256]{1,0:T(8,128)}, f32[256,256]{1,0:T(8,128)S(1)}, u32[]{:S(2)}) copy-start(f32[256,256]{1,0:T(8,128)S(1)} %collective-permute-done) | copy-start | bytes 786436
  23.1 9.8 %collective-permute-start.1 = (f32[256,256]{1,0:T(8,128)S(1)}, f32[256,256]{1,0:T(8,128)S(1)}, u32[]{:S(2)}, u32[]{:S(2)}) collective-permute-start(f32[256,256]{1,0:T(8,128)S(1)} %collective-permute-done), channel_id=1, source_target_pairs={{0,1},{1,2},{2,3},{3,4},{4,5},{5,6},{6,7},{7,8},{8,9},{9,10},{10,1... | collective-permute-start | bytes 786440 | tf_op jit(solution)/shard_map/ppermute | solution.py:20
  25.1 10.8 %collective-permute-start.3 = (f32[256,256]{1,0:T(8,128)}, f32[256,256]{1,0:T(8,128)S(1)}, u32[]{:S(2)}, u32[]{:S(2)}) collective-permute-start(f32[256,256]{1,0:T(8,128)} %collective-permute-done.2), channel_id=1, source_target_pairs={{0,63},{1,0},{2,1},{3,2},{4,3},{5,4},{6,5},{7,6},{8,7},{9,8},{10,9... | collective-permute-start | bytes 786440 | tf_op jit(solution)/shard_map/ppermute | solution.py:20
  38.6 2.9 copy-start.1
  41.5 2.7 copy-start.10
  44.2 19.8 %copy-start.8 = (f32[4,256,64,1]{1,2,3,0:T(8,128)}, f32[4,256,64,1]{1,2,3,0:T(8,128)S(1)}, u32[]{:S(2)}) copy-start(f32[4,256,64,1]{1,2,3,0:T(8,128)S(1)} %fusion.10) | copy-start | bytes 786436
  44.2 21.4 %copy-start.12 = (f32[256,256]{1,0:T(8,128)}, f32[256,256]{1,0:T(8,128)S(1)}, u32[]{:S(2)}) copy-start(f32[256,256]{1,0:T(8,128)S(1)} %fusion.3) | copy-start | bytes 786436
  44.2 9.8 %collective-permute-start.4 = (f32[256,256]{1,0:T(8,128)S(1)}, f32[256,256]{1,0:T(8,128)S(1)}, u32[]{:S(2)}, u32[]{:S(2)}) collective-permute-start(f32[256,256]{1,0:T(8,128)S(1)} %fusion.3), channel_id=1, source_target_pairs={{0,1},{1,2},{2,3},{3,4},{4,5},{5,6},{6,7},{7,8},{8,9},{9,10},{10,1... | collective-permute-start | bytes 786440 | tf_op jit(solution)/shard_map/ppermute | solution.py:20
  46.2 9.8 %collective-permute-start.6 = (f32[256,256]{1,0:T(8,128)S(1)}, f32[256,256]{1,0:T(8,128)S(1)}, u32[]{:S(2)}, u32[]{:S(2)}) collective-permute-start(f32[256,256]{1,0:T(8,128)S(1)} %fusion.3), channel_id=1, source_target_pairs={{0,63},{1,0},{2,1},{3,2},{4,3},{5,4},{6,5},{7,6},{8,7},{9,8},{10,9... | collective-permute-start | bytes 786440 | tf_op jit(solution)/shard_map/ppermute | solution.py:20
  54.0 9.8 %collective-permute-start.5 = (f32[256,256]{1,0:T(8,128)S(1)}, f32[256,256]{1,0:T(8,128)S(1)}, u32[]{:S(2)}, u32[]{:S(2)}) collective-permute-start(f32[256,256]{1,0:T(8,128)S(1)} %collective-permute-done.4), channel_id=1, source_target_pairs={{0,1},{1,2},{2,3},{3,4},{4,5},{5,6},{6,7},{7,8},{8,9},{9,10},{10,1... | collective-permute-start | bytes 786440 | tf_op jit(solution)/shard_map/ppermute | solution.py:20
  56.0 9.6 %collective-permute-start.7 = (f32[256,256]{1,0:T(8,128)S(1)}, f32[256,256]{1,0:T(8,128)S(1)}, u32[]{:S(2)}, u32[]{:S(2)}) collective-permute-start(f32[256,256]{1,0:T(8,128)S(1)} %collective-permute-done.6), channel_id=1, source_target_pairs={{0,63},{1,0},{2,1},{3,2},{4,3},{5,4},{6,5},{7,6},{8,7},{9,8},{10,9... | collective-permute-start | bytes 786440 | tf_op jit(solution)/shard_map/ppermute | solution.py:20
  68.4 2.9 copy-start.2
  71.3 2.7 copy-start.9
  71.3 2.7 copy-start.11
  74.0 21.6 %copy-start.5 = (f32[256,256]{1,0:T(8,128)}, f32[256,256]{1,0:T(8,128)S(1)}, u32[]{:S(2)}) copy-start(f32[256,256]{1,0:T(8,128)S(1)} %fusion.2) | copy-start | bytes 786436
  74.0 10.0 %collective-permute-start.8 = (f32[256,256]{1,0:T(8,128)S(1)}, f32[256,256]{1,0:T(8,128)S(1)}, u32[]{:S(2)}, u32[]{:S(2)}) collective-permute-start(f32[256,256]{1,0:T(8,128)S(1)} %fusion.2), channel_id=1, source_target_pairs={{0,1},{1,2},{2,3},{3,4},{4,5},{5,6},{6,7},{7,8},{8,9},{9,10},{10,1... | collective-permute-start | bytes 786440 | tf_op jit(solution)/shard_map/ppermute | solution.py:20
  75.9 10.0 %collective-permute-start.10 = (f32[256,256]{1,0:T(8,128)S(1)}, f32[256,256]{1,0:T(8,128)S(1)}, u32[]{:S(2)}, u32[]{:S(2)}) collective-permute-start(f32[256,256]{1,0:T(8,128)S(1)} %fusion.2), channel_id=1, source_target_pairs={{0,63},{1,0},{2,1},{3,2},{4,3},{5,4},{6,5},{7,6},{8,7},{9,8},{10,9... | collective-permute-start | bytes 786440 | tf_op jit(solution)/shard_map/ppermute | solution.py:20
  84.0 9.8 %collective-permute-start.9 = (f32[256,256]{1,0:T(8,128)S(1)}, f32[256,256]{1,0:T(8,128)S(1)}, u32[]{:S(2)}, u32[]{:S(2)}) collective-permute-start(f32[256,256]{1,0:T(8,128)S(1)} %collective-permute-done.8), channel_id=1, source_target_pairs={{0,1},{1,2},{2,3},{3,4},{4,5},{5,6},{6,7},{7,8},{8,9},{9,10},{10,1... | collective-permute-start | bytes 786440 | tf_op jit(solution)/shard_map/ppermute | solution.py:20
  85.9 9.6 %collective-permute-start.11 = (f32[256,256]{1,0:T(8,128)S(1)}, f32[256,256]{1,0:T(8,128)S(1)}, u32[]{:S(2)}, u32[]{:S(2)}) collective-permute-start(f32[256,256]{1,0:T(8,128)S(1)} %collective-permute-done.10), channel_id=1, source_target_pairs={{0,63},{1,0},{2,1},{3,2},{4,3},{5,4},{6,5},{7,6},{8,7},{9,8},{10,9... | collective-permute-start | bytes 786440 | tf_op jit(solution)/shard_map/ppermute | solution.py:20
  98.3 2.9 copy-start.3
  101.2 2.7 copy-start.6
  101.2 2.7 copy-start.13
  103.9 21.6 %copy-start.14 = (f32[256,256]{1,0:T(8,128)}, f32[256,256]{1,0:T(8,128)S(1)}, u32[]{:S(2)}) copy-start(f32[256,256]{1,0:T(8,128)S(1)} %fusion.1) | copy-start | bytes 786436
  103.9 10.0 %collective-permute-start.12 = (f32[256,256]{1,0:T(8,128)S(1)}, f32[256,256]{1,0:T(8,128)S(1)}, u32[]{:S(2)}, u32[]{:S(2)}) collective-permute-start(f32[256,256]{1,0:T(8,128)S(1)} %fusion.1), channel_id=1, source_target_pairs={{0,1},{1,2},{2,3},{3,4},{4,5},{5,6},{6,7},{7,8},{8,9},{9,10},{10,1... | collective-permute-start | bytes 786440 | tf_op jit(solution)/shard_map/ppermute | solution.py:20
  105.9 10.0 %collective-permute-start.14 = (f32[256,256]{1,0:T(8,128)S(1)}, f32[256,256]{1,0:T(8,128)S(1)}, u32[]{:S(2)}, u32[]{:S(2)}) collective-permute-start(f32[256,256]{1,0:T(8,128)S(1)} %fusion.1), channel_id=1, source_target_pairs={{0,63},{1,0},{2,1},{3,2},{4,3},{5,4},{6,5},{7,6},{8,7},{9,8},{10,9... | collective-permute-start | bytes 786440 | tf_op jit(solution)/shard_map/ppermute | solution.py:20
  113.9 9.8 %collective-permute-start.13 = (f32[256,256]{1,0:T(8,128)S(1)}, f32[256,256]{1,0:T(8,128)S(1)}, u32[]{:S(2)}, u32[]{:S(2)}) collective-permute-start(f32[256,256]{1,0:T(8,128)S(1)} %collective-permute-done.12), channel_id=1, source_target_pairs={{0,1},{1,2},{2,3},{3,4},{4,5},{5,6},{6,7},{7,8},{8,9},{9,10},{10,1... | collective-permute-start | bytes 786440 | tf_op jit(solution)/shard_map/ppermute | solution.py:20
  115.8 9.6 %collective-permute-start.15 = (f32[256,256]{1,0:T(8,128)S(1)}, f32[256,256]{1,0:T(8,128)S(1)}, u32[]{:S(2)}, u32[]{:S(2)}) collective-permute-start(f32[256,256]{1,0:T(8,128)S(1)} %collective-permute-done.14), channel_id=1, source_target_pairs={{0,63},{1,0},{2,1},{3,2},{4,3},{5,4},{6,5},{7,6},{8,7},{9,8},{10,9... | collective-permute-start | bytes 786440 | tf_op jit(solution)/shard_map/ppermute | solution.py:20
  128.3 2.9 copy-start.4
  131.1 2.7 copy-start.7
  131.1 2.7 copy-start.15
  135.2 195.8 %reduce-scatter.2.cloned.1.call-start = ((), (), s32[]{:S(2)}) async-start(), calls=%async_computation.1 | async-start | bytes 2359296 | tf_op jit(solution)/shard_map/reduce_scatter | solution.py:74
Sparse Core Ops, SparseCore 0:
  135.3 194.3 all-reduce.2
Sparse Core Ops, SparseCore 1:
  139.1 53.1 reduce-scatter.1
where the time goes:
time: 343 us; the launch traced here: 339 us
  waiting for transfers between devices  210 us (61%)
  starting transfers between devices  67 us (20%)
  between operations  16.7 us (5%)
  local copies, waits for them, and re-layouts  16.4 us (5%)
  matrix products  15.2 us (4%)
  other arithmetic  12.9 us (4%)
    unnamed x3, waiting for transfers between devices  189 us
    ppermute x16, starting transfers between devices, passed_along(): return lax.ppermute(value, axis, pairs)  67 us
    ppermute x16, waiting for transfers between devices, passed_along(): return lax.ppermute(value, axis, pairs)  21 us
    gather x4, local copies, waits for them, and re-layouts, apply_ham(): jnp.take(window, slot_index, axis=0).reshape(local_blocks, NB, B, width)  11.1 us
    select_n x5, other arithmetic, apply_ham(): jnp.take(window, slot_index, axis=0).reshape(local_blocks, NB, B, width)  10.7 us
    dot_general x4, matrix products, apply_ham(): jnp.einsum('asij,asjc->aic', hblocks, picked, precision=lax.Precision.HIG...  10.6 us
  transfers between devices with their start and end apart: 18, of which 12 were waited for; matrix products, arithmetic and copies ran while one was open for 3% of the time, Pallas kernels for 0%

commit v1 on v0

v1 whole, which is shorter than its diff:
```python
import jax
import jax.numpy as jnp
from jax import lax
from jax.sharding import PartitionSpec as P

B = 64
A_DEV = 4
NB = 16
HW = 2
DEGREE = 4


cheb_center = 0.25
cheb_half = 2.0

HI = lax.Precision.HIGHEST


def passed_along(value, axis, steps):
    count = lax.axis_size(axis)
    pairs = [(source, (source + steps) % count) for source in range(count)]
    return lax.ppermute(value, axis, pairs)


def dense_hamiltonian(hblocks, slot_index):
    local_blocks = hblocks.shape[0]
    window_blocks = (2 * HW + 1) * A_DEV
    onehot = (slot_index[:, :, None] == jnp.arange(window_blocks)[None, None, :]).astype(jnp.float32)
    hd = jnp.einsum("asp,asij->aipj", onehot, hblocks, precision=HI)
    return hd.reshape(local_blocks * B, window_blocks * B)


def apply_ham(field, hdense):
    rows = field.shape[0]
    pieces = [
        passed_along(field, "wide", 2),
        passed_along(field, "wide", 1),
        field,
        passed_along(field, "wide", -1),
        passed_along(field, "wide", -2),
    ]
    total = None
    for idx in (2, 1, 3, 0, 4):
        term = jnp.dot(hdense[:, idx * rows:(idx + 1) * rows], pieces[idx], precision=HI,
                       preferred_element_type=jnp.float32)
        total = term if total is None else total + term
    return total


def butterfly_scatter(value, axis):
    count = lax.axis_size(axis)
    me = lax.axis_index(axis)
    piece = value.shape[0] // count
    buf = value.reshape((count, piece) + value.shape[1:])
    bit = 0
    while (1 << bit) < count:
        n = buf.shape[0]
        buf = buf.reshape((n // 2, 2) + buf.shape[1:])
        mine = (me >> bit) & 1
        keep = jnp.where(mine == 0, buf[:, 0], buf[:, 1])
        send = jnp.where(mine == 0, buf[:, 1], buf[:, 0])
        pairs = [(i, i ^ (1 << bit)) for i in range(count)]
        buf = keep + lax.ppermute(send, axis, pairs)
        bit += 1
    return buf.reshape((piece,) + value.shape[1:])


def local(subspace, hblocks, pattern, rotation):
    devcount = lax.axis_size("wide")
    myself = lax.axis_index("wide")
    owner = pattern // A_DEV
    relative = (owner - myself + HW + devcount) % devcount
    slot_index = relative * A_DEV + pattern % A_DEV
    hdense = dense_hamiltonian(hblocks, slot_index)
    previous = subspace
    current = (apply_ham(subspace, hdense) - cheb_center * subspace) / cheb_half
    for step in range(DEGREE - 1):
        nextone = (
            2.0 * (apply_ham(current, hdense) - cheb_center * current) / cheb_half
            - previous
        )
        previous = current
        current = nextone
    total_rows = current.shape[0] * devcount
    gram_term = lax.dot_general(
        current,
        current,
        (((0,), (0,)), ((), ())),
        precision=HI,
        preferred_element_type=jnp.float32,
    )
    correlation = butterfly_scatter(gram_term, "wide") / total_rows
    rot_term = jnp.dot(
        current, rotation, precision=HI, preferred_element_type=jnp.float32
    )
    rotated = lax.psum_scatter(rot_term, "grp", scatter_dimension=1, tiled=True)
    return (rotated, correlation)


def solution(mesh):
    in_specs = (P("wide", "grp"), P("wide", None, None, None), P("wide", None), P("grp", None))
    out_specs = (P("wide", "grp"), P(("grp", "wide"), None))
    return jax.shard_map(local, mesh=mesh, in_specs=in_specs, out_specs=out_specs, check_vma=False)
```

time: 343 us -> 166 us (0.48); the launches traced: 339 us -> 165 us
  waiting for transfers between devices: 210 us -> 31.7 us
  starting transfers between devices: 67 us -> 91.4 us
  local copies, waits for them, and re-layouts: 16.4 us -> 3.92 us
  other arithmetic: 12.9 us -> 1.49 us
  matrix products: 15.2 us -> 22.1 us
    unnamed x3 -> x1, waiting for transfers between devices: 189 us -> 0.02 us
    ppermute x0 -> x6, starting transfers between devices: none -> 26.5 us  [butterfly_scatter(): buf = keep + lax.ppermute(send, axis, pairs)]
    ppermute x0 -> x6, waiting for transfers between devices: none -> 17.5 us  [butterfly_scatter(): buf = keep + lax.ppermute(send, axis, pairs)]
    ppermute x16, waiting for transfers between devices: 21 us -> 8.9 us  [passed_along(): return lax.ppermute(value, axis, pairs)]
    gather x4 -> x0, local copies, waits for them, and re-layouts: 11.1 us -> none  [apply_ham(): jnp.take(window, slot_index, axis=0).reshape(local_blocks, NB, B, width)]
    select_n x5 -> x6, other arithmetic: 10.7 us -> 0.09 us  [butterfly_scatter(): send = jnp.where(mine == 0, buf[:, 1], buf[:, 0])]
    dot_general x6 -> x23, matrix products: 15.2 us -> 22.1 us  [the longest x20 12.5 us: apply_ham(): jnp.dot(hdense[:, idx * rows:(idx + 1) * rows], pieces[idx], precision=HI...]
    reduce_scatter x1, waiting for transfers between devices: 0.01 us -> 5.28 us  [local(): rotated = lax.psum_scatter(rot_term, 'grp', scatter_dimension=1, tiled=True)]
  transfers between devices with their start and end apart: 18 -> 23, of which waited for: 12 -> 13; matrix products, arithmetic and copies ran while one was open for 3% -> 12% of each run, Pallas kernels for 0% -> 0%
where the time goes in v1:
time: 166 us; the launch traced here: 165 us
  starting transfers between devices  91.4 us (55%)
  waiting for transfers between devices  31.7 us (19%)
  matrix products  22.1 us (13%)
  between operations  14.6 us (9%)
  local copies, waits for them, and re-layouts  3.92 us (2%)
    ppermute x16, starting transfers between devices, passed_along(): return lax.ppermute(value, axis, pairs)  64.8 us
    ppermute x6, starting transfers between devices, butterfly_scatter(): buf = keep + lax.ppermute(send, axis, pairs)  26.5 us
    ppermute x6, waiting for transfers between devices, butterfly_scatter(): buf = keep + lax.ppermute(send, axis, pairs)  17.5 us
    dot_general x20, matrix products, apply_ham(): jnp.dot(hdense[:, idx * rows:(idx + 1) * rows], pieces[idx], precision=HI...  12.5 us
    ppermute x16, waiting for transfers between devices, passed_along(): return lax.ppermute(value, axis, pairs)  8.9 us
    dot_general x1, matrix products, dense_hamiltonian(): hd = jnp.einsum('asp,asij->aipj', onehot, hblocks, precision=HI)  5.74 us
    reduce_scatter x1, waiting for transfers between devices, local(): rotated = lax.psum_scatter(rot_term, 'grp', scatter_dimension=1, tiled=True)  5.28 us
  transfers between devices with their start and end apart: 23, of which 13 were waited for; matrix products, arithmetic and copies ran while one was open for 12% of the time, Pallas kernels for 0%

profile of v1, /device:TPU:6, one launch (start us, length us, event | category | flops | bytes accessed | tf_op | source)
XLA Modules:
  0.0 165.2 jit_solution(16368243658001271701)
XLA Ops:
  7.2 2.1 %collective-permute-start = (f32[256,256]{1,0:T(8,128)}, f32[256,256]{1,0:T(8,128)}, u32[]{:S(2)}, u32[]{:S(2)}) collective-permute-start(f32[256,256]{1,0:T(8,128)} %param.4), channel_id=1, source_target_pairs={{0,1},{1,2},{2,3},{3,4},{4,5},{5,6},{6,7},{7,8},{8,9},{9,10},{10,1... | collective-permute-start | bytes 786440 | tf_op jit(solution)/shard_map/ppermute | solution.py:22
  9.3 11.2 %collective-permute-start.3 = (f32[256,256]{1,0:T(8,128)}, f32[256,256]{1,0:T(8,128)}, u32[]{:S(2)}, u32[]{:S(2)}) collective-permute-start(f32[256,256]{1,0:T(8,128)} %param.4), channel_id=1, source_target_pairs={{0,62},{1,63},{2,0},{3,1},{4,2},{5,3},{6,4},{7,5},{8,6},{9,7},{10,... | collective-permute-start | bytes 786440 | tf_op jit(solution)/shard_map/ppermute | solution.py:22
  20.5 1.9 %collective-permute-start.2 = (f32[256,256]{1,0:T(8,128)}, f32[256,256]{1,0:T(8,128)}, u32[]{:S(2)}, u32[]{:S(2)}) collective-permute-start(f32[256,256]{1,0:T(8,128)} %param.4), channel_id=1, source_target_pairs={{0,2},{1,3},{2,4},{3,5},{4,6},{5,7},{6,8},{7,9},{8,10},{9,11},{10,... | collective-permute-start | bytes 786440 | tf_op jit(solution)/shard_map/ppermute | solution.py:22
  22.4 4.9 %collective-permute-start.1 = (f32[256,256]{1,0:T(8,128)}, f32[256,256]{1,0:T(8,128)}, u32[]{:S(2)}, u32[]{:S(2)}) collective-permute-start(f32[256,256]{1,0:T(8,128)} %param.4), channel_id=1, source_target_pairs={{0,63},{1,0},{2,1},{3,2},{4,3},{5,4},{6,5},{7,6},{8,7},{9,8},{10,9... | collective-permute-start | bytes 786440 | tf_op jit(solution)/shard_map/ppermute | solution.py:22
  27.4 0.7 fusion.70
  28.1 5.7 %fusion.2 = f32[4,64,20,64]{3,2,1,0:T(8,128)} fusion(f32[4,16,64,64]{3,2,1,0:T(8,128)} %param.5, s32[4,16]{1,0:T(4,128)S(1)} %fusion.70), kind=kOutput, calls=%fused_computation.2 | convolution fusion | flops 62915840 | bytes 2359552 | tf_op jit(solution)/shard_map/asp,asij->aipj/dot_general | solution.py:29
  33.8 2.2 %reshape.97 = f32[256,1280]{1,0:T(8,128)S(1)} reshape(f32[4,64,20,64]{3,2,1,0:T(8,128)} %fusion.2) | data formatting | bytes 2621440 | tf_op jit(solution)/shard_map/reshape | solution.py:30
  36.1 1.3 fusion.48
  37.4 1.4 fusion.24
  38.8 1.3 fusion.32
  40.1 1.3 convolution_add_fusion.7
  41.5 1.4 broadcast_multiply_fusion
  42.9 1.9 %collective-permute-start.6 = (f32[256,256]{1,0:T(8,128)S(1)}, f32[256,256]{1,0:T(8,128)S(1)}, u32[]{:S(2)}, u32[]{:S(2)}) collective-permute-start(f32[256,256]{1,0:T(8,128)S(1)} %get-tuple-element.2), channel_id=1, source_target_pairs={{0,2},{1,3},{2,4},{3,5},{4,6},{5,7},{6,8},{7,9},{8,10},{9,11},{10,... | collective-permute-start | bytes 786440 | tf_op jit(solution)/shard_map/ppermute | solution.py:22
  44.8 1.9 %collective-permute-start.4 = (f32[256,256]{1,0:T(8,128)S(1)}, f32[256,256]{1,0:T(8,128)S(1)}, u32[]{:S(2)}, u32[]{:S(2)}) collective-permute-start(f32[256,256]{1,0:T(8,128)S(1)} %get-tuple-element.2), channel_id=1, source_target_pairs={{0,1},{1,2},{2,3},{3,4},{4,5},{5,6},{6,7},{7,8},{8,9},{9,10},{10,1... | collective-permute-start | bytes 786440 | tf_op jit(solution)/shard_map/ppermute | solution.py:22
  46.7 6.0 %collective-permute-start.7 = (f32[256,256]{1,0:T(8,128)S(1)}, f32[256,256]{1,0:T(8,128)S(1)}, u32[]{:S(2)}, u32[]{:S(2)}) collective-permute-start(f32[256,256]{1,0:T(8,128)S(1)} %get-tuple-element.2), channel_id=1, source_target_pairs={{0,62},{1,63},{2,0},{3,1},{4,2},{5,3},{6,4},{7,5},{8,6},{9,7},{10,... | collective-permute-start | bytes 786440 | tf_op jit(solution)/shard_map/ppermute | solution.py:22
  52.8 3.4 %collective-permute-start.5 = (f32[256,256]{1,0:T(8,128)S(1)}, f32[256,256]{1,0:T(8,128)S(1)}, u32[]{:S(2)}, u32[]{:S(2)}) collective-permute-start(f32[256,256]{1,0:T(8,128)S(1)} %get-tuple-element.2), channel_id=1, source_target_pairs={{0,63},{1,0},{2,1},{3,2},{4,3},{5,4},{6,5},{7,6},{8,7},{9,8},{10,9... | collective-permute-start | bytes 786440 | tf_op jit(solution)/shard_map/ppermute | solution.py:22
  56.1 0.4 fusion.46
  56.5 0.4 fusion.30
  56.9 1.7 %collective-permute-done.7 = f32[256,256]{1,0:T(8,128)S(1)} collective-permute-done((f32[256,256]{1,0:T(8,128)S(1)}, f32[256,256]{1,0:T(8,128)S(1)}, u32[]{:S(2)}, u32[]{:S(2)}) %collective-permute-start.7) | collective-permute-done | bytes 262176 | tf_op jit(solution)/shard_map/ppermute | solution.py:22
  58.6 0.4 fusion.22
  59.0 0.4 convolution_add_fusion.5
  59.4 2.0 %collective-permute-done.5 = f32[256,256]{1,0:T(8,128)S(1)} collective-permute-done((f32[256,256]{1,0:T(8,128)S(1)}, f32[256,256]{1,0:T(8,128)S(1)}, u32[]{:S(2)}, u32[]{:S(2)}) %collective-permute-start.5) | collective-permute-done | bytes 262176 | tf_op jit(solution)/shard_map/ppermute | solution.py:22
  61.4 0.4 fusion.13
  61.8 1.9 %collective-permute-start.10 = (f32[256,256]{1,0:T(8,128)S(1)}, f32[256,256]{1,0:T(8,128)S(1)}, u32[]{:S(2)}, u32[]{:S(2)}) collective-permute-start(f32[256,256]{1,0:T(8,128)S(1)} %fusion.13), channel_id=1, source_target_pairs={{0,2},{1,3},{2,4},{3,5},{4,6},{5,7},{6,8},{7,9},{8,10},{9,11},{10,... | collective-permute-start | bytes 786440 | tf_op jit(solution)/shard_map/ppermute | solution.py:22
  63.7 6.0 %collective-permute-start.11 = (f32[256,256]{1,0:T(8,128)S(1)}, f32[256,256]{1,0:T(8,128)S(1)}, u32[]{:S(2)}, u32[]{:S(2)}) collective-permute-start(f32[256,256]{1,0:T(8,128)S(1)} %fusion.13), channel_id=1, source_target_pairs={{0,62},{1,63},{2,0},{3,1},{4,2},{5,3},{6,4},{7,5},{8,6},{9,7},{10,... | collective-permute-start | bytes 786440 | tf_op jit(solution)/shard_map/ppermute | solution.py:22
  69.8 0.4 fusion.44
  70.2 1.9 %collective-permute-start.8 = (f32[256,256]{1,0:T(8,128)S(1)}, f32[256,256]{1,0:T(8,128)S(1)}, u32[]{:S(2)}, u32[]{:S(2)}) collective-permute-start(f32[256,256]{1,0:T(8,128)S(1)} %fusion.13), channel_id=1, source_target_pairs={{0,1},{1,2},{2,3},{3,4},{4,5},{5,6},{6,7},{7,8},{8,9},{9,10},{10,1... | collective-permute-start | bytes 786440 | tf_op jit(solution)/shard_map/ppermute | solution.py:22
  72.1 5.8 %collective-permute-start.9 = (f32[256,256]{1,0:T(8,128)S(1)}, f32[256,256]{1,0:T(8,128)S(1)}, u32[]{:S(2)}, u32[]{:S(2)}) collective-permute-start(f32[256,256]{1,0:T(8,128)S(1)} %fusion.13), channel_id=1, source_target_pairs={{0,63},{1,0},{2,1},{3,2},{4,3},{5,4},{6,5},{7,6},{8,7},{9,8},{10,9... | collective-permute-start | bytes 786440 | tf_op jit(solution)/shard_map/ppermute | solution.py:22
  77.9 0.4 fusion.28
  78.3 0.4 fusion.20
  78.7 1.3 collective-permute-done.8
  80.0 0.4 convolution_add_fusion.3
  80.4 1.4 collective-permute-done.9
  81.7 0.4 fusion.16
  82.2 1.9 %collective-permute-start.14 = (f32[256,256]{1,0:T(8,128)S(1)}, f32[256,256]{1,0:T(8,128)S(1)}, u32[]{:S(2)}, u32[]{:S(2)}) collective-permute-start(f32[256,256]{1,0:T(8,128)S(1)} %fusion.16), channel_id=1, source_target_pairs={{0,2},{1,3},{2,4},{3,5},{4,6},{5,7},{6,8},{7,9},{8,10},{9,11},{10,... | collective-permute-start | bytes 786440 | tf_op jit(solution)/shard_map/ppermute | solution.py:22
  84.1 6.0 %collective-permute-start.15 = (f32[256,256]{1,0:T(8,128)S(1)}, f32[256,256]{1,0:T(8,128)S(1)}, u32[]{:S(2)}, u32[]{:S(2)}) collective-permute-start(f32[256,256]{1,0:T(8,128)S(1)} %fusion.16), channel_id=1, source_target_pairs={{0,62},{1,63},{2,0},{3,1},{4,2},{5,3},{6,4},{7,5},{8,6},{9,7},{10,... | collective-permute-start | bytes 786440 | tf_op jit(solution)/shard_map/ppermute | solution.py:22
  90.1 0.4 fusion.50
  90.5 1.9 %collective-permute-start.12 = (f32[256,256]{1,0:T(8,128)S(1)}, f32[256,256]{1,0:T(8,128)S(1)}, u32[]{:S(2)}, u32[]{:S(2)}) collective-permute-start(f32[256,256]{1,0:T(8,128)S(1)} %fusion.16), channel_id=1, source_target_pairs={{0,1},{1,2},{2,3},{3,4},{4,5},{5,6},{6,7},{7,8},{8,9},{9,10},{10,1... | collective-permute-start | bytes 786440 | tf_op jit(solution)/shard_map/ppermute | solution.py:22
  92.4 5.9 %collective-permute-start.13 = (f32[256,256]{1,0:T(8,128)S(1)}, f32[256,256]{1,0:T(8,128)S(1)}, u32[]{:S(2)}, u32[]{:S(2)}) collective-permute-start(f32[256,256]{1,0:T(8,128)S(1)} %fusion.16), channel_id=1, source_target_pairs={{0,63},{1,0},{2,1},{3,2},{4,3},{5,4},{6,5},{7,6},{8,7},{9,8},{10,9... | collective-permute-start | bytes 786440 | tf_op jit(solution)/shard_map/ppermute | solution.py:22
  98.4 0.4 fusion.34
  98.8 0.4 fusion.26
  99.2 1.1 collective-permute-done.12
  100.3 0.4 convolution_add_fusion.1
  100.7 1.4 collective-permute-done.13
  102.1 0.4 fusion.19
  102.5 0.7 copy-done.1
  103.2 3.2 %fusion.72 = f32[256,2048]{1,0:T(8,128)} fusion(f32[256,256]{1,0:T(8,128)S(1)} %fusion.19, f32[256,2048]{1,0:T(8,128)S(1)} %copy-done), kind=kOutput, calls=%fused_computation.102 | convolution fusion | flops 1610612736 | bytes 4456448 | tf_op jit(solution)/shard_map/dot_general | solution.py:93
  106.5 0.9 copy-done.2
  107.4 0.6 fusion.73
  108.0 0.1 reshape_reshape.3
  108.1 1.9 %collective-permute-start.16 = (f32[32,4,256]{2,1,0:T(4,128)S(1)}, f32[32,4,256]{2,1,0:T(4,128)S(1)}, u32[]{:S(2)}, u32[]{:S(2)}) collective-permute-start(f32[32,4,256]{2,1,0:T(4,128)S(1)} %select_bitcast_fusion), channel_id=1, source_target_pairs={{0,1},{1,0},{2,3},{3,2},{4,5},{5,4},{6,7},{7,6},{8,9},{9,8},{10,11... | collective-permute-start | bytes 393224 | tf_op jit(solution)/shard_map/ppermute | solution.py:63
  110.0 1.3 collective-permute-done.16
  111.4 1.9 %collective-permute-start.17 = (f32[16,4,256]{2,1,0:T(4,128)S(1)}, f32[16,4,256]{2,1,0:T(4,128)S(1)}, u32[]{:S(2)}, u32[]{:S(2)}) collective-permute-start(f32[16,4,256]{2,1,0:T(4,128)S(1)} %select_bitcast_fusion.1), channel_id=1, source_target_pairs={{0,2},{1,3},{2,0},{3,1},{4,6},{5,7},{6,4},{7,5},{8,10},{9,11},{10,... | collective-permute-start | bytes 196616 | tf_op jit(solution)/shard_map/ppermute | solution.py:63
  113.4 4.2 %collective-permute-done.17 = f32[16,4,256]{2,1,0:T(4,128)S(1)} collective-permute-done((f32[16,4,256]{2,1,0:T(4,128)S(1)}, f32[16,4,256]{2,1,0:T(4,128)S(1)}, u32[]{:S(2)}, u32[]{:S(2)}) %collective-permute-start.17) | collective-permute-done | bytes 65568 | tf_op jit(solution)/shard_map/ppermute | solution.py:63
  117.6 1.9 %collective-permute-start.18 = (f32[8,4,256]{2,1,0:T(4,128)S(1)}, f32[8,4,256]{2,1,0:T(4,128)S(1)}, u32[]{:S(2)}, u32[]{:S(2)}) collective-permute-start(f32[8,4,256]{2,1,0:T(4,128)S(1)} %select_bitcast_fusion.2), channel_id=1, source_target_pairs={{0,4},{1,5},{2,6},{3,7},{4,0},{5,1},{6,2},{7,3},{8,12},{9,13},{10,... | collective-permute-start | bytes 98312 | tf_op jit(solution)/shard_map/ppermute | solution.py:63
  119.6 4.8 %collective-permute-done.18 = f32[8,4,256]{2,1,0:T(4,128)S(1)} collective-permute-done((f32[8,4,256]{2,1,0:T(4,128)S(1)}, f32[8,4,256]{2,1,0:T(4,128)S(1)}, u32[]{:S(2)}, u32[]{:S(2)}) %collective-permute-start.18) | collective-permute-done | bytes 32800 | tf_op jit(solution)/shard_map/ppermute | solution.py:63
  124.4 13.8 %collective-permute-start.19 = (f32[4,4,256]{2,1,0:T(4,128)S(1)}, f32[4,4,256]{2,1,0:T(4,128)S(1)}, u32[]{:S(2)}, u32[]{:S(2)}) collective-permute-start(f32[4,4,256]{2,1,0:T(4,128)S(1)} %select_bitcast_fusion.3), channel_id=1, source_target_pairs={{0,8},{1,9},{2,10},{3,11},{4,12},{5,13},{6,14},{7,15},{8,0},{9,1},... | collective-permute-start | bytes 49160 | tf_op jit(solution)/shard_map/ppermute | solution.py:63
  138.2 1.7 %collective-permute-done.19 = f32[4,4,256]{2,1,0:T(4,128)S(1)} collective-permute-done((f32[4,4,256]{2,1,0:T(4,128)S(1)}, f32[4,4,256]{2,1,0:T(4,128)S(1)}, u32[]{:S(2)}, u32[]{:S(2)}) %collective-permute-start.19) | collective-permute-done | bytes 16416 | tf_op jit(solution)/shard_map/ppermute | solution.py:63
  139.9 1.9 %collective-permute-start.20 = (f32[2,4,256]{2,1,0:T(4,128)S(1)}, f32[2,4,256]{2,1,0:T(4,128)S(1)}, u32[]{:S(2)}, u32[]{:S(2)}) collective-permute-start(f32[2,4,256]{2,1,0:T(4,128)S(1)} %select_bitcast_fusion.4), channel_id=1, source_target_pairs={{0,16},{1,17},{2,18},{3,19},{4,20},{5,21},{6,22},{7,23},{8,24},{9,... | collective-permute-start | bytes 24584 | tf_op jit(solution)/shard_map/ppermute | solution.py:63
  141.8 3.6 %collective-permute-done.20 = f32[2,4,256]{2,1,0:T(4,128)S(1)} collective-permute-done((f32[2,4,256]{2,1,0:T(4,128)S(1)}, f32[2,4,256]{2,1,0:T(4,128)S(1)}, u32[]{:S(2)}, u32[]{:S(2)}) %collective-permute-start.20) | collective-permute-done | bytes 8224 | tf_op jit(solution)/shard_map/ppermute | solution.py:63
  145.5 5.1 %collective-permute-start.21 = (f32[1,4,256]{2,1,0:T(4,128)S(1)}, f32[1,4,256]{2,1,0:T(4,128)S(1)}, u32[]{:S(2)}, u32[]{:S(2)}) collective-permute-start(f32[1,4,256]{2,1,0:T(4,128)S(1)} %select_bitcast_fusion.5), channel_id=1, source_target_pairs={{0,32},{1,33},{2,34},{3,35},{4,36},{5,37},{6,38},{7,39},{8,40},{9,... | collective-permute-start | bytes 12296 | tf_op jit(solution)/shard_map/ppermute | solution.py:63
  150.5 1.9 %collective-permute-done.21 = f32[1,4,256]{2,1,0:T(4,128)S(1)} collective-permute-done((f32[1,4,256]{2,1,0:T(4,128)S(1)}, f32[1,4,256]{2,1,0:T(4,128)S(1)}, u32[]{:S(2)}, u32[]{:S(2)}) %collective-permute-start.21) | collective-permute-done | bytes 4128 | tf_op jit(solution)/shard_map/ppermute | solution.py:63
  152.5 0.6 fusion.65
  153.1 5.3 %reduce-scatter.2.cloned.1.call-done = f32[256,256]{1,0:T(8,128)} async-done(((f32[256,2048]{1,0:T(8,128)}), f32[256,256]{1,0:T(8,128)}) %reduce-scatter.2.cloned.1.call-update) | async-done | bytes 262160 | tf_op jit(solution)/shard_map/reduce_scatter | solution.py:96
  (29 shorter events, 0.3 us)
Async XLA Ops:
  7.2 96.0 %copy-start = (f32[256,2048]{1,0:T(8,128)S(1)}, f32[256,2048]{1,0:T(8,128)}, u32[]{:S(2)}) copy-start(f32[256,2048]{1,0:T(8,128)} %param.7) | copy-start | bytes 6291460
  7.2 151.2 %reduce-scatter.2.cloned.1.call-start = ((), (), s32[]{:S(2)}) async-start(), calls=%async_computation.1 | async-start | bytes 2359296 | tf_op jit(solution)/shard_map/reduce_scatter | solution.py:96
  7.2 32.9 %collective-permute-start = (f32[256,256]{1,0:T(8,128)}, f32[256,256]{1,0:T(8,128)}, u32[]{:S(2)}, u32[]{:S(2)}) collective-permute-start(f32[256,256]{1,0:T(8,128)} %param.4), channel_id=1, source_target_pairs={{0,1},{1,2},{2,3},{3,4},{4,5},{5,6},{6,7},{7,8},{8,9},{9,10},{10,1... | collective-permute-start | bytes 786440 | tf_op jit(solution)/shard_map/ppermute | solution.py:22
  9.3 28.1 %collective-permute-start.3 = (f32[256,256]{1,0:T(8,128)}, f32[256,256]{1,0:T(8,128)}, u32[]{:S(2)}, u32[]{:S(2)}) collective-permute-start(f32[256,256]{1,0:T(8,128)} %param.4), channel_id=1, source_target_pairs={{0,62},{1,63},{2,0},{3,1},{4,2},{5,3},{6,4},{7,5},{8,6},{9,7},{10,... | collective-permute-start | bytes 786440 | tf_op jit(solution)/shard_map/ppermute | solution.py:22
  20.5 18.3 %collective-permute-start.2 = (f32[256,256]{1,0:T(8,128)}, f32[256,256]{1,0:T(8,128)}, u32[]{:S(2)}, u32[]{:S(2)}) collective-permute-start(f32[256,256]{1,0:T(8,128)} %param.4), channel_id=1, source_target_pairs={{0,2},{1,3},{2,4},{3,5},{4,6},{5,7},{6,8},{7,9},{8,10},{9,11},{10,... | collective-permute-start | bytes 786440 | tf_op jit(solution)/shard_map/ppermute | solution.py:22
  22.4 19.0 %collective-permute-start.1 = (f32[256,256]{1,0:T(8,128)}, f32[256,256]{1,0:T(8,128)}, u32[]{:S(2)}, u32[]{:S(2)}) collective-permute-start(f32[256,256]{1,0:T(8,128)} %param.4), channel_id=1, source_target_pairs={{0,63},{1,0},{2,1},{3,2},{4,3},{5,4},{6,5},{7,6},{8,7},{9,8},{10,9... | collective-permute-start | bytes 786440 | tf_op jit(solution)/shard_map/ppermute | solution.py:22
  37.4 4.1 %copy-start.3 = (f32[256,256]{1,0:T(8,128)S(1)}, f32[256,256]{1,0:T(8,128)}, u32[]{:S(2)}) copy-start(f32[256,256]{1,0:T(8,128)} %param.4) | copy-start | bytes 786436
  42.9 13.7 %collective-permute-start.6 = (f32[256,256]{1,0:T(8,128)S(1)}, f32[256,256]{1,0:T(8,128)S(1)}, u32[]{:S(2)}, u32[]{:S(2)}) collective-permute-start(f32[256,256]{1,0:T(8,128)S(1)} %get-tuple-element.2), channel_id=1, source_target_pairs={{0,2},{1,3},{2,4},{3,5},{4,6},{5,7},{6,8},{7,9},{8,10},{9,11},{10,... | collective-permute-start | bytes 786440 | tf_op jit(solution)/shard_map/ppermute | solution.py:22
  44.8 14.2 %collective-permute-start.4 = (f32[256,256]{1,0:T(8,128)S(1)}, f32[256,256]{1,0:T(8,128)S(1)}, u32[]{:S(2)}, u32[]{:S(2)}) collective-permute-start(f32[256,256]{1,0:T(8,128)S(1)} %get-tuple-element.2), channel_id=1, source_target_pairs={{0,1},{1,2},{2,3},{3,4},{4,5},{5,6},{6,7},{7,8},{8,9},{9,10},{10,1... | collective-permute-start | bytes 786440 | tf_op jit(solution)/shard_map/ppermute | solution.py:22
  46.7 11.9 %collective-permute-start.7 = (f32[256,256]{1,0:T(8,128)S(1)}, f32[256,256]{1,0:T(8,128)S(1)}, u32[]{:S(2)}, u32[]{:S(2)}) collective-permute-start(f32[256,256]{1,0:T(8,128)S(1)} %get-tuple-element.2), channel_id=1, source_target_pairs={{0,62},{1,63},{2,0},{3,1},{4,2},{5,3},{6,4},{7,5},{8,6},{9,7},{10,... | collective-permute-start | bytes 786440 | tf_op jit(solution)/shard_map/ppermute | solution.py:22
  52.8 8.6 %collective-permute-start.5 = (f32[256,256]{1,0:T(8,128)S(1)}, f32[256,256]{1,0:T(8,128)S(1)}, u32[]{:S(2)}, u32[]{:S(2)}) collective-permute-start(f32[256,256]{1,0:T(8,128)S(1)} %get-tuple-element.2), channel_id=1, source_target_pairs={{0,63},{1,0},{2,1},{3,2},{4,3},{5,4},{6,5},{7,6},{8,7},{9,8},{10,9... | collective-permute-start | bytes 786440 | tf_op jit(solution)/shard_map/ppermute | solution.py:22
  61.8 16.0 %collective-permute-start.10 = (f32[256,256]{1,0:T(8,128)S(1)}, f32[256,256]{1,0:T(8,128)S(1)}, u32[]{:S(2)}, u32[]{:S(2)}) collective-permute-start(f32[256,256]{1,0:T(8,128)S(1)} %fusion.13), channel_id=1, source_target_pairs={{0,2},{1,3},{2,4},{3,5},{4,6},{5,7},{6,8},{7,9},{8,10},{9,11},{10,... | collective-permute-start | bytes 786440 | tf_op jit(solution)/shard_map/ppermute | solution.py:22
  63.7 14.5 %collective-permute-start.11 = (f32[256,256]{1,0:T(8,128)S(1)}, f32[256,256]{1,0:T(8,128)S(1)}, u32[]{:S(2)}, u32[]{:S(2)}) collective-permute-start(f32[256,256]{1,0:T(8,128)S(1)} %fusion.13), channel_id=1, source_target_pairs={{0,62},{1,63},{2,0},{3,1},{4,2},{5,3},{6,4},{7,5},{8,6},{9,7},{10,... | collective-permute-start | bytes 786440 | tf_op jit(solution)/shard_map/ppermute | solution.py:22
  70.2 9.8 %collective-permute-start.8 = (f32[256,256]{1,0:T(8,128)S(1)}, f32[256,256]{1,0:T(8,128)S(1)}, u32[]{:S(2)}, u32[]{:S(2)}) collective-permute-start(f32[256,256]{1,0:T(8,128)S(1)} %fusion.13), channel_id=1, source_target_pairs={{0,1},{1,2},{2,3},{3,4},{4,5},{5,6},{6,7},{7,8},{8,9},{9,10},{10,1... | collective-permute-start | bytes 786440 | tf_op jit(solution)/shard_map/ppermute | solution.py:22
  72.1 9.6 %collective-permute-start.9 = (f32[256,256]{1,0:T(8,128)S(1)}, f32[256,256]{1,0:T(8,128)S(1)}, u32[]{:S(2)}, u32[]{:S(2)}) collective-permute-start(f32[256,256]{1,0:T(8,128)S(1)} %fusion.13), channel_id=1, source_target_pairs={{0,63},{1,0},{2,1},{3,2},{4,3},{5,4},{6,5},{7,6},{8,7},{9,8},{10,9... | collective-permute-start | bytes 786440 | tf_op jit(solution)/shard_map/ppermute | solution.py:22
  82.2 16.2 %collective-permute-start.14 = (f32[256,256]{1,0:T(8,128)S(1)}, f32[256,256]{1,0:T(8,128)S(1)}, u32[]{:S(2)}, u32[]{:S(2)}) collective-permute-start(f32[256,256]{1,0:T(8,128)S(1)} %fusion.16), channel_id=1, source_target_pairs={{0,2},{1,3},{2,4},{3,5},{4,6},{5,7},{6,8},{7,9},{8,10},{9,11},{10,... | collective-permute-start | bytes 786440 | tf_op jit(solution)/shard_map/ppermute | solution.py:22
  84.1 14.7 %collective-permute-start.15 = (f32[256,256]{1,0:T(8,128)S(1)}, f32[256,256]{1,0:T(8,128)S(1)}, u32[]{:S(2)}, u32[]{:S(2)}) collective-permute-start(f32[256,256]{1,0:T(8,128)S(1)} %fusion.16), channel_id=1, source_target_pairs={{0,62},{1,63},{2,0},{3,1},{4,2},{5,3},{6,4},{7,5},{8,6},{9,7},{10,... | collective-permute-start | bytes 786440 | tf_op jit(solution)/shard_map/ppermute | solution.py:22
  90.5 9.8 %collective-permute-start.12 = (f32[256,256]{1,0:T(8,128)S(1)}, f32[256,256]{1,0:T(8,128)S(1)}, u32[]{:S(2)}, u32[]{:S(2)}) collective-permute-start(f32[256,256]{1,0:T(8,128)S(1)} %fusion.16), channel_id=1, source_target_pairs={{0,1},{1,2},{2,3},{3,4},{4,5},{5,6},{6,7},{7,8},{8,9},{9,10},{10,1... | collective-permute-start | bytes 786440 | tf_op jit(solution)/shard_map/ppermute | solution.py:22
  92.4 9.6 %collective-permute-start.13 = (f32[256,256]{1,0:T(8,128)S(1)}, f32[256,256]{1,0:T(8,128)S(1)}, u32[]{:S(2)}, u32[]{:S(2)}) collective-permute-start(f32[256,256]{1,0:T(8,128)S(1)} %fusion.16), channel_id=1, source_target_pairs={{0,63},{1,0},{2,1},{3,2},{4,3},{5,4},{6,5},{7,6},{8,7},{9,8},{10,9... | collective-permute-start | bytes 786440 | tf_op jit(solution)/shard_map/ppermute | solution.py:22
  102.5 0.7 copy-start.1
  106.4 0.9 copy-start.2
  108.1 3.2 %collective-permute-start.16 = (f32[32,4,256]{2,1,0:T(4,128)S(1)}, f32[32,4,256]{2,1,0:T(4,128)S(1)}, u32[]{:S(2)}, u32[]{:S(2)}) collective-permute-start(f32[32,4,256]{2,1,0:T(4,128)S(1)} %select_bitcast_fusion), channel_id=1, source_target_pairs={{0,1},{1,0},{2,3},{3,2},{4,5},{5,4},{6,7},{7,6},{8,9},{9,8},{10,11... | collective-permute-start | bytes 393224 | tf_op jit(solution)/shard_map/ppermute | solution.py:63
  111.4 6.2 %collective-permute-start.17 = (f32[16,4,256]{2,1,0:T(4,128)S(1)}, f32[16,4,256]{2,1,0:T(4,128)S(1)}, u32[]{:S(2)}, u32[]{:S(2)}) collective-permute-start(f32[16,4,256]{2,1,0:T(4,128)S(1)} %select_bitcast_fusion.1), channel_id=1, source_target_pairs={{0,2},{1,3},{2,0},{3,1},{4,6},{5,7},{6,4},{7,5},{8,10},{9,11},{10,... | collective-permute-start | bytes 196616 | tf_op jit(solution)/shard_map/ppermute | solution.py:63
  117.6 6.7 %collective-permute-start.18 = (f32[8,4,256]{2,1,0:T(4,128)S(1)}, f32[8,4,256]{2,1,0:T(4,128)S(1)}, u32[]{:S(2)}, u32[]{:S(2)}) collective-permute-start(f32[8,4,256]{2,1,0:T(4,128)S(1)} %select_bitcast_fusion.2), channel_id=1, source_target_pairs={{0,4},{1,5},{2,6},{3,7},{4,0},{5,1},{6,2},{7,3},{8,12},{9,13},{10,... | collective-permute-start | bytes 98312 | tf_op jit(solution)/shard_map/ppermute | solution.py:63
  124.4 15.5 %collective-permute-start.19 = (f32[4,4,256]{2,1,0:T(4,128)S(1)}, f32[4,4,256]{2,1,0:T(4,128)S(1)}, u32[]{:S(2)}, u32[]{:S(2)}) collective-permute-start(f32[4,4,256]{2,1,0:T(4,128)S(1)} %select_bitcast_fusion.3), channel_id=1, source_target_pairs={{0,8},{1,9},{2,10},{3,11},{4,12},{5,13},{6,14},{7,15},{8,0},{9,1},... | collective-permute-start | bytes 49160 | tf_op jit(solution)/shard_map/ppermute | solution.py:63
  139.9 5.5 %collective-permute-start.20 = (f32[2,4,256]{2,1,0:T(4,128)S(1)}, f32[2,4,256]{2,1,0:T(4,128)S(1)}, u32[]{:S(2)}, u32[]{:S(2)}) collective-permute-start(f32[2,4,256]{2,1,0:T(4,128)S(1)} %select_bitcast_fusion.4), channel_id=1, source_target_pairs={{0,16},{1,17},{2,18},{3,19},{4,20},{5,21},{6,22},{7,23},{8,24},{9,... | collective-permute-start | bytes 24584 | tf_op jit(solution)/shard_map/ppermute | solution.py:63
  145.5 7.0 %collective-permute-start.21 = (f32[1,4,256]{2,1,0:T(4,128)S(1)}, f32[1,4,256]{2,1,0:T(4,128)S(1)}, u32[]{:S(2)}, u32[]{:S(2)}) collective-permute-start(f32[1,4,256]{2,1,0:T(4,128)S(1)} %select_bitcast_fusion.5), channel_id=1, source_target_pairs={{0,32},{1,33},{2,34},{3,35},{4,36},{5,37},{6,38},{7,39},{8,40},{9,... | collective-permute-start | bytes 12296 | tf_op jit(solution)/shard_map/ppermute | solution.py:63
Sparse Core Ops, SparseCore 0:
  106.6 51.7 reduce-scatter.1

commit v2 on v1

--- a/solution.py
+++ b/solution.py
@@ -89,11 +89,20 @@
         precision=HI,
         preferred_element_type=jnp.float32,
     )
-    correlation = butterfly_scatter(gram_term, "wide") / total_rows
+    pieces = gram_term.reshape(devcount, -1, gram_term.shape[1])
+    gathered = lax.all_to_all(pieces, "wide", 0, 0, tiled=True)
+    correlation = jnp.sum(gathered, axis=0) / total_rows
     rot_term = jnp.dot(
         current, rotation, precision=HI, preferred_element_type=jnp.float32
     )
-    rotated = lax.psum_scatter(rot_term, "grp", scatter_dimension=1, tiled=True)
+    half = rot_term.shape[0] // 2
+    rotated = jnp.concatenate(
+        [
+            lax.psum_scatter(rot_term[:half], "grp", scatter_dimension=1, tiled=True),
+            lax.psum_scatter(rot_term[half:], "grp", scatter_dimension=1, tiled=True),
+        ],
+        axis=0,
+    )
     return (rotated, correlation)
 
 

time: 166 us -> 208 us (1.25)
  waiting for transfers between devices: 31.7 us -> 70.6 us
  blocking collectives: 0 us -> 28.3 us
  starting transfers between devices: 91.4 us -> 64.9 us
    reduce_scatter x1 -> x2, waiting for transfers between devices: 5.28 us -> 61 us  [the longest x1 42.9 us: local(): lax.psum_scatter(rot_term[half:], 'grp', scatter_dimension=1, tiled=True)]
    all_to_all x0 -> x1, blocking collectives: none -> 28.3 us  [local(): gathered = lax.all_to_all(pieces, 'wide', 0, 0, tiled=True)]
    ppermute x6 -> x0, starting transfers between devices: 26.5 us -> none  [butterfly_scatter(): buf = keep + lax.ppermute(send, axis, pairs)]
    ppermute x6 -> x0, waiting for transfers between devices: 17.5 us -> none  [butterfly_scatter(): buf = keep + lax.ppermute(send, axis, pairs)]
  transfers between devices with their start and end apart: 23 -> 18, of which waited for: 13 -> 8; matrix products, arithmetic and copies ran while one was open for 12% -> 10% of each run, Pallas kernels for 0% -> 0%
where the time goes in v2:
time: 208 us; the launch traced here: 207 us
  waiting for transfers between devices  70.6 us (34%)
  starting transfers between devices  64.9 us (31%)
  blocking collectives  28.3 us (14%)
  matrix products  20.8 us (10%)
  between operations  14.5 us (7%)
  local copies, waits for them, and re-layouts  4.68 us (2%)
  other arithmetic  3.08 us (1%)
    ppermute x16, starting transfers between devices, passed_along(): return lax.ppermute(value, axis, pairs)  64.8 us
    reduce_scatter x1, waiting for transfers between devices, local(): lax.psum_scatter(rot_term[half:], 'grp', scatter_dimension=1, tiled=True)  42.9 us
    all_to_all x1, blocking collectives, local(): gathered = lax.all_to_all(pieces, 'wide', 0, 0, tiled=True)  28.3 us
    reduce_scatter x1, waiting for transfers between devices, local(): lax.psum_scatter(rot_term[:half], 'grp', scatter_dimension=1, tiled=True)  18.1 us
    dot_general x20, matrix products, apply_ham(): jnp.dot(hdense[:, idx * rows:(idx + 1) * rows], pieces[idx], precision=HI...  12.5 us
    ppermute x16, waiting for transfers between devices, passed_along(): return lax.ppermute(value, axis, pairs)  8.9 us
    dot_general x1, matrix products, dense_hamiltonian(): hd = jnp.einsum('asp,asij->aipj', onehot, hblocks, precision=HI)  5.75 us
  transfers between devices with their start and end apart: 18, of which 8 were waited for; matrix products, arithmetic and copies ran while one was open for 10% of the time, Pallas kernels for 0%

profile of v2, /device:TPU:6, one launch (start us, length us, event | category | flops | bytes accessed | tf_op | source)
XLA Modules:
  0.0 206.8 jit_solution(12748139480240086695)
XLA Ops:
  7.2 0.0 copy-start
  7.2 0.0 reduce-scatter.3.cloned.1.call-start
  7.2 2.1 collective-permute-start
  9.3 11.2 %collective-permute-start.3 = (f32[256,256]{1,0:T(8,128)}, f32[256,256]{1,0:T(8,128)}, u32[]{:S(2)}, u32[]{:S(2)}) collective-permute-start(f32[256,256]{1,0:T(8,128)} %param.4), channel_id=1, source_target_pairs={{0,62},{1,63},{2,0},{3,1},{4,2},{5,3},{6,4},{7,5},{8,6},{9,7},{10,... | collective-permute-start | bytes 786440 | tf_op jit(solution)/shard_map/ppermute | solution.py:22
  20.5 1.9 collective-permute-start.2
  22.4 4.9 %collective-permute-start.1 = (f32[256,256]{1,0:T(8,128)}, f32[256,256]{1,0:T(8,128)}, u32[]{:S(2)}, u32[]{:S(2)}) collective-permute-start(f32[256,256]{1,0:T(8,128)} %param.4), channel_id=1, source_target_pairs={{0,63},{1,0},{2,1},{3,2},{4,3},{5,4},{6,5},{7,6},{8,7},{9,8},{10,9... | collective-permute-start | bytes 786440 | tf_op jit(solution)/shard_map/ppermute | solution.py:22
  27.4 0.7 fusion.59
  28.1 5.8 %fusion.2 = f32[4,64,20,64]{3,2,1,0:T(8,128)} fusion(f32[4,16,64,64]{3,2,1,0:T(8,128)} %param.5, s32[4,16]{1,0:T(4,128)S(1)} %fusion.59), kind=kOutput, calls=%fused_computation.2 | convolution fusion | flops 62915840 | bytes 2359552 | tf_op jit(solution)/shard_map/asp,asij->aipj/dot_general | solution.py:29
  33.8 2.2 %reshape.14 = f32[256,1280]{1,0:T(8,128)S(1)} reshape(f32[4,64,20,64]{3,2,1,0:T(8,128)} %fusion.2) | data formatting | bytes 2621440 | tf_op jit(solution)/shard_map/reshape | solution.py:30
  36.1 1.3 fusion.48
  37.4 0.0 copy-start.3
  37.4 1.4 fusion.24
  38.8 1.3 fusion.32
  40.2 1.3 convolution_add_fusion.7
  41.5 1.4 broadcast_multiply_fusion
  42.9 1.9 collective-permute-start.6
  44.8 1.9 collective-permute-start.4
  46.7 6.0 %collective-permute-start.7 = (f32[256,256]{1,0:T(8,128)S(1)}, f32[256,256]{1,0:T(8,128)S(1)}, u32[]{:S(2)}, u32[]{:S(2)}) collective-permute-start(f32[256,256]{1,0:T(8,128)S(1)} %get-tuple-element.4), channel_id=1, source_target_pairs={{0,62},{1,63},{2,0},{3,1},{4,2},{5,3},{6,4},{7,5},{8,6},{9,7},{10,... | collective-permute-start | bytes 786440 | tf_op jit(solution)/shard_map/ppermute | solution.py:22
  52.8 3.4 %collective-permute-start.5 = (f32[256,256]{1,0:T(8,128)S(1)}, f32[256,256]{1,0:T(8,128)S(1)}, u32[]{:S(2)}, u32[]{:S(2)}) collective-permute-start(f32[256,256]{1,0:T(8,128)S(1)} %get-tuple-element.4), channel_id=1, source_target_pairs={{0,63},{1,0},{2,1},{3,2},{4,3},{5,4},{6,5},{7,6},{8,7},{9,8},{10,9... | collective-permute-start | bytes 786440 | tf_op jit(solution)/shard_map/ppermute | solution.py:22
  56.1 0.4 fusion.46
  56.6 0.4 fusion.30
  56.9 1.7 collective-permute-done.7
  58.6 0.4 fusion.22
  59.0 0.4 convolution_add_fusion.5
  59.4 2.0 collective-permute-done.5
  61.4 0.4 fusion.13
  61.8 1.9 collective-permute-start.10
  63.8 6.0 %collective-permute-start.11 = (f32[256,256]{1,0:T(8,128)S(1)}, f32[256,256]{1,0:T(8,128)S(1)}, u32[]{:S(2)}, u32[]{:S(2)}) collective-permute-start(f32[256,256]{1,0:T(8,128)S(1)} %fusion.13), channel_id=1, source_target_pairs={{0,62},{1,63},{2,0},{3,1},{4,2},{5,3},{6,4},{7,5},{8,6},{9,7},{10,... | collective-permute-start | bytes 786440 | tf_op jit(solution)/shard_map/ppermute | solution.py:22
  69.8 0.4 fusion.44
  70.2 1.9 collective-permute-start.8
  72.1 5.8 %collective-permute-start.9 = (f32[256,256]{1,0:T(8,128)S(1)}, f32[256,256]{1,0:T(8,128)S(1)}, u32[]{:S(2)}, u32[]{:S(2)}) collective-permute-start(f32[256,256]{1,0:T(8,128)S(1)} %fusion.13), channel_id=1, source_target_pairs={{0,63},{1,0},{2,1},{3,2},{4,3},{5,4},{6,5},{7,6},{8,7},{9,8},{10,9... | collective-permute-start | bytes 786440 | tf_op jit(solution)/shard_map/ppermute | solution.py:22
  77.9 0.4 fusion.28
  78.3 0.4 fusion.20
  78.7 1.3 collective-permute-done.8
  80.0 0.4 convolution_add_fusion.3
  80.4 1.4 collective-permute-done.9
  81.7 0.4 fusion.16
  82.2 1.9 collective-permute-start.14
  84.1 6.0 %collective-permute-start.15 = (f32[256,256]{1,0:T(8,128)S(1)}, f32[256,256]{1,0:T(8,128)S(1)}, u32[]{:S(2)}, u32[]{:S(2)}) collective-permute-start(f32[256,256]{1,0:T(8,128)S(1)} %fusion.16), channel_id=1, source_target_pairs={{0,62},{1,63},{2,0},{3,1},{4,2},{5,3},{6,4},{7,5},{8,6},{9,7},{10,... | collective-permute-start | bytes 786440 | tf_op jit(solution)/shard_map/ppermute | solution.py:22
  90.1 0.4 fusion.50
  90.5 1.9 collective-permute-start.12
  92.4 5.9 %collective-permute-start.13 = (f32[256,256]{1,0:T(8,128)S(1)}, f32[256,256]{1,0:T(8,128)S(1)}, u32[]{:S(2)}, u32[]{:S(2)}) collective-permute-start(f32[256,256]{1,0:T(8,128)S(1)} %fusion.16), channel_id=1, source_target_pairs={{0,63},{1,0},{2,1},{3,2},{4,3},{5,4},{6,5},{7,6},{8,7},{9,8},{10,9... | collective-permute-start | bytes 786440 | tf_op jit(solution)/shard_map/ppermute | solution.py:22
  98.4 0.4 fusion.34
  98.8 0.4 fusion.26
  99.2 1.1 collective-permute-done.12
  100.3 0.4 convolution_add_fusion.1
  100.7 1.4 collective-permute-done.13
  102.1 0.4 fusion.19
  102.5 0.0 copy-start.1
  102.5 0.7 copy-done.1
  103.2 1.9 fusion.62
  105.1 1.5 fusion.61
  106.6 0.0 reduce-scatter.3.cloned.1.call-update
  106.7 0.0 reduce-scatter.5.cloned.1.call-start
  106.7 0.7 reduce-scatter.5.cloned.1.call-update
  107.4 0.2 copy-done.2
  107.6 0.6 fusion.63
  108.2 0.1 reshape.12
  108.3 28.3 %all_to_all.5 = f32[64,4,256]{2,1,0:T(4,128)S(1)} all-to-all(f32[64,4,256]{2,1,0:T(4,128)S(1)} %reshape.12), channel_id=1, replica_groups=mesh['grp'=8,'wide'=64] {'wide'}, dimensions={0} | all-to-all | bytes 524288 | tf_op jit(solution)/shard_map/all_to_all | solution.py:93
  136.6 0.1 reduce_sum.9
  136.6 0.6 broadcast_multiply_fusion.1
  137.2 18.1 %reduce-scatter.3.cloned.1.call-done = f32[128,256]{1,0:T(8,128)} async-done(((f32[128,2048]{1,0:T(8,128)}), f32[128,256]{1,0:T(8,128)}) %reduce-scatter.3.cloned.1.call-update) | async-done | bytes 131088 | tf_op jit(solution)/shard_map/reduce_scatter | solution.py:101
  155.3 42.9 %reduce-scatter.5.cloned.1.call-done = f32[128,256]{1,0:T(8,128)} async-done(((f32[128,2048]{1,0:T(8,128)}), f32[128,256]{1,0:T(8,128)}) %reduce-scatter.5.cloned.1.call-update) | async-done | bytes 131088 | tf_op jit(solution)/shard_map/reduce_scatter | solution.py:102
  198.3 1.7 pad_maximum_fusion
  (13 shorter events, 0.0 us)
Async XLA Ops:
  7.2 96.0 %copy-start = (f32[256,2048]{1,0:T(8,128)S(1)}, f32[256,2048]{1,0:T(8,128)}, u32[]{:S(2)}) copy-start(f32[256,2048]{1,0:T(8,128)} %param.7) | copy-start | bytes 6291460
  7.2 148.1 %reduce-scatter.3.cloned.1.call-start = ((), (), s32[]{:S(2)}) async-start(), calls=%async_computation.3 | async-start | bytes 1179648 | tf_op jit(solution)/shard_map/reduce_scatter | solution.py:101
  7.2 32.9 %collective-permute-start = (f32[256,256]{1,0:T(8,128)}, f32[256,256]{1,0:T(8,128)}, u32[]{:S(2)}, u32[]{:S(2)}) collective-permute-start(f32[256,256]{1,0:T(8,128)} %param.4), channel_id=1, source_target_pairs={{0,1},{1,2},{2,3},{3,4},{4,5},{5,6},{6,7},{7,8},{8,9},{9,10},{10,1... | collective-permute-start | bytes 786440 | tf_op jit(solution)/shard_map/ppermute | solution.py:22
  9.3 28.1 %collective-permute-start.3 = (f32[256,256]{1,0:T(8,128)}, f32[256,256]{1,0:T(8,128)}, u32[]{:S(2)}, u32[]{:S(2)}) collective-permute-start(f32[256,256]{1,0:T(8,128)} %param.4), channel_id=1, source_target_pairs={{0,62},{1,63},{2,0},{3,1},{4,2},{5,3},{6,4},{7,5},{8,6},{9,7},{10,... | collective-permute-start | bytes 786440 | tf_op jit(solution)/shard_map/ppermute | solution.py:22
  20.5 18.3 %collective-permute-start.2 = (f32[256,256]{1,0:T(8,128)}, f32[256,256]{1,0:T(8,128)}, u32[]{:S(2)}, u32[]{:S(2)}) collective-permute-start(f32[256,256]{1,0:T(8,128)} %param.4), channel_id=1, source_target_pairs={{0,2},{1,3},{2,4},{3,5},{4,6},{5,7},{6,8},{7,9},{8,10},{9,11},{10,... | collective-permute-start | bytes 786440 | tf_op jit(solution)/shard_map/ppermute | solution.py:22
  22.4 19.1 %collective-permute-start.1 = (f32[256,256]{1,0:T(8,128)}, f32[256,256]{1,0:T(8,128)}, u32[]{:S(2)}, u32[]{:S(2)}) collective-permute-start(f32[256,256]{1,0:T(8,128)} %param.4), channel_id=1, source_target_pairs={{0,63},{1,0},{2,1},{3,2},{4,3},{5,4},{6,5},{7,6},{8,7},{9,8},{10,9... | collective-permute-start | bytes 786440 | tf_op jit(solution)/shard_map/ppermute | solution.py:22
  37.4 4.1 %copy-start.3 = (f32[256,256]{1,0:T(8,128)S(1)}, f32[256,256]{1,0:T(8,128)}, u32[]{:S(2)}) copy-start(f32[256,256]{1,0:T(8,128)} %param.4) | copy-start | bytes 786436
  42.9 13.7 %collective-permute-start.6 = (f32[256,256]{1,0:T(8,128)S(1)}, f32[256,256]{1,0:T(8,128)S(1)}, u32[]{:S(2)}, u32[]{:S(2)}) collective-permute-start(f32[256,256]{1,0:T(8,128)S(1)} %get-tuple-element.4), channel_id=1, source_target_pairs={{0,2},{1,3},{2,4},{3,5},{4,6},{5,7},{6,8},{7,9},{8,10},{9,11},{10,... | collective-permute-start | bytes 786440 | tf_op jit(solution)/shard_map/ppermute | solution.py:22
  44.8 14.2 %collective-permute-start.4 = (f32[256,256]{1,0:T(8,128)S(1)}, f32[256,256]{1,0:T(8,128)S(1)}, u32[]{:S(2)}, u32[]{:S(2)}) collective-permute-start(f32[256,256]{1,0:T(8,128)S(1)} %get-tuple-element.4), channel_id=1, source_target_pairs={{0,1},{1,2},{2,3},{3,4},{4,5},{5,6},{6,7},{7,8},{8,9},{9,10},{10,1... | collective-permute-start | bytes 786440 | tf_op jit(solution)/shard_map/ppermute | solution.py:22
  46.7 11.9 %collective-permute-start.7 = (f32[256,256]{1,0:T(8,128)S(1)}, f32[256,256]{1,0:T(8,128)S(1)}, u32[]{:S(2)}, u32[]{:S(2)}) collective-permute-start(f32[256,256]{1,0:T(8,128)S(1)} %get-tuple-element.4), channel_id=1, source_target_pairs={{0,62},{1,63},{2,0},{3,1},{4,2},{5,3},{6,4},{7,5},{8,6},{9,7},{10,... | collective-permute-start | bytes 786440 | tf_op jit(solution)/shard_map/ppermute | solution.py:22
  52.8 8.6 %collective-permute-start.5 = (f32[256,256]{1,0:T(8,128)S(1)}, f32[256,256]{1,0:T(8,128)S(1)}, u32[]{:S(2)}, u32[]{:S(2)}) collective-permute-start(f32[256,256]{1,0:T(8,128)S(1)} %get-tuple-element.4), channel_id=1, source_target_pairs={{0,63},{1,0},{2,1},{3,2},{4,3},{5,4},{6,5},{7,6},{8,7},{9,8},{10,9... | collective-permute-start | bytes 786440 | tf_op jit(solution)/shard_map/ppermute | solution.py:22
  61.8 16.0 %collective-permute-start.10 = (f32[256,256]{1,0:T(8,128)S(1)}, f32[256,256]{1,0:T(8,128)S(1)}, u32[]{:S(2)}, u32[]{:S(2)}) collective-permute-start(f32[256,256]{1,0:T(8,128)S(1)} %fusion.13), channel_id=1, source_target_pairs={{0,2},{1,3},{2,4},{3,5},{4,6},{5,7},{6,8},{7,9},{8,10},{9,11},{10,... | collective-permute-start | bytes 786440 | tf_op jit(solution)/shard_map/ppermute | solution.py:22
  63.8 14.5 %collective-permute-start.11 = (f32[256,256]{1,0:T(8,128)S(1)}, f32[256,256]{1,0:T(8,128)S(1)}, u32[]{:S(2)}, u32[]{:S(2)}) collective-permute-start(f32[256,256]{1,0:T(8,128)S(1)} %fusion.13), channel_id=1, source_target_pairs={{0,62},{1,63},{2,0},{3,1},{4,2},{5,3},{6,4},{7,5},{8,6},{9,7},{10,... | collective-permute-start | bytes 786440 | tf_op jit(solution)/shard_map/ppermute | solution.py:22
  70.2 9.8 %collective-permute-start.8 = (f32[256,256]{1,0:T(8,128)S(1)}, f32[256,256]{1,0:T(8,128)S(1)}, u32[]{:S(2)}, u32[]{:S(2)}) collective-permute-start(f32[256,256]{1,0:T(8,128)S(1)} %fusion.13), channel_id=1, source_target_pairs={{0,1},{1,2},{2,3},{3,4},{4,5},{5,6},{6,7},{7,8},{8,9},{9,10},{10,1... | collective-permute-start | bytes 786440 | tf_op jit(solution)/shard_map/ppermute | solution.py:22
  72.1 9.6 %collective-permute-start.9 = (f32[256,256]{1,0:T(8,128)S(1)}, f32[256,256]{1,0:T(8,128)S(1)}, u32[]{:S(2)}, u32[]{:S(2)}) collective-permute-start(f32[256,256]{1,0:T(8,128)S(1)} %fusion.13), channel_id=1, source_target_pairs={{0,63},{1,0},{2,1},{3,2},{4,3},{5,4},{6,5},{7,6},{8,7},{9,8},{10,9... | collective-permute-start | bytes 786440 | tf_op jit(solution)/shard_map/ppermute | solution.py:22
  82.2 16.2 %collective-permute-start.14 = (f32[256,256]{1,0:T(8,128)S(1)}, f32[256,256]{1,0:T(8,128)S(1)}, u32[]{:S(2)}, u32[]{:S(2)}) collective-permute-start(f32[256,256]{1,0:T(8,128)S(1)} %fusion.16), channel_id=1, source_target_pairs={{0,2},{1,3},{2,4},{3,5},{4,6},{5,7},{6,8},{7,9},{8,10},{9,11},{10,... | collective-permute-start | bytes 786440 | tf_op jit(solution)/shard_map/ppermute | solution.py:22
  84.1 14.7 %collective-permute-start.15 = (f32[256,256]{1,0:T(8,128)S(1)}, f32[256,256]{1,0:T(8,128)S(1)}, u32[]{:S(2)}, u32[]{:S(2)}) collective-permute-start(f32[256,256]{1,0:T(8,128)S(1)} %fusion.16), channel_id=1, source_target_pairs={{0,62},{1,63},{2,0},{3,1},{4,2},{5,3},{6,4},{7,5},{8,6},{9,7},{10,... | collective-permute-start | bytes 786440 | tf_op jit(solution)/shard_map/ppermute | solution.py:22
  90.5 9.8 %collective-permute-start.12 = (f32[256,256]{1,0:T(8,128)S(1)}, f32[256,256]{1,0:T(8,128)S(1)}, u32[]{:S(2)}, u32[]{:S(2)}) collective-permute-start(f32[256,256]{1,0:T(8,128)S(1)} %fusion.16), channel_id=1, source_target_pairs={{0,1},{1,2},{2,3},{3,4},{4,5},{5,6},{6,7},{7,8},{8,9},{9,10},{10,1... | collective-permute-start | bytes 786440 | tf_op jit(solution)/shard_map/ppermute | solution.py:22
  92.4 9.6 %collective-permute-start.13 = (f32[256,256]{1,0:T(8,128)S(1)}, f32[256,256]{1,0:T(8,128)S(1)}, u32[]{:S(2)}, u32[]{:S(2)}) collective-permute-start(f32[256,256]{1,0:T(8,128)S(1)} %fusion.16), channel_id=1, source_target_pairs={{0,63},{1,0},{2,1},{3,2},{4,3},{5,4},{6,5},{7,6},{8,7},{9,8},{10,9... | collective-permute-start | bytes 786440 | tf_op jit(solution)/shard_map/ppermute | solution.py:22
  102.5 0.7 copy-start.1
  106.6 0.9 copy-start.2
  106.7 91.6 %reduce-scatter.5.cloned.1.call-start = ((), (), s32[]{:S(2)}) async-start(), calls=%async_computation.4 | async-start | bytes 1179648 | tf_op jit(solution)/shard_map/reduce_scatter | solution.py:102
Sparse Core Ops, SparseCore 0:
  106.8 48.4 reduce-scatter.2
  158.1 40.0 reduce-scatter.4

commit v3 on v1

--- a/solution.py
+++ b/solution.py
@@ -89,11 +89,17 @@
         precision=HI,
         preferred_element_type=jnp.float32,
     )
-    correlation = butterfly_scatter(gram_term, "wide") / total_rows
-    rot_term = jnp.dot(
-        current, rotation, precision=HI, preferred_element_type=jnp.float32
+    pieces = gram_term.reshape(devcount, -1, gram_term.shape[1])
+    gathered = lax.all_to_all(pieces, "wide", 0, 0, tiled=True)
+    correlation = jnp.sum(gathered, axis=0) / total_rows
+    ngrp = lax.axis_size("grp")
+    width = current.shape[1]
+    rot_blocks = jnp.einsum(
+        "rk,kgn->grn", current, rotation.reshape(rotation.shape[0], ngrp, width),
+        precision=HI, preferred_element_type=jnp.float32,
     )
-    rotated = lax.psum_scatter(rot_term, "grp", scatter_dimension=1, tiled=True)
+    rot_parts = lax.all_to_all(rot_blocks, "grp", 0, 0, tiled=True)
+    rotated = jnp.sum(rot_parts, axis=0)
     return (rotated, correlation)
 
 

time: 166 us -> 187 us (1.13)
  waiting for transfers between devices: 31.7 us -> 66.5 us
  between operations: 14.6 us -> 1.06 us
  starting transfers between devices: 91.4 us -> 88.8 us
  other arithmetic: 1.49 us -> 3.84 us
    all_to_all x0 -> x2, waiting for transfers between devices: none -> 57.6 us  [the longest x1 50.9 us: local(): rot_parts = lax.all_to_all(rot_blocks, 'grp', 0, 0, tiled=True)]
    ppermute x6 -> x0, starting transfers between devices: 26.5 us -> none  [butterfly_scatter(): buf = keep + lax.ppermute(send, axis, pairs)]
    all_to_all x0 -> x2, starting transfers between devices: none -> 24 us  [the longest x1 16.9 us: local(): gathered = lax.all_to_all(pieces, 'wide', 0, 0, tiled=True)]
    ppermute x6 -> x0, waiting for transfers between devices: 17.5 us -> none  [butterfly_scatter(): buf = keep + lax.ppermute(send, axis, pairs)]
    reduce_scatter x1 -> x0, waiting for transfers between devices: 5.28 us -> none  [local(): rotated = lax.psum_scatter(rot_term, 'grp', scatter_dimension=1, tiled=True)]
    reduce_sum x0 -> x2, other arithmetic: none -> 2.54 us  [the longest x1 2.45 us: local(): rotated = jnp.sum(rot_parts, axis=0)]
  transfers between devices with their start and end apart: 23 -> 18, of which waited for: 13 -> 8; matrix products, arithmetic and copies ran while one was open for 12% -> 12% of each run, Pallas kernels for 0% -> 0%
where the time goes in v3:
time: 187 us; the launch traced here: 186 us
  starting transfers between devices  88.8 us (47%)
  waiting for transfers between devices  66.5 us (36%)
  matrix products  22.3 us (12%)
  other arithmetic  3.84 us (2%)
  local copies, waits for them, and re-layouts  3.73 us (2%)
    ppermute x16, starting transfers between devices, passed_along(): return lax.ppermute(value, axis, pairs)  64.8 us
    all_to_all x1, waiting for transfers between devices, local(): rot_parts = lax.all_to_all(rot_blocks, 'grp', 0, 0, tiled=True)  50.9 us
    all_to_all x1, starting transfers between devices, local(): gathered = lax.all_to_all(pieces, 'wide', 0, 0, tiled=True)  16.9 us
    dot_general x20, matrix products, apply_ham(): jnp.dot(hdense[:, idx * rows:(idx + 1) * rows], pieces[idx], precision=HI...  12.5 us
    ppermute x16, waiting for transfers between devices, passed_along(): return lax.ppermute(value, axis, pairs)  8.9 us
    all_to_all x1, starting transfers between devices, local(): rot_parts = lax.all_to_all(rot_blocks, 'grp', 0, 0, tiled=True)  7.11 us
    all_to_all x1, waiting for transfers between devices, local(): gathered = lax.all_to_all(pieces, 'wide', 0, 0, tiled=True)  6.65 us
    dot_general x1, matrix products, local(): jnp.einsum('rk,kgn->grn', current, rotation.reshape(rotation.shape[0], ng...  4.91 us
  transfers between devices with their start and end apart: 18, of which 8 were waited for; matrix products, arithmetic and copies ran while one was open for 12% of the time, Pallas kernels for 0%

profile of v3, /device:TPU:6, one launch (start us, length us, event | category | flops | bytes accessed | tf_op | source)
XLA Modules:
  0.0 186.2 jit_solution(6118167888612358955)
XLA Ops:
  0.6 0.0 copy-start
  0.6 2.1 %collective-permute-start = (f32[256,256]{1,0:T(8,128)}, f32[256,256]{1,0:T(8,128)}, u32[]{:S(2)}, u32[]{:S(2)}) collective-permute-start(f32[256,256]{1,0:T(8,128)} %param.4), channel_id=1, source_target_pairs={{0,1},{1,2},{2,3},{3,4},{4,5},{5,6},{6,7},{7,8},{8,9},{9,10},{10,1... | collective-permute-start | bytes 786440 | tf_op jit(solution)/shard_map/ppermute | solution.py:22
  2.7 11.2 %collective-permute-start.3 = (f32[256,256]{1,0:T(8,128)}, f32[256,256]{1,0:T(8,128)}, u32[]{:S(2)}, u32[]{:S(2)}) collective-permute-start(f32[256,256]{1,0:T(8,128)} %param.4), channel_id=1, source_target_pairs={{0,62},{1,63},{2,0},{3,1},{4,2},{5,3},{6,4},{7,5},{8,6},{9,7},{10,... | collective-permute-start | bytes 786440 | tf_op jit(solution)/shard_map/ppermute | solution.py:22
  13.9 1.9 %collective-permute-start.2 = (f32[256,256]{1,0:T(8,128)}, f32[256,256]{1,0:T(8,128)}, u32[]{:S(2)}, u32[]{:S(2)}) collective-permute-start(f32[256,256]{1,0:T(8,128)} %param.4), channel_id=1, source_target_pairs={{0,2},{1,3},{2,4},{3,5},{4,6},{5,7},{6,8},{7,9},{8,10},{9,11},{10,... | collective-permute-start | bytes 786440 | tf_op jit(solution)/shard_map/ppermute | solution.py:22
  15.9 4.9 %collective-permute-start.1 = (f32[256,256]{1,0:T(8,128)}, f32[256,256]{1,0:T(8,128)}, u32[]{:S(2)}, u32[]{:S(2)}) collective-permute-start(f32[256,256]{1,0:T(8,128)} %param.4), channel_id=1, source_target_pairs={{0,63},{1,0},{2,1},{3,2},{4,3},{5,4},{6,5},{7,6},{8,7},{9,8},{10,9... | collective-permute-start | bytes 786440 | tf_op jit(solution)/shard_map/ppermute | solution.py:22
  20.8 0.7 fusion.66
  21.5 4.3 %fusion.5 = f32[4,64,20,64]{3,2,1,0:T(8,128)} fusion(f32[4,16,64,64]{3,2,1,0:T(8,128)S(1)} %copy-done, s32[4,16]{1,0:T(4,128)S(1)} %fusion.66), kind=kOutput, calls=%fused_computation.5 | convolution fusion | flops 62915840 | bytes 2359552 | tf_op jit(solution)/shard_map/asp,asij->aipj/dot_general | solution.py:29
  25.8 2.2 %reshape.19 = f32[256,1280]{1,0:T(8,128)S(1)} reshape(f32[4,64,20,64]{3,2,1,0:T(8,128)} %fusion.5) | data formatting | bytes 2621440 | tf_op jit(solution)/shard_map/reshape | solution.py:30
  28.0 1.3 fusion.55
  29.3 0.0 copy-start.2
  29.3 0.0 collective-permute-done.3
  29.4 1.4 fusion.31
  30.7 1.3 fusion.39
  32.1 0.0 collective-permute-done
  32.1 1.3 convolution_add_fusion.7
  33.4 0.0 collective-permute-done.1
  33.4 1.4 broadcast_multiply_fusion
  34.8 1.9 %collective-permute-start.6 = (f32[256,256]{1,0:T(8,128)S(1)}, f32[256,256]{1,0:T(8,128)S(1)}, u32[]{:S(2)}, u32[]{:S(2)}) collective-permute-start(f32[256,256]{1,0:T(8,128)S(1)} %get-tuple-element.2), channel_id=1, source_target_pairs={{0,2},{1,3},{2,4},{3,5},{4,6},{5,7},{6,8},{7,9},{8,10},{9,11},{10,... | collective-permute-start | bytes 786440 | tf_op jit(solution)/shard_map/ppermute | solution.py:22
  36.7 1.9 %collective-permute-start.4 = (f32[256,256]{1,0:T(8,128)S(1)}, f32[256,256]{1,0:T(8,128)S(1)}, u32[]{:S(2)}, u32[]{:S(2)}) collective-permute-start(f32[256,256]{1,0:T(8,128)S(1)} %get-tuple-element.2), channel_id=1, source_target_pairs={{0,1},{1,2},{2,3},{3,4},{4,5},{5,6},{6,7},{7,8},{8,9},{9,10},{10,1... | collective-permute-start | bytes 786440 | tf_op jit(solution)/shard_map/ppermute | solution.py:22
  38.7 6.0 %collective-permute-start.7 = (f32[256,256]{1,0:T(8,128)S(1)}, f32[256,256]{1,0:T(8,128)S(1)}, u32[]{:S(2)}, u32[]{:S(2)}) collective-permute-start(f32[256,256]{1,0:T(8,128)S(1)} %get-tuple-element.2), channel_id=1, source_target_pairs={{0,62},{1,63},{2,0},{3,1},{4,2},{5,3},{6,4},{7,5},{8,6},{9,7},{10,... | collective-permute-start | bytes 786440 | tf_op jit(solution)/shard_map/ppermute | solution.py:22
  44.7 3.4 %collective-permute-start.5 = (f32[256,256]{1,0:T(8,128)S(1)}, f32[256,256]{1,0:T(8,128)S(1)}, u32[]{:S(2)}, u32[]{:S(2)}) collective-permute-start(f32[256,256]{1,0:T(8,128)S(1)} %get-tuple-element.2), channel_id=1, source_target_pairs={{0,63},{1,0},{2,1},{3,2},{4,3},{5,4},{6,5},{7,6},{8,7},{9,8},{10,9... | collective-permute-start | bytes 786440 | tf_op jit(solution)/shard_map/ppermute | solution.py:22
  48.1 0.4 fusion.53
  48.5 0.0 collective-permute-done.6
  48.5 0.4 fusion.37
  48.9 1.7 collective-permute-done.7
  50.5 0.4 fusion.29
  50.9 0.0 collective-permute-done.4
  50.9 0.4 convolution_add_fusion.5
  51.3 2.0 %collective-permute-done.5 = f32[256,256]{1,0:T(8,128)S(1)} collective-permute-done((f32[256,256]{1,0:T(8,128)S(1)}, f32[256,256]{1,0:T(8,128)S(1)}, u32[]{:S(2)}, u32[]{:S(2)}) %collective-permute-start.5) | collective-permute-done | bytes 262176 | tf_op jit(solution)/shard_map/ppermute | solution.py:22
  53.3 0.4 fusion.19
  53.8 1.9 %collective-permute-start.10 = (f32[256,256]{1,0:T(8,128)S(1)}, f32[256,256]{1,0:T(8,128)S(1)}, u32[]{:S(2)}, u32[]{:S(2)}) collective-permute-start(f32[256,256]{1,0:T(8,128)S(1)} %fusion.19), channel_id=1, source_target_pairs={{0,2},{1,3},{2,4},{3,5},{4,6},{5,7},{6,8},{7,9},{8,10},{9,11},{10,... | collective-permute-start | bytes 786440 | tf_op jit(solution)/shard_map/ppermute | solution.py:22
  55.7 6.0 %collective-permute-start.11 = (f32[256,256]{1,0:T(8,128)S(1)}, f32[256,256]{1,0:T(8,128)S(1)}, u32[]{:S(2)}, u32[]{:S(2)}) collective-permute-start(f32[256,256]{1,0:T(8,128)S(1)} %fusion.19), channel_id=1, source_target_pairs={{0,62},{1,63},{2,0},{3,1},{4,2},{5,3},{6,4},{7,5},{8,6},{9,7},{10,... | collective-permute-start | bytes 786440 | tf_op jit(solution)/shard_map/ppermute | solution.py:22
  61.7 0.4 fusion.51
  62.1 1.9 %collective-permute-start.8 = (f32[256,256]{1,0:T(8,128)S(1)}, f32[256,256]{1,0:T(8,128)S(1)}, u32[]{:S(2)}, u32[]{:S(2)}) collective-permute-start(f32[256,256]{1,0:T(8,128)S(1)} %fusion.19), channel_id=1, source_target_pairs={{0,1},{1,2},{2,3},{3,4},{4,5},{5,6},{6,7},{7,8},{8,9},{9,10},{10,1... | collective-permute-start | bytes 786440 | tf_op jit(solution)/shard_map/ppermute | solution.py:22
  64.0 5.8 %collective-permute-start.9 = (f32[256,256]{1,0:T(8,128)S(1)}, f32[256,256]{1,0:T(8,128)S(1)}, u32[]{:S(2)}, u32[]{:S(2)}) collective-permute-start(f32[256,256]{1,0:T(8,128)S(1)} %fusion.19), channel_id=1, source_target_pairs={{0,63},{1,0},{2,1},{3,2},{4,3},{5,4},{6,5},{7,6},{8,7},{9,8},{10,9... | collective-permute-start | bytes 786440 | tf_op jit(solution)/shard_map/ppermute | solution.py:22
  69.8 0.4 fusion.35
  70.2 0.4 fusion.27
  70.6 1.3 collective-permute-done.8
  71.9 0.4 convolution_add_fusion.3
  72.3 1.4 collective-permute-done.9
  73.7 0.4 fusion.22
  74.1 1.9 %collective-permute-start.14 = (f32[256,256]{1,0:T(8,128)S(1)}, f32[256,256]{1,0:T(8,128)S(1)}, u32[]{:S(2)}, u32[]{:S(2)}) collective-permute-start(f32[256,256]{1,0:T(8,128)S(1)} %fusion.22), channel_id=1, source_target_pairs={{0,2},{1,3},{2,4},{3,5},{4,6},{5,7},{6,8},{7,9},{8,10},{9,11},{10,... | collective-permute-start | bytes 786440 | tf_op jit(solution)/shard_map/ppermute | solution.py:22
  76.0 6.0 %collective-permute-start.15 = (f32[256,256]{1,0:T(8,128)S(1)}, f32[256,256]{1,0:T(8,128)S(1)}, u32[]{:S(2)}, u32[]{:S(2)}) collective-permute-start(f32[256,256]{1,0:T(8,128)S(1)} %fusion.22), channel_id=1, source_target_pairs={{0,62},{1,63},{2,0},{3,1},{4,2},{5,3},{6,4},{7,5},{8,6},{9,7},{10,... | collective-permute-start | bytes 786440 | tf_op jit(solution)/shard_map/ppermute | solution.py:22
  82.1 0.4 fusion.57
  82.4 1.9 %collective-permute-start.12 = (f32[256,256]{1,0:T(8,128)S(1)}, f32[256,256]{1,0:T(8,128)S(1)}, u32[]{:S(2)}, u32[]{:S(2)}) collective-permute-start(f32[256,256]{1,0:T(8,128)S(1)} %fusion.22), channel_id=1, source_target_pairs={{0,1},{1,2},{2,3},{3,4},{4,5},{5,6},{6,7},{7,8},{8,9},{9,10},{10,1... | collective-permute-start | bytes 786440 | tf_op jit(solution)/shard_map/ppermute | solution.py:22
  84.4 5.9 %collective-permute-start.13 = (f32[256,256]{1,0:T(8,128)S(1)}, f32[256,256]{1,0:T(8,128)S(1)}, u32[]{:S(2)}, u32[]{:S(2)}) collective-permute-start(f32[256,256]{1,0:T(8,128)S(1)} %fusion.22), channel_id=1, source_target_pairs={{0,63},{1,0},{2,1},{3,2},{4,3},{5,4},{6,5},{7,6},{8,7},{9,8},{10,9... | collective-permute-start | bytes 786440 | tf_op jit(solution)/shard_map/ppermute | solution.py:22
  90.3 0.4 fusion.41
  90.7 0.4 fusion.33
  91.1 1.1 collective-permute-done.12
  92.2 0.4 convolution_add_fusion.1
  92.6 1.4 collective-permute-done.13
  94.0 0.4 fusion.25
  94.4 0.0 copy-start.1
  94.4 0.7 copy-done.1
  95.1 0.6 fusion.68
  95.7 0.8 reshape.16
  96.5 16.9 %all-to-all-start.1 = ((f32[64,4,256]{2,1,0:T(4,128)}), f32[64,4,256]{2,1,0:T(4,128)S(1)}, u32[]{:S(2)}, u32[]{:S(2)}) async-start(f32[64,4,256]{2,1,0:T(4,128)} %reshape.16), calls=%async_computation.1 | async-start | bytes 524288 | tf_op jit(solution)/shard_map/all_to_all | solution.py:93
  113.5 4.9 %fusion.8 = f32[8,256,256]{2,1,0:T(8,128)} fusion(f32[32,8,8,256]{3,2,1,0:T(8,128)} %bitcast.39, f32[256,256]{1,0:T(8,128)} %copy-done.1), kind=kOutput, calls=%fused_computation.6 | convolution fusion | flops 1610612736 | bytes 4456448 | tf_op jit(solution)/shard_map/rk,kgn->grn/dot_general | solution.py:97
  118.4 6.7 %all-to-all-done.1 = f32[64,4,256]{2,1,0:T(4,128)S(1)} async-done(((f32[64,4,256]{2,1,0:T(4,128)}), f32[64,4,256]{2,1,0:T(4,128)S(1)}, u32[]{:S(2)}, u32[]{:S(2)}) %all-to-all-start.1) | async-done | bytes 262176 | tf_op jit(solution)/shard_map/all_to_all | solution.py:93
  125.0 7.1 %all-to-all-start = ((f32[8,256,256]{2,1,0:T(8,128)}), f32[8,256,256]{2,1,0:T(8,128)}, u32[]{:S(2)}, u32[]{:S(2)}) async-start(f32[8,256,256]{2,1,0:T(8,128)} %fusion.8), calls=%async_computation | async-start | bytes 4194304 | tf_op jit(solution)/shard_map/all_to_all | solution.py:101
  132.1 0.1 reduce_sum.19
  132.2 0.6 broadcast_multiply_fusion.1
  132.8 50.9 %all-to-all-done = f32[8,256,256]{2,1,0:T(8,128)} async-done(((f32[8,256,256]{2,1,0:T(8,128)}), f32[8,256,256]{2,1,0:T(8,128)}, u32[]{:S(2)}, u32[]{:S(2)}) %all-to-all-start) | async-done | bytes 2097184 | tf_op jit(solution)/shard_map/all_to_all | solution.py:101
  183.7 2.5 %reduce_sum.18 = f32[256,256]{1,0:T(8,128)} reduce(f32[8,256,256]{2,1,0:T(8,128)} %all-to-all-done, f32[]{:T(128)} %constant.64.clone.1), dimensions={0}, to_apply=%region_0.1 | reduce | flops 458752 | bytes 2359300 | tf_op jit(solution)/shard_map/reduce_sum | solution.py:102
  (7 shorter events, 0.0 us)
Async XLA Ops:
  0.6 20.9 %copy-start = (f32[4,16,64,64]{3,2,1,0:T(8,128)S(1)}, f32[4,16,64,64]{3,2,1,0:T(8,128)}, u32[]{:S(2)}) copy-start(f32[4,16,64,64]{3,2,1,0:T(8,128)} %param.5) | copy-start | bytes 3145732
  0.6 31.4 %collective-permute-start = (f32[256,256]{1,0:T(8,128)}, f32[256,256]{1,0:T(8,128)}, u32[]{:S(2)}, u32[]{:S(2)}) collective-permute-start(f32[256,256]{1,0:T(8,128)} %param.4), channel_id=1, source_target_pairs={{0,1},{1,2},{2,3},{3,4},{4,5},{5,6},{6,7},{7,8},{8,9},{9,10},{10,1... | collective-permute-start | bytes 786440 | tf_op jit(solution)/shard_map/ppermute | solution.py:22
  2.7 26.6 %collective-permute-start.3 = (f32[256,256]{1,0:T(8,128)}, f32[256,256]{1,0:T(8,128)}, u32[]{:S(2)}, u32[]{:S(2)}) collective-permute-start(f32[256,256]{1,0:T(8,128)} %param.4), channel_id=1, source_target_pairs={{0,62},{1,63},{2,0},{3,1},{4,2},{5,3},{6,4},{7,5},{8,6},{9,7},{10,... | collective-permute-start | bytes 786440 | tf_op jit(solution)/shard_map/ppermute | solution.py:22
  13.9 16.8 %collective-permute-start.2 = (f32[256,256]{1,0:T(8,128)}, f32[256,256]{1,0:T(8,128)}, u32[]{:S(2)}, u32[]{:S(2)}) collective-permute-start(f32[256,256]{1,0:T(8,128)} %param.4), channel_id=1, source_target_pairs={{0,2},{1,3},{2,4},{3,5},{4,6},{5,7},{6,8},{7,9},{8,10},{9,11},{10,... | collective-permute-start | bytes 786440 | tf_op jit(solution)/shard_map/ppermute | solution.py:22
  15.9 17.6 %collective-permute-start.1 = (f32[256,256]{1,0:T(8,128)}, f32[256,256]{1,0:T(8,128)}, u32[]{:S(2)}, u32[]{:S(2)}) collective-permute-start(f32[256,256]{1,0:T(8,128)} %param.4), channel_id=1, source_target_pairs={{0,63},{1,0},{2,1},{3,2},{4,3},{5,4},{6,5},{7,6},{8,7},{9,8},{10,9... | collective-permute-start | bytes 786440 | tf_op jit(solution)/shard_map/ppermute | solution.py:22
  29.3 4.1 %copy-start.2 = (f32[256,256]{1,0:T(8,128)S(1)}, f32[256,256]{1,0:T(8,128)}, u32[]{:S(2)}) copy-start(f32[256,256]{1,0:T(8,128)} %param.4) | copy-start | bytes 786436
  34.8 13.7 %collective-permute-start.6 = (f32[256,256]{1,0:T(8,128)S(1)}, f32[256,256]{1,0:T(8,128)S(1)}, u32[]{:S(2)}, u32[]{:S(2)}) collective-permute-start(f32[256,256]{1,0:T(8,128)S(1)} %get-tuple-element.2), channel_id=1, source_target_pairs={{0,2},{1,3},{2,4},{3,5},{4,6},{5,7},{6,8},{7,9},{8,10},{9,11},{10,... | collective-permute-start | bytes 786440 | tf_op jit(solution)/shard_map/ppermute | solution.py:22
  36.7 14.2 %collective-permute-start.4 = (f32[256,256]{1,0:T(8,128)S(1)}, f32[256,256]{1,0:T(8,128)S(1)}, u32[]{:S(2)}, u32[]{:S(2)}) collective-permute-start(f32[256,256]{1,0:T(8,128)S(1)} %get-tuple-element.2), channel_id=1, source_target_pairs={{0,1},{1,2},{2,3},{3,4},{4,5},{5,6},{6,7},{7,8},{8,9},{9,10},{10,1... | collective-permute-start | bytes 786440 | tf_op jit(solution)/shard_map/ppermute | solution.py:22
  38.7 11.9 %collective-permute-start.7 = (f32[256,256]{1,0:T(8,128)S(1)}, f32[256,256]{1,0:T(8,128)S(1)}, u32[]{:S(2)}, u32[]{:S(2)}) collective-permute-start(f32[256,256]{1,0:T(8,128)S(1)} %get-tuple-element.2), channel_id=1, source_target_pairs={{0,62},{1,63},{2,0},{3,1},{4,2},{5,3},{6,4},{7,5},{8,6},{9,7},{10,... | collective-permute-start | bytes 786440 | tf_op jit(solution)/shard_map/ppermute | solution.py:22
  44.7 8.6 %collective-permute-start.5 = (f32[256,256]{1,0:T(8,128)S(1)}, f32[256,256]{1,0:T(8,128)S(1)}, u32[]{:S(2)}, u32[]{:S(2)}) collective-permute-start(f32[256,256]{1,0:T(8,128)S(1)} %get-tuple-element.2), channel_id=1, source_target_pairs={{0,63},{1,0},{2,1},{3,2},{4,3},{5,4},{6,5},{7,6},{8,7},{9,8},{10,9... | collective-permute-start | bytes 786440 | tf_op jit(solution)/shard_map/ppermute | solution.py:22
  53.8 16.0 %collective-permute-start.10 = (f32[256,256]{1,0:T(8,128)S(1)}, f32[256,256]{1,0:T(8,128)S(1)}, u32[]{:S(2)}, u32[]{:S(2)}) collective-permute-start(f32[256,256]{1,0:T(8,128)S(1)} %fusion.19), channel_id=1, source_target_pairs={{0,2},{1,3},{2,4},{3,5},{4,6},{5,7},{6,8},{7,9},{8,10},{9,11},{10,... | collective-permute-start | bytes 786440 | tf_op jit(solution)/shard_map/ppermute | solution.py:22
  55.7 14.5 %collective-permute-start.11 = (f32[256,256]{1,0:T(8,128)S(1)}, f32[256,256]{1,0:T(8,128)S(1)}, u32[]{:S(2)}, u32[]{:S(2)}) collective-permute-start(f32[256,256]{1,0:T(8,128)S(1)} %fusion.19), channel_id=1, source_target_pairs={{0,62},{1,63},{2,0},{3,1},{4,2},{5,3},{6,4},{7,5},{8,6},{9,7},{10,... | collective-permute-start | bytes 786440 | tf_op jit(solution)/shard_map/ppermute | solution.py:22
  62.1 9.8 %collective-permute-start.8 = (f32[256,256]{1,0:T(8,128)S(1)}, f32[256,256]{1,0:T(8,128)S(1)}, u32[]{:S(2)}, u32[]{:S(2)}) collective-permute-start(f32[256,256]{1,0:T(8,128)S(1)} %fusion.19), channel_id=1, source_target_pairs={{0,1},{1,2},{2,3},{3,4},{4,5},{5,6},{6,7},{7,8},{8,9},{9,10},{10,1... | collective-permute-start | bytes 786440 | tf_op jit(solution)/shard_map/ppermute | solution.py:22
  64.0 9.6 %collective-permute-start.9 = (f32[256,256]{1,0:T(8,128)S(1)}, f32[256,256]{1,0:T(8,128)S(1)}, u32[]{:S(2)}, u32[]{:S(2)}) collective-permute-start(f32[256,256]{1,0:T(8,128)S(1)} %fusion.19), channel_id=1, source_target_pairs={{0,63},{1,0},{2,1},{3,2},{4,3},{5,4},{6,5},{7,6},{8,7},{9,8},{10,9... | collective-permute-start | bytes 786440 | tf_op jit(solution)/shard_map/ppermute | solution.py:22
  74.1 16.2 %collective-permute-start.14 = (f32[256,256]{1,0:T(8,128)S(1)}, f32[256,256]{1,0:T(8,128)S(1)}, u32[]{:S(2)}, u32[]{:S(2)}) collective-permute-start(f32[256,256]{1,0:T(8,128)S(1)} %fusion.22), channel_id=1, source_target_pairs={{0,2},{1,3},{2,4},{3,5},{4,6},{5,7},{6,8},{7,9},{8,10},{9,11},{10,... | collective-permute-start | bytes 786440 | tf_op jit(solution)/shard_map/ppermute | solution.py:22
  76.0 14.7 %collective-permute-start.15 = (f32[256,256]{1,0:T(8,128)S(1)}, f32[256,256]{1,0:T(8,128)S(1)}, u32[]{:S(2)}, u32[]{:S(2)}) collective-permute-start(f32[256,256]{1,0:T(8,128)S(1)} %fusion.22), channel_id=1, source_target_pairs={{0,62},{1,63},{2,0},{3,1},{4,2},{5,3},{6,4},{7,5},{8,6},{9,7},{10,... | collective-permute-start | bytes 786440 | tf_op jit(solution)/shard_map/ppermute | solution.py:22
  82.4 9.8 %collective-permute-start.12 = (f32[256,256]{1,0:T(8,128)S(1)}, f32[256,256]{1,0:T(8,128)S(1)}, u32[]{:S(2)}, u32[]{:S(2)}) collective-permute-start(f32[256,256]{1,0:T(8,128)S(1)} %fusion.22), channel_id=1, source_target_pairs={{0,1},{1,2},{2,3},{3,4},{4,5},{5,6},{6,7},{7,8},{8,9},{9,10},{10,1... | collective-permute-start | bytes 786440 | tf_op jit(solution)/shard_map/ppermute | solution.py:22
  84.4 9.6 %collective-permute-start.13 = (f32[256,256]{1,0:T(8,128)S(1)}, f32[256,256]{1,0:T(8,128)S(1)}, u32[]{:S(2)}, u32[]{:S(2)}) collective-permute-start(f32[256,256]{1,0:T(8,128)S(1)} %fusion.22), channel_id=1, source_target_pairs={{0,63},{1,0},{2,1},{3,2},{4,3},{5,4},{6,5},{7,6},{8,7},{9,8},{10,9... | collective-permute-start | bytes 786440 | tf_op jit(solution)/shard_map/ppermute | solution.py:22
  94.4 0.7 copy-start.1
  96.5 28.5 %all-to-all-start.1 = ((f32[64,4,256]{2,1,0:T(4,128)}), f32[64,4,256]{2,1,0:T(4,128)S(1)}, u32[]{:S(2)}, u32[]{:S(2)}) async-start(f32[64,4,256]{2,1,0:T(4,128)} %reshape.16), calls=%async_computation.1 | async-start | bytes 524288 | tf_op jit(solution)/shard_map/all_to_all | solution.py:93
  125.0 58.7 %all-to-all-start = ((f32[8,256,256]{2,1,0:T(8,128)}), f32[8,256,256]{2,1,0:T(8,128)}, u32[]{:S(2)}, u32[]{:S(2)}) async-start(f32[8,256,256]{2,1,0:T(8,128)} %fusion.8), calls=%async_computation | async-start | bytes 4194304 | tf_op jit(solution)/shard_map/all_to_all | solution.py:101

commit v4 on v0

v4 whole, which is shorter than its diff:
```python
import jax
import jax.numpy as jnp
from jax import lax
from jax.sharding import PartitionSpec as P

B = 64
A_DEV = 4
NB = 16
HW = 2
DEGREE = 4


cheb_center = 0.25
cheb_half = 2.0

HI = lax.Precision.HIGHEST


def mm(a, b):
    return jnp.dot(a, b, precision=HI, preferred_element_type=jnp.float32)


def dense_hamiltonian(hblocks, slot_index):
    local_blocks = hblocks.shape[0]
    window_blocks = (2 * HW + 1) * A_DEV
    onehot = (slot_index[:, :, None] == jnp.arange(window_blocks)[None, None, :]).astype(jnp.float32)
    hd = jnp.einsum("asp,asij->aipj", onehot, hblocks, precision=HI)
    return hd.reshape(local_blocks * B, window_blocks * B)


def local(subspace, hblocks, pattern, rotation):
    devcount = lax.axis_size("wide")
    myself = lax.axis_index("wide")
    chips = devcount // 2
    core = myself % 2
    rows = subspace.shape[0]

    swap_pairs = [(i, i ^ 1) for i in range(devcount)]
    near_pairs = []
    for q in range(chips):
        near_pairs.append((2 * ((q - 1) % chips), 2 * q))
        near_pairs.append((2 * ((q + 1) % chips) + 1, 2 * q + 1))

    owner = pattern // A_DEV
    relative = (owner - myself + HW + devcount) % devcount
    slot_index = relative * A_DEV + pattern % A_DEV
    hd_own = dense_hamiltonian(hblocks, slot_index)
    zeros = jnp.zeros((rows, rows), jnp.float32)
    hc_own = jnp.where(core == 0,
                       jnp.concatenate([hd_own, zeros], axis=1),
                       jnp.concatenate([zeros, hd_own], axis=1))
    hc_other = lax.ppermute(hc_own, "wide", swap_pairs)
    sub_other = lax.ppermute(subspace, "wide", swap_pairs)
    first = core == 0
    h_chip = jnp.where(first, jnp.concatenate([hc_own, hc_other], axis=0),
                       jnp.concatenate([hc_other, hc_own], axis=0))
    y0 = jnp.where(first, jnp.concatenate([subspace, sub_other], axis=0),
                   jnp.concatenate([sub_other, subspace], axis=0))
    h_lo = h_chip[:, 0:2 * rows]
    h_self = h_chip[:, 2 * rows:4 * rows]
    h_hi = h_chip[:, 4 * rows:6 * rows]
    h_r1 = jnp.where(first, h_lo, h_hi)
    h_r2 = jnp.where(first, h_hi, h_lo)

    def apply_ham(field):
        r1 = lax.ppermute(field, "wide", near_pairs)
        total, r1 = lax.optimization_barrier((mm(h_self, field), r1))
        r2 = lax.ppermute(r1, "wide", swap_pairs)
        total, r2 = lax.optimization_barrier((total + mm(h_r1, r1), r2))
        return total + mm(h_r2, r2)

    previous = y0
    current = (apply_ham(y0) - cheb_center * y0) / cheb_half
    def cheb_step(step, carry):
        previous, current = carry
        nextone = (
            2.0 * (apply_ham(current) - cheb_center * current) / cheb_half
            - previous
        )
        return (current, nextone)

    previous, current = lax.fori_loop(0, DEGREE - 1, cheb_step, (previous, current))
    mine = lax.dynamic_slice_in_dim(current, core * rows, rows, axis=0)
    total_rows = rows * devcount
    gram_term = lax.dot_general(
        mine, mine, (((0,), (0,)), ((), ())), precision=HI, preferred_element_type=jnp.float32
    )
    pieces = gram_term.reshape(devcount, -1, gram_term.shape[1])
    gathered = lax.all_to_all(pieces, "wide", 0, 0, tiled=True)
    correlation = jnp.sum(gathered, axis=0) / total_rows
    rot_term = mm(mine, rotation)
    rotated = lax.psum_scatter(rot_term, "grp", scatter_dimension=1, tiled=True)
    return (rotated, correlation)


def solution(mesh):
    in_specs = (P("wide", "grp"), P("wide", None, None, None), P("wide", None), P("grp", None))
    out_specs = (P("wide", "grp"), P(("grp", "wide"), None))
    return jax.shard_map(local, mesh=mesh, in_specs=in_specs, out_specs=out_specs, check_vma=False)
```

time: 343 us -> 185 us (0.54)
  waiting for transfers between devices: 210 us -> 57.7 us
  starting transfers between devices: 67 us -> 22.2 us
  matrix products: 15.2 us -> 39.6 us
  blocking collectives: 0 us -> 21.2 us
    unnamed x3 -> x1, waiting for transfers between devices: 189 us -> 0.02 us
    ppermute x16 -> x10, starting transfers between devices: 67 us -> 22.2 us  [the longest x4 10 us: apply_ham(): r1 = lax.ppermute(field, 'wide', near_pairs)]
    dot_general x6 -> x15, matrix products: 15.2 us -> 39.6 us  [the longest x13 33.2 us: mm(): return jnp.dot(a, b, precision=HI, preferred_element_type=jnp.float32)]
    reduce_scatter x1, waiting for transfers between devices: 0.01 us -> 21.5 us  [local(): rotated = lax.psum_scatter(rot_term, 'grp', scatter_dimension=1, tiled=True)]
    all_to_all x0 -> x1, blocking collectives: none -> 21.2 us  [local(): gathered = lax.all_to_all(pieces, 'wide', 0, 0, tiled=True)]
    ppermute x16 -> x10, waiting for transfers between devices: 21 us -> 36.2 us  [the longest x4 34.6 us: apply_ham(): r1 = lax.ppermute(field, 'wide', near_pairs)]
    gather x4 -> x0, local copies, waits for them, and re-layouts: 11.1 us -> none  [apply_ham(): jnp.take(window, slot_index, axis=0).reshape(local_blocks, NB, B, width)]
    while x0 -> x12, local copies, waits for them, and re-layouts: none -> 8.89 us  [the longest x3 6.43 us: local(): lax.fori_loop(0, DEGREE - 1, cheb_step, (previous, current))]
  transfers between devices with their start and end apart: 18 -> 11, of which waited for: 12 -> 6; matrix products, arithmetic and copies ran while one was open for 3% -> 20% of each run, Pallas kernels for 0% -> 0%
where the time goes in v4:
time: 185 us; the launch traced here: 184 us
  waiting for transfers between devices  57.7 us (31%)
  matrix products  39.6 us (21%)
  starting transfers between devices  22.2 us (12%)
  blocking collectives  21.2 us (11%)
  other arithmetic  14.9 us (8%)
  between operations  14.2 us (8%)
  local copies, waits for them, and re-layouts  13.8 us (7%)
    ppermute x4, waiting for transfers between devices, apply_ham(): r1 = lax.ppermute(field, 'wide', near_pairs)  34.6 us
    dot_general x13, matrix products, mm(): return jnp.dot(a, b, precision=HI, preferred_element_type=jnp.float32)  33.2 us
    reduce_scatter x1, waiting for transfers between devices, local(): rotated = lax.psum_scatter(rot_term, 'grp', scatter_dimension=1, tiled=True)  21.5 us
    all_to_all x1, blocking collectives, local(): gathered = lax.all_to_all(pieces, 'wide', 0, 0, tiled=True)  21.2 us
    ppermute x4, starting transfers between devices, apply_ham(): r1 = lax.ppermute(field, 'wide', near_pairs)  10 us
    ppermute x4, starting transfers between devices, apply_ham(): r2 = lax.ppermute(r1, 'wide', swap_pairs)  7.82 us
    while x3, local copies, waits for them, and re-layouts, local(): lax.fori_loop(0, DEGREE - 1, cheb_step, (previous, current))  6.43 us
    dot_general x1, matrix products, dense_hamiltonian(): hd = jnp.einsum('asp,asij->aipj', onehot, hblocks, precision=HI)  5.76 us
  transfers between devices with their start and end apart: 11, of which 6 were waited for; matrix products, arithmetic and copies ran while one was open for 20% of the time, Pallas kernels for 0%

profile of v4, /device:TPU:6, one launch (start us, length us, event | category | flops | bytes accessed | tf_op | source)
XLA Modules:
  0.0 183.8 jit_solution(17666651954632682681)
XLA Ops:
  7.2 0.0 copy-start
  7.2 0.0 reduce-scatter.2.cloned.1.call-start
  7.2 0.8 fusion.16
  8.1 5.8 %fusion.2 = f32[4,64,20,64]{3,2,1,0:T(8,128)} fusion(f32[4,16,64,64]{3,2,1,0:T(8,128)} %param.7, s32[4,16]{1,0:T(4,128)S(1)} %fusion.16), kind=kOutput, calls=%fused_computation.6 | convolution fusion | flops 62915840 | bytes 2359552 | tf_op jit(solution)/shard_map/asp,asij->aipj/dot_general | solution.py:27
  13.8 3.0 %reshape.14 = f32[256,1280]{1,0:T(8,128)} reshape(f32[4,64,20,64]{3,2,1,0:T(8,128)} %fusion.2) | data formatting | bytes 2621440 | tf_op jit(solution)/shard_map/reshape | solution.py:28
  16.9 1.7 copy.19
  18.6 1.3 pad_select_fusion
  19.9 1.9 %collective-permute-start.3 = (f32[256,1536]{0,1:T(8,128)}, f32[256,1536]{0,1:T(8,128)}, u32[]{:S(2)}, u32[]{:S(2)}) collective-permute-start(f32[256,1536]{0,1:T(8,128)} %pad_select_fusion), channel_id=1, source_target_pairs={{0,1},{1,0},{2,3},{3,2},{4,5},{5,4},{6,7},{7,6},{8,9},{9,8},{10,11... | collective-permute-start | bytes 4718600 | tf_op jit(solution)/shard_map/ppermute | solution.py:52
  21.8 2.4 %collective-permute-start.2 = (f32[256,256]{1,0:T(8,128)}, f32[256,256]{1,0:T(8,128)S(1)}, u32[]{:S(2)}, u32[]{:S(2)}) collective-permute-start(f32[256,256]{1,0:T(8,128)} %param.6), channel_id=1, source_target_pairs={{0,1},{1,0},{2,3},{3,2},{4,5},{5,4},{6,7},{7,6},{8,9},{9,8},{10,11... | collective-permute-start | bytes 786440 | tf_op jit(solution)/shard_map/ppermute | solution.py:53
  24.2 1.5 collective-permute-done.2
  25.8 1.9 %maximum_select_fusion.1 = f32[512,256]{1,0:T(8,128)} fusion(f32[256,256]{1,0:T(8,128)S(1)} %collective-permute-done.2, f32[256,256]{1,0:T(8,128)} %param.6, pred[]{:T(512)S(6)} %eq.22), kind=kLoop, calls=%fused_computation.10 | loop fusion | flops 393216 | bytes 1048577 | tf_op jit(solution)/shard_map/jit(_where)/select_n | solution.py:57
  27.6 4.3 %collective-permute-start.4 = (f32[512,256]{1,0:T(8,128)}, f32[512,256]{1,0:T(8,128)}, u32[]{:S(2)}, u32[]{:S(2)}) collective-permute-start(f32[512,256]{1,0:T(8,128)} %maximum_select_fusion.1), channel_id=1, source_target_pairs={{62,0},{3,1},{0,2},{5,3},{2,4},{7,5},{4,6},{9,7},{6,8},{11,9},{8,1... | collective-permute-start | bytes 1572872 | tf_op jit(solution)/shard_map/ppermute | solution.py:66
  31.9 0.0 collective-permute-done.3
  31.9 3.5 %maximum_select_fusion = f32[512,1536]{0,1:T(8,128)S(1)} fusion(f32[256,1536]{0,1:T(8,128)} %collective-permute-done.3, f32[256,1536]{0,1:T(8,128)} %pad_select_fusion, pred[]{:T(512)S(6)} %eq.22), kind=kLoop, calls=%fused_computation.3 | loop fusion | flops 2359296 | bytes 6291457 | tf_op jit(solution)/shard_map/jit(_where)/select_n | solution.py:55
  35.5 3.7 %fusion.20 = f32[512,256]{1,0:T(8,128)} fusion(f32[512,256]{1,0:T(8,128)} %maximum_select_fusion.1, f32[512,1536]{0,1:T(8,128)S(1)} %maximum_select_fusion), kind=kOutput, calls=%fused_computation.37 | convolution fusion | flops 805306368 | bytes 2097152 | tf_op jit(solution)/shard_map/dot_general | solution.py:20
  39.1 7.2 %collective-permute-done.4 = f32[512,256]{1,0:T(8,128)} collective-permute-done((f32[512,256]{1,0:T(8,128)}, f32[512,256]{1,0:T(8,128)}, u32[]{:S(2)}, u32[]{:S(2)}) %collective-permute-start.4) | collective-permute-done | bytes 524320 | tf_op jit(solution)/shard_map/ppermute | solution.py:66
  46.3 2.1 %collective-permute-start.5 = (f32[512,256]{1,0:T(8,128)}, f32[512,256]{1,0:T(8,128)}, u32[]{:S(2)}, u32[]{:S(2)}) collective-permute-start(f32[512,256]{1,0:T(8,128)} %collective-permute-done.4), channel_id=1, source_target_pairs={{0,1},{1,0},{2,3},{3,2},{4,5},{5,4},{6,7},{7,6},{8,9},{9,8},{10,11... | collective-permute-start | bytes 1572872 | tf_op jit(solution)/shard_map/ppermute | solution.py:68
  48.4 1.7 fusion.22
  50.1 2.5 %copy.13 = f32[512,512]{1,0:T(8,128)} copy(f32[512,512]{0,1:T(8,128)} %get-tuple-element.110) | data formatting | bytes 2097152 | tf_op jit(solution)/shard_map/while | solution.py:82
  52.7 2.6 %copy.14 = f32[512,512]{1,0:T(8,128)} copy(f32[512,512]{0,1:T(8,128)} %get-tuple-element.111) | data formatting | bytes 2097152 | tf_op jit(solution)/shard_map/while | solution.py:82
  55.2 1.3 copy.15
  56.6 3.2 %fusion.24 = f32[512,256]{1,0:T(8,128)S(1)} fusion(f32[512,512]{0,1:T(8,128)} %get-tuple-element.111, f32[512,256]{1,0:T(8,128)} %collective-permute-done.4), kind=kOutput, calls=%fused_computation.41 | convolution fusion | flops 805306368 | bytes 2097152 | tf_op jit(solution)/shard_map/dot_general | solution.py:20
  59.8 0.1 add.67
  59.9 0.0 collective-permute-done.5
  59.9 2.9 %fusion.25 = f32[512,256]{1,0:T(8,128)S(1)} fusion(f32[512,512]{0,1:T(8,128)S(1)} %get-tuple-element.112, f32[512,256]{1,0:T(8,128)} %collective-permute-done.5), kind=kOutput, calls=%fused_computation.42 | convolution fusion | flops 805306368 | bytes 2097152 | tf_op jit(solution)/shard_map/dot_general | solution.py:20
  62.8 1.1 subtract_multiply_fusion
  63.9 65.7 %while.14 = (s32[]{:T(128)}, f32[512,256]{1,0:T(8,128)}, f32[512,256]{1,0:T(8,128)S(1)}, f32[512,512]{1,0:T(8,128)}, f32[512,512]{1,0:T(8,128)}, /*index=5*/f32[512,512]{1,0:T(8,128)}, s32[]{:T(128)}) while((s32[]{:T(128)}, f32[512,256]{1,0:T(8,128)}, f32[512,256]{1,0:T(8,128)S(1)}, f32[512,512]{1,0:T(8,128)}, f32[512,512]{1,0:T(8,128)}, ...), condition=%wide.region_1.2_spmd, body=%wide.region_0.1_spmd.sunk | while | flops 2416574464 | bytes 20971704 | solution.py:82
  64.0 1.9 %collective-permute-start = (f32[512,256]{1,0:T(8,128)S(1)}, f32[512,256]{1,0:T(8,128)}, u32[]{:S(2)}, u32[]{:S(2)}) collective-permute-start(f32[512,256]{1,0:T(8,128)S(1)} %copy.29), channel_id=1, source_target_pairs={{62,0},{3,1},{0,2},{5,3},{2,4},{7,5},{4,6},{9,7},{6,8},{11,9},{8,1... | collective-permute-start | bytes 1572872 | tf_op jit(solution)/shard_map/while/body/eval_jaxpr/ppermute | solution.py:66
  65.9 2.2 %fusion.51 = f32[512,256]{1,0:T(8,128)S(1)} fusion(f32[512,512]{1,0:T(8,128)} %get-tuple-element.175, f32[512,256]{1,0:T(8,128)S(1)} %copy.29), kind=kOutput, calls=%fused_computation.40.clone.1 | convolution fusion | flops 805306368 | bytes 2097152 | tf_op jit(solution)/shard_map/while/body/eval_jaxpr/dot_general | solution.py:20
  68.1 9.1 %collective-permute-done = f32[512,256]{1,0:T(8,128)} collective-permute-done((f32[512,256]{1,0:T(8,128)S(1)}, f32[512,256]{1,0:T(8,128)}, u32[]{:S(2)}, u32[]{:S(2)}) %collective-permute-start) | collective-permute-done | bytes 524320 | tf_op jit(solution)/shard_map/while/body/eval_jaxpr/ppermute | solution.py:66
  77.3 1.9 %collective-permute-start.1 = (f32[512,256]{1,0:T(8,128)}, f32[512,256]{1,0:T(8,128)}, u32[]{:S(2)}, u32[]{:S(2)}) collective-permute-start(f32[512,256]{1,0:T(8,128)} %collective-permute-done), channel_id=1, source_target_pairs={{0,1},{1,0},{2,3},{3,2},{4,5},{5,4},{6,7},{7,6},{8,9},{9,8},{10,11... | collective-permute-start | bytes 1572872 | tf_op jit(solution)/shard_map/while/body/eval_jaxpr/ppermute | solution.py:68
  79.2 2.5 %convolution_bitcast_fusion.4 = f32[512,256]{1,0:T(8,128)S(1)} fusion(f32[512,256]{1,0:T(8,128)} %collective-permute-done, f32[512,512]{1,0:T(8,128)} %get-tuple-element.176), kind=kOutput, calls=%fused_computation.1.clone.1 | convolution fusion | flops 805306368 | bytes 2097152 | tf_op jit(solution)/shard_map/while/body/eval_jaxpr/dot_general | solution.py:20
  81.7 0.1 add.92
  81.7 0.0 collective-permute-done.1
  81.8 2.1 %convolution_bitcast_fusion.5 = f32[512,256]{1,0:T(8,128)S(1)} fusion(f32[512,256]{1,0:T(8,128)} %collective-permute-done.1, f32[512,512]{1,0:T(8,128)S(1)} %copy-done.1), kind=kOutput, calls=%fused_computation.clone.1 | convolution fusion | flops 805306368 | bytes 2097152 | tf_op jit(solution)/shard_map/while/body/eval_jaxpr/dot_general | solution.py:20
  83.8 1.2 subtract_subtract_fusion.2
  85.0 0.8 copy.31
  85.9 1.9 %collective-permute-start = (f32[512,256]{1,0:T(8,128)S(1)}, f32[512,256]{1,0:T(8,128)}, u32[]{:S(2)}, u32[]{:S(2)}) collective-permute-start(f32[512,256]{1,0:T(8,128)S(1)} %copy.29), channel_id=1, source_target_pairs={{62,0},{3,1},{0,2},{5,3},{2,4},{7,5},{4,6},{9,7},{6,8},{11,9},{8,1... | collective-permute-start | bytes 1572872 | tf_op jit(solution)/shard_map/while/body/eval_jaxpr/ppermute | solution.py:66
  87.8 2.2 %fusion.51 = f32[512,256]{1,0:T(8,128)S(1)} fusion(f32[512,512]{1,0:T(8,128)} %get-tuple-element.175, f32[512,256]{1,0:T(8,128)S(1)} %copy.29), kind=kOutput, calls=%fused_computation.40.clone.1 | convolution fusion | flops 805306368 | bytes 2097152 | tf_op jit(solution)/shard_map/while/body/eval_jaxpr/dot_general | solution.py:20
  90.0 9.1 %collective-permute-done = f32[512,256]{1,0:T(8,128)} collective-permute-done((f32[512,256]{1,0:T(8,128)S(1)}, f32[512,256]{1,0:T(8,128)}, u32[]{:S(2)}, u32[]{:S(2)}) %collective-permute-start) | collective-permute-done | bytes 524320 | tf_op jit(solution)/shard_map/while/body/eval_jaxpr/ppermute | solution.py:66
  99.2 1.9 %collective-permute-start.1 = (f32[512,256]{1,0:T(8,128)}, f32[512,256]{1,0:T(8,128)}, u32[]{:S(2)}, u32[]{:S(2)}) collective-permute-start(f32[512,256]{1,0:T(8,128)} %collective-permute-done), channel_id=1, source_target_pairs={{0,1},{1,0},{2,3},{3,2},{4,5},{5,4},{6,7},{7,6},{8,9},{9,8},{10,11... | collective-permute-start | bytes 1572872 | tf_op jit(solution)/shard_map/while/body/eval_jaxpr/ppermute | solution.py:68
  101.1 2.5 %convolution_bitcast_fusion.4 = f32[512,256]{1,0:T(8,128)S(1)} fusion(f32[512,256]{1,0:T(8,128)} %collective-permute-done, f32[512,512]{1,0:T(8,128)} %get-tuple-element.176), kind=kOutput, calls=%fused_computation.1.clone.1 | convolution fusion | flops 805306368 | bytes 2097152 | tf_op jit(solution)/shard_map/while/body/eval_jaxpr/dot_general | solution.py:20
  103.6 0.1 add.92
  103.6 0.0 collective-permute-done.1
  103.7 2.1 %convolution_bitcast_fusion.5 = f32[512,256]{1,0:T(8,128)S(1)} fusion(f32[512,256]{1,0:T(8,128)} %collective-permute-done.1, f32[512,512]{1,0:T(8,128)S(1)} %copy-done.1), kind=kOutput, calls=%fused_computation.clone.1 | convolution fusion | flops 805306368 | bytes 2097152 | tf_op jit(solution)/shard_map/while/body/eval_jaxpr/dot_general | solution.py:20
  105.7 1.2 subtract_subtract_fusion.2
  106.9 0.8 copy.31
  107.8 1.9 %collective-permute-start = (f32[512,256]{1,0:T(8,128)S(1)}, f32[512,256]{1,0:T(8,128)}, u32[]{:S(2)}, u32[]{:S(2)}) collective-permute-start(f32[512,256]{1,0:T(8,128)S(1)} %copy.29), channel_id=1, source_target_pairs={{62,0},{3,1},{0,2},{5,3},{2,4},{7,5},{4,6},{9,7},{6,8},{11,9},{8,1... | collective-permute-start | bytes 1572872 | tf_op jit(solution)/shard_map/while/body/eval_jaxpr/ppermute | solution.py:66
  109.7 2.2 %fusion.51 = f32[512,256]{1,0:T(8,128)S(1)} fusion(f32[512,512]{1,0:T(8,128)} %get-tuple-element.175, f32[512,256]{1,0:T(8,128)S(1)} %copy.29), kind=kOutput, calls=%fused_computation.40.clone.1 | convolution fusion | flops 805306368 | bytes 2097152 | tf_op jit(solution)/shard_map/while/body/eval_jaxpr/dot_general | solution.py:20
  111.9 9.1 %collective-permute-done = f32[512,256]{1,0:T(8,128)} collective-permute-done((f32[512,256]{1,0:T(8,128)S(1)}, f32[512,256]{1,0:T(8,128)}, u32[]{:S(2)}, u32[]{:S(2)}) %collective-permute-start) | collective-permute-done | bytes 524320 | tf_op jit(solution)/shard_map/while/body/eval_jaxpr/ppermute | solution.py:66
  121.1 1.9 %collective-permute-start.1 = (f32[512,256]{1,0:T(8,128)}, f32[512,256]{1,0:T(8,128)}, u32[]{:S(2)}, u32[]{:S(2)}) collective-permute-start(f32[512,256]{1,0:T(8,128)} %collective-permute-done), channel_id=1, source_target_pairs={{0,1},{1,0},{2,3},{3,2},{4,5},{5,4},{6,7},{7,6},{8,9},{9,8},{10,11... | collective-permute-start | bytes 1572872 | tf_op jit(solution)/shard_map/while/body/eval_jaxpr/ppermute | solution.py:68
  123.0 2.5 %convolution_bitcast_fusion.4 = f32[512,256]{1,0:T(8,128)S(1)} fusion(f32[512,256]{1,0:T(8,128)} %collective-permute-done, f32[512,512]{1,0:T(8,128)} %get-tuple-element.176), kind=kOutput, calls=%fused_computation.1.clone.1 | convolution fusion | flops 805306368 | bytes 2097152 | tf_op jit(solution)/shard_map/while/body/eval_jaxpr/dot_general | solution.py:20
  125.5 0.1 add.92
  125.6 2.1 %convolution_bitcast_fusion.5 = f32[512,256]{1,0:T(8,128)S(1)} fusion(f32[512,256]{1,0:T(8,128)} %collective-permute-done.1, f32[512,512]{1,0:T(8,128)S(1)} %copy-done.1), kind=kOutput, calls=%fused_computation.clone.1 | convolution fusion | flops 805306368 | bytes 2097152 | tf_op jit(solution)/shard_map/while/body/eval_jaxpr/dot_general | solution.py:20
  127.6 1.2 subtract_subtract_fusion.2
  128.8 0.8 copy.31
  129.6 3.3 %fusion.7 = f32[256,2048]{1,0:T(8,128)} fusion(f32[256,2048]{1,0:T(8,128)S(1)} %copy-done, f32[512,256]{1,0:T(8,128)S(1)} %get-tuple-element.91, s32[]{:T(128)S(6)} %select_n.74), kind=kOutput, calls=%fused_computation.14 | convolution fusion | flops 1610612736 | bytes 4456452 | tf_op jit(solution)/shard_map/dot_general | solution.py:20
  132.9 0.0 reduce-scatter.2.cloned.1.call-update
  132.9 0.6 fusion.5
  133.5 0.1 reshape.12
  133.6 21.2 %all_to_all.5 = f32[64,4,256]{2,1,0:T(4,128)S(1)} all-to-all(f32[64,4,256]{2,1,0:T(4,128)S(1)} %reshape.12), channel_id=1, replica_groups=mesh['grp'=8,'wide'=64] {'wide'}, dimensions={0} | all-to-all | bytes 524288 | tf_op jit(solution)/shard_map/all_to_all | solution.py:89
  154.8 0.1 reduce_sum.9
  154.8 0.6 broadcast_multiply_fusion
  155.4 21.5 %reduce-scatter.2.cloned.1.call-done = f32[256,256]{1,0:T(8,128)} async-done(((f32[256,2048]{1,0:T(8,128)}), f32[256,256]{1,0:T(8,128)}) %reduce-scatter.2.cloned.1.call-update) | async-done | bytes 262160 | tf_op jit(solution)/shard_map/reduce_scatter | solution.py:92
  (13 shorter events, 0.1 us)
Async XLA Ops:
  7.2 122.5 %copy-start = (f32[256,2048]{1,0:T(8,128)S(1)}, f32[256,2048]{1,0:T(8,128)}, u32[]{:S(2)}) copy-start(f32[256,2048]{1,0:T(8,128)} %param.9) | copy-start | bytes 6291460
  7.2 169.8 %reduce-scatter.2.cloned.1.call-start = ((), (), s32[]{:S(2)}) async-start(), calls=%async_computation.2 | async-start | bytes 2359296 | tf_op jit(solution)/shard_map/reduce_scatter | solution.py:92
  19.9 12.0 %collective-permute-start.3 = (f32[256,1536]{0,1:T(8,128)}, f32[256,1536]{0,1:T(8,128)}, u32[]{:S(2)}, u32[]{:S(2)}) collective-permute-start(f32[256,1536]{0,1:T(8,128)} %pad_select_fusion), channel_id=1, source_target_pairs={{0,1},{1,0},{2,3},{3,2},{4,5},{5,4},{6,7},{7,6},{8,9},{9,8},{10,11... | collective-permute-start | bytes 4718600 | tf_op jit(solution)/shard_map/ppermute | solution.py:52
  21.8 4.0 %collective-permute-start.2 = (f32[256,256]{1,0:T(8,128)}, f32[256,256]{1,0:T(8,128)S(1)}, u32[]{:S(2)}, u32[]{:S(2)}) collective-permute-start(f32[256,256]{1,0:T(8,128)} %param.6), channel_id=1, source_target_pairs={{0,1},{1,0},{2,3},{3,2},{4,5},{5,4},{6,7},{7,6},{8,9},{9,8},{10,11... | collective-permute-start | bytes 786440 | tf_op jit(solution)/shard_map/ppermute | solution.py:53
  27.6 18.7 %collective-permute-start.4 = (f32[512,256]{1,0:T(8,128)}, f32[512,256]{1,0:T(8,128)}, u32[]{:S(2)}, u32[]{:S(2)}) collective-permute-start(f32[512,256]{1,0:T(8,128)} %maximum_select_fusion.1), channel_id=1, source_target_pairs={{62,0},{3,1},{0,2},{5,3},{2,4},{7,5},{4,6},{9,7},{6,8},{11,9},{8,1... | collective-permute-start | bytes 1572872 | tf_op jit(solution)/shard_map/ppermute | solution.py:66
  46.3 13.6 %collective-permute-start.5 = (f32[512,256]{1,0:T(8,128)}, f32[512,256]{1,0:T(8,128)}, u32[]{:S(2)}, u32[]{:S(2)}) collective-permute-start(f32[512,256]{1,0:T(8,128)} %collective-permute-done.4), channel_id=1, source_target_pairs={{0,1},{1,0},{2,3},{3,2},{4,5},{5,4},{6,7},{7,6},{8,9},{9,8},{10,11... | collective-permute-start | bytes 1572872 | tf_op jit(solution)/shard_map/ppermute | solution.py:68
  56.6 3.2 %copy-start.2 = (f32[512,256]{1,0:T(8,128)S(1)}, f32[512,256]{1,0:T(8,128)}, u32[]{:S(2)}) copy-start(f32[512,256]{1,0:T(8,128)} %fusion.20) | copy-start | bytes 1572868
  64.0 13.3 %collective-permute-start = (f32[512,256]{1,0:T(8,128)S(1)}, f32[512,256]{1,0:T(8,128)}, u32[]{:S(2)}, u32[]{:S(2)}) collective-permute-start(f32[512,256]{1,0:T(8,128)S(1)} %copy.29), channel_id=1, source_target_pairs={{62,0},{3,1},{0,2},{5,3},{2,4},{7,5},{4,6},{9,7},{6,8},{11,9},{8,1... | collective-permute-start | bytes 1572872 | tf_op jit(solution)/shard_map/while/body/eval_jaxpr/ppermute | solution.py:66
  77.3 4.5 %collective-permute-start.1 = (f32[512,256]{1,0:T(8,128)}, f32[512,256]{1,0:T(8,128)}, u32[]{:S(2)}, u32[]{:S(2)}) collective-permute-start(f32[512,256]{1,0:T(8,128)} %collective-permute-done), channel_id=1, source_target_pairs={{0,1},{1,0},{2,3},{3,2},{4,5},{5,4},{6,7},{7,6},{8,9},{9,8},{10,11... | collective-permute-start | bytes 1572872 | tf_op jit(solution)/shard_map/while/body/eval_jaxpr/ppermute | solution.py:68
  79.2 2.6 %copy-start.1 = (f32[512,512]{1,0:T(8,128)S(1)}, f32[512,512]{1,0:T(8,128)}, u32[]{:S(2)}) copy-start(f32[512,512]{1,0:T(8,128)} %get-tuple-element.177) | copy-start | bytes 3145732 | tf_op jit(solution)/shard_map/while
  85.9 13.3 %collective-permute-start = (f32[512,256]{1,0:T(8,128)S(1)}, f32[512,256]{1,0:T(8,128)}, u32[]{:S(2)}, u32[]{:S(2)}) collective-permute-start(f32[512,256]{1,0:T(8,128)S(1)} %copy.29), channel_id=1, source_target_pairs={{62,0},{3,1},{0,2},{5,3},{2,4},{7,5},{4,6},{9,7},{6,8},{11,9},{8,1... | collective-permute-start | bytes 1572872 | tf_op jit(solution)/shard_map/while/body/eval_jaxpr/ppermute | solution.py:66
  99.2 4.5 %collective-permute-start.1 = (f32[512,256]{1,0:T(8,128)}, f32[512,256]{1,0:T(8,128)}, u32[]{:S(2)}, u32[]{:S(2)}) collective-permute-start(f32[512,256]{1,0:T(8,128)} %collective-permute-done), channel_id=1, source_target_pairs={{0,1},{1,0},{2,3},{3,2},{4,5},{5,4},{6,7},{7,6},{8,9},{9,8},{10,11... | collective-permute-start | bytes 1572872 | tf_op jit(solution)/shard_map/while/body/eval_jaxpr/ppermute | solution.py:68
  101.1 2.6 %copy-start.1 = (f32[512,512]{1,0:T(8,128)S(1)}, f32[512,512]{1,0:T(8,128)}, u32[]{:S(2)}) copy-start(f32[512,512]{1,0:T(8,128)} %get-tuple-element.177) | copy-start | bytes 3145732 | tf_op jit(solution)/shard_map/while
  107.8 13.3 %collective-permute-start = (f32[512,256]{1,0:T(8,128)S(1)}, f32[512,256]{1,0:T(8,128)}, u32[]{:S(2)}, u32[]{:S(2)}) collective-permute-start(f32[512,256]{1,0:T(8,128)S(1)} %copy.29), channel_id=1, source_target_pairs={{62,0},{3,1},{0,2},{5,3},{2,4},{7,5},{4,6},{9,7},{6,8},{11,9},{8,1... | collective-permute-start | bytes 1572872 | tf_op jit(solution)/shard_map/while/body/eval_jaxpr/ppermute | solution.py:66
  121.1 4.5 %collective-permute-start.1 = (f32[512,256]{1,0:T(8,128)}, f32[512,256]{1,0:T(8,128)}, u32[]{:S(2)}, u32[]{:S(2)}) collective-permute-start(f32[512,256]{1,0:T(8,128)} %collective-permute-done), channel_id=1, source_target_pairs={{0,1},{1,0},{2,3},{3,2},{4,5},{5,4},{6,7},{7,6},{8,9},{9,8},{10,11... | collective-permute-start | bytes 1572872 | tf_op jit(solution)/shard_map/while/body/eval_jaxpr/ppermute | solution.py:68
  123.0 2.6 %copy-start.1 = (f32[512,512]{1,0:T(8,128)S(1)}, f32[512,512]{1,0:T(8,128)}, u32[]{:S(2)}) copy-start(f32[512,512]{1,0:T(8,128)} %get-tuple-element.177) | copy-start | bytes 3145732 | tf_op jit(solution)/shard_map/while
Sparse Core Ops, SparseCore 0:
  133.0 43.8 reduce-scatter.1

commit v5 on v1

--- a/solution.py
+++ b/solution.py
@@ -25,8 +25,8 @@
 def dense_hamiltonian(hblocks, slot_index):
     local_blocks = hblocks.shape[0]
     window_blocks = (2 * HW + 1) * A_DEV
-    onehot = (slot_index[:, :, None] == jnp.arange(window_blocks)[None, None, :]).astype(jnp.float32)
-    hd = jnp.einsum("asp,asij->aipj", onehot, hblocks, precision=HI)
+    hits = slot_index[:, :, None] == jnp.arange(window_blocks)[None, None, :]
+    hd = jnp.sum(jnp.where(hits[:, :, None, :, None], hblocks[:, :, :, None, :], 0.0), axis=1)
     return hd.reshape(local_blocks * B, window_blocks * B)
 
 
@@ -74,13 +74,15 @@
     hdense = dense_hamiltonian(hblocks, slot_index)
     previous = subspace
     current = (apply_ham(subspace, hdense) - cheb_center * subspace) / cheb_half
-    for step in range(DEGREE - 1):
+    def cheb_step(step, carry):
+        previous, current = carry
         nextone = (
             2.0 * (apply_ham(current, hdense) - cheb_center * current) / cheb_half
             - previous
         )
-        previous = current
-        current = nextone
+        return (current, nextone)
+
+    previous, current = lax.fori_loop(0, DEGREE - 1, cheb_step, (previous, current))
     total_rows = current.shape[0] * devcount
     gram_term = lax.dot_general(
         current,
@@ -89,7 +91,9 @@
         precision=HI,
         preferred_element_type=jnp.float32,
     )
-    correlation = butterfly_scatter(gram_term, "wide") / total_rows
+    pieces = gram_term.reshape(devcount, -1, gram_term.shape[1])
+    gathered = lax.all_to_all(pieces, "wide", 0, 0, tiled=True)
+    correlation = jnp.sum(gathered, axis=0) / total_rows
     rot_term = jnp.dot(
         current, rotation, precision=HI, preferred_element_type=jnp.float32
     )

time: 166 us -> 181 us (1.090)
  starting transfers between devices: 91.4 us -> 59.7 us
  blocking collectives: 0 us -> 24.1 us
  matrix products: 22.1 us -> 32.2 us
  other arithmetic: 1.49 us -> 9.79 us
  local copies, waits for them, and re-layouts: 3.92 us -> 12 us
  waiting for transfers between devices: 31.7 us -> 27.5 us
    ppermute x6 -> x0, starting transfers between devices: 26.5 us -> none  [butterfly_scatter(): buf = keep + lax.ppermute(send, axis, pairs)]
    all_to_all x0 -> x1, blocking collectives: none -> 24.1 us  [local(): gathered = lax.all_to_all(pieces, 'wide', 0, 0, tiled=True)]
    ppermute x6 -> x0, waiting for transfers between devices: 17.5 us -> none  [butterfly_scatter(): buf = keep + lax.ppermute(send, axis, pairs)]
    reduce_scatter x1, waiting for transfers between devices: 5.28 us -> 22.2 us  [local(): rotated = lax.psum_scatter(rot_term, 'grp', scatter_dimension=1, tiled=True)]
    dot_general x20, matrix products: 12.5 us -> 28.4 us  [apply_ham(): jnp.dot(hdense[:, idx * rows:(idx + 1) * rows], pieces[idx], precision=HI...]
    reduce_sum x0 -> x2, other arithmetic: none -> 8.41 us  [the longest x1 8.32 us: dense_hamiltonian(): jnp.sum(jnp.where(hits[:, :, None, :, None], hblocks[:, :, :, None, :], 0...]
    dot_general x1 -> x0, matrix products: 5.74 us -> none  [dense_hamiltonian(): hd = jnp.einsum('asp,asij->aipj', onehot, hblocks, precision=HI)]
    ppermute x16, starting transfers between devices: 64.8 us -> 59.7 us  [passed_along(): return lax.ppermute(value, axis, pairs)]
  transfers between devices with their start and end apart: 23 -> 17, of which waited for: 13 -> 4; matrix products, arithmetic and copies ran while one was open for 12% -> 24% of each run, Pallas kernels for 0% -> 0%
where the time goes in v5:
time: 181 us; the launch traced here: 180 us
  starting transfers between devices  59.7 us (33%)
  matrix products  32.2 us (18%)
  waiting for transfers between devices  27.5 us (15%)
  blocking collectives  24.1 us (13%)
  between operations  14.2 us (8%)
  local copies, waits for them, and re-layouts  12 us (7%)
  other arithmetic  9.79 us (5%)
    ppermute x16, starting transfers between devices, passed_along(): return lax.ppermute(value, axis, pairs)  59.7 us
    dot_general x20, matrix products, apply_ham(): jnp.dot(hdense[:, idx * rows:(idx + 1) * rows], pieces[idx], precision=HI...  28.4 us
    all_to_all x1, blocking collectives, local(): gathered = lax.all_to_all(pieces, 'wide', 0, 0, tiled=True)  24.1 us
    reduce_scatter x1, waiting for transfers between devices, local(): rotated = lax.psum_scatter(rot_term, 'grp', scatter_dimension=1, tiled=True)  22.2 us
    reduce_sum x1, other arithmetic, dense_hamiltonian(): jnp.sum(jnp.where(hits[:, :, None, :, None], hblocks[:, :, :, None, :], 0...  8.32 us
    ppermute x16, waiting for transfers between devices, passed_along(): return lax.ppermute(value, axis, pairs)  5.3 us
    reduce_sum x1, local copies, waits for them, and re-layouts, dense_hamiltonian(): jnp.sum(jnp.where(hits[:, :, None, :, None], hblocks[:, :, :, None, :], 0...  4.4 us
  transfers between devices with their start and end apart: 17, of which 4 were waited for; matrix products, arithmetic and copies ran while one was open for 24% of the time, Pallas kernels for 0%

profile of v5, /device:TPU:6, one launch (start us, length us, event | category | flops | bytes accessed | tf_op | source)
XLA Modules:
  0.0 179.8 jit_solution(14607421694333319331)
XLA Ops:
  7.2 0.0 copy-start
  7.2 0.0 reduce-scatter.2.cloned.1.call-start
  7.2 1.1 copy.20
  8.3 1.9 %collective-permute-start.4 = (f32[256,256]{1,0:T(8,128)S(1)}, f32[256,256]{1,0:T(8,128)}, u32[]{:S(2)}, u32[]{:S(2)}) collective-permute-start(f32[256,256]{1,0:T(8,128)S(1)} %copy.20), channel_id=1, source_target_pairs={{0,1},{1,2},{2,3},{3,4},{4,5},{5,6},{6,7},{7,8},{8,9},{9,10},{10,1... | collective-permute-start | bytes 786440 | tf_op jit(solution)/shard_map/ppermute | solution.py:22
  10.2 11.2 %collective-permute-start.7 = (f32[256,256]{1,0:T(8,128)S(1)}, f32[256,256]{1,0:T(8,128)S(1)}, u32[]{:S(2)}, u32[]{:S(2)}) collective-permute-start(f32[256,256]{1,0:T(8,128)S(1)} %copy.20), channel_id=1, source_target_pairs={{0,62},{1,63},{2,0},{3,1},{4,2},{5,3},{6,4},{7,5},{8,6},{9,7},{10,... | collective-permute-start | bytes 786440 | tf_op jit(solution)/shard_map/ppermute | solution.py:22
  21.5 1.9 %collective-permute-start.6 = (f32[256,256]{1,0:T(8,128)S(1)}, f32[256,256]{1,0:T(8,128)S(1)}, u32[]{:S(2)}, u32[]{:S(2)}) collective-permute-start(f32[256,256]{1,0:T(8,128)S(1)} %copy.20), channel_id=1, source_target_pairs={{0,2},{1,3},{2,4},{3,5},{4,6},{5,7},{6,8},{7,9},{8,10},{9,11},{10,... | collective-permute-start | bytes 786440 | tf_op jit(solution)/shard_map/ppermute | solution.py:22
  23.4 4.9 %collective-permute-start.5 = (f32[256,256]{1,0:T(8,128)S(1)}, f32[256,256]{1,0:T(8,128)S(1)}, u32[]{:S(2)}, u32[]{:S(2)}) collective-permute-start(f32[256,256]{1,0:T(8,128)S(1)} %copy.20), channel_id=1, source_target_pairs={{0,63},{1,0},{2,1},{3,2},{4,3},{5,4},{6,5},{7,6},{8,7},{9,8},{10,9... | collective-permute-start | bytes 786440 | tf_op jit(solution)/shard_map/ppermute | solution.py:22
  28.3 0.7 fusion.28
  29.0 0.1 iota_compare_fusion
  29.1 8.3 %select_reduce_fusion = f32[4,64,20,64]{3,1,2,0:T(8,128)} fusion(f32[4,16,64,64]{3,2,1,0:T(8,128)} %param.7, pred[4,16,20]{2,1,0:T(8,128)(4,1)S(1)} %iota_compare_fusion), kind=kLoop, calls=%fused_computation.14 | loop fusion | flops 10158080 | bytes 2360576 | tf_op jit(solution)/shard_map/reduce_sum | solution.py:29
  37.4 4.4 %copy.7 = f32[4,64,20,64]{1,0,3,2:T(4,128)} copy(f32[4,64,20,64]{3,1,2,0:T(8,128)} %select_reduce_fusion) | data formatting | bytes 2621440 | tf_op jit(solution)/shard_map/reduce_sum | solution.py:29
  41.8 3.6 %reshape.15 = f32[256,1280]{0,1:T(8,128)} reshape(f32[4,64,20,64]{1,0,3,2:T(4,128)} %copy.7) | data formatting | bytes 2621440 | tf_op jit(solution)/shard_map/reshape | solution.py:30
  45.4 1.5 fusion.22
  46.9 2.8 %copy.8 = f32[256,1280]{1,0:T(8,128)} copy(f32[256,1280]{0,1:T(8,128)} %reshape.15) | data formatting | bytes 2621440 | tf_op jit(solution)/shard_map/while | solution.py:85
  49.7 0.0 collective-permute-done.7
  49.7 1.5 fusion.16
  51.3 0.0 collective-permute-done.6
  51.3 1.5 fusion.18
  52.8 1.6 convolution_add_fusion.3
  54.5 0.0 collective-permute-done.5
  54.5 1.6 fusion.15
  56.1 66.0 %while.14 = (s32[]{:T(128)}, f32[256,256]{1,0:T(8,128)S(1)}, f32[256,256]{1,0:T(8,128)S(1)}, f32[256,1280]{1,0:T(8,128)}, s32[]{:T(128)}) while((s32[]{:T(128)}, f32[256,256]{1,0:T(8,128)S(1)}, f32[256,256]{1,0:T(8,128)S(1)}, f32[256,1280]{1,0:T(8,128)}, s32[]{:T(128)}) %tuple.32), condition=%wide.region_2.3_spmd, body=%wide.region_1.2_spmd.sunk | while | flops 1007091712 | bytes 10748125 | solution.py:85
  56.1 3.0 %collective-permute-start = (f32[256,256]{1,0:T(8,128)S(1)}, f32[256,256]{1,0:T(8,128)S(1)}, u32[]{:S(2)}, u32[]{:S(2)}) collective-permute-start(f32[256,256]{1,0:T(8,128)S(1)} %copy.14), channel_id=1, source_target_pairs={{0,62},{1,63},{2,0},{3,1},{4,2},{5,3},{6,4},{7,5},{8,6},{9,7},{10,... | collective-permute-start | bytes 786440 | tf_op jit(solution)/shard_map/while/body/eval_jaxpr/ppermute | solution.py:22
  59.1 2.1 %collective-permute-start.2 = (f32[256,256]{1,0:T(8,128)S(1)}, f32[256,256]{1,0:T(8,128)}, u32[]{:S(2)}, u32[]{:S(2)}) collective-permute-start(f32[256,256]{1,0:T(8,128)S(1)} %copy.14), channel_id=1, source_target_pairs={{0,1},{1,2},{2,3},{3,4},{4,5},{5,6},{6,7},{7,8},{8,9},{9,10},{10,1... | collective-permute-start | bytes 786440 | tf_op jit(solution)/shard_map/while/body/eval_jaxpr/ppermute | solution.py:22
  61.3 2.6 %collective-permute-start.1 = (f32[256,256]{1,0:T(8,128)S(1)}, f32[256,256]{1,0:T(8,128)S(1)}, u32[]{:S(2)}, u32[]{:S(2)}) collective-permute-start(f32[256,256]{1,0:T(8,128)S(1)} %copy.14), channel_id=1, source_target_pairs={{0,2},{1,3},{2,4},{3,5},{4,6},{5,7},{6,8},{7,9},{8,10},{9,11},{10,... | collective-permute-start | bytes 786440 | tf_op jit(solution)/shard_map/while/body/eval_jaxpr/ppermute | solution.py:22
  63.9 5.5 %collective-permute-start.3 = (f32[256,256]{1,0:T(8,128)S(1)}, f32[256,256]{1,0:T(8,128)}, u32[]{:S(2)}, u32[]{:S(2)}) collective-permute-start(f32[256,256]{1,0:T(8,128)S(1)} %copy.14), channel_id=1, source_target_pairs={{0,63},{1,0},{2,1},{3,2},{4,3},{5,4},{6,5},{7,6},{8,7},{9,8},{10,9... | collective-permute-start | bytes 786440 | tf_op jit(solution)/shard_map/while/body/eval_jaxpr/ppermute | solution.py:22
  69.4 1.3 fusion.72
  70.7 1.3 fusion.70
  72.0 2.5 %collective-permute-done.1 = f32[256,256]{1,0:T(8,128)S(1)} collective-permute-done((f32[256,256]{1,0:T(8,128)S(1)}, f32[256,256]{1,0:T(8,128)S(1)}, u32[]{:S(2)}, u32[]{:S(2)}) %collective-permute-start.1) | collective-permute-done | bytes 262176 | tf_op jit(solution)/shard_map/while/body/eval_jaxpr/ppermute | solution.py:22
  74.5 1.3 fusion.71
  75.9 0.0 collective-permute-done.2
  75.9 1.4 convolution_add_fusion.5
  77.3 1.5 fusion.73
  78.8 1.9 %collective-permute-start = (f32[256,256]{1,0:T(8,128)S(1)}, f32[256,256]{1,0:T(8,128)S(1)}, u32[]{:S(2)}, u32[]{:S(2)}) collective-permute-start(f32[256,256]{1,0:T(8,128)S(1)} %copy.14), channel_id=1, source_target_pairs={{0,62},{1,63},{2,0},{3,1},{4,2},{5,3},{6,4},{7,5},{8,6},{9,7},{10,... | collective-permute-start | bytes 786440 | tf_op jit(solution)/shard_map/while/body/eval_jaxpr/ppermute | solution.py:22
  80.8 2.1 %collective-permute-start.2 = (f32[256,256]{1,0:T(8,128)S(1)}, f32[256,256]{1,0:T(8,128)}, u32[]{:S(2)}, u32[]{:S(2)}) collective-permute-start(f32[256,256]{1,0:T(8,128)S(1)} %copy.14), channel_id=1, source_target_pairs={{0,1},{1,2},{2,3},{3,4},{4,5},{5,6},{6,7},{7,8},{8,9},{9,10},{10,1... | collective-permute-start | bytes 786440 | tf_op jit(solution)/shard_map/while/body/eval_jaxpr/ppermute | solution.py:22
  82.8 3.8 %collective-permute-start.1 = (f32[256,256]{1,0:T(8,128)S(1)}, f32[256,256]{1,0:T(8,128)S(1)}, u32[]{:S(2)}, u32[]{:S(2)}) collective-permute-start(f32[256,256]{1,0:T(8,128)S(1)} %copy.14), channel_id=1, source_target_pairs={{0,2},{1,3},{2,4},{3,5},{4,6},{5,7},{6,8},{7,9},{8,10},{9,11},{10,... | collective-permute-start | bytes 786440 | tf_op jit(solution)/shard_map/while/body/eval_jaxpr/ppermute | solution.py:22
  86.6 5.5 %collective-permute-start.3 = (f32[256,256]{1,0:T(8,128)S(1)}, f32[256,256]{1,0:T(8,128)}, u32[]{:S(2)}, u32[]{:S(2)}) collective-permute-start(f32[256,256]{1,0:T(8,128)S(1)} %copy.14), channel_id=1, source_target_pairs={{0,63},{1,0},{2,1},{3,2},{4,3},{5,4},{6,5},{7,6},{8,7},{9,8},{10,9... | collective-permute-start | bytes 786440 | tf_op jit(solution)/shard_map/while/body/eval_jaxpr/ppermute | solution.py:22
  92.1 1.3 fusion.72
  93.5 1.3 fusion.70
  94.8 0.6 collective-permute-done.1
  95.3 1.3 fusion.71
  96.7 0.0 collective-permute-done.2
  96.7 1.4 convolution_add_fusion.5
  98.1 0.0 collective-permute-done.3
  98.1 1.5 fusion.73
  99.6 1.9 %collective-permute-start = (f32[256,256]{1,0:T(8,128)S(1)}, f32[256,256]{1,0:T(8,128)S(1)}, u32[]{:S(2)}, u32[]{:S(2)}) collective-permute-start(f32[256,256]{1,0:T(8,128)S(1)} %copy.14), channel_id=1, source_target_pairs={{0,62},{1,63},{2,0},{3,1},{4,2},{5,3},{6,4},{7,5},{8,6},{9,7},{10,... | collective-permute-start | bytes 786440 | tf_op jit(solution)/shard_map/while/body/eval_jaxpr/ppermute | solution.py:22
  101.6 4.0 %collective-permute-start.2 = (f32[256,256]{1,0:T(8,128)S(1)}, f32[256,256]{1,0:T(8,128)}, u32[]{:S(2)}, u32[]{:S(2)}) collective-permute-start(f32[256,256]{1,0:T(8,128)S(1)} %copy.14), channel_id=1, source_target_pairs={{0,1},{1,2},{2,3},{3,4},{4,5},{5,6},{6,7},{7,8},{8,9},{9,10},{10,1... | collective-permute-start | bytes 786440 | tf_op jit(solution)/shard_map/while/body/eval_jaxpr/ppermute | solution.py:22
  105.6 2.2 %collective-permute-start.1 = (f32[256,256]{1,0:T(8,128)S(1)}, f32[256,256]{1,0:T(8,128)S(1)}, u32[]{:S(2)}, u32[]{:S(2)}) collective-permute-start(f32[256,256]{1,0:T(8,128)S(1)} %copy.14), channel_id=1, source_target_pairs={{0,2},{1,3},{2,4},{3,5},{4,6},{5,7},{6,8},{7,9},{8,10},{9,11},{10,... | collective-permute-start | bytes 786440 | tf_op jit(solution)/shard_map/while/body/eval_jaxpr/ppermute | solution.py:22
  107.8 5.1 %collective-permute-start.3 = (f32[256,256]{1,0:T(8,128)S(1)}, f32[256,256]{1,0:T(8,128)}, u32[]{:S(2)}, u32[]{:S(2)}) collective-permute-start(f32[256,256]{1,0:T(8,128)S(1)} %copy.14), channel_id=1, source_target_pairs={{0,63},{1,0},{2,1},{3,2},{4,3},{5,4},{6,5},{7,6},{8,7},{9,8},{10,9... | collective-permute-start | bytes 786440 | tf_op jit(solution)/shard_map/while/body/eval_jaxpr/ppermute | solution.py:22
  112.9 1.3 fusion.72
  114.3 1.3 fusion.70
  115.6 2.2 %collective-permute-done.1 = f32[256,256]{1,0:T(8,128)S(1)} collective-permute-done((f32[256,256]{1,0:T(8,128)S(1)}, f32[256,256]{1,0:T(8,128)S(1)}, u32[]{:S(2)}, u32[]{:S(2)}) %collective-permute-start.1) | collective-permute-done | bytes 262176 | tf_op jit(solution)/shard_map/while/body/eval_jaxpr/ppermute | solution.py:22
  117.8 1.3 fusion.71
  119.2 0.0 collective-permute-done.2
  119.2 1.4 convolution_add_fusion.5
  120.6 1.5 fusion.73
  122.1 3.2 %fusion.30 = f32[256,2048]{1,0:T(8,128)} fusion(f32[256,256]{1,0:T(8,128)S(1)} %get-tuple-element.55, f32[256,2048]{1,0:T(8,128)S(1)} %copy-done), kind=kOutput, calls=%fused_computation.46 | convolution fusion | flops 1610612736 | bytes 4456448 | tf_op jit(solution)/shard_map/dot_general | solution.py:97
  125.4 0.0 reduce-scatter.2.cloned.1.call-update
  125.4 0.6 fusion.31
  126.0 0.1 reshape.16
  126.1 24.1 %all_to_all.5 = f32[64,4,256]{2,1,0:T(4,128)S(1)} all-to-all(f32[64,4,256]{2,1,0:T(4,128)S(1)} %reshape.16), channel_id=1, replica_groups=mesh['grp'=8,'wide'=64] {'wide'}, dimensions={0} | all-to-all | bytes 524288 | tf_op jit(solution)/shard_map/all_to_all | solution.py:95
  150.1 0.1 reduce_sum.19
  150.2 0.6 broadcast_multiply_fusion
  150.8 22.2 %reduce-scatter.2.cloned.1.call-done = f32[256,256]{1,0:T(8,128)} async-done(((f32[256,2048]{1,0:T(8,128)}), f32[256,256]{1,0:T(8,128)}) %reduce-scatter.2.cloned.1.call-update) | async-done | bytes 262160 | tf_op jit(solution)/shard_map/reduce_scatter | solution.py:100
  (13 shorter events, 0.1 us)
Async XLA Ops:
  7.2 114.9 %copy-start = (f32[256,2048]{1,0:T(8,128)S(1)}, f32[256,2048]{1,0:T(8,128)}, u32[]{:S(2)}) copy-start(f32[256,2048]{1,0:T(8,128)} %param.9) | copy-start | bytes 6291460
  7.2 165.8 %reduce-scatter.2.cloned.1.call-start = ((), (), s32[]{:S(2)}) async-start(), calls=%async_computation.2 | async-start | bytes 2359296 | tf_op jit(solution)/shard_map/reduce_scatter | solution.py:100
  8.3 44.5 %collective-permute-start.4 = (f32[256,256]{1,0:T(8,128)S(1)}, f32[256,256]{1,0:T(8,128)}, u32[]{:S(2)}, u32[]{:S(2)}) collective-permute-start(f32[256,256]{1,0:T(8,128)S(1)} %copy.20), channel_id=1, source_target_pairs={{0,1},{1,2},{2,3},{3,4},{4,5},{5,6},{6,7},{7,8},{8,9},{9,10},{10,1... | collective-permute-start | bytes 786440 | tf_op jit(solution)/shard_map/ppermute | solution.py:22
  10.2 39.5 %collective-permute-start.7 = (f32[256,256]{1,0:T(8,128)S(1)}, f32[256,256]{1,0:T(8,128)S(1)}, u32[]{:S(2)}, u32[]{:S(2)}) collective-permute-start(f32[256,256]{1,0:T(8,128)S(1)} %copy.20), channel_id=1, source_target_pairs={{0,62},{1,63},{2,0},{3,1},{4,2},{5,3},{6,4},{7,5},{8,6},{9,7},{10,... | collective-permute-start | bytes 786440 | tf_op jit(solution)/shard_map/ppermute | solution.py:22
  21.5 29.8 %collective-permute-start.6 = (f32[256,256]{1,0:T(8,128)S(1)}, f32[256,256]{1,0:T(8,128)S(1)}, u32[]{:S(2)}, u32[]{:S(2)}) collective-permute-start(f32[256,256]{1,0:T(8,128)S(1)} %copy.20), channel_id=1, source_target_pairs={{0,2},{1,3},{2,4},{3,5},{4,6},{5,7},{6,8},{7,9},{8,10},{9,11},{10,... | collective-permute-start | bytes 786440 | tf_op jit(solution)/shard_map/ppermute | solution.py:22
  23.4 31.1 %collective-permute-start.5 = (f32[256,256]{1,0:T(8,128)S(1)}, f32[256,256]{1,0:T(8,128)S(1)}, u32[]{:S(2)}, u32[]{:S(2)}) collective-permute-start(f32[256,256]{1,0:T(8,128)S(1)} %copy.20), channel_id=1, source_target_pairs={{0,63},{1,0},{2,1},{3,2},{4,3},{5,4},{6,5},{7,6},{8,7},{9,8},{10,9... | collective-permute-start | bytes 786440 | tf_op jit(solution)/shard_map/ppermute | solution.py:22
  56.1 14.6 %collective-permute-start = (f32[256,256]{1,0:T(8,128)S(1)}, f32[256,256]{1,0:T(8,128)S(1)}, u32[]{:S(2)}, u32[]{:S(2)}) collective-permute-start(f32[256,256]{1,0:T(8,128)S(1)} %copy.14), channel_id=1, source_target_pairs={{0,62},{1,63},{2,0},{3,1},{4,2},{5,3},{6,4},{7,5},{8,6},{9,7},{10,... | collective-permute-start | bytes 786440 | tf_op jit(solution)/shard_map/while/body/eval_jaxpr/ppermute | solution.py:22
  59.1 16.7 %collective-permute-start.2 = (f32[256,256]{1,0:T(8,128)S(1)}, f32[256,256]{1,0:T(8,128)}, u32[]{:S(2)}, u32[]{:S(2)}) collective-permute-start(f32[256,256]{1,0:T(8,128)S(1)} %copy.14), channel_id=1, source_target_pairs={{0,1},{1,2},{2,3},{3,4},{4,5},{5,6},{6,7},{7,8},{8,9},{9,10},{10,1... | collective-permute-start | bytes 786440 | tf_op jit(solution)/shard_map/while/body/eval_jaxpr/ppermute | solution.py:22
  61.3 13.2 %collective-permute-start.1 = (f32[256,256]{1,0:T(8,128)S(1)}, f32[256,256]{1,0:T(8,128)S(1)}, u32[]{:S(2)}, u32[]{:S(2)}) collective-permute-start(f32[256,256]{1,0:T(8,128)S(1)} %copy.14), channel_id=1, source_target_pairs={{0,2},{1,3},{2,4},{3,5},{4,6},{5,7},{6,8},{7,9},{8,10},{9,11},{10,... | collective-permute-start | bytes 786440 | tf_op jit(solution)/shard_map/while/body/eval_jaxpr/ppermute | solution.py:22
  63.9 13.4 %collective-permute-start.3 = (f32[256,256]{1,0:T(8,128)S(1)}, f32[256,256]{1,0:T(8,128)}, u32[]{:S(2)}, u32[]{:S(2)}) collective-permute-start(f32[256,256]{1,0:T(8,128)S(1)} %copy.14), channel_id=1, source_target_pairs={{0,63},{1,0},{2,1},{3,2},{4,3},{5,4},{6,5},{7,6},{8,7},{9,8},{10,9... | collective-permute-start | bytes 786440 | tf_op jit(solution)/shard_map/while/body/eval_jaxpr/ppermute | solution.py:22
  78.8 14.6 %collective-permute-start = (f32[256,256]{1,0:T(8,128)S(1)}, f32[256,256]{1,0:T(8,128)S(1)}, u32[]{:S(2)}, u32[]{:S(2)}) collective-permute-start(f32[256,256]{1,0:T(8,128)S(1)} %copy.14), channel_id=1, source_target_pairs={{0,62},{1,63},{2,0},{3,1},{4,2},{5,3},{6,4},{7,5},{8,6},{9,7},{10,... | collective-permute-start | bytes 786440 | tf_op jit(solution)/shard_map/while/body/eval_jaxpr/ppermute | solution.py:22
  80.8 15.9 %collective-permute-start.2 = (f32[256,256]{1,0:T(8,128)S(1)}, f32[256,256]{1,0:T(8,128)}, u32[]{:S(2)}, u32[]{:S(2)}) collective-permute-start(f32[256,256]{1,0:T(8,128)S(1)} %copy.14), channel_id=1, source_target_pairs={{0,1},{1,2},{2,3},{3,4},{4,5},{5,6},{6,7},{7,8},{8,9},{9,10},{10,1... | collective-permute-start | bytes 786440 | tf_op jit(solution)/shard_map/while/body/eval_jaxpr/ppermute | solution.py:22
  82.8 12.5 %collective-permute-start.1 = (f32[256,256]{1,0:T(8,128)S(1)}, f32[256,256]{1,0:T(8,128)S(1)}, u32[]{:S(2)}, u32[]{:S(2)}) collective-permute-start(f32[256,256]{1,0:T(8,128)S(1)} %copy.14), channel_id=1, source_target_pairs={{0,2},{1,3},{2,4},{3,5},{4,6},{5,7},{6,8},{7,9},{8,10},{9,11},{10,... | collective-permute-start | bytes 786440 | tf_op jit(solution)/shard_map/while/body/eval_jaxpr/ppermute | solution.py:22
  86.6 11.5 %collective-permute-start.3 = (f32[256,256]{1,0:T(8,128)S(1)}, f32[256,256]{1,0:T(8,128)}, u32[]{:S(2)}, u32[]{:S(2)}) collective-permute-start(f32[256,256]{1,0:T(8,128)S(1)} %copy.14), channel_id=1, source_target_pairs={{0,63},{1,0},{2,1},{3,2},{4,3},{5,4},{6,5},{7,6},{8,7},{9,8},{10,9... | collective-permute-start | bytes 786440 | tf_op jit(solution)/shard_map/while/body/eval_jaxpr/ppermute | solution.py:22
  99.6 14.6 %collective-permute-start = (f32[256,256]{1,0:T(8,128)S(1)}, f32[256,256]{1,0:T(8,128)S(1)}, u32[]{:S(2)}, u32[]{:S(2)}) collective-permute-start(f32[256,256]{1,0:T(8,128)S(1)} %copy.14), channel_id=1, source_target_pairs={{0,62},{1,63},{2,0},{3,1},{4,2},{5,3},{6,4},{7,5},{8,6},{9,7},{10,... | collective-permute-start | bytes 786440 | tf_op jit(solution)/shard_map/while/body/eval_jaxpr/ppermute | solution.py:22
  101.6 17.6 %collective-permute-start.2 = (f32[256,256]{1,0:T(8,128)S(1)}, f32[256,256]{1,0:T(8,128)}, u32[]{:S(2)}, u32[]{:S(2)}) collective-permute-start(f32[256,256]{1,0:T(8,128)S(1)} %copy.14), channel_id=1, source_target_pairs={{0,1},{1,2},{2,3},{3,4},{4,5},{5,6},{6,7},{7,8},{8,9},{9,10},{10,1... | collective-permute-start | bytes 786440 | tf_op jit(solution)/shard_map/while/body/eval_jaxpr/ppermute | solution.py:22
  105.6 12.3 %collective-permute-start.1 = (f32[256,256]{1,0:T(8,128)S(1)}, f32[256,256]{1,0:T(8,128)S(1)}, u32[]{:S(2)}, u32[]{:S(2)}) collective-permute-start(f32[256,256]{1,0:T(8,128)S(1)} %copy.14), channel_id=1, source_target_pairs={{0,2},{1,3},{2,4},{3,5},{4,6},{5,7},{6,8},{7,9},{8,10},{9,11},{10,... | collective-permute-start | bytes 786440 | tf_op jit(solution)/shard_map/while/body/eval_jaxpr/ppermute | solution.py:22
  107.8 12.8 %collective-permute-start.3 = (f32[256,256]{1,0:T(8,128)S(1)}, f32[256,256]{1,0:T(8,128)}, u32[]{:S(2)}, u32[]{:S(2)}) collective-permute-start(f32[256,256]{1,0:T(8,128)S(1)} %copy.14), channel_id=1, source_target_pairs={{0,63},{1,0},{2,1},{3,2},{4,3},{5,4},{6,5},{7,6},{8,7},{9,8},{10,9... | collective-permute-start | bytes 786440 | tf_op jit(solution)/shard_map/while/body/eval_jaxpr/ppermute | solution.py:22
Sparse Core Ops, SparseCore 0:
  125.5 47.4 reduce-scatter.1

commit v6 on v1

--- a/solution.py
+++ b/solution.py
@@ -47,24 +47,6 @@
     return total
 
 
-def butterfly_scatter(value, axis):
-    count = lax.axis_size(axis)
-    me = lax.axis_index(axis)
-    piece = value.shape[0] // count
-    buf = value.reshape((count, piece) + value.shape[1:])
-    bit = 0
-    while (1 << bit) < count:
-        n = buf.shape[0]
-        buf = buf.reshape((n // 2, 2) + buf.shape[1:])
-        mine = (me >> bit) & 1
-        keep = jnp.where(mine == 0, buf[:, 0], buf[:, 1])
-        send = jnp.where(mine == 0, buf[:, 1], buf[:, 0])
-        pairs = [(i, i ^ (1 << bit)) for i in range(count)]
-        buf = keep + lax.ppermute(send, axis, pairs)
-        bit += 1
-    return buf.reshape((piece,) + value.shape[1:])
-
-
 def local(subspace, hblocks, pattern, rotation):
     devcount = lax.axis_size("wide")
     myself = lax.axis_index("wide")
@@ -89,7 +71,9 @@
         precision=HI,
         preferred_element_type=jnp.float32,
     )
-    correlation = butterfly_scatter(gram_term, "wide") / total_rows
+    pieces = gram_term.reshape(devcount, -1, gram_term.shape[1])
+    gathered = lax.all_to_all(pieces, "wide", 0, 0, tiled=True)
+    correlation = jnp.sum(gathered, axis=0) / total_rows
     rot_term = jnp.dot(
         current, rotation, precision=HI, preferred_element_type=jnp.float32
     )

time: 166 us -> 166 us (level)
  blocking collectives: 0 us -> 28.3 us
  starting transfers between devices: 91.4 us -> 64.8 us
    all_to_all x0 -> x1, blocking collectives: none -> 28.3 us  [local(): gathered = lax.all_to_all(pieces, 'wide', 0, 0, tiled=True)]
    ppermute x6 -> x0, starting transfers between devices: 26.5 us -> none  [butterfly_scatter(): buf = keep + lax.ppermute(send, axis, pairs)]
    ppermute x6 -> x0, waiting for transfers between devices: 17.5 us -> none  [butterfly_scatter(): buf = keep + lax.ppermute(send, axis, pairs)]
    reduce_scatter x1, waiting for transfers between devices: 5.28 us -> 21.4 us  [local(): rotated = lax.psum_scatter(rot_term, 'grp', scatter_dimension=1, tiled=True)]
  transfers between devices with their start and end apart: 23 -> 17, of which waited for: 13 -> 7; matrix products, arithmetic and copies ran while one was open for 12% -> 12% of each run, Pallas kernels for 0% -> 0%
where the time goes in v6:
time: 166 us; the launch traced here: 165 us
  starting transfers between devices  64.8 us (39%)
  waiting for transfers between devices  30.3 us (18%)
  blocking collectives  28.3 us (17%)
  matrix products  22.1 us (13%)
  between operations  14.5 us (9%)
  local copies, waits for them, and re-layouts  3.95 us (2%)
    ppermute x16, starting transfers between devices, passed_along(): return lax.ppermute(value, axis, pairs)  64.8 us
    all_to_all x1, blocking collectives, local(): gathered = lax.all_to_all(pieces, 'wide', 0, 0, tiled=True)  28.3 us
    reduce_scatter x1, waiting for transfers between devices, local(): rotated = lax.psum_scatter(rot_term, 'grp', scatter_dimension=1, tiled=True)  21.4 us
    dot_general x20, matrix products, apply_ham(): jnp.dot(hdense[:, idx * rows:(idx + 1) * rows], pieces[idx], precision=HI...  12.5 us
    ppermute x16, waiting for transfers between devices, passed_along(): return lax.ppermute(value, axis, pairs)  8.9 us
    dot_general x1, matrix products, dense_hamiltonian(): hd = jnp.einsum('asp,asij->aipj', onehot, hblocks, precision=HI)  5.76 us
  transfers between devices with their start and end apart: 17, of which 7 were waited for; matrix products, arithmetic and copies ran while one was open for 12% of the time, Pallas kernels for 0%

profile of v6, /device:TPU:6, one launch (start us, length us, event | category | flops | bytes accessed | tf_op | source)
XLA Modules:
  0.0 165.3 jit_solution(1314641378179955460)
XLA Ops:
  7.2 0.0 copy-start
  7.2 0.0 reduce-scatter.2.cloned.1.call-start
  7.2 2.1 %collective-permute-start = (f32[256,256]{1,0:T(8,128)}, f32[256,256]{1,0:T(8,128)}, u32[]{:S(2)}, u32[]{:S(2)}) collective-permute-start(f32[256,256]{1,0:T(8,128)} %param.4), channel_id=1, source_target_pairs={{0,1},{1,2},{2,3},{3,4},{4,5},{5,6},{6,7},{7,8},{8,9},{9,10},{10,1... | collective-permute-start | bytes 786440 | tf_op jit(solution)/shard_map/ppermute | solution.py:22
  9.3 11.2 %collective-permute-start.3 = (f32[256,256]{1,0:T(8,128)}, f32[256,256]{1,0:T(8,128)}, u32[]{:S(2)}, u32[]{:S(2)}) collective-permute-start(f32[256,256]{1,0:T(8,128)} %param.4), channel_id=1, source_target_pairs={{0,62},{1,63},{2,0},{3,1},{4,2},{5,3},{6,4},{7,5},{8,6},{9,7},{10,... | collective-permute-start | bytes 786440 | tf_op jit(solution)/shard_map/ppermute | solution.py:22
  20.5 1.9 %collective-permute-start.2 = (f32[256,256]{1,0:T(8,128)}, f32[256,256]{1,0:T(8,128)}, u32[]{:S(2)}, u32[]{:S(2)}) collective-permute-start(f32[256,256]{1,0:T(8,128)} %param.4), channel_id=1, source_target_pairs={{0,2},{1,3},{2,4},{3,5},{4,6},{5,7},{6,8},{7,9},{8,10},{9,11},{10,... | collective-permute-start | bytes 786440 | tf_op jit(solution)/shard_map/ppermute | solution.py:22
  22.4 4.9 %collective-permute-start.1 = (f32[256,256]{1,0:T(8,128)}, f32[256,256]{1,0:T(8,128)}, u32[]{:S(2)}, u32[]{:S(2)}) collective-permute-start(f32[256,256]{1,0:T(8,128)} %param.4), channel_id=1, source_target_pairs={{0,63},{1,0},{2,1},{3,2},{4,3},{5,4},{6,5},{7,6},{8,7},{9,8},{10,9... | collective-permute-start | bytes 786440 | tf_op jit(solution)/shard_map/ppermute | solution.py:22
  27.4 0.7 fusion.59
  28.1 5.8 %fusion.2 = f32[4,64,20,64]{3,2,1,0:T(8,128)} fusion(f32[4,16,64,64]{3,2,1,0:T(8,128)} %param.5, s32[4,16]{1,0:T(4,128)S(1)} %fusion.59), kind=kOutput, calls=%fused_computation.2 | convolution fusion | flops 62915840 | bytes 2359552 | tf_op jit(solution)/shard_map/asp,asij->aipj/dot_general | solution.py:29
  33.8 2.2 %reshape.14 = f32[256,1280]{1,0:T(8,128)S(1)} reshape(f32[4,64,20,64]{3,2,1,0:T(8,128)} %fusion.2) | data formatting | bytes 2621440 | tf_op jit(solution)/shard_map/reshape | solution.py:30
  36.1 1.3 fusion.48
  37.4 0.0 copy-start.3
  37.4 0.0 collective-permute-done.3
  37.4 1.4 fusion.24
  38.8 0.0 collective-permute-done.2
  38.8 1.3 fusion.32
  40.2 1.3 convolution_add_fusion.7
  41.5 1.4 broadcast_multiply_fusion
  42.9 1.9 %collective-permute-start.6 = (f32[256,256]{1,0:T(8,128)S(1)}, f32[256,256]{1,0:T(8,128)S(1)}, u32[]{:S(2)}, u32[]{:S(2)}) collective-permute-start(f32[256,256]{1,0:T(8,128)S(1)} %get-tuple-element.2), channel_id=1, source_target_pairs={{0,2},{1,3},{2,4},{3,5},{4,6},{5,7},{6,8},{7,9},{8,10},{9,11},{10,... | collective-permute-start | bytes 786440 | tf_op jit(solution)/shard_map/ppermute | solution.py:22
  44.8 1.9 %collective-permute-start.4 = (f32[256,256]{1,0:T(8,128)S(1)}, f32[256,256]{1,0:T(8,128)S(1)}, u32[]{:S(2)}, u32[]{:S(2)}) collective-permute-start(f32[256,256]{1,0:T(8,128)S(1)} %get-tuple-element.2), channel_id=1, source_target_pairs={{0,1},{1,2},{2,3},{3,4},{4,5},{5,6},{6,7},{7,8},{8,9},{9,10},{10,1... | collective-permute-start | bytes 786440 | tf_op jit(solution)/shard_map/ppermute | solution.py:22
  46.7 6.0 %collective-permute-start.7 = (f32[256,256]{1,0:T(8,128)S(1)}, f32[256,256]{1,0:T(8,128)S(1)}, u32[]{:S(2)}, u32[]{:S(2)}) collective-permute-start(f32[256,256]{1,0:T(8,128)S(1)} %get-tuple-element.2), channel_id=1, source_target_pairs={{0,62},{1,63},{2,0},{3,1},{4,2},{5,3},{6,4},{7,5},{8,6},{9,7},{10,... | collective-permute-start | bytes 786440 | tf_op jit(solution)/shard_map/ppermute | solution.py:22
  52.8 3.4 %collective-permute-start.5 = (f32[256,256]{1,0:T(8,128)S(1)}, f32[256,256]{1,0:T(8,128)S(1)}, u32[]{:S(2)}, u32[]{:S(2)}) collective-permute-start(f32[256,256]{1,0:T(8,128)S(1)} %get-tuple-element.2), channel_id=1, source_target_pairs={{0,63},{1,0},{2,1},{3,2},{4,3},{5,4},{6,5},{7,6},{8,7},{9,8},{10,9... | collective-permute-start | bytes 786440 | tf_op jit(solution)/shard_map/ppermute | solution.py:22
  56.1 0.4 fusion.46
  56.6 0.4 fusion.30
  56.9 1.7 %collective-permute-done.7 = f32[256,256]{1,0:T(8,128)S(1)} collective-permute-done((f32[256,256]{1,0:T(8,128)S(1)}, f32[256,256]{1,0:T(8,128)S(1)}, u32[]{:S(2)}, u32[]{:S(2)}) %collective-permute-start.7) | collective-permute-done | bytes 262176 | tf_op jit(solution)/shard_map/ppermute | solution.py:22
  58.6 0.4 fusion.22
  59.0 0.0 collective-permute-done.4
  59.0 0.4 convolution_add_fusion.5
  59.4 2.0 %collective-permute-done.5 = f32[256,256]{1,0:T(8,128)S(1)} collective-permute-done((f32[256,256]{1,0:T(8,128)S(1)}, f32[256,256]{1,0:T(8,128)S(1)}, u32[]{:S(2)}, u32[]{:S(2)}) %collective-permute-start.5) | collective-permute-done | bytes 262176 | tf_op jit(solution)/shard_map/ppermute | solution.py:22
  61.4 0.4 fusion.13
  61.8 1.9 %collective-permute-start.10 = (f32[256,256]{1,0:T(8,128)S(1)}, f32[256,256]{1,0:T(8,128)S(1)}, u32[]{:S(2)}, u32[]{:S(2)}) collective-permute-start(f32[256,256]{1,0:T(8,128)S(1)} %fusion.13), channel_id=1, source_target_pairs={{0,2},{1,3},{2,4},{3,5},{4,6},{5,7},{6,8},{7,9},{8,10},{9,11},{10,... | collective-permute-start | bytes 786440 | tf_op jit(solution)/shard_map/ppermute | solution.py:22
  63.8 6.0 %collective-permute-start.11 = (f32[256,256]{1,0:T(8,128)S(1)}, f32[256,256]{1,0:T(8,128)S(1)}, u32[]{:S(2)}, u32[]{:S(2)}) collective-permute-start(f32[256,256]{1,0:T(8,128)S(1)} %fusion.13), channel_id=1, source_target_pairs={{0,62},{1,63},{2,0},{3,1},{4,2},{5,3},{6,4},{7,5},{8,6},{9,7},{10,... | collective-permute-start | bytes 786440 | tf_op jit(solution)/shard_map/ppermute | solution.py:22
  69.8 0.4 fusion.44
  70.2 1.9 %collective-permute-start.8 = (f32[256,256]{1,0:T(8,128)S(1)}, f32[256,256]{1,0:T(8,128)S(1)}, u32[]{:S(2)}, u32[]{:S(2)}) collective-permute-start(f32[256,256]{1,0:T(8,128)S(1)} %fusion.13), channel_id=1, source_target_pairs={{0,1},{1,2},{2,3},{3,4},{4,5},{5,6},{6,7},{7,8},{8,9},{9,10},{10,1... | collective-permute-start | bytes 786440 | tf_op jit(solution)/shard_map/ppermute | solution.py:22
  72.1 5.8 %collective-permute-start.9 = (f32[256,256]{1,0:T(8,128)S(1)}, f32[256,256]{1,0:T(8,128)S(1)}, u32[]{:S(2)}, u32[]{:S(2)}) collective-permute-start(f32[256,256]{1,0:T(8,128)S(1)} %fusion.13), channel_id=1, source_target_pairs={{0,63},{1,0},{2,1},{3,2},{4,3},{5,4},{6,5},{7,6},{8,7},{9,8},{10,9... | collective-permute-start | bytes 786440 | tf_op jit(solution)/shard_map/ppermute | solution.py:22
  77.9 0.0 collective-permute-done.10
  77.9 0.4 fusion.28
  78.3 0.0 collective-permute-done.11
  78.3 0.4 fusion.20
  78.7 1.3 collective-permute-done.8
  80.0 0.4 convolution_add_fusion.3
  80.4 1.4 collective-permute-done.9
  81.7 0.4 fusion.16
  82.2 1.9 %collective-permute-start.14 = (f32[256,256]{1,0:T(8,128)S(1)}, f32[256,256]{1,0:T(8,128)S(1)}, u32[]{:S(2)}, u32[]{:S(2)}) collective-permute-start(f32[256,256]{1,0:T(8,128)S(1)} %fusion.16), channel_id=1, source_target_pairs={{0,2},{1,3},{2,4},{3,5},{4,6},{5,7},{6,8},{7,9},{8,10},{9,11},{10,... | collective-permute-start | bytes 786440 | tf_op jit(solution)/shard_map/ppermute | solution.py:22
  84.1 6.0 %collective-permute-start.15 = (f32[256,256]{1,0:T(8,128)S(1)}, f32[256,256]{1,0:T(8,128)S(1)}, u32[]{:S(2)}, u32[]{:S(2)}) collective-permute-start(f32[256,256]{1,0:T(8,128)S(1)} %fusion.16), channel_id=1, source_target_pairs={{0,62},{1,63},{2,0},{3,1},{4,2},{5,3},{6,4},{7,5},{8,6},{9,7},{10,... | collective-permute-start | bytes 786440 | tf_op jit(solution)/shard_map/ppermute | solution.py:22
  90.1 0.4 fusion.50
  90.5 1.9 %collective-permute-start.12 = (f32[256,256]{1,0:T(8,128)S(1)}, f32[256,256]{1,0:T(8,128)S(1)}, u32[]{:S(2)}, u32[]{:S(2)}) collective-permute-start(f32[256,256]{1,0:T(8,128)S(1)} %fusion.16), channel_id=1, source_target_pairs={{0,1},{1,2},{2,3},{3,4},{4,5},{5,6},{6,7},{7,8},{8,9},{9,10},{10,1... | collective-permute-start | bytes 786440 | tf_op jit(solution)/shard_map/ppermute | solution.py:22
  92.5 5.9 %collective-permute-start.13 = (f32[256,256]{1,0:T(8,128)S(1)}, f32[256,256]{1,0:T(8,128)S(1)}, u32[]{:S(2)}, u32[]{:S(2)}) collective-permute-start(f32[256,256]{1,0:T(8,128)S(1)} %fusion.16), channel_id=1, source_target_pairs={{0,63},{1,0},{2,1},{3,2},{4,3},{5,4},{6,5},{7,6},{8,7},{9,8},{10,9... | collective-permute-start | bytes 786440 | tf_op jit(solution)/shard_map/ppermute | solution.py:22
  98.4 0.4 fusion.34
  98.8 0.0 collective-permute-done.15
  98.8 0.4 fusion.26
  99.2 1.1 collective-permute-done.12
  100.3 0.4 convolution_add_fusion.1
  100.7 1.4 collective-permute-done.13
  102.1 0.4 fusion.19
  102.5 0.7 copy-done.1
  103.2 3.2 %fusion.61 = f32[256,2048]{1,0:T(8,128)} fusion(f32[256,256]{1,0:T(8,128)S(1)} %fusion.19, f32[256,2048]{1,0:T(8,128)S(1)} %copy-done), kind=kOutput, calls=%fused_computation.78 | convolution fusion | flops 1610612736 | bytes 4456448 | tf_op jit(solution)/shard_map/dot_general | solution.py:77
  106.5 0.0 reduce-scatter.2.cloned.1.call-update
  106.5 0.9 copy-done.2
  107.4 0.6 fusion.62
  108.0 0.1 reshape.12
  108.1 28.3 %all_to_all.5 = f32[64,4,256]{2,1,0:T(4,128)S(1)} all-to-all(f32[64,4,256]{2,1,0:T(4,128)S(1)} %reshape.12), channel_id=1, replica_groups=mesh['grp'=8,'wide'=64] {'wide'}, dimensions={0} | all-to-all | bytes 524288 | tf_op jit(solution)/shard_map/all_to_all | solution.py:75
  136.4 0.1 reduce_sum.9
  136.5 0.6 broadcast_multiply_fusion.1
  137.1 21.4 %reduce-scatter.2.cloned.1.call-done = f32[256,256]{1,0:T(8,128)} async-done(((f32[256,2048]{1,0:T(8,128)}), f32[256,256]{1,0:T(8,128)}) %reduce-scatter.2.cloned.1.call-update) | async-done | bytes 262160 | tf_op jit(solution)/shard_map/reduce_scatter | solution.py:80
  (8 shorter events, 0.0 us)
Async XLA Ops:
  7.2 96.1 %copy-start = (f32[256,2048]{1,0:T(8,128)S(1)}, f32[256,2048]{1,0:T(8,128)}, u32[]{:S(2)}) copy-start(f32[256,2048]{1,0:T(8,128)} %param.7) | copy-start | bytes 6291460
  7.2 151.3 %reduce-scatter.2.cloned.1.call-start = ((), (), s32[]{:S(2)}) async-start(), calls=%async_computation.2 | async-start | bytes 2359296 | tf_op jit(solution)/shard_map/reduce_scatter | solution.py:80
  7.2 32.9 %collective-permute-start = (f32[256,256]{1,0:T(8,128)}, f32[256,256]{1,0:T(8,128)}, u32[]{:S(2)}, u32[]{:S(2)}) collective-permute-start(f32[256,256]{1,0:T(8,128)} %param.4), channel_id=1, source_target_pairs={{0,1},{1,2},{2,3},{3,4},{4,5},{5,6},{6,7},{7,8},{8,9},{9,10},{10,1... | collective-permute-start | bytes 786440 | tf_op jit(solution)/shard_map/ppermute | solution.py:22
  9.3 28.1 %collective-permute-start.3 = (f32[256,256]{1,0:T(8,128)}, f32[256,256]{1,0:T(8,128)}, u32[]{:S(2)}, u32[]{:S(2)}) collective-permute-start(f32[256,256]{1,0:T(8,128)} %param.4), channel_id=1, source_target_pairs={{0,62},{1,63},{2,0},{3,1},{4,2},{5,3},{6,4},{7,5},{8,6},{9,7},{10,... | collective-permute-start | bytes 786440 | tf_op jit(solution)/shard_map/ppermute | solution.py:22
  20.5 18.3 %collective-permute-start.2 = (f32[256,256]{1,0:T(8,128)}, f32[256,256]{1,0:T(8,128)}, u32[]{:S(2)}, u32[]{:S(2)}) collective-permute-start(f32[256,256]{1,0:T(8,128)} %param.4), channel_id=1, source_target_pairs={{0,2},{1,3},{2,4},{3,5},{4,6},{5,7},{6,8},{7,9},{8,10},{9,11},{10,... | collective-permute-start | bytes 786440 | tf_op jit(solution)/shard_map/ppermute | solution.py:22
  22.4 19.1 %collective-permute-start.1 = (f32[256,256]{1,0:T(8,128)}, f32[256,256]{1,0:T(8,128)}, u32[]{:S(2)}, u32[]{:S(2)}) collective-permute-start(f32[256,256]{1,0:T(8,128)} %param.4), channel_id=1, source_target_pairs={{0,63},{1,0},{2,1},{3,2},{4,3},{5,4},{6,5},{7,6},{8,7},{9,8},{10,9... | collective-permute-start | bytes 786440 | tf_op jit(solution)/shard_map/ppermute | solution.py:22
  37.4 4.1 %copy-start.3 = (f32[256,256]{1,0:T(8,128)S(1)}, f32[256,256]{1,0:T(8,128)}, u32[]{:S(2)}) copy-start(f32[256,256]{1,0:T(8,128)} %param.4) | copy-start | bytes 786436
  42.9 13.7 %collective-permute-start.6 = (f32[256,256]{1,0:T(8,128)S(1)}, f32[256,256]{1,0:T(8,128)S(1)}, u32[]{:S(2)}, u32[]{:S(2)}) collective-permute-start(f32[256,256]{1,0:T(8,128)S(1)} %get-tuple-element.2), channel_id=1, source_target_pairs={{0,2},{1,3},{2,4},{3,5},{4,6},{5,7},{6,8},{7,9},{8,10},{9,11},{10,... | collective-permute-start | bytes 786440 | tf_op jit(solution)/shard_map/ppermute | solution.py:22
  44.8 14.2 %collective-permute-start.4 = (f32[256,256]{1,0:T(8,128)S(1)}, f32[256,256]{1,0:T(8,128)S(1)}, u32[]{:S(2)}, u32[]{:S(2)}) collective-permute-start(f32[256,256]{1,0:T(8,128)S(1)} %get-tuple-element.2), channel_id=1, source_target_pairs={{0,1},{1,2},{2,3},{3,4},{4,5},{5,6},{6,7},{7,8},{8,9},{9,10},{10,1... | collective-permute-start | bytes 786440 | tf_op jit(solution)/shard_map/ppermute | solution.py:22
  46.7 11.9 %collective-permute-start.7 = (f32[256,256]{1,0:T(8,128)S(1)}, f32[256,256]{1,0:T(8,128)S(1)}, u32[]{:S(2)}, u32[]{:S(2)}) collective-permute-start(f32[256,256]{1,0:T(8,128)S(1)} %get-tuple-element.2), channel_id=1, source_target_pairs={{0,62},{1,63},{2,0},{3,1},{4,2},{5,3},{6,4},{7,5},{8,6},{9,7},{10,... | collective-permute-start | bytes 786440 | tf_op jit(solution)/shard_map/ppermute | solution.py:22
  52.8 8.6 %collective-permute-start.5 = (f32[256,256]{1,0:T(8,128)S(1)}, f32[256,256]{1,0:T(8,128)S(1)}, u32[]{:S(2)}, u32[]{:S(2)}) collective-permute-start(f32[256,256]{1,0:T(8,128)S(1)} %get-tuple-element.2), channel_id=1, source_target_pairs={{0,63},{1,0},{2,1},{3,2},{4,3},{5,4},{6,5},{7,6},{8,7},{9,8},{10,9... | collective-permute-start | bytes 786440 | tf_op jit(solution)/shard_map/ppermute | solution.py:22
  61.8 16.0 %collective-permute-start.10 = (f32[256,256]{1,0:T(8,128)S(1)}, f32[256,256]{1,0:T(8,128)S(1)}, u32[]{:S(2)}, u32[]{:S(2)}) collective-permute-start(f32[256,256]{1,0:T(8,128)S(1)} %fusion.13), channel_id=1, source_target_pairs={{0,2},{1,3},{2,4},{3,5},{4,6},{5,7},{6,8},{7,9},{8,10},{9,11},{10,... | collective-permute-start | bytes 786440 | tf_op jit(solution)/shard_map/ppermute | solution.py:22
  63.8 14.5 %collective-permute-start.11 = (f32[256,256]{1,0:T(8,128)S(1)}, f32[256,256]{1,0:T(8,128)S(1)}, u32[]{:S(2)}, u32[]{:S(2)}) collective-permute-start(f32[256,256]{1,0:T(8,128)S(1)} %fusion.13), channel_id=1, source_target_pairs={{0,62},{1,63},{2,0},{3,1},{4,2},{5,3},{6,4},{7,5},{8,6},{9,7},{10,... | collective-permute-start | bytes 786440 | tf_op jit(solution)/shard_map/ppermute | solution.py:22
  70.2 9.8 %collective-permute-start.8 = (f32[256,256]{1,0:T(8,128)S(1)}, f32[256,256]{1,0:T(8,128)S(1)}, u32[]{:S(2)}, u32[]{:S(2)}) collective-permute-start(f32[256,256]{1,0:T(8,128)S(1)} %fusion.13), channel_id=1, source_target_pairs={{0,1},{1,2},{2,3},{3,4},{4,5},{5,6},{6,7},{7,8},{8,9},{9,10},{10,1... | collective-permute-start | bytes 786440 | tf_op jit(solution)/shard_map/ppermute | solution.py:22
  72.1 9.6 %collective-permute-start.9 = (f32[256,256]{1,0:T(8,128)S(1)}, f32[256,256]{1,0:T(8,128)S(1)}, u32[]{:S(2)}, u32[]{:S(2)}) collective-permute-start(f32[256,256]{1,0:T(8,128)S(1)} %fusion.13), channel_id=1, source_target_pairs={{0,63},{1,0},{2,1},{3,2},{4,3},{5,4},{6,5},{7,6},{8,7},{9,8},{10,9... | collective-permute-start | bytes 786440 | tf_op jit(solution)/shard_map/ppermute | solution.py:22
  82.2 16.2 %collective-permute-start.14 = (f32[256,256]{1,0:T(8,128)S(1)}, f32[256,256]{1,0:T(8,128)S(1)}, u32[]{:S(2)}, u32[]{:S(2)}) collective-permute-start(f32[256,256]{1,0:T(8,128)S(1)} %fusion.16), channel_id=1, source_target_pairs={{0,2},{1,3},{2,4},{3,5},{4,6},{5,7},{6,8},{7,9},{8,10},{9,11},{10,... | collective-permute-start | bytes 786440 | tf_op jit(solution)/shard_map/ppermute | solution.py:22
  84.1 14.7 %collective-permute-start.15 = (f32[256,256]{1,0:T(8,128)S(1)}, f32[256,256]{1,0:T(8,128)S(1)}, u32[]{:S(2)}, u32[]{:S(2)}) collective-permute-start(f32[256,256]{1,0:T(8,128)S(1)} %fusion.16), channel_id=1, source_target_pairs={{0,62},{1,63},{2,0},{3,1},{4,2},{5,3},{6,4},{7,5},{8,6},{9,7},{10,... | collective-permute-start | bytes 786440 | tf_op jit(solution)/shard_map/ppermute | solution.py:22
  90.5 9.8 %collective-permute-start.12 = (f32[256,256]{1,0:T(8,128)S(1)}, f32[256,256]{1,0:T(8,128)S(1)}, u32[]{:S(2)}, u32[]{:S(2)}) collective-permute-start(f32[256,256]{1,0:T(8,128)S(1)} %fusion.16), channel_id=1, source_target_pairs={{0,1},{1,2},{2,3},{3,4},{4,5},{5,6},{6,7},{7,8},{8,9},{9,10},{10,1... | collective-permute-start | bytes 786440 | tf_op jit(solution)/shard_map/ppermute | solution.py:22
  92.5 9.6 %collective-permute-start.13 = (f32[256,256]{1,0:T(8,128)S(1)}, f32[256,256]{1,0:T(8,128)S(1)}, u32[]{:S(2)}, u32[]{:S(2)}) collective-permute-start(f32[256,256]{1,0:T(8,128)S(1)} %fusion.16), channel_id=1, source_target_pairs={{0,63},{1,0},{2,1},{3,2},{4,3},{5,4},{6,5},{7,6},{8,7},{9,8},{10,9... | collective-permute-start | bytes 786440 | tf_op jit(solution)/shard_map/ppermute | solution.py:22
  102.5 0.7 copy-start.1
  106.5 0.9 copy-start.2
Sparse Core Ops, SparseCore 0:
  106.6 51.8 reduce-scatter.1

commit v7 on v6

v7 whole, which is shorter than its diff:
```python
import jax
import jax.numpy as jnp
from jax import lax
from jax.sharding import PartitionSpec as P

B = 64
A_DEV = 4
NB = 16
HW = 2
DEGREE = 4


cheb_center = 0.25
cheb_half = 2.0

HI = lax.Precision.HIGHEST


def dense_hamiltonian(hblocks, slot_index, window_blocks):
    local_blocks = hblocks.shape[0]
    onehot = (slot_index[:, :, None] == jnp.arange(window_blocks)[None, None, :]).astype(jnp.float32)
    hd = jnp.einsum("asp,asij->aipj", onehot, hblocks, precision=HI)
    return hd.reshape(local_blocks * B, window_blocks * B)


def group_exchange(field, groups):
    members = len(groups[0])
    spread = jnp.broadcast_to(field[None], (members,) + field.shape)
    got = lax.all_to_all(spread, "wide", 0, 0, tiled=True, axis_index_groups=groups)
    return got.reshape(members * field.shape[0], field.shape[1])


def apply_ham(field, hdense, groups_a, groups_b):
    got_a = group_exchange(field, groups_a)
    got_b = group_exchange(field, groups_b)
    half = got_a.shape[0]
    return (jnp.dot(hdense[:, :half], got_a, precision=HI, preferred_element_type=jnp.float32)
            + jnp.dot(hdense[:, half:], got_b, precision=HI, preferred_element_type=jnp.float32))


def local(subspace, hblocks, pattern, rotation):
    devcount = lax.axis_size("wide")
    myself = lax.axis_index("wide")
    span = 2 * HW
    groups_a = [[span * k + i for i in range(span)] for k in range(devcount // span)]
    groups_b = [[(span * k + HW + i) % devcount for i in range(span)] for k in range(devcount // span)]
    place = myself % span
    owner = pattern // A_DEV
    offset = (owner - myself + HW + devcount) % devcount - HW
    in_a = (offset + place >= 0) & (offset + place < span)
    piece = jnp.where(in_a, offset + place,
                      span + jnp.where(place < HW, offset + HW + place, offset - HW + place))
    slot_index = piece * A_DEV + pattern % A_DEV
    hdense = dense_hamiltonian(hblocks, slot_index, 2 * span * A_DEV)
    previous = subspace
    current = (apply_ham(subspace, hdense, groups_a, groups_b) - cheb_center * subspace) / cheb_half
    for step in range(DEGREE - 1):
        nextone = (
            2.0 * (apply_ham(current, hdense, groups_a, groups_b) - cheb_center * current) / cheb_half
            - previous
        )
        previous = current
        current = nextone
    total_rows = current.shape[0] * devcount
    gram_term = lax.dot_general(
        current,
        current,
        (((0,), (0,)), ((), ())),
        precision=HI,
        preferred_element_type=jnp.float32,
    )
    pieces = gram_term.reshape(devcount, -1, gram_term.shape[1])
    gathered = lax.all_to_all(pieces, "wide", 0, 0, tiled=True)
    correlation = jnp.sum(gathered, axis=0) / total_rows
    rot_term = jnp.dot(
        current, rotation, precision=HI, preferred_element_type=jnp.float32
    )
    rotated = lax.psum_scatter(rot_term, "grp", scatter_dimension=1, tiled=True)
    return (rotated, correlation)


def solution(mesh):
    in_specs = (P("wide", "grp"), P("wide", None, None, None), P("wide", None), P("grp", None))
    out_specs = (P("wide", "grp"), P(("grp", "wide"), None))
    return jax.shard_map(local, mesh=mesh, in_specs=in_specs, out_specs=out_specs, check_vma=False)
```

time: 166 us -> 238 us (1.43)
  blocking collectives: 28.3 us -> 99.7 us
  starting transfers between devices: 64.8 us -> 27.8 us
  waiting for transfers between devices: 30.3 us -> 50.6 us
  matrix products: 22.1 us -> 31.2 us
  local copies, waits for them, and re-layouts: 3.95 us -> 12.7 us
    all_to_all x0 -> x4, blocking collectives: none -> 75.3 us  [group_exchange(): lax.all_to_all(spread, 'wide', 0, 0, tiled=True, axis_index_groups=groups)]
    ppermute x16 -> x0, starting transfers between devices: 64.8 us -> none  [passed_along(): return lax.ppermute(value, axis, pairs)]
    all_to_all x0 -> x4, waiting for transfers between devices: none -> 29.1 us  [group_exchange(): lax.all_to_all(spread, 'wide', 0, 0, tiled=True, axis_index_groups=groups)]
    all_to_all x0 -> x4, starting transfers between devices: none -> 27.8 us  [group_exchange(): lax.all_to_all(spread, 'wide', 0, 0, tiled=True, axis_index_groups=groups)]
    dot_general x20 -> x8, matrix products: 12.5 us -> 23.4 us  [the longest x4 13.1 us: apply_ham(): jnp.dot(hdense[:, :half], got_a, precision=HI, preferred_element_type=jnp...]
    ppermute x16 -> x0, waiting for transfers between devices: 8.9 us -> none  [passed_along(): return lax.ppermute(value, axis, pairs)]
    broadcast_in_dim x0 -> x4, local copies, waits for them, and re-layouts: none -> 5.34 us  [group_exchange(): spread = jnp.broadcast_to(field[None], (members,) + field.shape)]
    all_to_all x1, blocking collectives: 28.3 us -> 24.4 us  [local(): gathered = lax.all_to_all(pieces, 'wide', 0, 0, tiled=True)]
  transfers between devices with their start and end apart: 17 -> 5, of which waited for: 7 -> 5; matrix products, arithmetic and copies ran while one was open for 12% -> 10% of each run, Pallas kernels for 0% -> 0%
where the time goes in v7:
time: 238 us; the launch traced here: 237 us
  blocking collectives  99.7 us (42%)
  waiting for transfers between devices  50.6 us (21%)
  matrix products  31.2 us (13%)
  starting transfers between devices  27.8 us (12%)
  between operations  14.1 us (6%)
  local copies, waits for them, and re-layouts  12.7 us (5%)
    all_to_all x4, blocking collectives, group_exchange(): lax.all_to_all(spread, 'wide', 0, 0, tiled=True, axis_index_groups=groups)  75.3 us
    all_to_all x4, waiting for transfers between devices, group_exchange(): lax.all_to_all(spread, 'wide', 0, 0, tiled=True, axis_index_groups=groups)  29.1 us
    all_to_all x4, starting transfers between devices, group_exchange(): lax.all_to_all(spread, 'wide', 0, 0, tiled=True, axis_index_groups=groups)  27.8 us
    all_to_all x1, blocking collectives, local(): gathered = lax.all_to_all(pieces, 'wide', 0, 0, tiled=True)  24.4 us
    reduce_scatter x1, waiting for transfers between devices, local(): rotated = lax.psum_scatter(rot_term, 'grp', scatter_dimension=1, tiled=True)  21.4 us
    dot_general x4, matrix products, apply_ham(): jnp.dot(hdense[:, :half], got_a, precision=HI, preferred_element_type=jnp...  13.1 us
    dot_general x4, matrix products, apply_ham(): jnp.dot(hdense[:, half:], got_b, precision=HI, preferred_element_type=jnp...  10.3 us
    broadcast_in_dim x4, local copies, waits for them, and re-layouts, group_exchange(): spread = jnp.broadcast_to(field[None], (members,) + field.shape)  5.34 us
  transfers between devices with their start and end apart: 5, of which 5 were waited for; matrix products, arithmetic and copies ran while one was open for 10% of the time, Pallas kernels for 0%

profile of v7, /device:TPU:6, one launch (start us, length us, event | category | flops | bytes accessed | tf_op | source)
XLA Modules:
  0.0 236.9 jit_solution(15486633722597093814)
XLA Ops:
  7.2 0.0 copy-start
  7.2 2.2 broadcast_in_dim.8
  9.4 0.0 copy-start.6
  9.4 19.0 %all_to_all.45 = f32[4,256,256]{2,1,0:T(8,128)} all-to-all(f32[4,256,256]{2,1,0:T(8,128)} %broadcast_in_dim.8), channel_id=1, replica_groups={{0,1,2,3},{4,5,6,7},{8,9,10,11},{12,13,14,15},{16,17,18,19},{20,21,22,2..., dimensions={0} | all-to-all | bytes 2097152 | tf_op jit(solution)/shard_map/all_to_all | solution.py:29
  28.3 11.6 %all-to-all-start.1 = ((f32[4,256,256]{2,1,0:T(8,128)}), f32[4,256,256]{2,1,0:T(8,128)S(1)}, u32[]{:S(2)}, u32[]{:S(2)}) async-start(f32[4,256,256]{2,1,0:T(8,128)} %broadcast_in_dim.8), calls=%async_computation.1 | async-start | bytes 2097152 | tf_op jit(solution)/shard_map/all_to_all | solution.py:29
  39.9 0.0 copy-done.6
  40.0 0.0 copy-done
  40.0 4.0 %convolution_bitcast_fusion = f32[4,64,32,64]{3,2,1,0:T(8,128)} fusion(f32[4,16,64,64]{3,2,1,0:T(8,128)S(1)} %copy-done, s32[4,16]{1,0:T(4,128)S(1)} %fusion.26), kind=kOutput, calls=%fused_computation | convolution fusion | flops 100665344 | bytes 3145984 | tf_op jit(solution)/shard_map/asp,asij->aipj/dot_general | solution.py:22
  43.9 5.0 %reshape.39 = f32[256,2048]{1,0:T(8,128)} reshape(f32[4,64,32,64]{3,2,1,0:T(8,128)} %convolution_bitcast_fusion) | data formatting | bytes 4194304 | tf_op jit(solution)/shard_map/reshape | solution.py:23
  48.9 0.0 copy-start.3
  48.9 3.3 %fusion.18 = f32[256,256]{1,0:T(8,128)} fusion(f32[1024,256]{1,0:T(8,128)} %bitcast.33, f32[256,2048]{1,0:T(8,128)} %reshape.39), kind=kOutput, calls=%fused_computation.23 | convolution fusion | flops 805306368 | bytes 2359296 | tf_op jit(solution)/shard_map/dot_general | solution.py:37
  52.2 0.5 all-to-all-done.1
  52.7 0.0 copy-done.3
  52.7 3.0 %broadcast_multiply_fusion = (f32[256,256]{1,0:T(8,128)S(1)}, f32[256,256]{1,0:T(8,128)}) fusion(f32[256,256]{1,0:T(8,128)S(1)} %copy-done.3, f32[256,256]{1,0:T(8,128)} %fusion.18, f32[1024,256]{1,0:T(8,128)S(1)} %bitcast.29, f32[256,2048]{1,0:T(8,128)} %reshape.39), kind=kOutput, calls=%fused_computation.25 | convolution fusion | flops 805568512 | bytes 3145728 | tf_op jit(solution)/shard_map/dot_general | solution.py:38
  55.7 1.1 broadcast_in_dim.9
  56.8 18.8 %all_to_all.46 = f32[4,256,256]{2,1,0:T(8,128)} all-to-all(f32[4,256,256]{2,1,0:T(8,128)} %broadcast_in_dim.9), channel_id=1, replica_groups={{0,1,2,3},{4,5,6,7},{8,9,10,11},{12,13,14,15},{16,17,18,19},{20,21,22,2..., dimensions={0} | all-to-all | bytes 2097152 | tf_op jit(solution)/shard_map/all_to_all | solution.py:29
  75.6 5.4 %all-to-all-start.3 = ((f32[4,256,256]{2,1,0:T(8,128)}), f32[4,256,256]{2,1,0:T(8,128)S(1)}, u32[]{:S(2)}, u32[]{:S(2)}) async-start(f32[4,256,256]{2,1,0:T(8,128)} %broadcast_in_dim.9), calls=%async_computation.3 | async-start | bytes 2097152 | tf_op jit(solution)/shard_map/all_to_all | solution.py:29
  81.0 3.3 %fusion.16 = f32[256,256]{1,0:T(8,128)} fusion(f32[1024,256]{1,0:T(8,128)} %bitcast.35, f32[256,2048]{1,0:T(8,128)} %reshape.39), kind=kOutput, calls=%fused_computation.21 | convolution fusion | flops 805306368 | bytes 2359296 | tf_op jit(solution)/shard_map/dot_general | solution.py:37
  84.2 9.5 %all-to-all-done.3 = f32[4,256,256]{2,1,0:T(8,128)S(1)} async-done(((f32[4,256,256]{2,1,0:T(8,128)}), f32[4,256,256]{2,1,0:T(8,128)S(1)}, u32[]{:S(2)}, u32[]{:S(2)}) %all-to-all-start.3) | async-done | bytes 1048608 | tf_op jit(solution)/shard_map/all_to_all | solution.py:29
  93.8 2.4 %fusion.6 = f32[256,256]{1,0:T(8,128)S(1)} fusion(f32[256,256]{1,0:T(8,128)} %param.4, f32[256,256]{1,0:T(8,128)} %fusion.16, f32[1024,256]{1,0:T(8,128)S(1)} %bitcast.31, f32[256,2048]{1,0:T(8,128)} %reshape.39, f32[256,256]{1,0:T(8,128)} %get-tuple-element.3), kind=kOutput, calls=%fused_computation.10 | convolution fusion | flops 805568512 | bytes 3145728 | tf_op jit(solution)/shard_map/dot_general | solution.py:38
  96.2 1.1 broadcast_in_dim.10
  97.3 18.8 %all_to_all.47 = f32[4,256,256]{2,1,0:T(8,128)} all-to-all(f32[4,256,256]{2,1,0:T(8,128)} %broadcast_in_dim.10), channel_id=1, replica_groups={{0,1,2,3},{4,5,6,7},{8,9,10,11},{12,13,14,15},{16,17,18,19},{20,21,22,2..., dimensions={0} | all-to-all | bytes 2097152 | tf_op jit(solution)/shard_map/all_to_all | solution.py:29
  116.1 5.4 %all-to-all-start.5 = ((f32[4,256,256]{2,1,0:T(8,128)}), f32[4,256,256]{2,1,0:T(8,128)S(1)}, u32[]{:S(2)}, u32[]{:S(2)}) async-start(f32[4,256,256]{2,1,0:T(8,128)} %broadcast_in_dim.10), calls=%async_computation.5 | async-start | bytes 2097152 | tf_op jit(solution)/shard_map/all_to_all | solution.py:29
  121.5 3.3 %fusion.14 = f32[256,256]{1,0:T(8,128)} fusion(f32[1024,256]{1,0:T(8,128)} %bitcast.36, f32[256,2048]{1,0:T(8,128)} %reshape.39), kind=kOutput, calls=%fused_computation.19 | convolution fusion | flops 805306368 | bytes 2359296 | tf_op jit(solution)/shard_map/dot_general | solution.py:37
  124.7 9.5 %all-to-all-done.5 = f32[4,256,256]{2,1,0:T(8,128)S(1)} async-done(((f32[4,256,256]{2,1,0:T(8,128)}), f32[4,256,256]{2,1,0:T(8,128)S(1)}, u32[]{:S(2)}, u32[]{:S(2)}) %all-to-all-start.5) | async-done | bytes 1048608 | tf_op jit(solution)/shard_map/all_to_all | solution.py:29
  134.3 2.4 %fusion.4 = f32[256,256]{1,0:T(8,128)S(1)} fusion(f32[256,256]{1,0:T(8,128)} %fusion.14, f32[1024,256]{1,0:T(8,128)S(1)} %bitcast.32, f32[256,2048]{1,0:T(8,128)} %reshape.39, f32[256,256]{1,0:T(8,128)S(1)} %fusion.6, f32[256,256]{1,0:T(8,128)} %get-tuple-element.3), kind=kOutput, calls=%fused_computation.7 | convolution fusion | flops 805634048 | bytes 3145728 | tf_op jit(solution)/shard_map/dot_general | solution.py:38
  136.6 0.0 copy-start.4
  136.7 0.7 copy-done.4
  137.3 1.1 broadcast_in_dim.11
  138.4 18.8 %all_to_all.48 = f32[4,256,256]{2,1,0:T(8,128)} all-to-all(f32[4,256,256]{2,1,0:T(8,128)} %broadcast_in_dim.11), channel_id=1, replica_groups={{0,1,2,3},{4,5,6,7},{8,9,10,11},{12,13,14,15},{16,17,18,19},{20,21,22,2..., dimensions={0} | all-to-all | bytes 2097152 | tf_op jit(solution)/shard_map/all_to_all | solution.py:29
  157.2 5.4 %all-to-all-start.7 = ((f32[4,256,256]{2,1,0:T(8,128)}), f32[4,256,256]{2,1,0:T(8,128)S(1)}, u32[]{:S(2)}, u32[]{:S(2)}) async-start(f32[4,256,256]{2,1,0:T(8,128)} %broadcast_in_dim.11), calls=%async_computation.7 | async-start | bytes 2097152 | tf_op jit(solution)/shard_map/all_to_all | solution.py:29
  162.6 0.0 reduce-scatter.2.cloned.1.call-start
  162.6 3.3 %fusion.12 = f32[256,256]{1,0:T(8,128)} fusion(f32[1024,256]{1,0:T(8,128)} %bitcast.34, f32[256,2048]{1,0:T(8,128)} %reshape.39), kind=kOutput, calls=%fused_computation.17 | convolution fusion | flops 805306368 | bytes 2359296 | tf_op jit(solution)/shard_map/dot_general | solution.py:37
  165.9 9.5 %all-to-all-done.7 = f32[4,256,256]{2,1,0:T(8,128)S(1)} async-done(((f32[4,256,256]{2,1,0:T(8,128)}), f32[4,256,256]{2,1,0:T(8,128)S(1)}, u32[]{:S(2)}, u32[]{:S(2)}) %all-to-all-start.7) | async-done | bytes 1048608 | tf_op jit(solution)/shard_map/all_to_all | solution.py:29
  175.4 0.0 copy-start.5
  175.4 2.5 %fusion.2 = f32[256,256]{1,0:T(8,128)S(1)} fusion(f32[256,256]{1,0:T(8,128)S(1)} %fusion.6, f32[256,256]{1,0:T(8,128)} %fusion.12, f32[1024,256]{1,0:T(8,128)S(1)} %bitcast.30, f32[256,2048]{1,0:T(8,128)} %reshape.39, f32[256,256]{1,0:T(8,128)} %copy-done.4), kind=kOutput, calls=%fused_computation.4 | convolution fusion | flops 805568512 | bytes 3145728 | tf_op jit(solution)/shard_map/dot_general | solution.py:38
  177.9 0.0 copy-start.1
  177.9 0.7 copy-done.1
  178.6 0.0 copy-done.5
  178.6 3.2 %fusion.31 = f32[256,2048]{1,0:T(8,128)} fusion(f32[256,256]{1,0:T(8,128)S(1)} %fusion.2, f32[256,2048]{1,0:T(8,128)S(1)} %copy-done.5), kind=kOutput, calls=%fused_computation.48 | convolution fusion | flops 1610612736 | bytes 4456448 | tf_op jit(solution)/shard_map/dot_general | solution.py:75
  181.8 0.0 copy-start.2
  181.8 0.0 reduce-scatter.2.cloned.1.call-update
  181.9 0.9 copy-done.2
  182.8 0.6 fusion.32
  183.4 0.1 reshape.48
  183.5 24.4 %all_to_all.49 = f32[64,4,256]{2,1,0:T(4,128)S(1)} all-to-all(f32[64,4,256]{2,1,0:T(4,128)S(1)} %reshape.48), channel_id=1, replica_groups=mesh['grp'=8,'wide'=64] {'wide'}, dimensions={0} | all-to-all | bytes 524288 | tf_op jit(solution)/shard_map/all_to_all | solution.py:73
  207.9 0.1 reduce_sum.9
  208.0 0.6 broadcast_multiply_fusion.1
  208.6 21.4 %reduce-scatter.2.cloned.1.call-done = f32[256,256]{1,0:T(8,128)} async-done(((f32[256,2048]{1,0:T(8,128)}), f32[256,256]{1,0:T(8,128)}) %reduce-scatter.2.cloned.1.call-update) | async-done | bytes 262160 | tf_op jit(solution)/shard_map/reduce_scatter | solution.py:78
  (1 shorter events, 0.0 us)
Async XLA Ops:
  7.2 32.8 %copy-start = (f32[4,16,64,64]{3,2,1,0:T(8,128)S(1)}, f32[4,16,64,64]{3,2,1,0:T(8,128)}, u32[]{:S(2)}) copy-start(f32[4,16,64,64]{3,2,1,0:T(8,128)} %param.5) | copy-start | bytes 3145732
  9.4 30.6 %copy-start.6 = (s32[4,16]{1,0:T(4,128)S(1)}, s32[4,16]{1,0:T(4,128)}, u32[]{:S(2)}) copy-start(s32[4,16]{1,0:T(4,128)} %param.6) | copy-start | bytes 772
  28.3 24.4 %all-to-all-start.1 = ((f32[4,256,256]{2,1,0:T(8,128)}), f32[4,256,256]{2,1,0:T(8,128)S(1)}, u32[]{:S(2)}, u32[]{:S(2)}) async-start(f32[4,256,256]{2,1,0:T(8,128)} %broadcast_in_dim.8), calls=%async_computation.1 | async-start | bytes 2097152 | tf_op jit(solution)/shard_map/all_to_all | solution.py:29
  48.9 3.8 %copy-start.3 = (f32[256,256]{1,0:T(8,128)S(1)}, f32[256,256]{1,0:T(8,128)}, u32[]{:S(2)}) copy-start(f32[256,256]{1,0:T(8,128)} %param.4) | copy-start | bytes 786436
  75.6 18.2 %all-to-all-start.3 = ((f32[4,256,256]{2,1,0:T(8,128)}), f32[4,256,256]{2,1,0:T(8,128)S(1)}, u32[]{:S(2)}, u32[]{:S(2)}) async-start(f32[4,256,256]{2,1,0:T(8,128)} %broadcast_in_dim.9), calls=%async_computation.3 | async-start | bytes 2097152 | tf_op jit(solution)/shard_map/all_to_all | solution.py:29
  116.1 18.2 %all-to-all-start.5 = ((f32[4,256,256]{2,1,0:T(8,128)}), f32[4,256,256]{2,1,0:T(8,128)S(1)}, u32[]{:S(2)}, u32[]{:S(2)}) async-start(f32[4,256,256]{2,1,0:T(8,128)} %broadcast_in_dim.10), calls=%async_computation.5 | async-start | bytes 2097152 | tf_op jit(solution)/shard_map/all_to_all | solution.py:29
  136.6 0.7 copy-start.4
  157.2 18.2 %all-to-all-start.7 = ((f32[4,256,256]{2,1,0:T(8,128)}), f32[4,256,256]{2,1,0:T(8,128)S(1)}, u32[]{:S(2)}, u32[]{:S(2)}) async-start(f32[4,256,256]{2,1,0:T(8,128)} %broadcast_in_dim.11), calls=%async_computation.7 | async-start | bytes 2097152 | tf_op jit(solution)/shard_map/all_to_all | solution.py:29
  162.6 67.5 %reduce-scatter.2.cloned.1.call-start = ((), (), s32[]{:S(2)}) async-start(), calls=%async_computation.10 | async-start | bytes 2359296 | tf_op jit(solution)/shard_map/reduce_scatter | solution.py:78
  175.4 3.2 %copy-start.5 = (f32[256,2048]{1,0:T(8,128)S(1)}, f32[256,2048]{1,0:T(8,128)}, u32[]{:S(2)}) copy-start(f32[256,2048]{1,0:T(8,128)} %param.7) | copy-start | bytes 6291460
  177.9 0.7 copy-start.1
  181.8 0.9 copy-start.2
Sparse Core Ops, SparseCore 0:
  182.0 47.9 reduce-scatter.1

commit v8 on v6

--- a/solution.py
+++ b/solution.py
@@ -1,6 +1,8 @@
 import jax
 import jax.numpy as jnp
 from jax import lax
+from jax.experimental import pallas as pl
+from jax.experimental.pallas import tpu as pltpu
 from jax.sharding import PartitionSpec as P
 
 B = 64
@@ -22,12 +24,28 @@
     return lax.ppermute(value, axis, pairs)
 
 
+def hbuild_kernel(slot_ref, h_ref, o_ref):
+    o_ref[...] = jnp.zeros(o_ref.shape, o_ref.dtype)
+    for a in range(h_ref.shape[0]):
+        for s in range(h_ref.shape[1]):
+            p = slot_ref[a, s]
+            o_ref[a, p] = o_ref[a, p] + h_ref[a, s]
+
+
 def dense_hamiltonian(hblocks, slot_index):
     local_blocks = hblocks.shape[0]
     window_blocks = (2 * HW + 1) * A_DEV
-    onehot = (slot_index[:, :, None] == jnp.arange(window_blocks)[None, None, :]).astype(jnp.float32)
-    hd = jnp.einsum("asp,asij->aipj", onehot, hblocks, precision=HI)
-    return hd.reshape(local_blocks * B, window_blocks * B)
+    out_bytes = local_blocks * window_blocks * B * B * 4
+    hd = pl.pallas_call(
+        hbuild_kernel,
+        out_shape=jax.ShapeDtypeStruct((local_blocks, window_blocks, B, B), jnp.float32),
+        in_specs=[pl.BlockSpec(memory_space=pltpu.SMEM), pl.BlockSpec(memory_space=pltpu.VMEM)],
+        out_specs=pl.BlockSpec(memory_space=pltpu.VMEM),
+        cost_estimate=pl.CostEstimate(
+            flops=hblocks.size, bytes_accessed=hblocks.size * 4 + out_bytes, transcendentals=0
+        ),
+    )(slot_index, hblocks)
+    return hd.transpose(0, 2, 1, 3).reshape(local_blocks * B, window_blocks * B)
 
 
 def apply_ham(field, hdense):
@@ -75,7 +93,7 @@
     gathered = lax.all_to_all(pieces, "wide", 0, 0, tiled=True)
     correlation = jnp.sum(gathered, axis=0) / total_rows
     rot_term = jnp.dot(
-        current, rotation, precision=HI, preferred_element_type=jnp.float32
+        current, rotation, precision=lax.Precision.HIGH, preferred_element_type=jnp.float32
     )
     rotated = lax.psum_scatter(rot_term, "grp", scatter_dimension=1, tiled=True)
     return (rotated, correlation)

time: 166 us -> 171 us (1.030)
  local copies, waits for them, and re-layouts: 3.95 us -> 8.88 us
  Pallas kernels: 0 us -> 3.54 us
  matrix products: 22.1 us -> 19.8 us
  waiting for transfers between devices: 30.3 us -> 28.1 us
    dot_general x2 -> x1, matrix products: 9.01 us -> 2.45 us  [local(): jnp.dot(current, rotation, precision=lax.Precision.HIGH, preferred_elemen...]
    transpose x0 -> x1, local copies, waits for them, and re-layouts: none -> 4.41 us  [dense_hamiltonian(): return hd.transpose(0, 2, 1, 3).reshape(local_blocks * B, window_blocks * B)]
    dot_general x20, matrix products: 12.5 us -> 16.8 us  [apply_ham(): jnp.dot(hdense[:, idx * rows:(idx + 1) * rows], pieces[idx], precision=HI...]
    pallas_call x0 -> x1, Pallas kernels: none -> 3.54 us  [dense_hamiltonian(): pl.pallas_call(hbuild_kernel, out_shape=jax.ShapeDtypeStruct((local_block...]
    ppermute x16, waiting for transfers between devices: 8.9 us -> 6.73 us  [passed_along(): return lax.ppermute(value, axis, pairs)]
  transfers between devices with their start and end apart: 17 -> 17, of which waited for: 7 -> 7; matrix products, arithmetic and copies ran while one was open for 12% -> 14% of each run, Pallas kernels for 0% -> 2%
where the time goes in v8:
time: 171 us; the launch traced here: 170 us
  starting transfers between devices  64.8 us (38%)
  blocking collectives  28.3 us (17%)
  waiting for transfers between devices  28.1 us (16%)
  matrix products  19.8 us (12%)
  between operations  14.5 us (8%)
  local copies, waits for them, and re-layouts  8.88 us (5%)
  Pallas kernels  3.54 us (2%)
  other arithmetic  1.97 us (1%)
    ppermute x16, starting transfers between devices, passed_along(): return lax.ppermute(value, axis, pairs)  64.8 us
    all_to_all x1, blocking collectives, local(): gathered = lax.all_to_all(pieces, 'wide', 0, 0, tiled=True)  28.3 us
    reduce_scatter x1, waiting for transfers between devices, local(): rotated = lax.psum_scatter(rot_term, 'grp', scatter_dimension=1, tiled=True)  21.3 us
    dot_general x20, matrix products, apply_ham(): jnp.dot(hdense[:, idx * rows:(idx + 1) * rows], pieces[idx], precision=HI...  16.8 us
    ppermute x16, waiting for transfers between devices, passed_along(): return lax.ppermute(value, axis, pairs)  6.73 us
    transpose x1, local copies, waits for them, and re-layouts, dense_hamiltonian(): return hd.transpose(0, 2, 1, 3).reshape(local_blocks * B, window_blocks * B)  4.41 us
    pallas_call x1, Pallas kernels, dense_hamiltonian(): pl.pallas_call(hbuild_kernel, out_shape=jax.ShapeDtypeStruct((local_block...  3.54 us
  transfers between devices with their start and end apart: 17, of which 7 were waited for; matrix products, arithmetic and copies ran while one was open for 14% of the time, Pallas kernels for 2%

profile of v8, /device:TPU:6, one launch (start us, length us, event | category | flops | bytes accessed | tf_op | source)
XLA Modules:
  0.0 169.8 jit_solution(12255876094647809427)
XLA Ops:
  7.2 0.0 copy-start
  7.2 0.0 reduce-scatter.2.cloned.1.call-start
  7.2 2.1 %collective-permute-start = (f32[256,256]{1,0:T(8,128)}, f32[256,256]{1,0:T(8,128)}, u32[]{:S(2)}, u32[]{:S(2)}) collective-permute-start(f32[256,256]{1,0:T(8,128)} %param.4), channel_id=1, source_target_pairs={{0,1},{1,2},{2,3},{3,4},{4,5},{5,6},{6,7},{7,8},{8,9},{9,10},{10,1... | collective-permute-start | bytes 786440 | tf_op jit(solution)/shard_map/ppermute | solution.py:24
  9.3 11.2 %collective-permute-start.3 = (f32[256,256]{1,0:T(8,128)}, f32[256,256]{1,0:T(8,128)}, u32[]{:S(2)}, u32[]{:S(2)}) collective-permute-start(f32[256,256]{1,0:T(8,128)} %param.4), channel_id=1, source_target_pairs={{0,62},{1,63},{2,0},{3,1},{4,2},{5,3},{6,4},{7,5},{8,6},{9,7},{10,... | collective-permute-start | bytes 786440 | tf_op jit(solution)/shard_map/ppermute | solution.py:24
  20.5 1.9 %collective-permute-start.2 = (f32[256,256]{1,0:T(8,128)}, f32[256,256]{1,0:T(8,128)}, u32[]{:S(2)}, u32[]{:S(2)}) collective-permute-start(f32[256,256]{1,0:T(8,128)} %param.4), channel_id=1, source_target_pairs={{0,2},{1,3},{2,4},{3,5},{4,6},{5,7},{6,8},{7,9},{8,10},{9,11},{10,... | collective-permute-start | bytes 786440 | tf_op jit(solution)/shard_map/ppermute | solution.py:24
  22.4 4.9 %collective-permute-start.1 = (f32[256,256]{1,0:T(8,128)}, f32[256,256]{1,0:T(8,128)}, u32[]{:S(2)}, u32[]{:S(2)}) collective-permute-start(f32[256,256]{1,0:T(8,128)} %param.4), channel_id=1, source_target_pairs={{0,63},{1,0},{2,1},{3,2},{4,3},{5,4},{6,5},{7,6},{8,7},{9,8},{10,9... | collective-permute-start | bytes 786440 | tf_op jit(solution)/shard_map/ppermute | solution.py:24
  27.4 1.3 fusion.51.slot_ref
  28.6 3.5 %shard_map.59 = f32[4,20,64,64]{3,2,1,0:T(8,128)} custom-call(s32[4,16]{1,0:T(4,128)} %fusion.51.slot_ref, f32[4,16,64,64]{3,2,1,0:T(8,128)} %h_ref.1), custom_call_target="tpu_custom_call" | custom-call | flops 262144 | bytes 2359296 | tf_op jit(solution)/shard_map/pallas_call | solution.py:39
  32.2 4.4 %copy.6 = f32[4,64,20,64]{1,0,3,2:T(4,128)} copy(f32[4,64,20,64]{3,1,2,0:T(8,128)} %bitcast.26) | data formatting | bytes 2621440 | tf_op jit(solution)/shard_map/transpose | solution.py:48
  36.6 2.8 %reshape.10 = f32[256,1280]{0,1:T(8,128)S(1)} reshape(f32[4,64,20,64]{1,0,3,2:T(4,128)} %copy.6) | data formatting | bytes 2621440 | tf_op jit(solution)/shard_map/reshape | solution.py:48
  39.4 1.5 fusion.45
  40.9 0.0 copy-start.3
  40.9 1.6 fusion.21
  42.5 1.5 fusion.29
  44.1 0.0 collective-permute-done
  44.1 1.5 convolution_add_fusion.7
  45.6 0.0 collective-permute-done.1
  45.7 1.6 broadcast_multiply_fusion
  47.2 1.9 %collective-permute-start.6 = (f32[256,256]{1,0:T(8,128)S(1)}, f32[256,256]{1,0:T(8,128)S(1)}, u32[]{:S(2)}, u32[]{:S(2)}) collective-permute-start(f32[256,256]{1,0:T(8,128)S(1)} %get-tuple-element.2), channel_id=1, source_target_pairs={{0,2},{1,3},{2,4},{3,5},{4,6},{5,7},{6,8},{7,9},{8,10},{9,11},{10,... | collective-permute-start | bytes 786440 | tf_op jit(solution)/shard_map/ppermute | solution.py:24
  49.2 1.9 %collective-permute-start.4 = (f32[256,256]{1,0:T(8,128)S(1)}, f32[256,256]{1,0:T(8,128)S(1)}, u32[]{:S(2)}, u32[]{:S(2)}) collective-permute-start(f32[256,256]{1,0:T(8,128)S(1)} %get-tuple-element.2), channel_id=1, source_target_pairs={{0,1},{1,2},{2,3},{3,4},{4,5},{5,6},{6,7},{7,8},{8,9},{9,10},{10,1... | collective-permute-start | bytes 786440 | tf_op jit(solution)/shard_map/ppermute | solution.py:24
  51.1 6.0 %collective-permute-start.7 = (f32[256,256]{1,0:T(8,128)S(1)}, f32[256,256]{1,0:T(8,128)S(1)}, u32[]{:S(2)}, u32[]{:S(2)}) collective-permute-start(f32[256,256]{1,0:T(8,128)S(1)} %get-tuple-element.2), channel_id=1, source_target_pairs={{0,62},{1,63},{2,0},{3,1},{4,2},{5,3},{6,4},{7,5},{8,6},{9,7},{10,... | collective-permute-start | bytes 786440 | tf_op jit(solution)/shard_map/ppermute | solution.py:24
  57.1 3.4 %collective-permute-start.5 = (f32[256,256]{1,0:T(8,128)S(1)}, f32[256,256]{1,0:T(8,128)S(1)}, u32[]{:S(2)}, u32[]{:S(2)}) collective-permute-start(f32[256,256]{1,0:T(8,128)S(1)} %get-tuple-element.2), channel_id=1, source_target_pairs={{0,63},{1,0},{2,1},{3,2},{4,3},{5,4},{6,5},{7,6},{8,7},{9,8},{10,9... | collective-permute-start | bytes 786440 | tf_op jit(solution)/shard_map/ppermute | solution.py:24
  60.5 0.6 fusion.43
  61.1 0.6 fusion.27
  61.7 1.2 collective-permute-done.7
  63.0 0.6 fusion.19
  63.6 0.0 collective-permute-done.4
  63.6 0.6 convolution_add_fusion.5
  64.2 1.6 collective-permute-done.5
  65.8 0.6 fusion.8
  66.4 1.9 %collective-permute-start.10 = (f32[256,256]{1,0:T(8,128)S(1)}, f32[256,256]{1,0:T(8,128)S(1)}, u32[]{:S(2)}, u32[]{:S(2)}) collective-permute-start(f32[256,256]{1,0:T(8,128)S(1)} %fusion.8), channel_id=1, source_target_pairs={{0,2},{1,3},{2,4},{3,5},{4,6},{5,7},{6,8},{7,9},{8,10},{9,11},{10,... | collective-permute-start | bytes 786440 | tf_op jit(solution)/shard_map/ppermute | solution.py:24
  68.3 6.0 %collective-permute-start.11 = (f32[256,256]{1,0:T(8,128)S(1)}, f32[256,256]{1,0:T(8,128)S(1)}, u32[]{:S(2)}, u32[]{:S(2)}) collective-permute-start(f32[256,256]{1,0:T(8,128)S(1)} %fusion.8), channel_id=1, source_target_pairs={{0,62},{1,63},{2,0},{3,1},{4,2},{5,3},{6,4},{7,5},{8,6},{9,7},{10,... | collective-permute-start | bytes 786440 | tf_op jit(solution)/shard_map/ppermute | solution.py:24
  74.3 0.6 fusion.41
  75.0 1.9 %collective-permute-start.8 = (f32[256,256]{1,0:T(8,128)S(1)}, f32[256,256]{1,0:T(8,128)S(1)}, u32[]{:S(2)}, u32[]{:S(2)}) collective-permute-start(f32[256,256]{1,0:T(8,128)S(1)} %fusion.8), channel_id=1, source_target_pairs={{0,1},{1,2},{2,3},{3,4},{4,5},{5,6},{6,7},{7,8},{8,9},{9,10},{10,1... | collective-permute-start | bytes 786440 | tf_op jit(solution)/shard_map/ppermute | solution.py:24
  76.9 5.9 %collective-permute-start.9 = (f32[256,256]{1,0:T(8,128)S(1)}, f32[256,256]{1,0:T(8,128)S(1)}, u32[]{:S(2)}, u32[]{:S(2)}) collective-permute-start(f32[256,256]{1,0:T(8,128)S(1)} %fusion.8), channel_id=1, source_target_pairs={{0,63},{1,0},{2,1},{3,2},{4,3},{5,4},{6,5},{7,6},{8,7},{9,8},{10,9... | collective-permute-start | bytes 786440 | tf_op jit(solution)/shard_map/ppermute | solution.py:24
  82.8 0.0 collective-permute-done.10
  82.8 0.6 fusion.25
  83.4 0.6 fusion.17
  84.1 0.7 collective-permute-done.8
  84.8 0.6 convolution_add_fusion.3
  85.4 1.1 collective-permute-done.9
  86.5 0.6 fusion.11
  87.1 1.9 %collective-permute-start.14 = (f32[256,256]{1,0:T(8,128)S(1)}, f32[256,256]{1,0:T(8,128)S(1)}, u32[]{:S(2)}, u32[]{:S(2)}) collective-permute-start(f32[256,256]{1,0:T(8,128)S(1)} %fusion.11), channel_id=1, source_target_pairs={{0,2},{1,3},{2,4},{3,5},{4,6},{5,7},{6,8},{7,9},{8,10},{9,11},{10,... | collective-permute-start | bytes 786440 | tf_op jit(solution)/shard_map/ppermute | solution.py:24
  89.1 6.0 %collective-permute-start.15 = (f32[256,256]{1,0:T(8,128)S(1)}, f32[256,256]{1,0:T(8,128)S(1)}, u32[]{:S(2)}, u32[]{:S(2)}) collective-permute-start(f32[256,256]{1,0:T(8,128)S(1)} %fusion.11), channel_id=1, source_target_pairs={{0,62},{1,63},{2,0},{3,1},{4,2},{5,3},{6,4},{7,5},{8,6},{9,7},{10,... | collective-permute-start | bytes 786440 | tf_op jit(solution)/shard_map/ppermute | solution.py:24
  95.1 0.6 fusion.39
  95.7 1.9 %collective-permute-start.12 = (f32[256,256]{1,0:T(8,128)S(1)}, f32[256,256]{1,0:T(8,128)S(1)}, u32[]{:S(2)}, u32[]{:S(2)}) collective-permute-start(f32[256,256]{1,0:T(8,128)S(1)} %fusion.11), channel_id=1, source_target_pairs={{0,1},{1,2},{2,3},{3,4},{4,5},{5,6},{6,7},{7,8},{8,9},{9,10},{10,1... | collective-permute-start | bytes 786440 | tf_op jit(solution)/shard_map/ppermute | solution.py:24
  97.6 5.8 %collective-permute-start.13 = (f32[256,256]{1,0:T(8,128)S(1)}, f32[256,256]{1,0:T(8,128)S(1)}, u32[]{:S(2)}, u32[]{:S(2)}) collective-permute-start(f32[256,256]{1,0:T(8,128)S(1)} %fusion.11), channel_id=1, source_target_pairs={{0,63},{1,0},{2,1},{3,2},{4,3},{5,4},{6,5},{7,6},{8,7},{9,8},{10,9... | collective-permute-start | bytes 786440 | tf_op jit(solution)/shard_map/ppermute | solution.py:24
  103.4 0.0 collective-permute-done.14
  103.4 0.6 fusion.23
  104.0 0.6 fusion.15
  104.6 0.9 collective-permute-done.12
  105.5 0.6 convolution_add_fusion.1
  106.1 1.2 collective-permute-done.13
  107.3 0.6 fusion.14
  107.9 0.7 copy-done.1
  108.6 2.4 %fusion.53 = f32[256,2048]{1,0:T(8,128)} fusion(f32[256,256]{1,0:T(8,128)S(1)} %fusion.14, f32[256,2048]{1,0:T(8,128)S(1)} %copy-done), kind=kOutput, calls=%fused_computation.72 | convolution fusion | flops 805306368 | bytes 4456448 | tf_op jit(solution)/shard_map/dot_general | solution.py:95
  111.0 0.0 reduce-scatter.2.cloned.1.call-update
  111.1 0.9 copy-done.2
  112.0 0.6 fusion.54
  112.6 0.1 reshape.11
  112.7 28.3 %all_to_all.5 = f32[64,4,256]{2,1,0:T(4,128)S(1)} all-to-all(f32[64,4,256]{2,1,0:T(4,128)S(1)} %reshape.11), channel_id=1, replica_groups=mesh['grp'=8,'wide'=64] {'wide'}, dimensions={0} | all-to-all | bytes 524288 | tf_op jit(solution)/shard_map/all_to_all | solution.py:93
  141.0 0.1 reduce_sum.9
  141.1 0.6 broadcast_multiply_fusion.1
  141.7 21.3 %reduce-scatter.2.cloned.1.call-done = f32[256,256]{1,0:T(8,128)} async-done(((f32[256,2048]{1,0:T(8,128)}), f32[256,256]{1,0:T(8,128)}) %reduce-scatter.2.cloned.1.call-update) | async-done | bytes 262160 | tf_op jit(solution)/shard_map/reduce_scatter | solution.py:98
  (9 shorter events, 0.0 us)
Async XLA Ops:
  7.2 101.4 %copy-start = (f32[256,2048]{1,0:T(8,128)S(1)}, f32[256,2048]{1,0:T(8,128)}, u32[]{:S(2)}) copy-start(f32[256,2048]{1,0:T(8,128)} %param.7) | copy-start | bytes 6291460
  7.2 155.8 %reduce-scatter.2.cloned.1.call-start = ((), (), s32[]{:S(2)}) async-start(), calls=%async_computation.2 | async-start | bytes 2359296 | tf_op jit(solution)/shard_map/reduce_scatter | solution.py:98
  7.2 36.9 %collective-permute-start = (f32[256,256]{1,0:T(8,128)}, f32[256,256]{1,0:T(8,128)}, u32[]{:S(2)}, u32[]{:S(2)}) collective-permute-start(f32[256,256]{1,0:T(8,128)} %param.4), channel_id=1, source_target_pairs={{0,1},{1,2},{2,3},{3,4},{4,5},{5,6},{6,7},{7,8},{8,9},{9,10},{10,1... | collective-permute-start | bytes 786440 | tf_op jit(solution)/shard_map/ppermute | solution.py:24
  9.3 31.6 %collective-permute-start.3 = (f32[256,256]{1,0:T(8,128)}, f32[256,256]{1,0:T(8,128)}, u32[]{:S(2)}, u32[]{:S(2)}) collective-permute-start(f32[256,256]{1,0:T(8,128)} %param.4), channel_id=1, source_target_pairs={{0,62},{1,63},{2,0},{3,1},{4,2},{5,3},{6,4},{7,5},{8,6},{9,7},{10,... | collective-permute-start | bytes 786440 | tf_op jit(solution)/shard_map/ppermute | solution.py:24
  20.5 22.0 %collective-permute-start.2 = (f32[256,256]{1,0:T(8,128)}, f32[256,256]{1,0:T(8,128)}, u32[]{:S(2)}, u32[]{:S(2)}) collective-permute-start(f32[256,256]{1,0:T(8,128)} %param.4), channel_id=1, source_target_pairs={{0,2},{1,3},{2,4},{3,5},{4,6},{5,7},{6,8},{7,9},{8,10},{9,11},{10,... | collective-permute-start | bytes 786440 | tf_op jit(solution)/shard_map/ppermute | solution.py:24
  22.4 23.2 %collective-permute-start.1 = (f32[256,256]{1,0:T(8,128)}, f32[256,256]{1,0:T(8,128)}, u32[]{:S(2)}, u32[]{:S(2)}) collective-permute-start(f32[256,256]{1,0:T(8,128)} %param.4), channel_id=1, source_target_pairs={{0,63},{1,0},{2,1},{3,2},{4,3},{5,4},{6,5},{7,6},{8,7},{9,8},{10,9... | collective-permute-start | bytes 786440 | tf_op jit(solution)/shard_map/ppermute | solution.py:24
  40.9 4.8 %copy-start.3 = (f32[256,256]{1,0:T(8,128)S(1)}, f32[256,256]{1,0:T(8,128)}, u32[]{:S(2)}) copy-start(f32[256,256]{1,0:T(8,128)} %param.4) | copy-start | bytes 786436
  47.2 13.9 %collective-permute-start.6 = (f32[256,256]{1,0:T(8,128)S(1)}, f32[256,256]{1,0:T(8,128)S(1)}, u32[]{:S(2)}, u32[]{:S(2)}) collective-permute-start(f32[256,256]{1,0:T(8,128)S(1)} %get-tuple-element.2), channel_id=1, source_target_pairs={{0,2},{1,3},{2,4},{3,5},{4,6},{5,7},{6,8},{7,9},{8,10},{9,11},{10,... | collective-permute-start | bytes 786440 | tf_op jit(solution)/shard_map/ppermute | solution.py:24
  49.2 14.4 %collective-permute-start.4 = (f32[256,256]{1,0:T(8,128)S(1)}, f32[256,256]{1,0:T(8,128)S(1)}, u32[]{:S(2)}, u32[]{:S(2)}) collective-permute-start(f32[256,256]{1,0:T(8,128)S(1)} %get-tuple-element.2), channel_id=1, source_target_pairs={{0,1},{1,2},{2,3},{3,4},{4,5},{5,6},{6,7},{7,8},{8,9},{9,10},{10,1... | collective-permute-start | bytes 786440 | tf_op jit(solution)/shard_map/ppermute | solution.py:24
  51.1 11.9 %collective-permute-start.7 = (f32[256,256]{1,0:T(8,128)S(1)}, f32[256,256]{1,0:T(8,128)S(1)}, u32[]{:S(2)}, u32[]{:S(2)}) collective-permute-start(f32[256,256]{1,0:T(8,128)S(1)} %get-tuple-element.2), channel_id=1, source_target_pairs={{0,62},{1,63},{2,0},{3,1},{4,2},{5,3},{6,4},{7,5},{8,6},{9,7},{10,... | collective-permute-start | bytes 786440 | tf_op jit(solution)/shard_map/ppermute | solution.py:24
  57.1 8.6 %collective-permute-start.5 = (f32[256,256]{1,0:T(8,128)S(1)}, f32[256,256]{1,0:T(8,128)S(1)}, u32[]{:S(2)}, u32[]{:S(2)}) collective-permute-start(f32[256,256]{1,0:T(8,128)S(1)} %get-tuple-element.2), channel_id=1, source_target_pairs={{0,63},{1,0},{2,1},{3,2},{4,3},{5,4},{6,5},{7,6},{8,7},{9,8},{10,9... | collective-permute-start | bytes 786440 | tf_op jit(solution)/shard_map/ppermute | solution.py:24
  66.4 16.4 %collective-permute-start.10 = (f32[256,256]{1,0:T(8,128)S(1)}, f32[256,256]{1,0:T(8,128)S(1)}, u32[]{:S(2)}, u32[]{:S(2)}) collective-permute-start(f32[256,256]{1,0:T(8,128)S(1)} %fusion.8), channel_id=1, source_target_pairs={{0,2},{1,3},{2,4},{3,5},{4,6},{5,7},{6,8},{7,9},{8,10},{9,11},{10,... | collective-permute-start | bytes 786440 | tf_op jit(solution)/shard_map/ppermute | solution.py:24
  68.3 15.1 %collective-permute-start.11 = (f32[256,256]{1,0:T(8,128)S(1)}, f32[256,256]{1,0:T(8,128)S(1)}, u32[]{:S(2)}, u32[]{:S(2)}) collective-permute-start(f32[256,256]{1,0:T(8,128)S(1)} %fusion.8), channel_id=1, source_target_pairs={{0,62},{1,63},{2,0},{3,1},{4,2},{5,3},{6,4},{7,5},{8,6},{9,7},{10,... | collective-permute-start | bytes 786440 | tf_op jit(solution)/shard_map/ppermute | solution.py:24
  75.0 9.8 %collective-permute-start.8 = (f32[256,256]{1,0:T(8,128)S(1)}, f32[256,256]{1,0:T(8,128)S(1)}, u32[]{:S(2)}, u32[]{:S(2)}) collective-permute-start(f32[256,256]{1,0:T(8,128)S(1)} %fusion.8), channel_id=1, source_target_pairs={{0,1},{1,2},{2,3},{3,4},{4,5},{5,6},{6,7},{7,8},{8,9},{9,10},{10,1... | collective-permute-start | bytes 786440 | tf_op jit(solution)/shard_map/ppermute | solution.py:24
  76.9 9.6 %collective-permute-start.9 = (f32[256,256]{1,0:T(8,128)S(1)}, f32[256,256]{1,0:T(8,128)S(1)}, u32[]{:S(2)}, u32[]{:S(2)}) collective-permute-start(f32[256,256]{1,0:T(8,128)S(1)} %fusion.8), channel_id=1, source_target_pairs={{0,63},{1,0},{2,1},{3,2},{4,3},{5,4},{6,5},{7,6},{8,7},{9,8},{10,9... | collective-permute-start | bytes 786440 | tf_op jit(solution)/shard_map/ppermute | solution.py:24
  87.1 16.3 %collective-permute-start.14 = (f32[256,256]{1,0:T(8,128)S(1)}, f32[256,256]{1,0:T(8,128)S(1)}, u32[]{:S(2)}, u32[]{:S(2)}) collective-permute-start(f32[256,256]{1,0:T(8,128)S(1)} %fusion.11), channel_id=1, source_target_pairs={{0,2},{1,3},{2,4},{3,5},{4,6},{5,7},{6,8},{7,9},{8,10},{9,11},{10,... | collective-permute-start | bytes 786440 | tf_op jit(solution)/shard_map/ppermute | solution.py:24
  89.1 15.0 %collective-permute-start.15 = (f32[256,256]{1,0:T(8,128)S(1)}, f32[256,256]{1,0:T(8,128)S(1)}, u32[]{:S(2)}, u32[]{:S(2)}) collective-permute-start(f32[256,256]{1,0:T(8,128)S(1)} %fusion.11), channel_id=1, source_target_pairs={{0,62},{1,63},{2,0},{3,1},{4,2},{5,3},{6,4},{7,5},{8,6},{9,7},{10,... | collective-permute-start | bytes 786440 | tf_op jit(solution)/shard_map/ppermute | solution.py:24
  95.7 9.8 %collective-permute-start.12 = (f32[256,256]{1,0:T(8,128)S(1)}, f32[256,256]{1,0:T(8,128)S(1)}, u32[]{:S(2)}, u32[]{:S(2)}) collective-permute-start(f32[256,256]{1,0:T(8,128)S(1)} %fusion.11), channel_id=1, source_target_pairs={{0,1},{1,2},{2,3},{3,4},{4,5},{5,6},{6,7},{7,8},{8,9},{9,10},{10,1... | collective-permute-start | bytes 786440 | tf_op jit(solution)/shard_map/ppermute | solution.py:24
  97.6 9.6 %collective-permute-start.13 = (f32[256,256]{1,0:T(8,128)S(1)}, f32[256,256]{1,0:T(8,128)S(1)}, u32[]{:S(2)}, u32[]{:S(2)}) collective-permute-start(f32[256,256]{1,0:T(8,128)S(1)} %fusion.11), channel_id=1, source_target_pairs={{0,63},{1,0},{2,1},{3,2},{4,3},{5,4},{6,5},{7,6},{8,7},{9,8},{10,9... | collective-permute-start | bytes 786440 | tf_op jit(solution)/shard_map/ppermute | solution.py:24
  107.9 0.7 copy-start.1
  111.0 0.9 copy-start.2
Sparse Core Ops, SparseCore 0:
  111.2 51.7 reduce-scatter.1

commit v9 on v6

--- a/solution.py
+++ b/solution.py
@@ -30,21 +30,25 @@
     return hd.reshape(local_blocks * B, window_blocks * B)
 
 
-def apply_ham(field, hdense):
+def apply_ham(field, hdense, build=None):
     rows = field.shape[0]
+    far_up = passed_along(field, "wide", 2)
+    far_down = passed_along(field, "wide", -2)
+    if build is not None:
+        hdense, field = lax.optimization_barrier((build(), field))
     pieces = [
-        passed_along(field, "wide", 2),
+        far_up,
         passed_along(field, "wide", 1),
         field,
         passed_along(field, "wide", -1),
-        passed_along(field, "wide", -2),
+        far_down,
     ]
     total = None
     for idx in (2, 1, 3, 0, 4):
         term = jnp.dot(hdense[:, idx * rows:(idx + 1) * rows], pieces[idx], precision=HI,
                        preferred_element_type=jnp.float32)
         total = term if total is None else total + term
-    return total
+    return total, hdense
 
 
 def local(subspace, hblocks, pattern, rotation):
@@ -53,12 +57,12 @@
     owner = pattern // A_DEV
     relative = (owner - myself + HW + devcount) % devcount
     slot_index = relative * A_DEV + pattern % A_DEV
-    hdense = dense_hamiltonian(hblocks, slot_index)
     previous = subspace
-    current = (apply_ham(subspace, hdense) - cheb_center * subspace) / cheb_half
+    first, hdense = apply_ham(subspace, None, lambda: dense_hamiltonian(hblocks, slot_index))
+    current = (first - cheb_center * subspace) / cheb_half
     for step in range(DEGREE - 1):
         nextone = (
-            2.0 * (apply_ham(current, hdense) - cheb_center * current) / cheb_half
+            2.0 * (apply_ham(current, hdense)[0] - cheb_center * current) / cheb_half
             - previous
         )
         previous = current
@@ -75,7 +79,7 @@
     gathered = lax.all_to_all(pieces, "wide", 0, 0, tiled=True)
     correlation = jnp.sum(gathered, axis=0) / total_rows
     rot_term = jnp.dot(
-        current, rotation, precision=HI, preferred_element_type=jnp.float32
+        current, rotation, precision=lax.Precision.HIGH, preferred_element_type=jnp.float32
     )
     rotated = lax.psum_scatter(rot_term, "grp", scatter_dimension=1, tiled=True)
     return (rotated, correlation)

time: 166 us -> 169 us (1.018)
  local copies, waits for them, and re-layouts: 3.95 us -> 6.48 us
  waiting for transfers between devices: 30.3 us -> 28.2 us
    reshape x1 -> x2, local copies, waits for them, and re-layouts: 2.23 us -> 4.76 us  [dense_hamiltonian(): return hd.reshape(local_blocks * B, window_blocks * B)]
    dot_general x20, matrix products: 12.5 us -> 14.9 us  [apply_ham(): jnp.dot(hdense[:, idx * rows:(idx + 1) * rows], pieces[idx], precision=HI...]
    ppermute x16, waiting for transfers between devices: 8.9 us -> 6.73 us  [passed_along(): return lax.ppermute(value, axis, pairs)]
  transfers between devices with their start and end apart: 17 -> 17, of which waited for: 7 -> 7; matrix products, arithmetic and copies ran while one was open for 12% -> 15% of each run, Pallas kernels for 0% -> 0%
where the time goes in v9:
time: 169 us; the launch traced here: 168 us
  starting transfers between devices  65.6 us (39%)
  blocking collectives  28.3 us (17%)
  waiting for transfers between devices  28.2 us (17%)
  matrix products  23.7 us (14%)
  between operations  14.5 us (9%)
  local copies, waits for them, and re-layouts  6.48 us (4%)
    ppermute x16, starting transfers between devices, passed_along(): return lax.ppermute(value, axis, pairs)  65.6 us
    all_to_all x1, blocking collectives, local(): gathered = lax.all_to_all(pieces, 'wide', 0, 0, tiled=True)  28.3 us
    reduce_scatter x1, waiting for transfers between devices, local(): rotated = lax.psum_scatter(rot_term, 'grp', scatter_dimension=1, tiled=True)  21.4 us
    dot_general x20, matrix products, apply_ham(): jnp.dot(hdense[:, idx * rows:(idx + 1) * rows], pieces[idx], precision=HI...  14.9 us
    ppermute x16, waiting for transfers between devices, passed_along(): return lax.ppermute(value, axis, pairs)  6.73 us
    dot_general x1, matrix products, dense_hamiltonian(): hd = jnp.einsum('asp,asij->aipj', onehot, hblocks, precision=HI)  5.76 us
    reshape x2, local copies, waits for them, and re-layouts, dense_hamiltonian(): return hd.reshape(local_blocks * B, window_blocks * B)  4.76 us
  transfers between devices with their start and end apart: 17, of which 7 were waited for; matrix products, arithmetic and copies ran while one was open for 15% of the time, Pallas kernels for 0%

profile of v9, /device:TPU:6, one launch (start us, length us, event | category | flops | bytes accessed | tf_op | source)
XLA Modules:
  0.0 168.1 jit_solution(13226888252500809999)
XLA Ops:
  7.2 0.0 copy-start
  7.2 0.0 reduce-scatter.2.cloned.1.call-start
  7.2 11.3 %collective-permute-start.3 = (f32[256,256]{1,0:T(8,128)}, f32[256,256]{1,0:T(8,128)}, u32[]{:S(2)}, u32[]{:S(2)}) collective-permute-start(f32[256,256]{1,0:T(8,128)} %param.4), channel_id=1, source_target_pairs={{0,62},{1,63},{2,0},{3,1},{4,2},{5,3},{6,4},{7,5},{8,6},{9,7},{10,... | collective-permute-start | bytes 786440 | tf_op jit(solution)/shard_map/ppermute | solution.py:22
  18.6 1.9 %collective-permute-start.2 = (f32[256,256]{1,0:T(8,128)}, f32[256,256]{1,0:T(8,128)}, u32[]{:S(2)}, u32[]{:S(2)}) collective-permute-start(f32[256,256]{1,0:T(8,128)} %param.4), channel_id=1, source_target_pairs={{0,2},{1,3},{2,4},{3,5},{4,6},{5,7},{6,8},{7,9},{8,10},{9,11},{10,... | collective-permute-start | bytes 786440 | tf_op jit(solution)/shard_map/ppermute | solution.py:22
  20.5 0.7 fusion.59
  21.2 5.8 %fusion.2 = f32[4,64,20,64]{3,2,1,0:T(8,128)} fusion(f32[4,16,64,64]{3,2,1,0:T(8,128)} %param.5, s32[4,16]{1,0:T(4,128)S(1)} %fusion.59), kind=kOutput, calls=%fused_computation.2 | convolution fusion | flops 62915840 | bytes 2359552 | tf_op jit(solution)/shard_map/asp,asij->aipj/dot_general | solution.py:29
  27.0 3.0 %reshape.14 = f32[256,1280]{1,0:T(8,128)} reshape(f32[4,64,20,64]{3,2,1,0:T(8,128)} %fusion.2) | data formatting | bytes 2621440 | tf_op jit(solution)/shard_map/reshape | solution.py:30
  30.0 1.7 %copy.10 = f32[256,1280]{0,1:T(8,128)S(1)} copy(f32[256,1280]{1,0:T(8,128)} %reshape.14) | data formatting | bytes 2621440 | tf_op jit(solution)/shard_map/reshape | solution.py:30
  31.7 1.9 %collective-permute-start = (f32[256,256]{1,0:T(8,128)}, f32[256,256]{1,0:T(8,128)S(1)}, u32[]{:S(2)}, u32[]{:S(2)}) collective-permute-start(f32[256,256]{1,0:T(8,128)} %param.4), channel_id=1, source_target_pairs={{0,1},{1,2},{2,3},{3,4},{4,5},{5,6},{6,7},{7,8},{8,9},{9,10},{10,1... | collective-permute-start | bytes 786440 | tf_op jit(solution)/shard_map/ppermute | solution.py:22
  33.7 5.8 %collective-permute-start.1 = (f32[256,256]{1,0:T(8,128)}, f32[256,256]{1,0:T(8,128)S(1)}, u32[]{:S(2)}, u32[]{:S(2)}) collective-permute-start(f32[256,256]{1,0:T(8,128)} %param.4), channel_id=1, source_target_pairs={{0,63},{1,0},{2,1},{3,2},{4,3},{5,4},{6,5},{7,6},{8,7},{9,8},{10,9... | collective-permute-start | bytes 786440 | tf_op jit(solution)/shard_map/ppermute | solution.py:22
  39.4 1.6 fusion.50
  41.0 0.0 copy-start.3
  41.0 1.6 fusion.26
  42.6 0.0 collective-permute-done.2
  42.6 1.5 fusion.34
  44.2 0.0 collective-permute-done
  44.2 0.6 convolution_add_fusion.7
  44.8 0.6 broadcast_multiply_fusion
  45.4 1.9 %collective-permute-start.6 = (f32[256,256]{1,0:T(8,128)S(1)}, f32[256,256]{1,0:T(8,128)S(1)}, u32[]{:S(2)}, u32[]{:S(2)}) collective-permute-start(f32[256,256]{1,0:T(8,128)S(1)} %get-tuple-element.6), channel_id=1, source_target_pairs={{0,2},{1,3},{2,4},{3,5},{4,6},{5,7},{6,8},{7,9},{8,10},{9,11},{10,... | collective-permute-start | bytes 786440 | tf_op jit(solution)/shard_map/ppermute | solution.py:22
  47.4 1.9 %collective-permute-start.4 = (f32[256,256]{1,0:T(8,128)S(1)}, f32[256,256]{1,0:T(8,128)S(1)}, u32[]{:S(2)}, u32[]{:S(2)}) collective-permute-start(f32[256,256]{1,0:T(8,128)S(1)} %get-tuple-element.6), channel_id=1, source_target_pairs={{0,1},{1,2},{2,3},{3,4},{4,5},{5,6},{6,7},{7,8},{8,9},{9,10},{10,1... | collective-permute-start | bytes 786440 | tf_op jit(solution)/shard_map/ppermute | solution.py:22
  49.3 6.0 %collective-permute-start.7 = (f32[256,256]{1,0:T(8,128)S(1)}, f32[256,256]{1,0:T(8,128)S(1)}, u32[]{:S(2)}, u32[]{:S(2)}) collective-permute-start(f32[256,256]{1,0:T(8,128)S(1)} %get-tuple-element.6), channel_id=1, source_target_pairs={{0,62},{1,63},{2,0},{3,1},{4,2},{5,3},{6,4},{7,5},{8,6},{9,7},{10,... | collective-permute-start | bytes 786440 | tf_op jit(solution)/shard_map/ppermute | solution.py:22
  55.3 3.4 %collective-permute-start.5 = (f32[256,256]{1,0:T(8,128)S(1)}, f32[256,256]{1,0:T(8,128)S(1)}, u32[]{:S(2)}, u32[]{:S(2)}) collective-permute-start(f32[256,256]{1,0:T(8,128)S(1)} %get-tuple-element.6), channel_id=1, source_target_pairs={{0,63},{1,0},{2,1},{3,2},{4,3},{5,4},{6,5},{7,6},{8,7},{9,8},{10,9... | collective-permute-start | bytes 786440 | tf_op jit(solution)/shard_map/ppermute | solution.py:22
  58.7 0.6 fusion.48
  59.3 0.0 collective-permute-done.6
  59.3 0.6 fusion.32
  59.9 1.2 collective-permute-done.7
  61.1 0.6 fusion.24
  61.7 0.0 collective-permute-done.4
  61.8 0.6 convolution_add_fusion.5
  62.4 1.6 collective-permute-done.5
  64.0 0.6 fusion.13
  64.6 1.9 %collective-permute-start.10 = (f32[256,256]{1,0:T(8,128)S(1)}, f32[256,256]{1,0:T(8,128)S(1)}, u32[]{:S(2)}, u32[]{:S(2)}) collective-permute-start(f32[256,256]{1,0:T(8,128)S(1)} %fusion.13), channel_id=1, source_target_pairs={{0,2},{1,3},{2,4},{3,5},{4,6},{5,7},{6,8},{7,9},{8,10},{9,11},{10,... | collective-permute-start | bytes 786440 | tf_op jit(solution)/shard_map/ppermute | solution.py:22
  66.5 6.0 %collective-permute-start.11 = (f32[256,256]{1,0:T(8,128)S(1)}, f32[256,256]{1,0:T(8,128)S(1)}, u32[]{:S(2)}, u32[]{:S(2)}) collective-permute-start(f32[256,256]{1,0:T(8,128)S(1)} %fusion.13), channel_id=1, source_target_pairs={{0,62},{1,63},{2,0},{3,1},{4,2},{5,3},{6,4},{7,5},{8,6},{9,7},{10,... | collective-permute-start | bytes 786440 | tf_op jit(solution)/shard_map/ppermute | solution.py:22
  72.5 0.6 fusion.46
  73.1 1.9 %collective-permute-start.8 = (f32[256,256]{1,0:T(8,128)S(1)}, f32[256,256]{1,0:T(8,128)S(1)}, u32[]{:S(2)}, u32[]{:S(2)}) collective-permute-start(f32[256,256]{1,0:T(8,128)S(1)} %fusion.13), channel_id=1, source_target_pairs={{0,1},{1,2},{2,3},{3,4},{4,5},{5,6},{6,7},{7,8},{8,9},{9,10},{10,1... | collective-permute-start | bytes 786440 | tf_op jit(solution)/shard_map/ppermute | solution.py:22
  75.1 5.9 %collective-permute-start.9 = (f32[256,256]{1,0:T(8,128)S(1)}, f32[256,256]{1,0:T(8,128)S(1)}, u32[]{:S(2)}, u32[]{:S(2)}) collective-permute-start(f32[256,256]{1,0:T(8,128)S(1)} %fusion.13), channel_id=1, source_target_pairs={{0,63},{1,0},{2,1},{3,2},{4,3},{5,4},{6,5},{7,6},{8,7},{9,8},{10,9... | collective-permute-start | bytes 786440 | tf_op jit(solution)/shard_map/ppermute | solution.py:22
  81.0 0.0 collective-permute-done.10
  81.0 0.6 fusion.30
  81.6 0.6 fusion.22
  82.2 0.7 collective-permute-done.8
  82.9 0.6 convolution_add_fusion.3
  83.5 1.1 collective-permute-done.9
  84.7 0.6 fusion.16
  85.3 1.9 %collective-permute-start.14 = (f32[256,256]{1,0:T(8,128)S(1)}, f32[256,256]{1,0:T(8,128)S(1)}, u32[]{:S(2)}, u32[]{:S(2)}) collective-permute-start(f32[256,256]{1,0:T(8,128)S(1)} %fusion.16), channel_id=1, source_target_pairs={{0,2},{1,3},{2,4},{3,5},{4,6},{5,7},{6,8},{7,9},{8,10},{9,11},{10,... | collective-permute-start | bytes 786440 | tf_op jit(solution)/shard_map/ppermute | solution.py:22
  87.3 6.0 %collective-permute-start.15 = (f32[256,256]{1,0:T(8,128)S(1)}, f32[256,256]{1,0:T(8,128)S(1)}, u32[]{:S(2)}, u32[]{:S(2)}) collective-permute-start(f32[256,256]{1,0:T(8,128)S(1)} %fusion.16), channel_id=1, source_target_pairs={{0,62},{1,63},{2,0},{3,1},{4,2},{5,3},{6,4},{7,5},{8,6},{9,7},{10,... | collective-permute-start | bytes 786440 | tf_op jit(solution)/shard_map/ppermute | solution.py:22
  93.3 0.6 fusion.44
  93.9 1.9 %collective-permute-start.12 = (f32[256,256]{1,0:T(8,128)S(1)}, f32[256,256]{1,0:T(8,128)S(1)}, u32[]{:S(2)}, u32[]{:S(2)}) collective-permute-start(f32[256,256]{1,0:T(8,128)S(1)} %fusion.16), channel_id=1, source_target_pairs={{0,1},{1,2},{2,3},{3,4},{4,5},{5,6},{6,7},{7,8},{8,9},{9,10},{10,1... | collective-permute-start | bytes 786440 | tf_op jit(solution)/shard_map/ppermute | solution.py:22
  95.8 5.8 %collective-permute-start.13 = (f32[256,256]{1,0:T(8,128)S(1)}, f32[256,256]{1,0:T(8,128)S(1)}, u32[]{:S(2)}, u32[]{:S(2)}) collective-permute-start(f32[256,256]{1,0:T(8,128)S(1)} %fusion.16), channel_id=1, source_target_pairs={{0,63},{1,0},{2,1},{3,2},{4,3},{5,4},{6,5},{7,6},{8,7},{9,8},{10,9... | collective-permute-start | bytes 786440 | tf_op jit(solution)/shard_map/ppermute | solution.py:22
  101.6 0.6 fusion.28
  102.2 0.6 fusion.20
  102.8 0.9 collective-permute-done.12
  103.7 0.6 convolution_add_fusion.1
  104.3 1.2 collective-permute-done.13
  105.5 0.6 fusion.19
  106.1 0.7 copy-done.1
  106.8 2.4 %fusion.61 = f32[256,2048]{1,0:T(8,128)} fusion(f32[256,256]{1,0:T(8,128)S(1)} %fusion.19, f32[256,2048]{1,0:T(8,128)S(1)} %copy-done), kind=kOutput, calls=%fused_computation.78 | convolution fusion | flops 805306368 | bytes 4456448 | tf_op jit(solution)/shard_map/dot_general | solution.py:81
  109.2 0.0 reduce-scatter.2.cloned.1.call-update
  109.3 0.9 copy-done.2
  110.2 0.6 fusion.62
  110.8 0.1 reshape.12
  110.9 28.3 %all_to_all.5 = f32[64,4,256]{2,1,0:T(4,128)S(1)} all-to-all(f32[64,4,256]{2,1,0:T(4,128)S(1)} %reshape.12), channel_id=1, replica_groups=mesh['grp'=8,'wide'=64] {'wide'}, dimensions={0} | all-to-all | bytes 524288 | tf_op jit(solution)/shard_map/all_to_all | solution.py:79
  139.2 0.1 reduce_sum.9
  139.2 0.6 broadcast_multiply_fusion.1
  139.8 21.4 %reduce-scatter.2.cloned.1.call-done = f32[256,256]{1,0:T(8,128)} async-done(((f32[256,2048]{1,0:T(8,128)}), f32[256,256]{1,0:T(8,128)}) %reduce-scatter.2.cloned.1.call-update) | async-done | bytes 262160 | tf_op jit(solution)/shard_map/reduce_scatter | solution.py:84
  (9 shorter events, 0.0 us)
Async XLA Ops:
  7.2 99.6 %copy-start = (f32[256,2048]{1,0:T(8,128)S(1)}, f32[256,2048]{1,0:T(8,128)}, u32[]{:S(2)}) copy-start(f32[256,2048]{1,0:T(8,128)} %param.7) | copy-start | bytes 6291460
  7.2 154.1 %reduce-scatter.2.cloned.1.call-start = ((), (), s32[]{:S(2)}) async-start(), calls=%async_computation.2 | async-start | bytes 2359296 | tf_op jit(solution)/shard_map/reduce_scatter | solution.py:84
  7.2 33.8 %collective-permute-start.3 = (f32[256,256]{1,0:T(8,128)}, f32[256,256]{1,0:T(8,128)}, u32[]{:S(2)}, u32[]{:S(2)}) collective-permute-start(f32[256,256]{1,0:T(8,128)} %param.4), channel_id=1, source_target_pairs={{0,62},{1,63},{2,0},{3,1},{4,2},{5,3},{6,4},{7,5},{8,6},{9,7},{10,... | collective-permute-start | bytes 786440 | tf_op jit(solution)/shard_map/ppermute | solution.py:22
  18.6 24.0 %collective-permute-start.2 = (f32[256,256]{1,0:T(8,128)}, f32[256,256]{1,0:T(8,128)}, u32[]{:S(2)}, u32[]{:S(2)}) collective-permute-start(f32[256,256]{1,0:T(8,128)} %param.4), channel_id=1, source_target_pairs={{0,2},{1,3},{2,4},{3,5},{4,6},{5,7},{6,8},{7,9},{8,10},{9,11},{10,... | collective-permute-start | bytes 786440 | tf_op jit(solution)/shard_map/ppermute | solution.py:22
  31.7 12.4 %collective-permute-start = (f32[256,256]{1,0:T(8,128)}, f32[256,256]{1,0:T(8,128)S(1)}, u32[]{:S(2)}, u32[]{:S(2)}) collective-permute-start(f32[256,256]{1,0:T(8,128)} %param.4), channel_id=1, source_target_pairs={{0,1},{1,2},{2,3},{3,4},{4,5},{5,6},{6,7},{7,8},{8,9},{9,10},{10,1... | collective-permute-start | bytes 786440 | tf_op jit(solution)/shard_map/ppermute | solution.py:22
  33.7 11.1 %collective-permute-start.1 = (f32[256,256]{1,0:T(8,128)}, f32[256,256]{1,0:T(8,128)S(1)}, u32[]{:S(2)}, u32[]{:S(2)}) collective-permute-start(f32[256,256]{1,0:T(8,128)} %param.4), channel_id=1, source_target_pairs={{0,63},{1,0},{2,1},{3,2},{4,3},{5,4},{6,5},{7,6},{8,7},{9,8},{10,9... | collective-permute-start | bytes 786440 | tf_op jit(solution)/shard_map/ppermute | solution.py:22
  41.0 3.8 %copy-start.3 = (f32[256,256]{1,0:T(8,128)S(1)}, f32[256,256]{1,0:T(8,128)}, u32[]{:S(2)}) copy-start(f32[256,256]{1,0:T(8,128)} %param.4) | copy-start | bytes 786436
  45.4 13.9 %collective-permute-start.6 = (f32[256,256]{1,0:T(8,128)S(1)}, f32[256,256]{1,0:T(8,128)S(1)}, u32[]{:S(2)}, u32[]{:S(2)}) collective-permute-start(f32[256,256]{1,0:T(8,128)S(1)} %get-tuple-element.6), channel_id=1, source_target_pairs={{0,2},{1,3},{2,4},{3,5},{4,6},{5,7},{6,8},{7,9},{8,10},{9,11},{10,... | collective-permute-start | bytes 786440 | tf_op jit(solution)/shard_map/ppermute | solution.py:22
  47.4 14.4 %collective-permute-start.4 = (f32[256,256]{1,0:T(8,128)S(1)}, f32[256,256]{1,0:T(8,128)S(1)}, u32[]{:S(2)}, u32[]{:S(2)}) collective-permute-start(f32[256,256]{1,0:T(8,128)S(1)} %get-tuple-element.6), channel_id=1, source_target_pairs={{0,1},{1,2},{2,3},{3,4},{4,5},{5,6},{6,7},{7,8},{8,9},{9,10},{10,1... | collective-permute-start | bytes 786440 | tf_op jit(solution)/shard_map/ppermute | solution.py:22
  49.3 11.9 %collective-permute-start.7 = (f32[256,256]{1,0:T(8,128)S(1)}, f32[256,256]{1,0:T(8,128)S(1)}, u32[]{:S(2)}, u32[]{:S(2)}) collective-permute-start(f32[256,256]{1,0:T(8,128)S(1)} %get-tuple-element.6), channel_id=1, source_target_pairs={{0,62},{1,63},{2,0},{3,1},{4,2},{5,3},{6,4},{7,5},{8,6},{9,7},{10,... | collective-permute-start | bytes 786440 | tf_op jit(solution)/shard_map/ppermute | solution.py:22
  55.3 8.6 %collective-permute-start.5 = (f32[256,256]{1,0:T(8,128)S(1)}, f32[256,256]{1,0:T(8,128)S(1)}, u32[]{:S(2)}, u32[]{:S(2)}) collective-permute-start(f32[256,256]{1,0:T(8,128)S(1)} %get-tuple-element.6), channel_id=1, source_target_pairs={{0,63},{1,0},{2,1},{3,2},{4,3},{5,4},{6,5},{7,6},{8,7},{9,8},{10,9... | collective-permute-start | bytes 786440 | tf_op jit(solution)/shard_map/ppermute | solution.py:22
  64.6 16.4 %collective-permute-start.10 = (f32[256,256]{1,0:T(8,128)S(1)}, f32[256,256]{1,0:T(8,128)S(1)}, u32[]{:S(2)}, u32[]{:S(2)}) collective-permute-start(f32[256,256]{1,0:T(8,128)S(1)} %fusion.13), channel_id=1, source_target_pairs={{0,2},{1,3},{2,4},{3,5},{4,6},{5,7},{6,8},{7,9},{8,10},{9,11},{10,... | collective-permute-start | bytes 786440 | tf_op jit(solution)/shard_map/ppermute | solution.py:22
  66.5 15.1 %collective-permute-start.11 = (f32[256,256]{1,0:T(8,128)S(1)}, f32[256,256]{1,0:T(8,128)S(1)}, u32[]{:S(2)}, u32[]{:S(2)}) collective-permute-start(f32[256,256]{1,0:T(8,128)S(1)} %fusion.13), channel_id=1, source_target_pairs={{0,62},{1,63},{2,0},{3,1},{4,2},{5,3},{6,4},{7,5},{8,6},{9,7},{10,... | collective-permute-start | bytes 786440 | tf_op jit(solution)/shard_map/ppermute | solution.py:22
  73.1 9.8 %collective-permute-start.8 = (f32[256,256]{1,0:T(8,128)S(1)}, f32[256,256]{1,0:T(8,128)S(1)}, u32[]{:S(2)}, u32[]{:S(2)}) collective-permute-start(f32[256,256]{1,0:T(8,128)S(1)} %fusion.13), channel_id=1, source_target_pairs={{0,1},{1,2},{2,3},{3,4},{4,5},{5,6},{6,7},{7,8},{8,9},{9,10},{10,1... | collective-permute-start | bytes 786440 | tf_op jit(solution)/shard_map/ppermute | solution.py:22
  75.1 9.6 %collective-permute-start.9 = (f32[256,256]{1,0:T(8,128)S(1)}, f32[256,256]{1,0:T(8,128)S(1)}, u32[]{:S(2)}, u32[]{:S(2)}) collective-permute-start(f32[256,256]{1,0:T(8,128)S(1)} %fusion.13), channel_id=1, source_target_pairs={{0,63},{1,0},{2,1},{3,2},{4,3},{5,4},{6,5},{7,6},{8,7},{9,8},{10,9... | collective-permute-start | bytes 786440 | tf_op jit(solution)/shard_map/ppermute | solution.py:22
  85.3 16.3 %collective-permute-start.14 = (f32[256,256]{1,0:T(8,128)S(1)}, f32[256,256]{1,0:T(8,128)S(1)}, u32[]{:S(2)}, u32[]{:S(2)}) collective-permute-start(f32[256,256]{1,0:T(8,128)S(1)} %fusion.16), channel_id=1, source_target_pairs={{0,2},{1,3},{2,4},{3,5},{4,6},{5,7},{6,8},{7,9},{8,10},{9,11},{10,... | collective-permute-start | bytes 786440 | tf_op jit(solution)/shard_map/ppermute | solution.py:22
  87.3 15.0 %collective-permute-start.15 = (f32[256,256]{1,0:T(8,128)S(1)}, f32[256,256]{1,0:T(8,128)S(1)}, u32[]{:S(2)}, u32[]{:S(2)}) collective-permute-start(f32[256,256]{1,0:T(8,128)S(1)} %fusion.16), channel_id=1, source_target_pairs={{0,62},{1,63},{2,0},{3,1},{4,2},{5,3},{6,4},{7,5},{8,6},{9,7},{10,... | collective-permute-start | bytes 786440 | tf_op jit(solution)/shard_map/ppermute | solution.py:22
  93.9 9.8 %collective-permute-start.12 = (f32[256,256]{1,0:T(8,128)S(1)}, f32[256,256]{1,0:T(8,128)S(1)}, u32[]{:S(2)}, u32[]{:S(2)}) collective-permute-start(f32[256,256]{1,0:T(8,128)S(1)} %fusion.16), channel_id=1, source_target_pairs={{0,1},{1,2},{2,3},{3,4},{4,5},{5,6},{6,7},{7,8},{8,9},{9,10},{10,1... | collective-permute-start | bytes 786440 | tf_op jit(solution)/shard_map/ppermute | solution.py:22
  95.8 9.6 %collective-permute-start.13 = (f32[256,256]{1,0:T(8,128)S(1)}, f32[256,256]{1,0:T(8,128)S(1)}, u32[]{:S(2)}, u32[]{:S(2)}) collective-permute-start(f32[256,256]{1,0:T(8,128)S(1)} %fusion.16), channel_id=1, source_target_pairs={{0,63},{1,0},{2,1},{3,2},{4,3},{5,4},{6,5},{7,6},{8,7},{9,8},{10,9... | collective-permute-start | bytes 786440 | tf_op jit(solution)/shard_map/ppermute | solution.py:22
  106.1 0.7 copy-start.1
  109.2 0.9 copy-start.2
Sparse Core Ops, SparseCore 0:
  109.4 51.8 reduce-scatter.1

commit v10 on v6

--- a/solution.py
+++ b/solution.py
@@ -25,8 +25,16 @@
 def dense_hamiltonian(hblocks, slot_index):
     local_blocks = hblocks.shape[0]
     window_blocks = (2 * HW + 1) * A_DEV
-    onehot = (slot_index[:, :, None] == jnp.arange(window_blocks)[None, None, :]).astype(jnp.float32)
-    hd = jnp.einsum("asp,asij->aipj", onehot, hblocks, precision=HI)
+    onehot = (slot_index[:, :, None] == jnp.arange(window_blocks)[None, None, :]).astype(jnp.bfloat16)
+    h1 = lax.reduce_precision(hblocks, exponent_bits=8, mantissa_bits=7)
+    rest = hblocks - h1
+    h2 = lax.reduce_precision(rest, exponent_bits=8, mantissa_bits=7)
+    h3 = rest - h2
+    hd = None
+    for part in (h3, h2, h1):
+        term = jnp.einsum("asp,asij->aipj", onehot, part.astype(jnp.bfloat16),
+                          preferred_element_type=jnp.float32)
+        hd = term if hd is None else hd + term
     return hd.reshape(local_blocks * B, window_blocks * B)
 
 

time: 166 us -> 167 us (level)
  other arithmetic: 1.39 us -> 4.53 us
    convert_element_type x0 -> x1, other arithmetic: none -> 3.83 us  [dense_hamiltonian(): part.astype(jnp.bfloat16)]
    dot_general x1 -> x3, matrix products: 5.76 us -> 5.73 us  [dense_hamiltonian(): jnp.einsum('asp,asij->aipj', onehot, part.astype(jnp.bfloat16), preferred...]
  transfers between devices with their start and end apart: 17 -> 17, of which waited for: 7 -> 7; matrix products, arithmetic and copies ran while one was open for 12% -> 14% of each run, Pallas kernels for 0% -> 0%
where the time goes in v10:
time: 167 us; the launch traced here: 166 us
  starting transfers between devices  63.3 us (38%)
  waiting for transfers between devices  30.2 us (18%)
  blocking collectives  27.1 us (16%)
  matrix products  22.1 us (13%)
  between operations  14.5 us (9%)
  other arithmetic  4.53 us (3%)
  local copies, waits for them, and re-layouts  4.29 us (3%)
    ppermute x16, starting transfers between devices, passed_along(): return lax.ppermute(value, axis, pairs)  63.2 us
    all_to_all x1, blocking collectives, local(): gathered = lax.all_to_all(pieces, 'wide', 0, 0, tiled=True)  27.1 us
    reduce_scatter x1, waiting for transfers between devices, local(): rotated = lax.psum_scatter(rot_term, 'grp', scatter_dimension=1, tiled=True)  21.3 us
    dot_general x20, matrix products, apply_ham(): jnp.dot(hdense[:, idx * rows:(idx + 1) * rows], pieces[idx], precision=HI...  12.5 us
    ppermute x16, waiting for transfers between devices, passed_along(): return lax.ppermute(value, axis, pairs)  8.9 us
    dot_general x3, matrix products, dense_hamiltonian(): jnp.einsum('asp,asij->aipj', onehot, part.astype(jnp.bfloat16), preferred...  5.73 us
    convert_element_type x1, other arithmetic, dense_hamiltonian(): part.astype(jnp.bfloat16)  3.83 us
  transfers between devices with their start and end apart: 17, of which 7 were waited for; matrix products, arithmetic and copies ran while one was open for 14% of the time, Pallas kernels for 0%

profile of v10, /device:TPU:6, one launch (start us, length us, event | category | flops | bytes accessed | tf_op | source)
XLA Modules:
  0.0 165.9 jit_solution(2798419501371841269)
XLA Ops:
  7.2 0.0 copy-start
  7.2 0.0 reduce-scatter.2.cloned.1.call-start
  7.2 2.1 %collective-permute-start = (f32[256,256]{1,0:T(8,128)}, f32[256,256]{1,0:T(8,128)}, u32[]{:S(2)}, u32[]{:S(2)}) collective-permute-start(f32[256,256]{1,0:T(8,128)} %param.4), channel_id=1, source_target_pairs={{0,1},{1,2},{2,3},{3,4},{4,5},{5,6},{6,7},{7,8},{8,9},{9,10},{10,1... | collective-permute-start | bytes 786440 | tf_op jit(solution)/shard_map/ppermute | solution.py:22
  9.3 4.3 %collective-permute-start.2 = (f32[256,256]{1,0:T(8,128)}, f32[256,256]{1,0:T(8,128)}, u32[]{:S(2)}, u32[]{:S(2)}) collective-permute-start(f32[256,256]{1,0:T(8,128)} %param.4), channel_id=1, source_target_pairs={{0,2},{1,3},{2,4},{3,5},{4,6},{5,7},{6,8},{7,9},{8,10},{9,11},{10,... | collective-permute-start | bytes 786440 | tf_op jit(solution)/shard_map/ppermute | solution.py:22
  13.6 8.9 %collective-permute-start.3 = (f32[256,256]{1,0:T(8,128)}, f32[256,256]{1,0:T(8,128)}, u32[]{:S(2)}, u32[]{:S(2)}) collective-permute-start(f32[256,256]{1,0:T(8,128)} %param.4), channel_id=1, source_target_pairs={{0,62},{1,63},{2,0},{3,1},{4,2},{5,3},{6,4},{7,5},{8,6},{9,7},{10,... | collective-permute-start | bytes 786440 | tf_op jit(solution)/shard_map/ppermute | solution.py:22
  22.4 3.4 %collective-permute-start.1 = (f32[256,256]{1,0:T(8,128)}, f32[256,256]{1,0:T(8,128)}, u32[]{:S(2)}, u32[]{:S(2)}) collective-permute-start(f32[256,256]{1,0:T(8,128)} %param.4), channel_id=1, source_target_pairs={{0,63},{1,0},{2,1},{3,2},{4,3},{5,4},{6,5},{7,6},{8,7},{9,8},{10,9... | collective-permute-start | bytes 786440 | tf_op jit(solution)/shard_map/ppermute | solution.py:22
  25.8 3.8 %reduce-precision_convert_fusion.1 = (bf16[4,16,64,64]{3,2,1,0:T(8,128)(2,1)}, bf16[4,16,64,64]{3,2,1,0:T(8,128)(2,1)S(1)}, bf16[4,16,64,64]{3,2,1,0:T(8,128)(2,1)}) fusion(f32[4,16,64,64]{3,2,1,0:T(8,128)} %param.5), kind=kLoop, calls=%fused_computation.3 | loop fusion | flops 1835008 | bytes 2621440 | tf_op jit(solution)/shard_map/convert_element_type | solution.py:35
  29.7 2.1 %fusion.17 = f32[4,64,64,20]{2,3,1,0:T(8,128)S(1)} fusion(bf16[4,16,64,64]{3,2,1,0:T(8,128)(2,1)} %get-tuple-element.4, s32[4,16]{1,0:T(4,128)S(1)} %fusion.64), kind=kOutput, calls=%fused_computation.30 | convolution fusion | flops 10487040 | bytes 1835264 | tf_op jit(solution)/shard_map/asp,asij->aipj/dot_general | solution.py:35
  31.8 0.9 fusion.19
  32.7 0.3 copy-done.3
  33.0 2.8 %bitcast_add_fusion = f32[4,64,20,64]{3,2,1,0:T(8,128)} fusion(f32[4,64,64,20]{2,3,1,0:T(8,128)S(1)} %fusion.19, f32[4,64,64,20]{2,3,1,0:T(8,128)S(1)} %fusion.17, bf16[4,16,64,64]{3,2,1,0:T(8,128)(2,1)S(1)} %copy-done.3, s32[4,16]{1,0:T(4,128)S(1)} %fusion.64), kind=kOutput, calls=%fused_computation | convolution fusion | flops 11142400 | bytes 4456704 | tf_op jit(solution)/shard_map/asp,asij->aipj/dot_general | solution.py:35
  35.8 2.2 %reshape.14 = f32[256,1280]{1,0:T(8,128)S(1)} reshape(f32[4,64,20,64]{3,2,1,0:T(8,128)} %bitcast_add_fusion) | data formatting | bytes 2621440 | tf_op jit(solution)/shard_map/reshape | solution.py:38
  38.0 1.3 fusion.49
  39.4 0.0 copy-start.4
  39.4 1.4 fusion.33
  40.7 0.0 collective-permute-done.3
  40.8 1.3 fusion.25
  42.1 1.3 convolution_add_fusion.7
  43.5 1.4 broadcast_multiply_fusion
  44.8 1.9 %collective-permute-start.6 = (f32[256,256]{1,0:T(8,128)S(1)}, f32[256,256]{1,0:T(8,128)S(1)}, u32[]{:S(2)}, u32[]{:S(2)}) collective-permute-start(f32[256,256]{1,0:T(8,128)S(1)} %get-tuple-element.5), channel_id=1, source_target_pairs={{0,2},{1,3},{2,4},{3,5},{4,6},{5,7},{6,8},{7,9},{8,10},{9,11},{10,... | collective-permute-start | bytes 786440 | tf_op jit(solution)/shard_map/ppermute | solution.py:22
  46.8 1.9 %collective-permute-start.4 = (f32[256,256]{1,0:T(8,128)S(1)}, f32[256,256]{1,0:T(8,128)S(1)}, u32[]{:S(2)}, u32[]{:S(2)}) collective-permute-start(f32[256,256]{1,0:T(8,128)S(1)} %get-tuple-element.5), channel_id=1, source_target_pairs={{0,1},{1,2},{2,3},{3,4},{4,5},{5,6},{6,7},{7,8},{8,9},{9,10},{10,1... | collective-permute-start | bytes 786440 | tf_op jit(solution)/shard_map/ppermute | solution.py:22
  48.7 6.0 %collective-permute-start.7 = (f32[256,256]{1,0:T(8,128)S(1)}, f32[256,256]{1,0:T(8,128)S(1)}, u32[]{:S(2)}, u32[]{:S(2)}) collective-permute-start(f32[256,256]{1,0:T(8,128)S(1)} %get-tuple-element.5), channel_id=1, source_target_pairs={{0,62},{1,63},{2,0},{3,1},{4,2},{5,3},{6,4},{7,5},{8,6},{9,7},{10,... | collective-permute-start | bytes 786440 | tf_op jit(solution)/shard_map/ppermute | solution.py:22
  54.7 3.4 %collective-permute-start.5 = (f32[256,256]{1,0:T(8,128)S(1)}, f32[256,256]{1,0:T(8,128)S(1)}, u32[]{:S(2)}, u32[]{:S(2)}) collective-permute-start(f32[256,256]{1,0:T(8,128)S(1)} %get-tuple-element.5), channel_id=1, source_target_pairs={{0,63},{1,0},{2,1},{3,2},{4,3},{5,4},{6,5},{7,6},{8,7},{9,8},{10,9... | collective-permute-start | bytes 786440 | tf_op jit(solution)/shard_map/ppermute | solution.py:22
  58.1 0.4 fusion.47
  58.5 0.4 fusion.31
  58.9 1.7 %collective-permute-done.7 = f32[256,256]{1,0:T(8,128)S(1)} collective-permute-done((f32[256,256]{1,0:T(8,128)S(1)}, f32[256,256]{1,0:T(8,128)S(1)}, u32[]{:S(2)}, u32[]{:S(2)}) %collective-permute-start.7) | collective-permute-done | bytes 262176 | tf_op jit(solution)/shard_map/ppermute | solution.py:22
  60.5 0.4 fusion.23
  60.9 0.4 convolution_add_fusion.5
  61.3 2.0 %collective-permute-done.5 = f32[256,256]{1,0:T(8,128)S(1)} collective-permute-done((f32[256,256]{1,0:T(8,128)S(1)}, f32[256,256]{1,0:T(8,128)S(1)}, u32[]{:S(2)}, u32[]{:S(2)}) %collective-permute-start.5) | collective-permute-done | bytes 262176 | tf_op jit(solution)/shard_map/ppermute | solution.py:22
  63.4 0.4 fusion.9
  63.8 1.9 %collective-permute-start.10 = (f32[256,256]{1,0:T(8,128)S(1)}, f32[256,256]{1,0:T(8,128)S(1)}, u32[]{:S(2)}, u32[]{:S(2)}) collective-permute-start(f32[256,256]{1,0:T(8,128)S(1)} %fusion.9), channel_id=1, source_target_pairs={{0,2},{1,3},{2,4},{3,5},{4,6},{5,7},{6,8},{7,9},{8,10},{9,11},{10,... | collective-permute-start | bytes 786440 | tf_op jit(solution)/shard_map/ppermute | solution.py:22
  65.7 6.0 %collective-permute-start.11 = (f32[256,256]{1,0:T(8,128)S(1)}, f32[256,256]{1,0:T(8,128)S(1)}, u32[]{:S(2)}, u32[]{:S(2)}) collective-permute-start(f32[256,256]{1,0:T(8,128)S(1)} %fusion.9), channel_id=1, source_target_pairs={{0,62},{1,63},{2,0},{3,1},{4,2},{5,3},{6,4},{7,5},{8,6},{9,7},{10,... | collective-permute-start | bytes 786440 | tf_op jit(solution)/shard_map/ppermute | solution.py:22
  71.7 0.4 fusion.45
  72.1 1.9 %collective-permute-start.8 = (f32[256,256]{1,0:T(8,128)S(1)}, f32[256,256]{1,0:T(8,128)S(1)}, u32[]{:S(2)}, u32[]{:S(2)}) collective-permute-start(f32[256,256]{1,0:T(8,128)S(1)} %fusion.9), channel_id=1, source_target_pairs={{0,1},{1,2},{2,3},{3,4},{4,5},{5,6},{6,7},{7,8},{8,9},{9,10},{10,1... | collective-permute-start | bytes 786440 | tf_op jit(solution)/shard_map/ppermute | solution.py:22
  74.1 5.8 %collective-permute-start.9 = (f32[256,256]{1,0:T(8,128)S(1)}, f32[256,256]{1,0:T(8,128)S(1)}, u32[]{:S(2)}, u32[]{:S(2)}) collective-permute-start(f32[256,256]{1,0:T(8,128)S(1)} %fusion.9), channel_id=1, source_target_pairs={{0,63},{1,0},{2,1},{3,2},{4,3},{5,4},{6,5},{7,6},{8,7},{9,8},{10,9... | collective-permute-start | bytes 786440 | tf_op jit(solution)/shard_map/ppermute | solution.py:22
  79.8 0.0 collective-permute-done.10
  79.8 0.4 fusion.29
  80.2 0.0 collective-permute-done.11
  80.2 0.4 fusion.21
  80.6 1.3 collective-permute-done.8
  81.9 0.4 convolution_add_fusion.3
  82.3 1.4 collective-permute-done.9
  83.7 0.4 fusion.12
  84.1 1.9 %collective-permute-start.14 = (f32[256,256]{1,0:T(8,128)S(1)}, f32[256,256]{1,0:T(8,128)S(1)}, u32[]{:S(2)}, u32[]{:S(2)}) collective-permute-start(f32[256,256]{1,0:T(8,128)S(1)} %fusion.12), channel_id=1, source_target_pairs={{0,2},{1,3},{2,4},{3,5},{4,6},{5,7},{6,8},{7,9},{8,10},{9,11},{10,... | collective-permute-start | bytes 786440 | tf_op jit(solution)/shard_map/ppermute | solution.py:22
  86.0 6.0 %collective-permute-start.15 = (f32[256,256]{1,0:T(8,128)S(1)}, f32[256,256]{1,0:T(8,128)S(1)}, u32[]{:S(2)}, u32[]{:S(2)}) collective-permute-start(f32[256,256]{1,0:T(8,128)S(1)} %fusion.12), channel_id=1, source_target_pairs={{0,62},{1,63},{2,0},{3,1},{4,2},{5,3},{6,4},{7,5},{8,6},{9,7},{10,... | collective-permute-start | bytes 786440 | tf_op jit(solution)/shard_map/ppermute | solution.py:22
  92.1 0.4 fusion.51
  92.5 1.9 %collective-permute-start.12 = (f32[256,256]{1,0:T(8,128)S(1)}, f32[256,256]{1,0:T(8,128)S(1)}, u32[]{:S(2)}, u32[]{:S(2)}) collective-permute-start(f32[256,256]{1,0:T(8,128)S(1)} %fusion.12), channel_id=1, source_target_pairs={{0,1},{1,2},{2,3},{3,4},{4,5},{5,6},{6,7},{7,8},{8,9},{9,10},{10,1... | collective-permute-start | bytes 786440 | tf_op jit(solution)/shard_map/ppermute | solution.py:22
  94.4 5.9 %collective-permute-start.13 = (f32[256,256]{1,0:T(8,128)S(1)}, f32[256,256]{1,0:T(8,128)S(1)}, u32[]{:S(2)}, u32[]{:S(2)}) collective-permute-start(f32[256,256]{1,0:T(8,128)S(1)} %fusion.12), channel_id=1, source_target_pairs={{0,63},{1,0},{2,1},{3,2},{4,3},{5,4},{6,5},{7,6},{8,7},{9,8},{10,9... | collective-permute-start | bytes 786440 | tf_op jit(solution)/shard_map/ppermute | solution.py:22
  100.3 0.4 fusion.35
  100.7 0.4 fusion.27
  101.1 1.1 collective-permute-done.12
  102.3 0.4 convolution_add_fusion.1
  102.7 1.4 collective-permute-done.13
  104.0 0.4 fusion.15
  104.5 0.7 copy-done.1
  105.2 3.2 %fusion.66 = f32[256,2048]{1,0:T(8,128)} fusion(f32[256,256]{1,0:T(8,128)S(1)} %fusion.15, f32[256,2048]{1,0:T(8,128)S(1)} %copy-done), kind=kOutput, calls=%fused_computation.88 | convolution fusion | flops 1610612736 | bytes 4456448 | tf_op jit(solution)/shard_map/dot_general | solution.py:85
  108.4 0.0 reduce-scatter.2.cloned.1.call-update
  108.4 0.9 copy-done.2
  109.3 0.6 fusion.67
  109.9 0.1 reshape.12
  110.0 27.1 %all_to_all.5 = f32[64,4,256]{2,1,0:T(4,128)S(1)} all-to-all(f32[64,4,256]{2,1,0:T(4,128)S(1)} %reshape.12), channel_id=1, replica_groups=mesh['grp'=8,'wide'=64] {'wide'}, dimensions={0} | all-to-all | bytes 524288 | tf_op jit(solution)/shard_map/all_to_all | solution.py:83
  137.1 0.1 reduce_sum.9
  137.2 0.6 broadcast_multiply_fusion.1
  137.8 21.3 %reduce-scatter.2.cloned.1.call-done = f32[256,256]{1,0:T(8,128)} async-done(((f32[256,2048]{1,0:T(8,128)}), f32[256,256]{1,0:T(8,128)}) %reduce-scatter.2.cloned.1.call-update) | async-done | bytes 262160 | tf_op jit(solution)/shard_map/reduce_scatter | solution.py:88
  (15 shorter events, 0.1 us)
Async XLA Ops:
  7.2 98.0 %copy-start = (f32[256,2048]{1,0:T(8,128)S(1)}, f32[256,2048]{1,0:T(8,128)}, u32[]{:S(2)}) copy-start(f32[256,2048]{1,0:T(8,128)} %param.7) | copy-start | bytes 6291460
  7.2 151.9 %reduce-scatter.2.cloned.1.call-start = ((), (), s32[]{:S(2)}) async-start(), calls=%async_computation.2 | async-start | bytes 2359296 | tf_op jit(solution)/shard_map/reduce_scatter | solution.py:88
  7.2 34.9 %collective-permute-start = (f32[256,256]{1,0:T(8,128)}, f32[256,256]{1,0:T(8,128)}, u32[]{:S(2)}, u32[]{:S(2)}) collective-permute-start(f32[256,256]{1,0:T(8,128)} %param.4), channel_id=1, source_target_pairs={{0,1},{1,2},{2,3},{3,4},{4,5},{5,6},{6,7},{7,8},{8,9},{9,10},{10,1... | collective-permute-start | bytes 786440 | tf_op jit(solution)/shard_map/ppermute | solution.py:22
  9.3 30.1 %collective-permute-start.2 = (f32[256,256]{1,0:T(8,128)}, f32[256,256]{1,0:T(8,128)}, u32[]{:S(2)}, u32[]{:S(2)}) collective-permute-start(f32[256,256]{1,0:T(8,128)} %param.4), channel_id=1, source_target_pairs={{0,2},{1,3},{2,4},{3,5},{4,6},{5,7},{6,8},{7,9},{8,10},{9,11},{10,... | collective-permute-start | bytes 786440 | tf_op jit(solution)/shard_map/ppermute | solution.py:22
  13.6 27.2 %collective-permute-start.3 = (f32[256,256]{1,0:T(8,128)}, f32[256,256]{1,0:T(8,128)}, u32[]{:S(2)}, u32[]{:S(2)}) collective-permute-start(f32[256,256]{1,0:T(8,128)} %param.4), channel_id=1, source_target_pairs={{0,62},{1,63},{2,0},{3,1},{4,2},{5,3},{6,4},{7,5},{8,6},{9,7},{10,... | collective-permute-start | bytes 786440 | tf_op jit(solution)/shard_map/ppermute | solution.py:22
  22.4 21.0 %collective-permute-start.1 = (f32[256,256]{1,0:T(8,128)}, f32[256,256]{1,0:T(8,128)}, u32[]{:S(2)}, u32[]{:S(2)}) collective-permute-start(f32[256,256]{1,0:T(8,128)} %param.4), channel_id=1, source_target_pairs={{0,63},{1,0},{2,1},{3,2},{4,3},{5,4},{6,5},{7,6},{8,7},{9,8},{10,9... | collective-permute-start | bytes 786440 | tf_op jit(solution)/shard_map/ppermute | solution.py:22
  25.8 3.8 %copy-start.5 = (s32[4,16]{1,0:T(4,128)S(1)}, s32[4,16]{1,0:T(4,128)}, u32[]{:S(2)}) copy-start(s32[4,16]{1,0:T(4,128)} %param.6) | copy-start | bytes 772
  31.8 1.2 copy-start.3
  39.4 4.1 %copy-start.4 = (f32[256,256]{1,0:T(8,128)S(1)}, f32[256,256]{1,0:T(8,128)}, u32[]{:S(2)}) copy-start(f32[256,256]{1,0:T(8,128)} %param.4) | copy-start | bytes 786436
  44.8 13.7 %collective-permute-start.6 = (f32[256,256]{1,0:T(8,128)S(1)}, f32[256,256]{1,0:T(8,128)S(1)}, u32[]{:S(2)}, u32[]{:S(2)}) collective-permute-start(f32[256,256]{1,0:T(8,128)S(1)} %get-tuple-element.5), channel_id=1, source_target_pairs={{0,2},{1,3},{2,4},{3,5},{4,6},{5,7},{6,8},{7,9},{8,10},{9,11},{10,... | collective-permute-start | bytes 786440 | tf_op jit(solution)/shard_map/ppermute | solution.py:22
  46.8 14.2 %collective-permute-start.4 = (f32[256,256]{1,0:T(8,128)S(1)}, f32[256,256]{1,0:T(8,128)S(1)}, u32[]{:S(2)}, u32[]{:S(2)}) collective-permute-start(f32[256,256]{1,0:T(8,128)S(1)} %get-tuple-element.5), channel_id=1, source_target_pairs={{0,1},{1,2},{2,3},{3,4},{4,5},{5,6},{6,7},{7,8},{8,9},{9,10},{10,1... | collective-permute-start | bytes 786440 | tf_op jit(solution)/shard_map/ppermute | solution.py:22
  48.7 11.9 %collective-permute-start.7 = (f32[256,256]{1,0:T(8,128)S(1)}, f32[256,256]{1,0:T(8,128)S(1)}, u32[]{:S(2)}, u32[]{:S(2)}) collective-permute-start(f32[256,256]{1,0:T(8,128)S(1)} %get-tuple-element.5), channel_id=1, source_target_pairs={{0,62},{1,63},{2,0},{3,1},{4,2},{5,3},{6,4},{7,5},{8,6},{9,7},{10,... | collective-permute-start | bytes 786440 | tf_op jit(solution)/shard_map/ppermute | solution.py:22
  54.7 8.6 %collective-permute-start.5 = (f32[256,256]{1,0:T(8,128)S(1)}, f32[256,256]{1,0:T(8,128)S(1)}, u32[]{:S(2)}, u32[]{:S(2)}) collective-permute-start(f32[256,256]{1,0:T(8,128)S(1)} %get-tuple-element.5), channel_id=1, source_target_pairs={{0,63},{1,0},{2,1},{3,2},{4,3},{5,4},{6,5},{7,6},{8,7},{9,8},{10,9... | collective-permute-start | bytes 786440 | tf_op jit(solution)/shard_map/ppermute | solution.py:22
  63.8 16.0 %collective-permute-start.10 = (f32[256,256]{1,0:T(8,128)S(1)}, f32[256,256]{1,0:T(8,128)S(1)}, u32[]{:S(2)}, u32[]{:S(2)}) collective-permute-start(f32[256,256]{1,0:T(8,128)S(1)} %fusion.9), channel_id=1, source_target_pairs={{0,2},{1,3},{2,4},{3,5},{4,6},{5,7},{6,8},{7,9},{8,10},{9,11},{10,... | collective-permute-start | bytes 786440 | tf_op jit(solution)/shard_map/ppermute | solution.py:22
  65.7 14.5 %collective-permute-start.11 = (f32[256,256]{1,0:T(8,128)S(1)}, f32[256,256]{1,0:T(8,128)S(1)}, u32[]{:S(2)}, u32[]{:S(2)}) collective-permute-start(f32[256,256]{1,0:T(8,128)S(1)} %fusion.9), channel_id=1, source_target_pairs={{0,62},{1,63},{2,0},{3,1},{4,2},{5,3},{6,4},{7,5},{8,6},{9,7},{10,... | collective-permute-start | bytes 786440 | tf_op jit(solution)/shard_map/ppermute | solution.py:22
  72.1 9.8 %collective-permute-start.8 = (f32[256,256]{1,0:T(8,128)S(1)}, f32[256,256]{1,0:T(8,128)S(1)}, u32[]{:S(2)}, u32[]{:S(2)}) collective-permute-start(f32[256,256]{1,0:T(8,128)S(1)} %fusion.9), channel_id=1, source_target_pairs={{0,1},{1,2},{2,3},{3,4},{4,5},{5,6},{6,7},{7,8},{8,9},{9,10},{10,1... | collective-permute-start | bytes 786440 | tf_op jit(solution)/shard_map/ppermute | solution.py:22
  74.1 9.6 %collective-permute-start.9 = (f32[256,256]{1,0:T(8,128)S(1)}, f32[256,256]{1,0:T(8,128)S(1)}, u32[]{:S(2)}, u32[]{:S(2)}) collective-permute-start(f32[256,256]{1,0:T(8,128)S(1)} %fusion.9), channel_id=1, source_target_pairs={{0,63},{1,0},{2,1},{3,2},{4,3},{5,4},{6,5},{7,6},{8,7},{9,8},{10,9... | collective-permute-start | bytes 786440 | tf_op jit(solution)/shard_map/ppermute | solution.py:22
  84.1 16.2 %collective-permute-start.14 = (f32[256,256]{1,0:T(8,128)S(1)}, f32[256,256]{1,0:T(8,128)S(1)}, u32[]{:S(2)}, u32[]{:S(2)}) collective-permute-start(f32[256,256]{1,0:T(8,128)S(1)} %fusion.12), channel_id=1, source_target_pairs={{0,2},{1,3},{2,4},{3,5},{4,6},{5,7},{6,8},{7,9},{8,10},{9,11},{10,... | collective-permute-start | bytes 786440 | tf_op jit(solution)/shard_map/ppermute | solution.py:22
  86.0 14.7 %collective-permute-start.15 = (f32[256,256]{1,0:T(8,128)S(1)}, f32[256,256]{1,0:T(8,128)S(1)}, u32[]{:S(2)}, u32[]{:S(2)}) collective-permute-start(f32[256,256]{1,0:T(8,128)S(1)} %fusion.12), channel_id=1, source_target_pairs={{0,62},{1,63},{2,0},{3,1},{4,2},{5,3},{6,4},{7,5},{8,6},{9,7},{10,... | collective-permute-start | bytes 786440 | tf_op jit(solution)/shard_map/ppermute | solution.py:22
  92.5 9.8 %collective-permute-start.12 = (f32[256,256]{1,0:T(8,128)S(1)}, f32[256,256]{1,0:T(8,128)S(1)}, u32[]{:S(2)}, u32[]{:S(2)}) collective-permute-start(f32[256,256]{1,0:T(8,128)S(1)} %fusion.12), channel_id=1, source_target_pairs={{0,1},{1,2},{2,3},{3,4},{4,5},{5,6},{6,7},{7,8},{8,9},{9,10},{10,1... | collective-permute-start | bytes 786440 | tf_op jit(solution)/shard_map/ppermute | solution.py:22
  94.4 9.6 %collective-permute-start.13 = (f32[256,256]{1,0:T(8,128)S(1)}, f32[256,256]{1,0:T(8,128)S(1)}, u32[]{:S(2)}, u32[]{:S(2)}) collective-permute-start(f32[256,256]{1,0:T(8,128)S(1)} %fusion.12), channel_id=1, source_target_pairs={{0,63},{1,0},{2,1},{3,2},{4,3},{5,4},{6,5},{7,6},{8,7},{9,8},{10,9... | collective-permute-start | bytes 786440 | tf_op jit(solution)/shard_map/ppermute | solution.py:22
  104.4 0.7 copy-start.1
  108.4 0.9 copy-start.2
Sparse Core Ops, SparseCore 0:
  108.5 50.4 reduce-scatter.1

commit v11 on v6

--- a/solution.py
+++ b/solution.py
@@ -41,7 +41,7 @@
     ]
     total = None
     for idx in (2, 1, 3, 0, 4):
-        term = jnp.dot(hdense[:, idx * rows:(idx + 1) * rows], pieces[idx], precision=HI,
+        term = jnp.dot(hdense[:, idx * rows:(idx + 1) * rows], pieces[idx], precision=lax.Precision.HIGH,
                        preferred_element_type=jnp.float32)
         total = term if total is None else total + term
     return total
@@ -75,7 +75,7 @@
     gathered = lax.all_to_all(pieces, "wide", 0, 0, tiled=True)
     correlation = jnp.sum(gathered, axis=0) / total_rows
     rot_term = jnp.dot(
-        current, rotation, precision=HI, preferred_element_type=jnp.float32
+        current, rotation, precision=lax.Precision.HIGH, preferred_element_type=jnp.float32
     )
     rotated = lax.psum_scatter(rot_term, "grp", scatter_dimension=1, tiled=True)
     return (rotated, correlation)

time: 166 us -> 164 us (0.988)
  matrix products: 22.1 us -> 19.1 us
    dot_general x21, matrix products: 15.8 us -> 12.8 us  [the longest x20 10.3 us: apply_ham(): jnp.dot(hdense[:, idx * rows:(idx + 1) * rows], pieces[idx], precision=la...]
  transfers between devices with their start and end apart: 17 -> 17, of which waited for: 7 -> 7; matrix products, arithmetic and copies ran while one was open for 12% -> 11% of each run, Pallas kernels for 0% -> 0%
where the time goes in v11:
time: 164 us; the launch traced here: 163 us
  starting transfers between devices  64.6 us (39%)
  waiting for transfers between devices  31.5 us (19%)
  blocking collectives  28.3 us (17%)
  matrix products  19.1 us (12%)
  between operations  14.5 us (9%)
  local copies, waits for them, and re-layouts  3.95 us (2%)
    ppermute x16, starting transfers between devices, passed_along(): return lax.ppermute(value, axis, pairs)  64.6 us
    all_to_all x1, blocking collectives, local(): gathered = lax.all_to_all(pieces, 'wide', 0, 0, tiled=True)  28.3 us
    reduce_scatter x1, waiting for transfers between devices, local(): rotated = lax.psum_scatter(rot_term, 'grp', scatter_dimension=1, tiled=True)  21.4 us
    dot_general x20, matrix products, apply_ham(): jnp.dot(hdense[:, idx * rows:(idx + 1) * rows], pieces[idx], precision=la...  10.3 us
    ppermute x16, waiting for transfers between devices, passed_along(): return lax.ppermute(value, axis, pairs)  10.2 us
    dot_general x1, matrix products, dense_hamiltonian(): hd = jnp.einsum('asp,asij->aipj', onehot, hblocks, precision=HI)  5.76 us
  transfers between devices with their start and end apart: 17, of which 7 were waited for; matrix products, arithmetic and copies ran while one was open for 11% of the time, Pallas kernels for 0%

profile of v11, /device:TPU:6, one launch (start us, length us, event | category | flops | bytes accessed | tf_op | source)
XLA Modules:
  0.0 163.4 jit_solution(8652037244802407724)
XLA Ops:
  7.2 0.0 copy-start
  7.2 0.0 reduce-scatter.2.cloned.1.call-start
  7.2 2.1 %collective-permute-start = (f32[256,256]{1,0:T(8,128)}, f32[256,256]{1,0:T(8,128)}, u32[]{:S(2)}, u32[]{:S(2)}) collective-permute-start(f32[256,256]{1,0:T(8,128)} %param.4), channel_id=1, source_target_pairs={{0,1},{1,2},{2,3},{3,4},{4,5},{5,6},{6,7},{7,8},{8,9},{9,10},{10,1... | collective-permute-start | bytes 786440 | tf_op jit(solution)/shard_map/ppermute | solution.py:22
  9.3 11.2 %collective-permute-start.3 = (f32[256,256]{1,0:T(8,128)}, f32[256,256]{1,0:T(8,128)}, u32[]{:S(2)}, u32[]{:S(2)}) collective-permute-start(f32[256,256]{1,0:T(8,128)} %param.4), channel_id=1, source_target_pairs={{0,62},{1,63},{2,0},{3,1},{4,2},{5,3},{6,4},{7,5},{8,6},{9,7},{10,... | collective-permute-start | bytes 786440 | tf_op jit(solution)/shard_map/ppermute | solution.py:22
  20.5 1.9 %collective-permute-start.2 = (f32[256,256]{1,0:T(8,128)}, f32[256,256]{1,0:T(8,128)}, u32[]{:S(2)}, u32[]{:S(2)}) collective-permute-start(f32[256,256]{1,0:T(8,128)} %param.4), channel_id=1, source_target_pairs={{0,2},{1,3},{2,4},{3,5},{4,6},{5,7},{6,8},{7,9},{8,10},{9,11},{10,... | collective-permute-start | bytes 786440 | tf_op jit(solution)/shard_map/ppermute | solution.py:22
  22.4 4.9 %collective-permute-start.1 = (f32[256,256]{1,0:T(8,128)}, f32[256,256]{1,0:T(8,128)}, u32[]{:S(2)}, u32[]{:S(2)}) collective-permute-start(f32[256,256]{1,0:T(8,128)} %param.4), channel_id=1, source_target_pairs={{0,63},{1,0},{2,1},{3,2},{4,3},{5,4},{6,5},{7,6},{8,7},{9,8},{10,9... | collective-permute-start | bytes 786440 | tf_op jit(solution)/shard_map/ppermute | solution.py:22
  27.4 0.7 fusion.59
  28.1 5.8 %fusion.2 = f32[4,64,20,64]{3,2,1,0:T(8,128)} fusion(f32[4,16,64,64]{3,2,1,0:T(8,128)} %param.5, s32[4,16]{1,0:T(4,128)S(1)} %fusion.59), kind=kOutput, calls=%fused_computation.2 | convolution fusion | flops 62915840 | bytes 2359552 | tf_op jit(solution)/shard_map/asp,asij->aipj/dot_general | solution.py:29
  33.8 2.2 %reshape.14 = f32[256,1280]{1,0:T(8,128)S(1)} reshape(f32[4,64,20,64]{3,2,1,0:T(8,128)} %fusion.2) | data formatting | bytes 2621440 | tf_op jit(solution)/shard_map/reshape | solution.py:30
  36.1 1.2 fusion.48
  37.3 0.0 copy-start.3
  37.3 0.0 collective-permute-done.3
  37.3 1.3 fusion.24
  38.6 0.0 collective-permute-done.2
  38.6 1.2 fusion.32
  39.9 0.0 collective-permute-done
  39.9 1.2 convolution_add_fusion.7
  41.1 0.0 collective-permute-done.1
  41.1 1.2 broadcast_multiply_fusion
  42.4 1.9 %collective-permute-start.6 = (f32[256,256]{1,0:T(8,128)S(1)}, f32[256,256]{1,0:T(8,128)S(1)}, u32[]{:S(2)}, u32[]{:S(2)}) collective-permute-start(f32[256,256]{1,0:T(8,128)S(1)} %get-tuple-element.2), channel_id=1, source_target_pairs={{0,2},{1,3},{2,4},{3,5},{4,6},{5,7},{6,8},{7,9},{8,10},{9,11},{10,... | collective-permute-start | bytes 786440 | tf_op jit(solution)/shard_map/ppermute | solution.py:22
  44.3 1.9 %collective-permute-start.4 = (f32[256,256]{1,0:T(8,128)S(1)}, f32[256,256]{1,0:T(8,128)S(1)}, u32[]{:S(2)}, u32[]{:S(2)}) collective-permute-start(f32[256,256]{1,0:T(8,128)S(1)} %get-tuple-element.2), channel_id=1, source_target_pairs={{0,1},{1,2},{2,3},{3,4},{4,5},{5,6},{6,7},{7,8},{8,9},{9,10},{10,1... | collective-permute-start | bytes 786440 | tf_op jit(solution)/shard_map/ppermute | solution.py:22
  46.2 6.0 %collective-permute-start.7 = (f32[256,256]{1,0:T(8,128)S(1)}, f32[256,256]{1,0:T(8,128)S(1)}, u32[]{:S(2)}, u32[]{:S(2)}) collective-permute-start(f32[256,256]{1,0:T(8,128)S(1)} %get-tuple-element.2), channel_id=1, source_target_pairs={{0,62},{1,63},{2,0},{3,1},{4,2},{5,3},{6,4},{7,5},{8,6},{9,7},{10,... | collective-permute-start | bytes 786440 | tf_op jit(solution)/shard_map/ppermute | solution.py:22
  52.3 3.4 %collective-permute-start.5 = (f32[256,256]{1,0:T(8,128)S(1)}, f32[256,256]{1,0:T(8,128)S(1)}, u32[]{:S(2)}, u32[]{:S(2)}) collective-permute-start(f32[256,256]{1,0:T(8,128)S(1)} %get-tuple-element.2), channel_id=1, source_target_pairs={{0,63},{1,0},{2,1},{3,2},{4,3},{5,4},{6,5},{7,6},{8,7},{9,8},{10,9... | collective-permute-start | bytes 786440 | tf_op jit(solution)/shard_map/ppermute | solution.py:22
  55.6 0.3 fusion.46
  55.9 0.3 fusion.30
  56.2 1.9 %collective-permute-done.7 = f32[256,256]{1,0:T(8,128)S(1)} collective-permute-done((f32[256,256]{1,0:T(8,128)S(1)}, f32[256,256]{1,0:T(8,128)S(1)}, u32[]{:S(2)}, u32[]{:S(2)}) %collective-permute-start.7) | collective-permute-done | bytes 262176 | tf_op jit(solution)/shard_map/ppermute | solution.py:22
  58.1 0.3 fusion.22
  58.4 0.3 convolution_add_fusion.5
  58.6 2.2 %collective-permute-done.5 = f32[256,256]{1,0:T(8,128)S(1)} collective-permute-done((f32[256,256]{1,0:T(8,128)S(1)}, f32[256,256]{1,0:T(8,128)S(1)}, u32[]{:S(2)}, u32[]{:S(2)}) %collective-permute-start.5) | collective-permute-done | bytes 262176 | tf_op jit(solution)/shard_map/ppermute | solution.py:22
  60.9 0.3 fusion.13
  61.2 1.9 %collective-permute-start.10 = (f32[256,256]{1,0:T(8,128)S(1)}, f32[256,256]{1,0:T(8,128)S(1)}, u32[]{:S(2)}, u32[]{:S(2)}) collective-permute-start(f32[256,256]{1,0:T(8,128)S(1)} %fusion.13), channel_id=1, source_target_pairs={{0,2},{1,3},{2,4},{3,5},{4,6},{5,7},{6,8},{7,9},{8,10},{9,11},{10,... | collective-permute-start | bytes 786440 | tf_op jit(solution)/shard_map/ppermute | solution.py:22
  63.1 6.0 %collective-permute-start.11 = (f32[256,256]{1,0:T(8,128)S(1)}, f32[256,256]{1,0:T(8,128)S(1)}, u32[]{:S(2)}, u32[]{:S(2)}) collective-permute-start(f32[256,256]{1,0:T(8,128)S(1)} %fusion.13), channel_id=1, source_target_pairs={{0,62},{1,63},{2,0},{3,1},{4,2},{5,3},{6,4},{7,5},{8,6},{9,7},{10,... | collective-permute-start | bytes 786440 | tf_op jit(solution)/shard_map/ppermute | solution.py:22
  69.2 0.3 fusion.44
  69.4 1.9 %collective-permute-start.8 = (f32[256,256]{1,0:T(8,128)S(1)}, f32[256,256]{1,0:T(8,128)S(1)}, u32[]{:S(2)}, u32[]{:S(2)}) collective-permute-start(f32[256,256]{1,0:T(8,128)S(1)} %fusion.13), channel_id=1, source_target_pairs={{0,1},{1,2},{2,3},{3,4},{4,5},{5,6},{6,7},{7,8},{8,9},{9,10},{10,1... | collective-permute-start | bytes 786440 | tf_op jit(solution)/shard_map/ppermute | solution.py:22
  71.4 5.8 %collective-permute-start.9 = (f32[256,256]{1,0:T(8,128)S(1)}, f32[256,256]{1,0:T(8,128)S(1)}, u32[]{:S(2)}, u32[]{:S(2)}) collective-permute-start(f32[256,256]{1,0:T(8,128)S(1)} %fusion.13), channel_id=1, source_target_pairs={{0,63},{1,0},{2,1},{3,2},{4,3},{5,4},{6,5},{7,6},{8,7},{9,8},{10,9... | collective-permute-start | bytes 786440 | tf_op jit(solution)/shard_map/ppermute | solution.py:22
  77.1 0.0 collective-permute-done.10
  77.1 0.3 fusion.28
  77.4 0.0 collective-permute-done.11
  77.4 0.3 fusion.20
  77.7 1.5 collective-permute-done.8
  79.2 0.3 convolution_add_fusion.3
  79.5 1.5 collective-permute-done.9
  81.0 0.3 fusion.16
  81.3 1.9 %collective-permute-start.14 = (f32[256,256]{1,0:T(8,128)S(1)}, f32[256,256]{1,0:T(8,128)S(1)}, u32[]{:S(2)}, u32[]{:S(2)}) collective-permute-start(f32[256,256]{1,0:T(8,128)S(1)} %fusion.16), channel_id=1, source_target_pairs={{0,2},{1,3},{2,4},{3,5},{4,6},{5,7},{6,8},{7,9},{8,10},{9,11},{10,... | collective-permute-start | bytes 786440 | tf_op jit(solution)/shard_map/ppermute | solution.py:22
  83.2 6.0 %collective-permute-start.15 = (f32[256,256]{1,0:T(8,128)S(1)}, f32[256,256]{1,0:T(8,128)S(1)}, u32[]{:S(2)}, u32[]{:S(2)}) collective-permute-start(f32[256,256]{1,0:T(8,128)S(1)} %fusion.16), channel_id=1, source_target_pairs={{0,62},{1,63},{2,0},{3,1},{4,2},{5,3},{6,4},{7,5},{8,6},{9,7},{10,... | collective-permute-start | bytes 786440 | tf_op jit(solution)/shard_map/ppermute | solution.py:22
  89.3 0.3 fusion.50
  89.6 1.9 %collective-permute-start.12 = (f32[256,256]{1,0:T(8,128)S(1)}, f32[256,256]{1,0:T(8,128)S(1)}, u32[]{:S(2)}, u32[]{:S(2)}) collective-permute-start(f32[256,256]{1,0:T(8,128)S(1)} %fusion.16), channel_id=1, source_target_pairs={{0,1},{1,2},{2,3},{3,4},{4,5},{5,6},{6,7},{7,8},{8,9},{9,10},{10,1... | collective-permute-start | bytes 786440 | tf_op jit(solution)/shard_map/ppermute | solution.py:22
  91.5 5.8 %collective-permute-start.13 = (f32[256,256]{1,0:T(8,128)S(1)}, f32[256,256]{1,0:T(8,128)S(1)}, u32[]{:S(2)}, u32[]{:S(2)}) collective-permute-start(f32[256,256]{1,0:T(8,128)S(1)} %fusion.16), channel_id=1, source_target_pairs={{0,63},{1,0},{2,1},{3,2},{4,3},{5,4},{6,5},{7,6},{8,7},{9,8},{10,9... | collective-permute-start | bytes 786440 | tf_op jit(solution)/shard_map/ppermute | solution.py:22
  97.3 0.3 fusion.34
  97.5 0.3 fusion.26
  97.8 1.5 collective-permute-done.12
  99.4 0.3 convolution_add_fusion.1
  99.6 1.5 collective-permute-done.13
  101.1 0.3 fusion.19
  101.4 0.7 copy-done.1
  102.1 2.4 %fusion.61 = f32[256,2048]{1,0:T(8,128)} fusion(f32[256,256]{1,0:T(8,128)S(1)} %fusion.19, f32[256,2048]{1,0:T(8,128)S(1)} %copy-done), kind=kOutput, calls=%fused_computation.78 | convolution fusion | flops 805306368 | bytes 4456448 | tf_op jit(solution)/shard_map/dot_general | solution.py:77
  104.6 0.0 reduce-scatter.2.cloned.1.call-update
  104.6 0.9 copy-done.2
  105.5 0.6 fusion.62
  106.1 0.1 reshape.12
  106.2 28.3 %all_to_all.5 = f32[64,4,256]{2,1,0:T(4,128)S(1)} all-to-all(f32[64,4,256]{2,1,0:T(4,128)S(1)} %reshape.12), channel_id=1, replica_groups=mesh['grp'=8,'wide'=64] {'wide'}, dimensions={0} | all-to-all | bytes 524288 | tf_op jit(solution)/shard_map/all_to_all | solution.py:75
  134.5 0.1 reduce_sum.9
  134.6 0.6 broadcast_multiply_fusion.1
  135.2 21.4 %reduce-scatter.2.cloned.1.call-done = f32[256,256]{1,0:T(8,128)} async-done(((f32[256,2048]{1,0:T(8,128)}), f32[256,256]{1,0:T(8,128)}) %reduce-scatter.2.cloned.1.call-update) | async-done | bytes 262160 | tf_op jit(solution)/shard_map/reduce_scatter | solution.py:80
  (8 shorter events, 0.0 us)
Async XLA Ops:
  7.2 95.0 %copy-start = (f32[256,2048]{1,0:T(8,128)S(1)}, f32[256,2048]{1,0:T(8,128)}, u32[]{:S(2)}) copy-start(f32[256,2048]{1,0:T(8,128)} %param.7) | copy-start | bytes 6291460
  7.2 149.4 %reduce-scatter.2.cloned.1.call-start = ((), (), s32[]{:S(2)}) async-start(), calls=%async_computation.2 | async-start | bytes 2359296 | tf_op jit(solution)/shard_map/reduce_scatter | solution.py:80
  7.2 32.6 %collective-permute-start = (f32[256,256]{1,0:T(8,128)}, f32[256,256]{1,0:T(8,128)}, u32[]{:S(2)}, u32[]{:S(2)}) collective-permute-start(f32[256,256]{1,0:T(8,128)} %param.4), channel_id=1, source_target_pairs={{0,1},{1,2},{2,3},{3,4},{4,5},{5,6},{6,7},{7,8},{8,9},{9,10},{10,1... | collective-permute-start | bytes 786440 | tf_op jit(solution)/shard_map/ppermute | solution.py:22
  9.3 28.0 %collective-permute-start.3 = (f32[256,256]{1,0:T(8,128)}, f32[256,256]{1,0:T(8,128)}, u32[]{:S(2)}, u32[]{:S(2)}) collective-permute-start(f32[256,256]{1,0:T(8,128)} %param.4), channel_id=1, source_target_pairs={{0,62},{1,63},{2,0},{3,1},{4,2},{5,3},{6,4},{7,5},{8,6},{9,7},{10,... | collective-permute-start | bytes 786440 | tf_op jit(solution)/shard_map/ppermute | solution.py:22
  20.5 18.1 %collective-permute-start.2 = (f32[256,256]{1,0:T(8,128)}, f32[256,256]{1,0:T(8,128)}, u32[]{:S(2)}, u32[]{:S(2)}) collective-permute-start(f32[256,256]{1,0:T(8,128)} %param.4), channel_id=1, source_target_pairs={{0,2},{1,3},{2,4},{3,5},{4,6},{5,7},{6,8},{7,9},{8,10},{9,11},{10,... | collective-permute-start | bytes 786440 | tf_op jit(solution)/shard_map/ppermute | solution.py:22
  22.4 18.7 %collective-permute-start.1 = (f32[256,256]{1,0:T(8,128)}, f32[256,256]{1,0:T(8,128)}, u32[]{:S(2)}, u32[]{:S(2)}) collective-permute-start(f32[256,256]{1,0:T(8,128)} %param.4), channel_id=1, source_target_pairs={{0,63},{1,0},{2,1},{3,2},{4,3},{5,4},{6,5},{7,6},{8,7},{9,8},{10,9... | collective-permute-start | bytes 786440 | tf_op jit(solution)/shard_map/ppermute | solution.py:22
  37.3 3.8 %copy-start.3 = (f32[256,256]{1,0:T(8,128)S(1)}, f32[256,256]{1,0:T(8,128)}, u32[]{:S(2)}) copy-start(f32[256,256]{1,0:T(8,128)} %param.4) | copy-start | bytes 786436
  42.4 13.6 %collective-permute-start.6 = (f32[256,256]{1,0:T(8,128)S(1)}, f32[256,256]{1,0:T(8,128)S(1)}, u32[]{:S(2)}, u32[]{:S(2)}) collective-permute-start(f32[256,256]{1,0:T(8,128)S(1)} %get-tuple-element.2), channel_id=1, source_target_pairs={{0,2},{1,3},{2,4},{3,5},{4,6},{5,7},{6,8},{7,9},{8,10},{9,11},{10,... | collective-permute-start | bytes 786440 | tf_op jit(solution)/shard_map/ppermute | solution.py:22
  44.3 14.1 %collective-permute-start.4 = (f32[256,256]{1,0:T(8,128)S(1)}, f32[256,256]{1,0:T(8,128)S(1)}, u32[]{:S(2)}, u32[]{:S(2)}) collective-permute-start(f32[256,256]{1,0:T(8,128)S(1)} %get-tuple-element.2), channel_id=1, source_target_pairs={{0,1},{1,2},{2,3},{3,4},{4,5},{5,6},{6,7},{7,8},{8,9},{9,10},{10,1... | collective-permute-start | bytes 786440 | tf_op jit(solution)/shard_map/ppermute | solution.py:22
  46.2 11.9 %collective-permute-start.7 = (f32[256,256]{1,0:T(8,128)S(1)}, f32[256,256]{1,0:T(8,128)S(1)}, u32[]{:S(2)}, u32[]{:S(2)}) collective-permute-start(f32[256,256]{1,0:T(8,128)S(1)} %get-tuple-element.2), channel_id=1, source_target_pairs={{0,62},{1,63},{2,0},{3,1},{4,2},{5,3},{6,4},{7,5},{8,6},{9,7},{10,... | collective-permute-start | bytes 786440 | tf_op jit(solution)/shard_map/ppermute | solution.py:22
  52.3 8.6 %collective-permute-start.5 = (f32[256,256]{1,0:T(8,128)S(1)}, f32[256,256]{1,0:T(8,128)S(1)}, u32[]{:S(2)}, u32[]{:S(2)}) collective-permute-start(f32[256,256]{1,0:T(8,128)S(1)} %get-tuple-element.2), channel_id=1, source_target_pairs={{0,63},{1,0},{2,1},{3,2},{4,3},{5,4},{6,5},{7,6},{8,7},{9,8},{10,9... | collective-permute-start | bytes 786440 | tf_op jit(solution)/shard_map/ppermute | solution.py:22
  61.2 15.9 %collective-permute-start.10 = (f32[256,256]{1,0:T(8,128)S(1)}, f32[256,256]{1,0:T(8,128)S(1)}, u32[]{:S(2)}, u32[]{:S(2)}) collective-permute-start(f32[256,256]{1,0:T(8,128)S(1)} %fusion.13), channel_id=1, source_target_pairs={{0,2},{1,3},{2,4},{3,5},{4,6},{5,7},{6,8},{7,9},{8,10},{9,11},{10,... | collective-permute-start | bytes 786440 | tf_op jit(solution)/shard_map/ppermute | solution.py:22
  63.1 14.3 %collective-permute-start.11 = (f32[256,256]{1,0:T(8,128)S(1)}, f32[256,256]{1,0:T(8,128)S(1)}, u32[]{:S(2)}, u32[]{:S(2)}) collective-permute-start(f32[256,256]{1,0:T(8,128)S(1)} %fusion.13), channel_id=1, source_target_pairs={{0,62},{1,63},{2,0},{3,1},{4,2},{5,3},{6,4},{7,5},{8,6},{9,7},{10,... | collective-permute-start | bytes 786440 | tf_op jit(solution)/shard_map/ppermute | solution.py:22
  69.4 9.8 %collective-permute-start.8 = (f32[256,256]{1,0:T(8,128)S(1)}, f32[256,256]{1,0:T(8,128)S(1)}, u32[]{:S(2)}, u32[]{:S(2)}) collective-permute-start(f32[256,256]{1,0:T(8,128)S(1)} %fusion.13), channel_id=1, source_target_pairs={{0,1},{1,2},{2,3},{3,4},{4,5},{5,6},{6,7},{7,8},{8,9},{9,10},{10,1... | collective-permute-start | bytes 786440 | tf_op jit(solution)/shard_map/ppermute | solution.py:22
  71.4 9.6 %collective-permute-start.9 = (f32[256,256]{1,0:T(8,128)S(1)}, f32[256,256]{1,0:T(8,128)S(1)}, u32[]{:S(2)}, u32[]{:S(2)}) collective-permute-start(f32[256,256]{1,0:T(8,128)S(1)} %fusion.13), channel_id=1, source_target_pairs={{0,63},{1,0},{2,1},{3,2},{4,3},{5,4},{6,5},{7,6},{8,7},{9,8},{10,9... | collective-permute-start | bytes 786440 | tf_op jit(solution)/shard_map/ppermute | solution.py:22
  81.3 15.9 %collective-permute-start.14 = (f32[256,256]{1,0:T(8,128)S(1)}, f32[256,256]{1,0:T(8,128)S(1)}, u32[]{:S(2)}, u32[]{:S(2)}) collective-permute-start(f32[256,256]{1,0:T(8,128)S(1)} %fusion.16), channel_id=1, source_target_pairs={{0,2},{1,3},{2,4},{3,5},{4,6},{5,7},{6,8},{7,9},{8,10},{9,11},{10,... | collective-permute-start | bytes 786440 | tf_op jit(solution)/shard_map/ppermute | solution.py:22
  83.2 14.3 %collective-permute-start.15 = (f32[256,256]{1,0:T(8,128)S(1)}, f32[256,256]{1,0:T(8,128)S(1)}, u32[]{:S(2)}, u32[]{:S(2)}) collective-permute-start(f32[256,256]{1,0:T(8,128)S(1)} %fusion.16), channel_id=1, source_target_pairs={{0,62},{1,63},{2,0},{3,1},{4,2},{5,3},{6,4},{7,5},{8,6},{9,7},{10,... | collective-permute-start | bytes 786440 | tf_op jit(solution)/shard_map/ppermute | solution.py:22
  89.6 9.8 %collective-permute-start.12 = (f32[256,256]{1,0:T(8,128)S(1)}, f32[256,256]{1,0:T(8,128)S(1)}, u32[]{:S(2)}, u32[]{:S(2)}) collective-permute-start(f32[256,256]{1,0:T(8,128)S(1)} %fusion.16), channel_id=1, source_target_pairs={{0,1},{1,2},{2,3},{3,4},{4,5},{5,6},{6,7},{7,8},{8,9},{9,10},{10,1... | collective-permute-start | bytes 786440 | tf_op jit(solution)/shard_map/ppermute | solution.py:22
  91.5 9.6 %collective-permute-start.13 = (f32[256,256]{1,0:T(8,128)S(1)}, f32[256,256]{1,0:T(8,128)S(1)}, u32[]{:S(2)}, u32[]{:S(2)}) collective-permute-start(f32[256,256]{1,0:T(8,128)S(1)} %fusion.16), channel_id=1, source_target_pairs={{0,63},{1,0},{2,1},{3,2},{4,3},{5,4},{6,5},{7,6},{8,7},{9,8},{10,9... | collective-permute-start | bytes 786440 | tf_op jit(solution)/shard_map/ppermute | solution.py:22
  101.4 0.7 copy-start.1
  104.6 0.9 copy-start.2
Sparse Core Ops, SparseCore 0:
  104.7 51.7 reduce-scatter.1

commit v12 on v6

--- a/solution.py
+++ b/solution.py
@@ -25,8 +25,14 @@
 def dense_hamiltonian(hblocks, slot_index):
     local_blocks = hblocks.shape[0]
     window_blocks = (2 * HW + 1) * A_DEV
-    onehot = (slot_index[:, :, None] == jnp.arange(window_blocks)[None, None, :]).astype(jnp.float32)
-    hd = jnp.einsum("asp,asij->aipj", onehot, hblocks, precision=HI)
+    slots = hblocks.shape[1]
+    hits = slot_index[:, :, None] == jnp.arange(window_blocks)[None, None, :]
+    same = jnp.eye(local_blocks, dtype=bool)
+    select = (jnp.transpose(hits, (0, 2, 1))[:, :, None, :] & same[:, None, :, None]).astype(jnp.float32)
+    select = select.reshape(local_blocks * window_blocks, local_blocks * slots)
+    hd = jnp.dot(select, hblocks.reshape(local_blocks * slots, B * B), precision=HI,
+                 preferred_element_type=jnp.float32)
+    hd = hd.reshape(local_blocks, window_blocks, B, B).transpose(0, 2, 1, 3)
     return hd.reshape(local_blocks * B, window_blocks * B)
 
 

time: 166 us -> 171 us (1.030)
  local copies, waits for them, and re-layouts: 3.95 us -> 8.16 us
    reshape x0 -> x1, local copies, waits for them, and re-layouts: none -> 2.13 us  [dense_hamiltonian(): hblocks.reshape(local_blocks * slots, B * B)]
    dot_general x0 -> x1, local copies, waits for them, and re-layouts: none -> 1.97 us  [dense_hamiltonian(): jnp.dot(select, hblocks.reshape(local_blocks * slots, B * B), precision=H...]
  transfers between devices with their start and end apart: 17 -> 17, of which waited for: 7 -> 7; matrix products, arithmetic and copies ran while one was open for 12% -> 14% of each run, Pallas kernels for 0% -> 0%
where the time goes in v12:
time: 171 us; the launch traced here: 170 us
  starting transfers between devices  64.8 us (38%)
  waiting for transfers between devices  30.5 us (18%)
  blocking collectives  28.3 us (17%)
  matrix products  22.7 us (13%)
  between operations  14.5 us (8%)
  local copies, waits for them, and re-layouts  8.16 us (5%)
    ppermute x16, starting transfers between devices, passed_along(): return lax.ppermute(value, axis, pairs)  64.8 us
    all_to_all x1, blocking collectives, local(): gathered = lax.all_to_all(pieces, 'wide', 0, 0, tiled=True)  28.3 us
    reduce_scatter x1, waiting for transfers between devices, local(): rotated = lax.psum_scatter(rot_term, 'grp', scatter_dimension=1, tiled=True)  21.6 us
    dot_general x20, matrix products, apply_ham(): jnp.dot(hdense[:, idx * rows:(idx + 1) * rows], pieces[idx], precision=HI...  12.5 us
    ppermute x16, waiting for transfers between devices, passed_along(): return lax.ppermute(value, axis, pairs)  8.9 us
    dot_general x1, matrix products, dense_hamiltonian(): jnp.dot(select, hblocks.reshape(local_blocks * slots, B * B), precision=H...  6.37 us
  transfers between devices with their start and end apart: 17, of which 7 were waited for; matrix products, arithmetic and copies ran while one was open for 14% of the time, Pallas kernels for 0%

profile of v12, /device:TPU:6, one launch (start us, length us, event | category | flops | bytes accessed | tf_op | source)
XLA Modules:
  0.0 169.8 jit_solution(4351415544261339365)
XLA Ops:
  7.2 0.0 copy-start
  7.2 0.0 reduce-scatter.2.cloned.1.call-start
  7.2 2.1 %collective-permute-start = (f32[256,256]{1,0:T(8,128)}, f32[256,256]{1,0:T(8,128)}, u32[]{:S(2)}, u32[]{:S(2)}) collective-permute-start(f32[256,256]{1,0:T(8,128)} %param.4), channel_id=1, source_target_pairs={{0,1},{1,2},{2,3},{3,4},{4,5},{5,6},{6,7},{7,8},{8,9},{9,10},{10,1... | collective-permute-start | bytes 786440 | tf_op jit(solution)/shard_map/ppermute | solution.py:22
  9.3 11.2 %collective-permute-start.3 = (f32[256,256]{1,0:T(8,128)}, f32[256,256]{1,0:T(8,128)}, u32[]{:S(2)}, u32[]{:S(2)}) collective-permute-start(f32[256,256]{1,0:T(8,128)} %param.4), channel_id=1, source_target_pairs={{0,62},{1,63},{2,0},{3,1},{4,2},{5,3},{6,4},{7,5},{8,6},{9,7},{10,... | collective-permute-start | bytes 786440 | tf_op jit(solution)/shard_map/ppermute | solution.py:22
  20.5 1.9 %collective-permute-start.2 = (f32[256,256]{1,0:T(8,128)}, f32[256,256]{1,0:T(8,128)}, u32[]{:S(2)}, u32[]{:S(2)}) collective-permute-start(f32[256,256]{1,0:T(8,128)} %param.4), channel_id=1, source_target_pairs={{0,2},{1,3},{2,4},{3,5},{4,6},{5,7},{6,8},{7,9},{8,10},{9,11},{10,... | collective-permute-start | bytes 786440 | tf_op jit(solution)/shard_map/ppermute | solution.py:22
  22.4 4.9 %collective-permute-start.1 = (f32[256,256]{1,0:T(8,128)}, f32[256,256]{1,0:T(8,128)}, u32[]{:S(2)}, u32[]{:S(2)}) collective-permute-start(f32[256,256]{1,0:T(8,128)} %param.4), channel_id=1, source_target_pairs={{0,63},{1,0},{2,1},{3,2},{4,3},{5,4},{6,5},{7,6},{8,7},{9,8},{10,9... | collective-permute-start | bytes 786440 | tf_op jit(solution)/shard_map/ppermute | solution.py:22
  27.4 2.1 %reshape.49 = f32[64,4096]{1,0:T(8,128)S(1)} reshape(f32[4,16,64,64]{3,2,1,0:T(8,128)} %param.5) | data formatting | bytes 2097152 | tf_op jit(solution)/shard_map/reshape | solution.py:33
  29.5 0.0 copy-start.4
  29.5 2.0 %copy.7 = f32[4096,64]{1,0:T(8,128)} copy(f32[4096,64]{0,1:T(8,128)S(1)} %bitcast.36) | data formatting | bytes 2097152 | tf_op jit(solution)/shard_map/dot_general | solution.py:33
  31.5 0.1 broadcast_and_fusion
  31.7 0.1 and.45
  31.8 6.4 %convolution_bitcast_fusion = f32[4,64,20,64]{3,2,1,0:T(8,128)} fusion(f32[64,64,64,1]{2,1,0,3:T(8,128)} %bitcast.35, pred[4,20,64,1]{2,0,1,3:T(4,128)(4,1)S(1)} %bitcast.37), kind=kOutput, calls=%fused_computation | convolution fusion | flops 251658240 | bytes 2364416 | tf_op jit(solution)/shard_map/dot_general | solution.py:33
  38.2 2.2 %reshape.54 = f32[256,1280]{1,0:T(8,128)S(1)} reshape(f32[4,64,20,64]{3,2,1,0:T(8,128)} %convolution_bitcast_fusion) | data formatting | bytes 2621440 | tf_op jit(solution)/shard_map/reshape | solution.py:36
  40.4 1.3 fusion.43
  41.7 0.0 copy-start.3
  41.8 1.4 fusion.19
  43.1 0.0 collective-permute-done.2
  43.1 1.3 fusion.27
  44.5 1.3 convolution_add_fusion.7
  45.8 1.4 broadcast_multiply_fusion
  47.2 1.9 %collective-permute-start.6 = (f32[256,256]{1,0:T(8,128)S(1)}, f32[256,256]{1,0:T(8,128)S(1)}, u32[]{:S(2)}, u32[]{:S(2)}) collective-permute-start(f32[256,256]{1,0:T(8,128)S(1)} %get-tuple-element.2), channel_id=1, source_target_pairs={{0,2},{1,3},{2,4},{3,5},{4,6},{5,7},{6,8},{7,9},{8,10},{9,11},{10,... | collective-permute-start | bytes 786440 | tf_op jit(solution)/shard_map/ppermute | solution.py:22
  49.1 1.9 %collective-permute-start.4 = (f32[256,256]{1,0:T(8,128)S(1)}, f32[256,256]{1,0:T(8,128)S(1)}, u32[]{:S(2)}, u32[]{:S(2)}) collective-permute-start(f32[256,256]{1,0:T(8,128)S(1)} %get-tuple-element.2), channel_id=1, source_target_pairs={{0,1},{1,2},{2,3},{3,4},{4,5},{5,6},{6,7},{7,8},{8,9},{9,10},{10,1... | collective-permute-start | bytes 786440 | tf_op jit(solution)/shard_map/ppermute | solution.py:22
  51.1 6.0 %collective-permute-start.7 = (f32[256,256]{1,0:T(8,128)S(1)}, f32[256,256]{1,0:T(8,128)S(1)}, u32[]{:S(2)}, u32[]{:S(2)}) collective-permute-start(f32[256,256]{1,0:T(8,128)S(1)} %get-tuple-element.2), channel_id=1, source_target_pairs={{0,62},{1,63},{2,0},{3,1},{4,2},{5,3},{6,4},{7,5},{8,6},{9,7},{10,... | collective-permute-start | bytes 786440 | tf_op jit(solution)/shard_map/ppermute | solution.py:22
  57.1 3.4 %collective-permute-start.5 = (f32[256,256]{1,0:T(8,128)S(1)}, f32[256,256]{1,0:T(8,128)S(1)}, u32[]{:S(2)}, u32[]{:S(2)}) collective-permute-start(f32[256,256]{1,0:T(8,128)S(1)} %get-tuple-element.2), channel_id=1, source_target_pairs={{0,63},{1,0},{2,1},{3,2},{4,3},{5,4},{6,5},{7,6},{8,7},{9,8},{10,9... | collective-permute-start | bytes 786440 | tf_op jit(solution)/shard_map/ppermute | solution.py:22
  60.5 0.4 fusion.41
  60.9 0.0 collective-permute-done.6
  60.9 0.4 fusion.25
  61.3 1.7 collective-permute-done.7
  62.9 0.4 fusion.17
  63.3 0.4 convolution_add_fusion.5
  63.7 2.0 %collective-permute-done.5 = f32[256,256]{1,0:T(8,128)S(1)} collective-permute-done((f32[256,256]{1,0:T(8,128)S(1)}, f32[256,256]{1,0:T(8,128)S(1)}, u32[]{:S(2)}, u32[]{:S(2)}) %collective-permute-start.5) | collective-permute-done | bytes 262176 | tf_op jit(solution)/shard_map/ppermute | solution.py:22
  65.7 0.4 fusion.8
  66.2 1.9 %collective-permute-start.10 = (f32[256,256]{1,0:T(8,128)S(1)}, f32[256,256]{1,0:T(8,128)S(1)}, u32[]{:S(2)}, u32[]{:S(2)}) collective-permute-start(f32[256,256]{1,0:T(8,128)S(1)} %fusion.8), channel_id=1, source_target_pairs={{0,2},{1,3},{2,4},{3,5},{4,6},{5,7},{6,8},{7,9},{8,10},{9,11},{10,... | collective-permute-start | bytes 786440 | tf_op jit(solution)/shard_map/ppermute | solution.py:22
  68.1 6.0 %collective-permute-start.11 = (f32[256,256]{1,0:T(8,128)S(1)}, f32[256,256]{1,0:T(8,128)S(1)}, u32[]{:S(2)}, u32[]{:S(2)}) collective-permute-start(f32[256,256]{1,0:T(8,128)S(1)} %fusion.8), channel_id=1, source_target_pairs={{0,62},{1,63},{2,0},{3,1},{4,2},{5,3},{6,4},{7,5},{8,6},{9,7},{10,... | collective-permute-start | bytes 786440 | tf_op jit(solution)/shard_map/ppermute | solution.py:22
  74.1 0.4 fusion.39
  74.5 1.9 %collective-permute-start.8 = (f32[256,256]{1,0:T(8,128)S(1)}, f32[256,256]{1,0:T(8,128)S(1)}, u32[]{:S(2)}, u32[]{:S(2)}) collective-permute-start(f32[256,256]{1,0:T(8,128)S(1)} %fusion.8), channel_id=1, source_target_pairs={{0,1},{1,2},{2,3},{3,4},{4,5},{5,6},{6,7},{7,8},{8,9},{9,10},{10,1... | collective-permute-start | bytes 786440 | tf_op jit(solution)/shard_map/ppermute | solution.py:22
  76.4 5.8 %collective-permute-start.9 = (f32[256,256]{1,0:T(8,128)S(1)}, f32[256,256]{1,0:T(8,128)S(1)}, u32[]{:S(2)}, u32[]{:S(2)}) collective-permute-start(f32[256,256]{1,0:T(8,128)S(1)} %fusion.8), channel_id=1, source_target_pairs={{0,63},{1,0},{2,1},{3,2},{4,3},{5,4},{6,5},{7,6},{8,7},{9,8},{10,9... | collective-permute-start | bytes 786440 | tf_op jit(solution)/shard_map/ppermute | solution.py:22
  82.2 0.4 fusion.23
  82.6 0.4 fusion.15
  83.0 1.3 collective-permute-done.8
  84.3 0.4 convolution_add_fusion.3
  84.7 1.4 collective-permute-done.9
  86.1 0.4 fusion.11
  86.5 1.9 %collective-permute-start.14 = (f32[256,256]{1,0:T(8,128)S(1)}, f32[256,256]{1,0:T(8,128)S(1)}, u32[]{:S(2)}, u32[]{:S(2)}) collective-permute-start(f32[256,256]{1,0:T(8,128)S(1)} %fusion.11), channel_id=1, source_target_pairs={{0,2},{1,3},{2,4},{3,5},{4,6},{5,7},{6,8},{7,9},{8,10},{9,11},{10,... | collective-permute-start | bytes 786440 | tf_op jit(solution)/shard_map/ppermute | solution.py:22
  88.4 6.0 %collective-permute-start.15 = (f32[256,256]{1,0:T(8,128)S(1)}, f32[256,256]{1,0:T(8,128)S(1)}, u32[]{:S(2)}, u32[]{:S(2)}) collective-permute-start(f32[256,256]{1,0:T(8,128)S(1)} %fusion.11), channel_id=1, source_target_pairs={{0,62},{1,63},{2,0},{3,1},{4,2},{5,3},{6,4},{7,5},{8,6},{9,7},{10,... | collective-permute-start | bytes 786440 | tf_op jit(solution)/shard_map/ppermute | solution.py:22
  94.5 0.4 fusion.45
  94.8 1.9 %collective-permute-start.12 = (f32[256,256]{1,0:T(8,128)S(1)}, f32[256,256]{1,0:T(8,128)S(1)}, u32[]{:S(2)}, u32[]{:S(2)}) collective-permute-start(f32[256,256]{1,0:T(8,128)S(1)} %fusion.11), channel_id=1, source_target_pairs={{0,1},{1,2},{2,3},{3,4},{4,5},{5,6},{6,7},{7,8},{8,9},{9,10},{10,1... | collective-permute-start | bytes 786440 | tf_op jit(solution)/shard_map/ppermute | solution.py:22
  96.8 5.9 %collective-permute-start.13 = (f32[256,256]{1,0:T(8,128)S(1)}, f32[256,256]{1,0:T(8,128)S(1)}, u32[]{:S(2)}, u32[]{:S(2)}) collective-permute-start(f32[256,256]{1,0:T(8,128)S(1)} %fusion.11), channel_id=1, source_target_pairs={{0,63},{1,0},{2,1},{3,2},{4,3},{5,4},{6,5},{7,6},{8,7},{9,8},{10,9... | collective-permute-start | bytes 786440 | tf_op jit(solution)/shard_map/ppermute | solution.py:22
  102.7 0.4 fusion.29
  103.1 0.4 fusion.21
  103.5 1.1 collective-permute-done.12
  104.6 0.4 convolution_add_fusion.1
  105.0 1.4 collective-permute-done.13
  106.4 0.4 fusion.14
  106.8 0.7 copy-done.1
  107.5 3.3 %fusion.54 = f32[256,2048]{1,0:T(8,128)} fusion(f32[256,256]{1,0:T(8,128)S(1)} %fusion.14, f32[256,2048]{1,0:T(8,128)S(1)} %copy-done), kind=kOutput, calls=%fused_computation.77 | convolution fusion | flops 1610612736 | bytes 4456448 | tf_op jit(solution)/shard_map/dot_general | solution.py:83
  110.8 0.0 reduce-scatter.2.cloned.1.call-update
  110.8 0.9 copy-done.2
  111.7 0.6 fusion.55
  112.3 0.1 reshape.51
  112.4 28.3 %all_to_all.5 = f32[64,4,256]{2,1,0:T(4,128)S(1)} all-to-all(f32[64,4,256]{2,1,0:T(4,128)S(1)} %reshape.51), channel_id=1, replica_groups=mesh['grp'=8,'wide'=64] {'wide'}, dimensions={0} | all-to-all | bytes 524288 | tf_op jit(solution)/shard_map/all_to_all | solution.py:81
  140.7 0.1 reduce_sum.9
  140.8 0.6 broadcast_multiply_fusion.1
  141.4 21.6 %reduce-scatter.2.cloned.1.call-done = f32[256,256]{1,0:T(8,128)} async-done(((f32[256,2048]{1,0:T(8,128)}), f32[256,256]{1,0:T(8,128)}) %reduce-scatter.2.cloned.1.call-update) | async-done | bytes 262160 | tf_op jit(solution)/shard_map/reduce_scatter | solution.py:86
  (16 shorter events, 0.1 us)
Async XLA Ops:
  7.2 100.4 %copy-start = (f32[256,2048]{1,0:T(8,128)S(1)}, f32[256,2048]{1,0:T(8,128)}, u32[]{:S(2)}) copy-start(f32[256,2048]{1,0:T(8,128)} %param.7) | copy-start | bytes 6291460
  7.2 155.8 %reduce-scatter.2.cloned.1.call-start = ((), (), s32[]{:S(2)}) async-start(), calls=%async_computation.2 | async-start | bytes 2359296 | tf_op jit(solution)/shard_map/reduce_scatter | solution.py:86
  7.2 37.3 %collective-permute-start = (f32[256,256]{1,0:T(8,128)}, f32[256,256]{1,0:T(8,128)}, u32[]{:S(2)}, u32[]{:S(2)}) collective-permute-start(f32[256,256]{1,0:T(8,128)} %param.4), channel_id=1, source_target_pairs={{0,1},{1,2},{2,3},{3,4},{4,5},{5,6},{6,7},{7,8},{8,9},{9,10},{10,1... | collective-permute-start | bytes 786440 | tf_op jit(solution)/shard_map/ppermute | solution.py:22
  9.3 32.5 %collective-permute-start.3 = (f32[256,256]{1,0:T(8,128)}, f32[256,256]{1,0:T(8,128)}, u32[]{:S(2)}, u32[]{:S(2)}) collective-permute-start(f32[256,256]{1,0:T(8,128)} %param.4), channel_id=1, source_target_pairs={{0,62},{1,63},{2,0},{3,1},{4,2},{5,3},{6,4},{7,5},{8,6},{9,7},{10,... | collective-permute-start | bytes 786440 | tf_op jit(solution)/shard_map/ppermute | solution.py:22
  20.5 22.6 %collective-permute-start.2 = (f32[256,256]{1,0:T(8,128)}, f32[256,256]{1,0:T(8,128)}, u32[]{:S(2)}, u32[]{:S(2)}) collective-permute-start(f32[256,256]{1,0:T(8,128)} %param.4), channel_id=1, source_target_pairs={{0,2},{1,3},{2,4},{3,5},{4,6},{5,7},{6,8},{7,9},{8,10},{9,11},{10,... | collective-permute-start | bytes 786440 | tf_op jit(solution)/shard_map/ppermute | solution.py:22
  22.4 23.4 %collective-permute-start.1 = (f32[256,256]{1,0:T(8,128)}, f32[256,256]{1,0:T(8,128)}, u32[]{:S(2)}, u32[]{:S(2)}) collective-permute-start(f32[256,256]{1,0:T(8,128)} %param.4), channel_id=1, source_target_pairs={{0,63},{1,0},{2,1},{3,2},{4,3},{5,4},{6,5},{7,6},{8,7},{9,8},{10,9... | collective-permute-start | bytes 786440 | tf_op jit(solution)/shard_map/ppermute | solution.py:22
  29.5 2.0 %copy-start.4 = (s32[4,16]{1,0:T(4,128)S(1)}, s32[4,16]{1,0:T(4,128)}, u32[]{:S(2)}) copy-start(s32[4,16]{1,0:T(4,128)} %param.6) | copy-start | bytes 772
  41.7 4.1 %copy-start.3 = (f32[256,256]{1,0:T(8,128)S(1)}, f32[256,256]{1,0:T(8,128)}, u32[]{:S(2)}) copy-start(f32[256,256]{1,0:T(8,128)} %param.4) | copy-start | bytes 786436
  47.2 13.7 %collective-permute-start.6 = (f32[256,256]{1,0:T(8,128)S(1)}, f32[256,256]{1,0:T(8,128)S(1)}, u32[]{:S(2)}, u32[]{:S(2)}) collective-permute-start(f32[256,256]{1,0:T(8,128)S(1)} %get-tuple-element.2), channel_id=1, source_target_pairs={{0,2},{1,3},{2,4},{3,5},{4,6},{5,7},{6,8},{7,9},{8,10},{9,11},{10,... | collective-permute-start | bytes 786440 | tf_op jit(solution)/shard_map/ppermute | solution.py:22
  49.1 14.2 %collective-permute-start.4 = (f32[256,256]{1,0:T(8,128)S(1)}, f32[256,256]{1,0:T(8,128)S(1)}, u32[]{:S(2)}, u32[]{:S(2)}) collective-permute-start(f32[256,256]{1,0:T(8,128)S(1)} %get-tuple-element.2), channel_id=1, source_target_pairs={{0,1},{1,2},{2,3},{3,4},{4,5},{5,6},{6,7},{7,8},{8,9},{9,10},{10,1... | collective-permute-start | bytes 786440 | tf_op jit(solution)/shard_map/ppermute | solution.py:22
  51.1 11.9 %collective-permute-start.7 = (f32[256,256]{1,0:T(8,128)S(1)}, f32[256,256]{1,0:T(8,128)S(1)}, u32[]{:S(2)}, u32[]{:S(2)}) collective-permute-start(f32[256,256]{1,0:T(8,128)S(1)} %get-tuple-element.2), channel_id=1, source_target_pairs={{0,62},{1,63},{2,0},{3,1},{4,2},{5,3},{6,4},{7,5},{8,6},{9,7},{10,... | collective-permute-start | bytes 786440 | tf_op jit(solution)/shard_map/ppermute | solution.py:22
  57.1 8.6 %collective-permute-start.5 = (f32[256,256]{1,0:T(8,128)S(1)}, f32[256,256]{1,0:T(8,128)S(1)}, u32[]{:S(2)}, u32[]{:S(2)}) collective-permute-start(f32[256,256]{1,0:T(8,128)S(1)} %get-tuple-element.2), channel_id=1, source_target_pairs={{0,63},{1,0},{2,1},{3,2},{4,3},{5,4},{6,5},{7,6},{8,7},{9,8},{10,9... | collective-permute-start | bytes 786440 | tf_op jit(solution)/shard_map/ppermute | solution.py:22
  66.2 16.0 %collective-permute-start.10 = (f32[256,256]{1,0:T(8,128)S(1)}, f32[256,256]{1,0:T(8,128)S(1)}, u32[]{:S(2)}, u32[]{:S(2)}) collective-permute-start(f32[256,256]{1,0:T(8,128)S(1)} %fusion.8), channel_id=1, source_target_pairs={{0,2},{1,3},{2,4},{3,5},{4,6},{5,7},{6,8},{7,9},{8,10},{9,11},{10,... | collective-permute-start | bytes 786440 | tf_op jit(solution)/shard_map/ppermute | solution.py:22
  68.1 14.5 %collective-permute-start.11 = (f32[256,256]{1,0:T(8,128)S(1)}, f32[256,256]{1,0:T(8,128)S(1)}, u32[]{:S(2)}, u32[]{:S(2)}) collective-permute-start(f32[256,256]{1,0:T(8,128)S(1)} %fusion.8), channel_id=1, source_target_pairs={{0,62},{1,63},{2,0},{3,1},{4,2},{5,3},{6,4},{7,5},{8,6},{9,7},{10,... | collective-permute-start | bytes 786440 | tf_op jit(solution)/shard_map/ppermute | solution.py:22
  74.5 9.8 %collective-permute-start.8 = (f32[256,256]{1,0:T(8,128)S(1)}, f32[256,256]{1,0:T(8,128)S(1)}, u32[]{:S(2)}, u32[]{:S(2)}) collective-permute-start(f32[256,256]{1,0:T(8,128)S(1)} %fusion.8), channel_id=1, source_target_pairs={{0,1},{1,2},{2,3},{3,4},{4,5},{5,6},{6,7},{7,8},{8,9},{9,10},{10,1... | collective-permute-start | bytes 786440 | tf_op jit(solution)/shard_map/ppermute | solution.py:22
  76.4 9.6 %collective-permute-start.9 = (f32[256,256]{1,0:T(8,128)S(1)}, f32[256,256]{1,0:T(8,128)S(1)}, u32[]{:S(2)}, u32[]{:S(2)}) collective-permute-start(f32[256,256]{1,0:T(8,128)S(1)} %fusion.8), channel_id=1, source_target_pairs={{0,63},{1,0},{2,1},{3,2},{4,3},{5,4},{6,5},{7,6},{8,7},{9,8},{10,9... | collective-permute-start | bytes 786440 | tf_op jit(solution)/shard_map/ppermute | solution.py:22
  86.5 16.2 %collective-permute-start.14 = (f32[256,256]{1,0:T(8,128)S(1)}, f32[256,256]{1,0:T(8,128)S(1)}, u32[]{:S(2)}, u32[]{:S(2)}) collective-permute-start(f32[256,256]{1,0:T(8,128)S(1)} %fusion.11), channel_id=1, source_target_pairs={{0,2},{1,3},{2,4},{3,5},{4,6},{5,7},{6,8},{7,9},{8,10},{9,11},{10,... | collective-permute-start | bytes 786440 | tf_op jit(solution)/shard_map/ppermute | solution.py:22
  88.4 14.7 %collective-permute-start.15 = (f32[256,256]{1,0:T(8,128)S(1)}, f32[256,256]{1,0:T(8,128)S(1)}, u32[]{:S(2)}, u32[]{:S(2)}) collective-permute-start(f32[256,256]{1,0:T(8,128)S(1)} %fusion.11), channel_id=1, source_target_pairs={{0,62},{1,63},{2,0},{3,1},{4,2},{5,3},{6,4},{7,5},{8,6},{9,7},{10,... | collective-permute-start | bytes 786440 | tf_op jit(solution)/shard_map/ppermute | solution.py:22
  94.8 9.8 %collective-permute-start.12 = (f32[256,256]{1,0:T(8,128)S(1)}, f32[256,256]{1,0:T(8,128)S(1)}, u32[]{:S(2)}, u32[]{:S(2)}) collective-permute-start(f32[256,256]{1,0:T(8,128)S(1)} %fusion.11), channel_id=1, source_target_pairs={{0,1},{1,2},{2,3},{3,4},{4,5},{5,6},{6,7},{7,8},{8,9},{9,10},{10,1... | collective-permute-start | bytes 786440 | tf_op jit(solution)/shard_map/ppermute | solution.py:22
  96.8 9.6 %collective-permute-start.13 = (f32[256,256]{1,0:T(8,128)S(1)}, f32[256,256]{1,0:T(8,128)S(1)}, u32[]{:S(2)}, u32[]{:S(2)}) collective-permute-start(f32[256,256]{1,0:T(8,128)S(1)} %fusion.11), channel_id=1, source_target_pairs={{0,63},{1,0},{2,1},{3,2},{4,3},{5,4},{6,5},{7,6},{8,7},{9,8},{10,9... | collective-permute-start | bytes 786440 | tf_op jit(solution)/shard_map/ppermute | solution.py:22
  106.8 0.7 copy-start.1
  110.8 0.9 copy-start.2
Sparse Core Ops, SparseCore 0:
  110.9 52.0 reduce-scatter.1

commit v13 on v6

--- a/solution.py
+++ b/solution.py
@@ -53,14 +53,17 @@
     owner = pattern // A_DEV
     relative = (owner - myself + HW + devcount) % devcount
     slot_index = relative * A_DEV + pattern % A_DEV
-    hdense = dense_hamiltonian(hblocks, slot_index)
+    local_blocks = hblocks.shape[0]
+    shift = jnp.broadcast_to(-cheb_center * jnp.eye(B, dtype=jnp.float32), (local_blocks, 1, B, B))
+    blocks_ext = (2.0 / cheb_half) * jnp.concatenate([hblocks, shift], axis=1)
+    self_slot = HW * A_DEV + jnp.arange(local_blocks, dtype=slot_index.dtype)[:, None]
+    hdense = dense_hamiltonian(blocks_ext, jnp.concatenate([slot_index, self_slot], axis=1))
+    rows = subspace.shape[0]
+    step_op = hdense
     previous = subspace
-    current = (apply_ham(subspace, hdense) - cheb_center * subspace) / cheb_half
+    current = 0.5 * apply_ham(subspace, step_op)
     for step in range(DEGREE - 1):
-        nextone = (
-            2.0 * (apply_ham(current, hdense) - cheb_center * current) / cheb_half
-            - previous
-        )
+        nextone = apply_ham(current, step_op) - previous
         previous = current
         current = nextone
     total_rows = current.shape[0] * devcount

time: 166 us -> 172 us (1.036)
  local copies, waits for them, and re-layouts: 3.95 us -> 8.2 us
  starting transfers between devices: 64.8 us -> 67.3 us
    unnamed x8 -> x11, local copies, waits for them, and re-layouts: 1.64 us -> 5.82 us
    ppermute x16, starting transfers between devices: 64.8 us -> 67.3 us  [passed_along(): return lax.ppermute(value, axis, pairs)]
  transfers between devices with their start and end apart: 17 -> 17, of which waited for: 7 -> 7; matrix products, arithmetic and copies ran while one was open for 12% -> 13% of each run, Pallas kernels for 0% -> 0%
where the time goes in v13:
time: 172 us; the launch traced here: 171 us
  starting transfers between devices  67.3 us (39%)
  blocking collectives  29.5 us (17%)
  waiting for transfers between devices  29.4 us (17%)
  matrix products  21.2 us (12%)
  between operations  14.5 us (8%)
  local copies, waits for them, and re-layouts  8.2 us (5%)
    ppermute x16, starting transfers between devices, passed_along(): return lax.ppermute(value, axis, pairs)  67.3 us
    all_to_all x1, blocking collectives, local(): gathered = lax.all_to_all(pieces, 'wide', 0, 0, tiled=True)  29.5 us
    reduce_scatter x1, waiting for transfers between devices, local(): rotated = lax.psum_scatter(rot_term, 'grp', scatter_dimension=1, tiled=True)  21.5 us
    dot_general x20, matrix products, apply_ham(): jnp.dot(hdense[:, idx * rows:(idx + 1) * rows], pieces[idx], precision=HI...  12.4 us
    ppermute x16, waiting for transfers between devices, passed_along(): return lax.ppermute(value, axis, pairs)  7.9 us
    unnamed x11, local copies, waits for them, and re-layouts  5.82 us
    dot_general x1, matrix products, dense_hamiltonian(): hd = jnp.einsum('asp,asij->aipj', onehot, hblocks, precision=HI)  5.01 us
  transfers between devices with their start and end apart: 17, of which 7 were waited for; matrix products, arithmetic and copies ran while one was open for 13% of the time, Pallas kernels for 0%

profile of v13, /device:TPU:6, one launch (start us, length us, event | category | flops | bytes accessed | tf_op | source)
XLA Modules:
  0.0 170.9 jit_solution(18204167260649260779)
XLA Ops:
  7.2 0.0 copy-start
  7.2 0.0 reduce-scatter.2.cloned.1.call-start
  7.2 2.1 %collective-permute-start = (f32[256,256]{1,0:T(8,128)}, f32[256,256]{1,0:T(8,128)}, u32[]{:S(2)}, u32[]{:S(2)}) collective-permute-start(f32[256,256]{1,0:T(8,128)} %param.4), channel_id=1, source_target_pairs={{0,1},{1,2},{2,3},{3,4},{4,5},{5,6},{6,7},{7,8},{8,9},{9,10},{10,1... | collective-permute-start | bytes 786440 | tf_op jit(solution)/shard_map/ppermute | solution.py:22
  9.3 11.2 %collective-permute-start.3 = (f32[256,256]{1,0:T(8,128)}, f32[256,256]{1,0:T(8,128)}, u32[]{:S(2)}, u32[]{:S(2)}) collective-permute-start(f32[256,256]{1,0:T(8,128)} %param.4), channel_id=1, source_target_pairs={{0,62},{1,63},{2,0},{3,1},{4,2},{5,3},{6,4},{7,5},{8,6},{9,7},{10,... | collective-permute-start | bytes 786440 | tf_op jit(solution)/shard_map/ppermute | solution.py:22
  20.5 1.9 %collective-permute-start.2 = (f32[256,256]{1,0:T(8,128)}, f32[256,256]{1,0:T(8,128)}, u32[]{:S(2)}, u32[]{:S(2)}) collective-permute-start(f32[256,256]{1,0:T(8,128)} %param.4), channel_id=1, source_target_pairs={{0,2},{1,3},{2,4},{3,5},{4,6},{5,7},{6,8},{7,9},{8,10},{9,11},{10,... | collective-permute-start | bytes 786440 | tf_op jit(solution)/shard_map/ppermute | solution.py:22
  22.4 4.9 %collective-permute-start.1 = (f32[256,256]{1,0:T(8,128)}, f32[256,256]{1,0:T(8,128)}, u32[]{:S(2)}, u32[]{:S(2)}) collective-permute-start(f32[256,256]{1,0:T(8,128)} %param.4), channel_id=1, source_target_pairs={{0,63},{1,0},{2,1},{3,2},{4,3},{5,4},{6,5},{7,6},{8,7},{9,8},{10,9... | collective-permute-start | bytes 786440 | tf_op jit(solution)/shard_map/ppermute | solution.py:22
  27.4 0.0 copy-start.4
  27.4 4.2 %copy.7 = f32[4,16,64,64]{3,1,2,0:T(8,128)} copy(f32[4,16,64,64]{3,2,1,0:T(8,128)} %param.5) | data formatting | bytes 2097152 | tf_op args[1]
  31.6 0.1 pad_add_fusion
  31.7 0.1 broadcast_in_dim.2
  31.8 5.0 %fusion.4 = f32[4,64,20,64]{3,2,1,0:T(8,128)} fusion(f32[4,1,64,64]{3,1,2,0:T(1,128)S(1)} %broadcast_in_dim.2, f32[4,16,64,64]{3,1,2,0:T(8,128)} %copy.7, s32[4,17]{1,0:T(4,128)S(1)} %pad_add_fusion), kind=kOutput, calls=%fused_computation.4 | convolution fusion | flops 67126608 | bytes 2425104 | tf_op jit(solution)/shard_map/asp,asij->aipj/dot_general | solution.py:29
  36.8 2.2 %reshape.22 = f32[256,1280]{1,0:T(8,128)S(1)} reshape(f32[4,64,20,64]{3,2,1,0:T(8,128)} %fusion.4) | data formatting | bytes 2621440 | tf_op jit(solution)/shard_map/reshape | solution.py:30
  39.0 1.3 fusion.47
  40.4 1.3 fusion.23
  41.7 0.0 collective-permute-done.2
  41.7 1.3 fusion.31
  43.0 0.0 collective-permute-done
  43.0 1.3 convolution_add_fusion.7
  44.4 0.0 collective-permute-done.1
  44.4 1.3 fusion.12
  45.7 1.9 %collective-permute-start.6 = (f32[256,256]{1,0:T(8,128)S(1)}, f32[256,256]{1,0:T(8,128)S(1)}, u32[]{:S(2)}, u32[]{:S(2)}) collective-permute-start(f32[256,256]{1,0:T(8,128)S(1)} %fusion.12), channel_id=1, source_target_pairs={{0,2},{1,3},{2,4},{3,5},{4,6},{5,7},{6,8},{7,9},{8,10},{9,11},{10,... | collective-permute-start | bytes 786440 | tf_op jit(solution)/shard_map/ppermute | solution.py:22
  47.7 6.0 %collective-permute-start.7 = (f32[256,256]{1,0:T(8,128)S(1)}, f32[256,256]{1,0:T(8,128)S(1)}, u32[]{:S(2)}, u32[]{:S(2)}) collective-permute-start(f32[256,256]{1,0:T(8,128)S(1)} %fusion.12), channel_id=1, source_target_pairs={{0,62},{1,63},{2,0},{3,1},{4,2},{5,3},{6,4},{7,5},{8,6},{9,7},{10,... | collective-permute-start | bytes 786440 | tf_op jit(solution)/shard_map/ppermute | solution.py:22
  53.7 0.4 fusion.45
  54.1 0.0 copy-start.3
  54.1 2.1 %collective-permute-start.4 = (f32[256,256]{1,0:T(8,128)S(1)}, f32[256,256]{1,0:T(8,128)S(1)}, u32[]{:S(2)}, u32[]{:S(2)}) collective-permute-start(f32[256,256]{1,0:T(8,128)S(1)} %fusion.12), channel_id=1, source_target_pairs={{0,1},{1,2},{2,3},{3,4},{4,5},{5,6},{6,7},{7,8},{8,9},{9,10},{10,1... | collective-permute-start | bytes 786440 | tf_op jit(solution)/shard_map/ppermute | solution.py:22
  56.2 5.8 %collective-permute-start.5 = (f32[256,256]{1,0:T(8,128)S(1)}, f32[256,256]{1,0:T(8,128)S(1)}, u32[]{:S(2)}, u32[]{:S(2)}) collective-permute-start(f32[256,256]{1,0:T(8,128)S(1)} %fusion.12), channel_id=1, source_target_pairs={{0,63},{1,0},{2,1},{3,2},{4,3},{5,4},{6,5},{7,6},{8,7},{9,8},{10,9... | collective-permute-start | bytes 786440 | tf_op jit(solution)/shard_map/ppermute | solution.py:22
  61.9 0.4 fusion.29
  62.3 0.4 fusion.21
  62.7 1.3 collective-permute-done.4
  64.0 0.4 convolution_add_fusion.5
  64.4 1.4 collective-permute-done.5
  65.8 0.4 fusion.14
  66.2 1.9 %collective-permute-start.10 = (f32[256,256]{1,0:T(8,128)S(1)}, f32[256,256]{1,0:T(8,128)S(1)}, u32[]{:S(2)}, u32[]{:S(2)}) collective-permute-start(f32[256,256]{1,0:T(8,128)S(1)} %fusion.14), channel_id=1, source_target_pairs={{0,2},{1,3},{2,4},{3,5},{4,6},{5,7},{6,8},{7,9},{8,10},{9,11},{10,... | collective-permute-start | bytes 786440 | tf_op jit(solution)/shard_map/ppermute | solution.py:22
  68.1 6.0 %collective-permute-start.11 = (f32[256,256]{1,0:T(8,128)S(1)}, f32[256,256]{1,0:T(8,128)S(1)}, u32[]{:S(2)}, u32[]{:S(2)}) collective-permute-start(f32[256,256]{1,0:T(8,128)S(1)} %fusion.14), channel_id=1, source_target_pairs={{0,62},{1,63},{2,0},{3,1},{4,2},{5,3},{6,4},{7,5},{8,6},{9,7},{10,... | collective-permute-start | bytes 786440 | tf_op jit(solution)/shard_map/ppermute | solution.py:22
  74.2 0.4 fusion.43
  74.5 1.9 %collective-permute-start.8 = (f32[256,256]{1,0:T(8,128)S(1)}, f32[256,256]{1,0:T(8,128)S(1)}, u32[]{:S(2)}, u32[]{:S(2)}) collective-permute-start(f32[256,256]{1,0:T(8,128)S(1)} %fusion.14), channel_id=1, source_target_pairs={{0,1},{1,2},{2,3},{3,4},{4,5},{5,6},{6,7},{7,8},{8,9},{9,10},{10,1... | collective-permute-start | bytes 786440 | tf_op jit(solution)/shard_map/ppermute | solution.py:22
  76.5 5.8 %collective-permute-start.9 = (f32[256,256]{1,0:T(8,128)S(1)}, f32[256,256]{1,0:T(8,128)S(1)}, u32[]{:S(2)}, u32[]{:S(2)}) collective-permute-start(f32[256,256]{1,0:T(8,128)S(1)} %fusion.14), channel_id=1, source_target_pairs={{0,63},{1,0},{2,1},{3,2},{4,3},{5,4},{6,5},{7,6},{8,7},{9,8},{10,9... | collective-permute-start | bytes 786440 | tf_op jit(solution)/shard_map/ppermute | solution.py:22
  82.2 0.4 fusion.27
  82.6 0.4 fusion.19
  83.0 1.3 collective-permute-done.8
  84.3 0.4 convolution_add_fusion.3
  84.7 1.4 collective-permute-done.9
  86.1 0.4 fusion.16
  86.5 1.9 %collective-permute-start.14 = (f32[256,256]{1,0:T(8,128)S(1)}, f32[256,256]{1,0:T(8,128)S(1)}, u32[]{:S(2)}, u32[]{:S(2)}) collective-permute-start(f32[256,256]{1,0:T(8,128)S(1)} %fusion.16), channel_id=1, source_target_pairs={{0,2},{1,3},{2,4},{3,5},{4,6},{5,7},{6,8},{7,9},{8,10},{9,11},{10,... | collective-permute-start | bytes 786440 | tf_op jit(solution)/shard_map/ppermute | solution.py:22
  88.4 6.0 %collective-permute-start.15 = (f32[256,256]{1,0:T(8,128)S(1)}, f32[256,256]{1,0:T(8,128)S(1)}, u32[]{:S(2)}, u32[]{:S(2)}) collective-permute-start(f32[256,256]{1,0:T(8,128)S(1)} %fusion.16), channel_id=1, source_target_pairs={{0,62},{1,63},{2,0},{3,1},{4,2},{5,3},{6,4},{7,5},{8,6},{9,7},{10,... | collective-permute-start | bytes 786440 | tf_op jit(solution)/shard_map/ppermute | solution.py:22
  94.5 0.4 fusion.49
  94.8 1.9 %collective-permute-start.12 = (f32[256,256]{1,0:T(8,128)S(1)}, f32[256,256]{1,0:T(8,128)S(1)}, u32[]{:S(2)}, u32[]{:S(2)}) collective-permute-start(f32[256,256]{1,0:T(8,128)S(1)} %fusion.16), channel_id=1, source_target_pairs={{0,1},{1,2},{2,3},{3,4},{4,5},{5,6},{6,7},{7,8},{8,9},{9,10},{10,1... | collective-permute-start | bytes 786440 | tf_op jit(solution)/shard_map/ppermute | solution.py:22
  96.8 5.9 %collective-permute-start.13 = (f32[256,256]{1,0:T(8,128)S(1)}, f32[256,256]{1,0:T(8,128)S(1)}, u32[]{:S(2)}, u32[]{:S(2)}) collective-permute-start(f32[256,256]{1,0:T(8,128)S(1)} %fusion.16), channel_id=1, source_target_pairs={{0,63},{1,0},{2,1},{3,2},{4,3},{5,4},{6,5},{7,6},{8,7},{9,8},{10,9... | collective-permute-start | bytes 786440 | tf_op jit(solution)/shard_map/ppermute | solution.py:22
  102.7 0.4 fusion.33
  103.1 0.4 fusion.25
  103.5 1.1 collective-permute-done.12
  104.6 0.4 convolution_add_fusion.1
  105.0 1.4 collective-permute-done.13
  106.4 0.4 fusion.18
  106.8 0.7 copy-done.1
  107.5 3.2 %fusion.62 = f32[256,2048]{1,0:T(8,128)} fusion(f32[256,256]{1,0:T(8,128)S(1)} %fusion.18, f32[256,2048]{1,0:T(8,128)S(1)} %copy-done), kind=kOutput, calls=%fused_computation.81 | convolution fusion | flops 1610612736 | bytes 4456448 | tf_op jit(solution)/shard_map/dot_general | solution.py:80
  110.8 0.0 reduce-scatter.2.cloned.1.call-update
  110.8 0.9 copy-done.2
  111.7 0.6 fusion.63
  112.3 0.1 reshape.20
  112.4 29.5 %all_to_all.5 = f32[64,4,256]{2,1,0:T(4,128)S(1)} all-to-all(f32[64,4,256]{2,1,0:T(4,128)S(1)} %reshape.20), channel_id=1, replica_groups=mesh['grp'=8,'wide'=64] {'wide'}, dimensions={0} | all-to-all | bytes 524288 | tf_op jit(solution)/shard_map/all_to_all | solution.py:78
  141.9 0.1 reduce_sum.9
  142.0 0.6 broadcast_multiply_fusion
  142.6 21.5 %reduce-scatter.2.cloned.1.call-done = f32[256,256]{1,0:T(8,128)} async-done(((f32[256,2048]{1,0:T(8,128)}), f32[256,256]{1,0:T(8,128)}) %reduce-scatter.2.cloned.1.call-update) | async-done | bytes 262160 | tf_op jit(solution)/shard_map/reduce_scatter | solution.py:83
  (15 shorter events, 0.1 us)
Async XLA Ops:
  7.2 100.3 %copy-start = (f32[256,2048]{1,0:T(8,128)S(1)}, f32[256,2048]{1,0:T(8,128)}, u32[]{:S(2)}) copy-start(f32[256,2048]{1,0:T(8,128)} %param.7) | copy-start | bytes 6291460
  7.2 156.9 %reduce-scatter.2.cloned.1.call-start = ((), (), s32[]{:S(2)}) async-start(), calls=%async_computation.2 | async-start | bytes 2359296 | tf_op jit(solution)/shard_map/reduce_scatter | solution.py:83
  7.2 35.8 %collective-permute-start = (f32[256,256]{1,0:T(8,128)}, f32[256,256]{1,0:T(8,128)}, u32[]{:S(2)}, u32[]{:S(2)}) collective-permute-start(f32[256,256]{1,0:T(8,128)} %param.4), channel_id=1, source_target_pairs={{0,1},{1,2},{2,3},{3,4},{4,5},{5,6},{6,7},{7,8},{8,9},{9,10},{10,1... | collective-permute-start | bytes 786440 | tf_op jit(solution)/shard_map/ppermute | solution.py:22
  9.3 31.1 %collective-permute-start.3 = (f32[256,256]{1,0:T(8,128)}, f32[256,256]{1,0:T(8,128)}, u32[]{:S(2)}, u32[]{:S(2)}) collective-permute-start(f32[256,256]{1,0:T(8,128)} %param.4), channel_id=1, source_target_pairs={{0,62},{1,63},{2,0},{3,1},{4,2},{5,3},{6,4},{7,5},{8,6},{9,7},{10,... | collective-permute-start | bytes 786440 | tf_op jit(solution)/shard_map/ppermute | solution.py:22
  20.5 21.2 %collective-permute-start.2 = (f32[256,256]{1,0:T(8,128)}, f32[256,256]{1,0:T(8,128)}, u32[]{:S(2)}, u32[]{:S(2)}) collective-permute-start(f32[256,256]{1,0:T(8,128)} %param.4), channel_id=1, source_target_pairs={{0,2},{1,3},{2,4},{3,5},{4,6},{5,7},{6,8},{7,9},{8,10},{9,11},{10,... | collective-permute-start | bytes 786440 | tf_op jit(solution)/shard_map/ppermute | solution.py:22
  22.4 21.9 %collective-permute-start.1 = (f32[256,256]{1,0:T(8,128)}, f32[256,256]{1,0:T(8,128)}, u32[]{:S(2)}, u32[]{:S(2)}) collective-permute-start(f32[256,256]{1,0:T(8,128)} %param.4), channel_id=1, source_target_pairs={{0,63},{1,0},{2,1},{3,2},{4,3},{5,4},{6,5},{7,6},{8,7},{9,8},{10,9... | collective-permute-start | bytes 786440 | tf_op jit(solution)/shard_map/ppermute | solution.py:22
  27.4 4.2 %copy-start.4 = (s32[4,16]{1,0:T(4,128)S(1)}, s32[4,16]{1,0:T(4,128)}, u32[]{:S(2)}) copy-start(s32[4,16]{1,0:T(4,128)} %param.6) | copy-start | bytes 772
  45.7 16.2 %collective-permute-start.6 = (f32[256,256]{1,0:T(8,128)S(1)}, f32[256,256]{1,0:T(8,128)S(1)}, u32[]{:S(2)}, u32[]{:S(2)}) collective-permute-start(f32[256,256]{1,0:T(8,128)S(1)} %fusion.12), channel_id=1, source_target_pairs={{0,2},{1,3},{2,4},{3,5},{4,6},{5,7},{6,8},{7,9},{8,10},{9,11},{10,... | collective-permute-start | bytes 786440 | tf_op jit(solution)/shard_map/ppermute | solution.py:22
  47.7 14.7 %collective-permute-start.7 = (f32[256,256]{1,0:T(8,128)S(1)}, f32[256,256]{1,0:T(8,128)S(1)}, u32[]{:S(2)}, u32[]{:S(2)}) collective-permute-start(f32[256,256]{1,0:T(8,128)S(1)} %fusion.12), channel_id=1, source_target_pairs={{0,62},{1,63},{2,0},{3,1},{4,2},{5,3},{6,4},{7,5},{8,6},{9,7},{10,... | collective-permute-start | bytes 786440 | tf_op jit(solution)/shard_map/ppermute | solution.py:22
  54.1 11.7 %copy-start.3 = (f32[256,256]{1,0:T(8,128)S(1)}, f32[256,256]{1,0:T(8,128)}, u32[]{:S(2)}) copy-start(f32[256,256]{1,0:T(8,128)} %param.4) | copy-start | bytes 786436
  54.1 9.9 %collective-permute-start.4 = (f32[256,256]{1,0:T(8,128)S(1)}, f32[256,256]{1,0:T(8,128)S(1)}, u32[]{:S(2)}, u32[]{:S(2)}) collective-permute-start(f32[256,256]{1,0:T(8,128)S(1)} %fusion.12), channel_id=1, source_target_pairs={{0,1},{1,2},{2,3},{3,4},{4,5},{5,6},{6,7},{7,8},{8,9},{9,10},{10,1... | collective-permute-start | bytes 786440 | tf_op jit(solution)/shard_map/ppermute | solution.py:22
  56.2 9.6 %collective-permute-start.5 = (f32[256,256]{1,0:T(8,128)S(1)}, f32[256,256]{1,0:T(8,128)S(1)}, u32[]{:S(2)}, u32[]{:S(2)}) collective-permute-start(f32[256,256]{1,0:T(8,128)S(1)} %fusion.12), channel_id=1, source_target_pairs={{0,63},{1,0},{2,1},{3,2},{4,3},{5,4},{6,5},{7,6},{8,7},{9,8},{10,9... | collective-permute-start | bytes 786440 | tf_op jit(solution)/shard_map/ppermute | solution.py:22
  66.2 16.0 %collective-permute-start.10 = (f32[256,256]{1,0:T(8,128)S(1)}, f32[256,256]{1,0:T(8,128)S(1)}, u32[]{:S(2)}, u32[]{:S(2)}) collective-permute-start(f32[256,256]{1,0:T(8,128)S(1)} %fusion.14), channel_id=1, source_target_pairs={{0,2},{1,3},{2,4},{3,5},{4,6},{5,7},{6,8},{7,9},{8,10},{9,11},{10,... | collective-permute-start | bytes 786440 | tf_op jit(solution)/shard_map/ppermute | solution.py:22
  68.1 14.5 %collective-permute-start.11 = (f32[256,256]{1,0:T(8,128)S(1)}, f32[256,256]{1,0:T(8,128)S(1)}, u32[]{:S(2)}, u32[]{:S(2)}) collective-permute-start(f32[256,256]{1,0:T(8,128)S(1)} %fusion.14), channel_id=1, source_target_pairs={{0,62},{1,63},{2,0},{3,1},{4,2},{5,3},{6,4},{7,5},{8,6},{9,7},{10,... | collective-permute-start | bytes 786440 | tf_op jit(solution)/shard_map/ppermute | solution.py:22
  74.5 9.8 %collective-permute-start.8 = (f32[256,256]{1,0:T(8,128)S(1)}, f32[256,256]{1,0:T(8,128)S(1)}, u32[]{:S(2)}, u32[]{:S(2)}) collective-permute-start(f32[256,256]{1,0:T(8,128)S(1)} %fusion.14), channel_id=1, source_target_pairs={{0,1},{1,2},{2,3},{3,4},{4,5},{5,6},{6,7},{7,8},{8,9},{9,10},{10,1... | collective-permute-start | bytes 786440 | tf_op jit(solution)/shard_map/ppermute | solution.py:22
  76.5 9.6 %collective-permute-start.9 = (f32[256,256]{1,0:T(8,128)S(1)}, f32[256,256]{1,0:T(8,128)S(1)}, u32[]{:S(2)}, u32[]{:S(2)}) collective-permute-start(f32[256,256]{1,0:T(8,128)S(1)} %fusion.14), channel_id=1, source_target_pairs={{0,63},{1,0},{2,1},{3,2},{4,3},{5,4},{6,5},{7,6},{8,7},{9,8},{10,9... | collective-permute-start | bytes 786440 | tf_op jit(solution)/shard_map/ppermute | solution.py:22
  86.5 16.2 %collective-permute-start.14 = (f32[256,256]{1,0:T(8,128)S(1)}, f32[256,256]{1,0:T(8,128)S(1)}, u32[]{:S(2)}, u32[]{:S(2)}) collective-permute-start(f32[256,256]{1,0:T(8,128)S(1)} %fusion.16), channel_id=1, source_target_pairs={{0,2},{1,3},{2,4},{3,5},{4,6},{5,7},{6,8},{7,9},{8,10},{9,11},{10,... | collective-permute-start | bytes 786440 | tf_op jit(solution)/shard_map/ppermute | solution.py:22
  88.4 14.7 %collective-permute-start.15 = (f32[256,256]{1,0:T(8,128)S(1)}, f32[256,256]{1,0:T(8,128)S(1)}, u32[]{:S(2)}, u32[]{:S(2)}) collective-permute-start(f32[256,256]{1,0:T(8,128)S(1)} %fusion.16), channel_id=1, source_target_pairs={{0,62},{1,63},{2,0},{3,1},{4,2},{5,3},{6,4},{7,5},{8,6},{9,7},{10,... | collective-permute-start | bytes 786440 | tf_op jit(solution)/shard_map/ppermute | solution.py:22
  94.8 9.8 %collective-permute-start.12 = (f32[256,256]{1,0:T(8,128)S(1)}, f32[256,256]{1,0:T(8,128)S(1)}, u32[]{:S(2)}, u32[]{:S(2)}) collective-permute-start(f32[256,256]{1,0:T(8,128)S(1)} %fusion.16), channel_id=1, source_target_pairs={{0,1},{1,2},{2,3},{3,4},{4,5},{5,6},{6,7},{7,8},{8,9},{9,10},{10,1... | collective-permute-start | bytes 786440 | tf_op jit(solution)/shard_map/ppermute | solution.py:22
  96.8 9.6 %collective-permute-start.13 = (f32[256,256]{1,0:T(8,128)S(1)}, f32[256,256]{1,0:T(8,128)S(1)}, u32[]{:S(2)}, u32[]{:S(2)}) collective-permute-start(f32[256,256]{1,0:T(8,128)S(1)} %fusion.16), channel_id=1, source_target_pairs={{0,63},{1,0},{2,1},{3,2},{4,3},{5,4},{6,5},{7,6},{8,7},{9,8},{10,9... | collective-permute-start | bytes 786440 | tf_op jit(solution)/shard_map/ppermute | solution.py:22
  106.8 0.7 copy-start.1
  110.8 0.9 copy-start.2
Sparse Core Ops, SparseCore 0:
  110.9 53.0 reduce-scatter.1

commit v14 on v6

--- a/solution.py
+++ b/solution.py
@@ -32,11 +32,14 @@
 
 def apply_ham(field, hdense):
     rows = field.shape[0]
+    count = lax.axis_size("wide")
+    swap_pairs = [(i, i ^ 1) for i in range(count)]
+    cross_pairs = [(i, (i - 1) % count if i % 2 == 0 else (i + 1) % count) for i in range(count)]
     pieces = [
         passed_along(field, "wide", 2),
-        passed_along(field, "wide", 1),
+        lax.ppermute(field, "wide", swap_pairs),
         field,
-        passed_along(field, "wide", -1),
+        lax.ppermute(field, "wide", cross_pairs),
         passed_along(field, "wide", -2),
     ]
     total = None
@@ -52,6 +55,7 @@
     myself = lax.axis_index("wide")
     owner = pattern // A_DEV
     relative = (owner - myself + HW + devcount) % devcount
+    relative = jnp.where(myself % 2 == 0, jnp.where(relative == 1, 3, jnp.where(relative == 3, 1, relative)), relative)
     slot_index = relative * A_DEV + pattern % A_DEV
     hdense = dense_hamiltonian(hblocks, slot_index)
     previous = subspace

time: 166 us -> 162 us (0.976)
  starting transfers between devices: 64.8 us -> 55 us
  waiting for transfers between devices: 30.3 us -> 39.1 us
  blocking collectives: 28.3 us -> 24.8 us
    ppermute x16 -> x8, starting transfers between devices: 64.8 us -> 37 us  [passed_along(): return lax.ppermute(value, axis, pairs)]
    ppermute x0 -> x8, starting transfers between devices: none -> 18 us  [the longest x4 10.2 us: apply_ham(): lax.ppermute(field, 'wide', cross_pairs)]
    ppermute x0 -> x8, waiting for transfers between devices: none -> 15.3 us  [the longest x4 15.3 us: apply_ham(): lax.ppermute(field, 'wide', cross_pairs)]
    ppermute x16 -> x8, waiting for transfers between devices: 8.9 us -> 3.42 us  [passed_along(): return lax.ppermute(value, axis, pairs)]
    all_to_all x1, blocking collectives: 28.3 us -> 24.8 us  [local(): gathered = lax.all_to_all(pieces, 'wide', 0, 0, tiled=True)]
  transfers between devices with their start and end apart: 17 -> 17, of which waited for: 7 -> 5; matrix products, arithmetic and copies ran while one was open for 12% -> 12% of each run, Pallas kernels for 0% -> 0%
where the time goes in v14:
time: 162 us; the launch traced here: 161 us
  starting transfers between devices  55 us (34%)
  waiting for transfers between devices  39.1 us (24%)
  blocking collectives  24.8 us (15%)
  matrix products  22.1 us (14%)
  between operations  14.5 us (9%)
  local copies, waits for them, and re-layouts  3.95 us (2%)
    ppermute x8, starting transfers between devices, passed_along(): return lax.ppermute(value, axis, pairs)  37 us
    all_to_all x1, blocking collectives, local(): gathered = lax.all_to_all(pieces, 'wide', 0, 0, tiled=True)  24.8 us
    reduce_scatter x1, waiting for transfers between devices, local(): rotated = lax.psum_scatter(rot_term, 'grp', scatter_dimension=1, tiled=True)  20.3 us
    ppermute x4, waiting for transfers between devices, apply_ham(): lax.ppermute(field, 'wide', cross_pairs)  15.3 us
    dot_general x20, matrix products, apply_ham(): jnp.dot(hdense[:, idx * rows:(idx + 1) * rows], pieces[idx], precision=HI...  12.5 us
    ppermute x4, starting transfers between devices, apply_ham(): lax.ppermute(field, 'wide', cross_pairs)  10.2 us
    ppermute x4, starting transfers between devices, apply_ham(): lax.ppermute(field, 'wide', swap_pairs)  7.82 us
    dot_general x1, matrix products, dense_hamiltonian(): hd = jnp.einsum('asp,asij->aipj', onehot, hblocks, precision=HI)  5.77 us
  transfers between devices with their start and end apart: 17, of which 5 were waited for; matrix products, arithmetic and copies ran while one was open for 12% of the time, Pallas kernels for 0%

profile of v14, /device:TPU:6, one launch (start us, length us, event | category | flops | bytes accessed | tf_op | source)
XLA Modules:
  0.0 160.8 jit_solution(5805325373656663757)
XLA Ops:
  7.2 0.0 copy-start
  7.2 0.0 reduce-scatter.2.cloned.1.call-start
  7.2 2.1 %collective-permute-start = (f32[256,256]{1,0:T(8,128)}, f32[256,256]{1,0:T(8,128)}, u32[]{:S(2)}, u32[]{:S(2)}) collective-permute-start(f32[256,256]{1,0:T(8,128)} %param.4), channel_id=1, source_target_pairs={{0,1},{1,0},{2,3},{3,2},{4,5},{5,4},{6,7},{7,6},{8,9},{9,8},{10,11... | collective-permute-start | bytes 786440 | tf_op jit(solution)/shard_map/ppermute | solution.py:40
  9.3 4.3 %collective-permute-start.2 = (f32[256,256]{1,0:T(8,128)}, f32[256,256]{1,0:T(8,128)}, u32[]{:S(2)}, u32[]{:S(2)}) collective-permute-start(f32[256,256]{1,0:T(8,128)} %param.4), channel_id=1, source_target_pairs={{0,2},{1,3},{2,4},{3,5},{4,6},{5,7},{6,8},{7,9},{8,10},{9,11},{10,... | collective-permute-start | bytes 786440 | tf_op jit(solution)/shard_map/ppermute | solution.py:22
  13.6 8.9 %collective-permute-start.3 = (f32[256,256]{1,0:T(8,128)}, f32[256,256]{1,0:T(8,128)}, u32[]{:S(2)}, u32[]{:S(2)}) collective-permute-start(f32[256,256]{1,0:T(8,128)} %param.4), channel_id=1, source_target_pairs={{0,62},{1,63},{2,0},{3,1},{4,2},{5,3},{6,4},{7,5},{8,6},{9,7},{10,... | collective-permute-start | bytes 786440 | tf_op jit(solution)/shard_map/ppermute | solution.py:22
  22.4 3.5 %collective-permute-start.1 = (f32[256,256]{1,0:T(8,128)}, f32[256,256]{1,0:T(8,128)}, u32[]{:S(2)}, u32[]{:S(2)}) collective-permute-start(f32[256,256]{1,0:T(8,128)} %param.4), channel_id=1, source_target_pairs={{0,63},{1,2},{2,1},{3,4},{4,3},{5,6},{6,5},{7,8},{8,7},{9,10},{10,... | collective-permute-start | bytes 786440 | tf_op jit(solution)/shard_map/ppermute | solution.py:42
  25.9 0.7 fusion.58
  26.6 5.8 %fusion.2 = f32[4,64,20,64]{3,2,1,0:T(8,128)} fusion(f32[4,16,64,64]{3,2,1,0:T(8,128)} %param.5, s32[4,16]{1,0:T(4,128)S(1)} %fusion.58), kind=kOutput, calls=%fused_computation.2 | convolution fusion | flops 62915840 | bytes 2359552 | tf_op jit(solution)/shard_map/asp,asij->aipj/dot_general | solution.py:29
  32.4 2.2 %reshape.14 = f32[256,1280]{1,0:T(8,128)S(1)} reshape(f32[4,64,20,64]{3,2,1,0:T(8,128)} %fusion.2) | data formatting | bytes 2621440 | tf_op jit(solution)/shard_map/reshape | solution.py:30
  34.6 1.3 fusion.48
  36.0 0.0 copy-start.3
  36.0 0.0 collective-permute-done.2
  36.0 1.4 fusion.32
  37.4 0.0 collective-permute-done.3
  37.4 1.3 fusion.24
  38.7 0.0 collective-permute-done
  38.7 1.3 convolution_add_fusion.7
  40.1 0.0 collective-permute-done.1
  40.1 1.4 broadcast_multiply_fusion
  41.5 2.2 %collective-permute-start.6 = (f32[256,256]{1,0:T(8,128)S(1)}, f32[256,256]{1,0:T(8,128)S(1)}, u32[]{:S(2)}, u32[]{:S(2)}) collective-permute-start(f32[256,256]{1,0:T(8,128)S(1)} %get-tuple-element.2), channel_id=1, source_target_pairs={{0,2},{1,3},{2,4},{3,5},{4,6},{5,7},{6,8},{7,9},{8,10},{9,11},{10,... | collective-permute-start | bytes 786440 | tf_op jit(solution)/shard_map/ppermute | solution.py:22
  43.7 1.9 %collective-permute-start.4 = (f32[256,256]{1,0:T(8,128)S(1)}, f32[256,256]{1,0:T(8,128)S(1)}, u32[]{:S(2)}, u32[]{:S(2)}) collective-permute-start(f32[256,256]{1,0:T(8,128)S(1)} %get-tuple-element.2), channel_id=1, source_target_pairs={{0,1},{1,0},{2,3},{3,2},{4,5},{5,4},{6,7},{7,6},{8,9},{9,8},{10,11... | collective-permute-start | bytes 786440 | tf_op jit(solution)/shard_map/ppermute | solution.py:40
  45.6 5.8 %collective-permute-start.7 = (f32[256,256]{1,0:T(8,128)S(1)}, f32[256,256]{1,0:T(8,128)S(1)}, u32[]{:S(2)}, u32[]{:S(2)}) collective-permute-start(f32[256,256]{1,0:T(8,128)S(1)} %get-tuple-element.2), channel_id=1, source_target_pairs={{0,62},{1,63},{2,0},{3,1},{4,2},{5,3},{6,4},{7,5},{8,6},{9,7},{10,... | collective-permute-start | bytes 786440 | tf_op jit(solution)/shard_map/ppermute | solution.py:22
  51.4 2.0 %collective-permute-start.5 = (f32[256,256]{1,0:T(8,128)S(1)}, f32[256,256]{1,0:T(8,128)S(1)}, u32[]{:S(2)}, u32[]{:S(2)}) collective-permute-start(f32[256,256]{1,0:T(8,128)S(1)} %get-tuple-element.2), channel_id=1, source_target_pairs={{0,63},{1,2},{2,1},{3,4},{4,3},{5,6},{6,5},{7,8},{8,7},{9,10},{10,... | collective-permute-start | bytes 786440 | tf_op jit(solution)/shard_map/ppermute | solution.py:42
  53.4 0.4 fusion.46
  53.8 0.0 collective-permute-done.6
  53.8 0.4 fusion.30
  54.2 3.4 %collective-permute-done.7 = f32[256,256]{1,0:T(8,128)S(1)} collective-permute-done((f32[256,256]{1,0:T(8,128)S(1)}, f32[256,256]{1,0:T(8,128)S(1)}, u32[]{:S(2)}, u32[]{:S(2)}) %collective-permute-start.7) | collective-permute-done | bytes 262176 | tf_op jit(solution)/shard_map/ppermute | solution.py:22
  57.6 0.4 fusion.22
  57.9 0.0 collective-permute-done.4
  58.0 0.4 convolution_add_fusion.5
  58.3 2.8 %collective-permute-done.5 = f32[256,256]{1,0:T(8,128)S(1)} collective-permute-done((f32[256,256]{1,0:T(8,128)S(1)}, f32[256,256]{1,0:T(8,128)S(1)}, u32[]{:S(2)}, u32[]{:S(2)}) %collective-permute-start.5) | collective-permute-done | bytes 262176 | tf_op jit(solution)/shard_map/ppermute | solution.py:42
  61.2 0.4 fusion.13
  61.6 1.9 %collective-permute-start.10 = (f32[256,256]{1,0:T(8,128)S(1)}, f32[256,256]{1,0:T(8,128)S(1)}, u32[]{:S(2)}, u32[]{:S(2)}) collective-permute-start(f32[256,256]{1,0:T(8,128)S(1)} %fusion.13), channel_id=1, source_target_pairs={{0,2},{1,3},{2,4},{3,5},{4,6},{5,7},{6,8},{7,9},{8,10},{9,11},{10,... | collective-permute-start | bytes 786440 | tf_op jit(solution)/shard_map/ppermute | solution.py:22
  63.5 6.0 %collective-permute-start.11 = (f32[256,256]{1,0:T(8,128)S(1)}, f32[256,256]{1,0:T(8,128)S(1)}, u32[]{:S(2)}, u32[]{:S(2)}) collective-permute-start(f32[256,256]{1,0:T(8,128)S(1)} %fusion.13), channel_id=1, source_target_pairs={{0,62},{1,63},{2,0},{3,1},{4,2},{5,3},{6,4},{7,5},{8,6},{9,7},{10,... | collective-permute-start | bytes 786440 | tf_op jit(solution)/shard_map/ppermute | solution.py:22
  69.5 0.4 fusion.44
  69.9 1.9 %collective-permute-start.8 = (f32[256,256]{1,0:T(8,128)S(1)}, f32[256,256]{1,0:T(8,128)S(1)}, u32[]{:S(2)}, u32[]{:S(2)}) collective-permute-start(f32[256,256]{1,0:T(8,128)S(1)} %fusion.13), channel_id=1, source_target_pairs={{0,1},{1,0},{2,3},{3,2},{4,5},{5,4},{6,7},{7,6},{8,9},{9,8},{10,11... | collective-permute-start | bytes 786440 | tf_op jit(solution)/shard_map/ppermute | solution.py:40
  71.9 2.5 %collective-permute-start.9 = (f32[256,256]{1,0:T(8,128)S(1)}, f32[256,256]{1,0:T(8,128)S(1)}, u32[]{:S(2)}, u32[]{:S(2)}) collective-permute-start(f32[256,256]{1,0:T(8,128)S(1)} %fusion.13), channel_id=1, source_target_pairs={{0,63},{1,2},{2,1},{3,4},{4,3},{5,6},{6,5},{7,8},{8,7},{9,10},{10,... | collective-permute-start | bytes 786440 | tf_op jit(solution)/shard_map/ppermute | solution.py:42
  74.3 0.4 fusion.28
  74.7 0.0 collective-permute-done.11
  74.7 0.4 fusion.20
  75.1 0.0 collective-permute-done.8
  75.1 0.4 convolution_add_fusion.3
  75.5 6.1 %collective-permute-done.9 = f32[256,256]{1,0:T(8,128)S(1)} collective-permute-done((f32[256,256]{1,0:T(8,128)S(1)}, f32[256,256]{1,0:T(8,128)S(1)}, u32[]{:S(2)}, u32[]{:S(2)}) %collective-permute-start.9) | collective-permute-done | bytes 262176 | tf_op jit(solution)/shard_map/ppermute | solution.py:42
  81.7 0.4 fusion.16
  82.1 1.9 %collective-permute-start.14 = (f32[256,256]{1,0:T(8,128)S(1)}, f32[256,256]{1,0:T(8,128)S(1)}, u32[]{:S(2)}, u32[]{:S(2)}) collective-permute-start(f32[256,256]{1,0:T(8,128)S(1)} %fusion.16), channel_id=1, source_target_pairs={{0,2},{1,3},{2,4},{3,5},{4,6},{5,7},{6,8},{7,9},{8,10},{9,11},{10,... | collective-permute-start | bytes 786440 | tf_op jit(solution)/shard_map/ppermute | solution.py:22
  84.0 6.0 %collective-permute-start.15 = (f32[256,256]{1,0:T(8,128)S(1)}, f32[256,256]{1,0:T(8,128)S(1)}, u32[]{:S(2)}, u32[]{:S(2)}) collective-permute-start(f32[256,256]{1,0:T(8,128)S(1)} %fusion.16), channel_id=1, source_target_pairs={{0,62},{1,63},{2,0},{3,1},{4,2},{5,3},{6,4},{7,5},{8,6},{9,7},{10,... | collective-permute-start | bytes 786440 | tf_op jit(solution)/shard_map/ppermute | solution.py:22
  90.1 0.4 fusion.50
  90.4 1.9 %collective-permute-start.12 = (f32[256,256]{1,0:T(8,128)S(1)}, f32[256,256]{1,0:T(8,128)S(1)}, u32[]{:S(2)}, u32[]{:S(2)}) collective-permute-start(f32[256,256]{1,0:T(8,128)S(1)} %fusion.16), channel_id=1, source_target_pairs={{0,1},{1,0},{2,3},{3,2},{4,5},{5,4},{6,7},{7,6},{8,9},{9,8},{10,11... | collective-permute-start | bytes 786440 | tf_op jit(solution)/shard_map/ppermute | solution.py:40
  92.4 2.2 %collective-permute-start.13 = (f32[256,256]{1,0:T(8,128)S(1)}, f32[256,256]{1,0:T(8,128)S(1)}, u32[]{:S(2)}, u32[]{:S(2)}) collective-permute-start(f32[256,256]{1,0:T(8,128)S(1)} %fusion.16), channel_id=1, source_target_pairs={{0,63},{1,2},{2,1},{3,4},{4,3},{5,6},{6,5},{7,8},{8,7},{9,10},{10,... | collective-permute-start | bytes 786440 | tf_op jit(solution)/shard_map/ppermute | solution.py:42
  94.6 0.4 fusion.34
  95.0 0.4 fusion.26
  95.4 0.4 convolution_add_fusion.1
  95.8 6.4 %collective-permute-done.13 = f32[256,256]{1,0:T(8,128)S(1)} collective-permute-done((f32[256,256]{1,0:T(8,128)S(1)}, f32[256,256]{1,0:T(8,128)S(1)}, u32[]{:S(2)}, u32[]{:S(2)}) %collective-permute-start.13) | collective-permute-done | bytes 262176 | tf_op jit(solution)/shard_map/ppermute | solution.py:42
  102.2 0.4 fusion.19
  102.6 0.7 copy-done.1
  103.3 3.2 %fusion.63 = f32[256,2048]{1,0:T(8,128)} fusion(f32[256,256]{1,0:T(8,128)S(1)} %fusion.19, f32[256,2048]{1,0:T(8,128)S(1)} %copy-done), kind=kOutput, calls=%fused_computation.81 | convolution fusion | flops 1610612736 | bytes 4456448 | tf_op jit(solution)/shard_map/dot_general | solution.py:81
  106.6 0.0 reduce-scatter.2.cloned.1.call-update
  106.6 0.9 copy-done.2
  107.5 0.6 fusion.64
  108.1 0.1 reshape.12
  108.2 24.8 %all_to_all.5 = f32[64,4,256]{2,1,0:T(4,128)S(1)} all-to-all(f32[64,4,256]{2,1,0:T(4,128)S(1)} %reshape.12), channel_id=1, replica_groups=mesh['grp'=8,'wide'=64] {'wide'}, dimensions={0} | all-to-all | bytes 524288 | tf_op jit(solution)/shard_map/all_to_all | solution.py:79
  133.0 0.1 reduce_sum.9
  133.1 0.6 broadcast_multiply_fusion.1
  133.7 20.3 %reduce-scatter.2.cloned.1.call-done = f32[256,256]{1,0:T(8,128)} async-done(((f32[256,2048]{1,0:T(8,128)}), f32[256,256]{1,0:T(8,128)}) %reduce-scatter.2.cloned.1.call-update) | async-done | bytes 262160 | tf_op jit(solution)/shard_map/reduce_scatter | solution.py:84
  (8 shorter events, 0.0 us)
Async XLA Ops:
  7.2 96.1 %copy-start = (f32[256,2048]{1,0:T(8,128)S(1)}, f32[256,2048]{1,0:T(8,128)}, u32[]{:S(2)}) copy-start(f32[256,2048]{1,0:T(8,128)} %param.7) | copy-start | bytes 6291460
  7.2 146.8 %reduce-scatter.2.cloned.1.call-start = ((), (), s32[]{:S(2)}) async-start(), calls=%async_computation.2 | async-start | bytes 2359296 | tf_op jit(solution)/shard_map/reduce_scatter | solution.py:84
  7.2 31.5 %collective-permute-start = (f32[256,256]{1,0:T(8,128)}, f32[256,256]{1,0:T(8,128)}, u32[]{:S(2)}, u32[]{:S(2)}) collective-permute-start(f32[256,256]{1,0:T(8,128)} %param.4), channel_id=1, source_target_pairs={{0,1},{1,0},{2,3},{3,2},{4,5},{5,4},{6,7},{7,6},{8,9},{9,8},{10,11... | collective-permute-start | bytes 786440 | tf_op jit(solution)/shard_map/ppermute | solution.py:40
  9.3 26.7 %collective-permute-start.2 = (f32[256,256]{1,0:T(8,128)}, f32[256,256]{1,0:T(8,128)}, u32[]{:S(2)}, u32[]{:S(2)}) collective-permute-start(f32[256,256]{1,0:T(8,128)} %param.4), channel_id=1, source_target_pairs={{0,2},{1,3},{2,4},{3,5},{4,6},{5,7},{6,8},{7,9},{8,10},{9,11},{10,... | collective-permute-start | bytes 786440 | tf_op jit(solution)/shard_map/ppermute | solution.py:22
  13.6 23.8 %collective-permute-start.3 = (f32[256,256]{1,0:T(8,128)}, f32[256,256]{1,0:T(8,128)}, u32[]{:S(2)}, u32[]{:S(2)}) collective-permute-start(f32[256,256]{1,0:T(8,128)} %param.4), channel_id=1, source_target_pairs={{0,62},{1,63},{2,0},{3,1},{4,2},{5,3},{6,4},{7,5},{8,6},{9,7},{10,... | collective-permute-start | bytes 786440 | tf_op jit(solution)/shard_map/ppermute | solution.py:22
  22.4 17.6 %collective-permute-start.1 = (f32[256,256]{1,0:T(8,128)}, f32[256,256]{1,0:T(8,128)}, u32[]{:S(2)}, u32[]{:S(2)}) collective-permute-start(f32[256,256]{1,0:T(8,128)} %param.4), channel_id=1, source_target_pairs={{0,63},{1,2},{2,1},{3,4},{4,3},{5,6},{6,5},{7,8},{8,7},{9,10},{10,... | collective-permute-start | bytes 786440 | tf_op jit(solution)/shard_map/ppermute | solution.py:42
  36.0 4.1 %copy-start.3 = (f32[256,256]{1,0:T(8,128)S(1)}, f32[256,256]{1,0:T(8,128)}, u32[]{:S(2)}) copy-start(f32[256,256]{1,0:T(8,128)} %param.4) | copy-start | bytes 786436
  41.5 12.3 %collective-permute-start.6 = (f32[256,256]{1,0:T(8,128)S(1)}, f32[256,256]{1,0:T(8,128)S(1)}, u32[]{:S(2)}, u32[]{:S(2)}) collective-permute-start(f32[256,256]{1,0:T(8,128)S(1)} %get-tuple-element.2), channel_id=1, source_target_pairs={{0,2},{1,3},{2,4},{3,5},{4,6},{5,7},{6,8},{7,9},{8,10},{9,11},{10,... | collective-permute-start | bytes 786440 | tf_op jit(solution)/shard_map/ppermute | solution.py:22
  43.7 14.3 %collective-permute-start.4 = (f32[256,256]{1,0:T(8,128)S(1)}, f32[256,256]{1,0:T(8,128)S(1)}, u32[]{:S(2)}, u32[]{:S(2)}) collective-permute-start(f32[256,256]{1,0:T(8,128)S(1)} %get-tuple-element.2), channel_id=1, source_target_pairs={{0,1},{1,0},{2,3},{3,2},{4,5},{5,4},{6,7},{7,6},{8,9},{9,8},{10,11... | collective-permute-start | bytes 786440 | tf_op jit(solution)/shard_map/ppermute | solution.py:40
  45.6 12.0 %collective-permute-start.7 = (f32[256,256]{1,0:T(8,128)S(1)}, f32[256,256]{1,0:T(8,128)S(1)}, u32[]{:S(2)}, u32[]{:S(2)}) collective-permute-start(f32[256,256]{1,0:T(8,128)S(1)} %get-tuple-element.2), channel_id=1, source_target_pairs={{0,62},{1,63},{2,0},{3,1},{4,2},{5,3},{6,4},{7,5},{8,6},{9,7},{10,... | collective-permute-start | bytes 786440 | tf_op jit(solution)/shard_map/ppermute | solution.py:22
  51.4 9.8 %collective-permute-start.5 = (f32[256,256]{1,0:T(8,128)S(1)}, f32[256,256]{1,0:T(8,128)S(1)}, u32[]{:S(2)}, u32[]{:S(2)}) collective-permute-start(f32[256,256]{1,0:T(8,128)S(1)} %get-tuple-element.2), channel_id=1, source_target_pairs={{0,63},{1,2},{2,1},{3,4},{4,3},{5,6},{6,5},{7,8},{8,7},{9,10},{10,... | collective-permute-start | bytes 786440 | tf_op jit(solution)/shard_map/ppermute | solution.py:42
  61.6 12.8 %collective-permute-start.10 = (f32[256,256]{1,0:T(8,128)S(1)}, f32[256,256]{1,0:T(8,128)S(1)}, u32[]{:S(2)}, u32[]{:S(2)}) collective-permute-start(f32[256,256]{1,0:T(8,128)S(1)} %fusion.13), channel_id=1, source_target_pairs={{0,2},{1,3},{2,4},{3,5},{4,6},{5,7},{6,8},{7,9},{8,10},{9,11},{10,... | collective-permute-start | bytes 786440 | tf_op jit(solution)/shard_map/ppermute | solution.py:22
  63.5 11.2 %collective-permute-start.11 = (f32[256,256]{1,0:T(8,128)S(1)}, f32[256,256]{1,0:T(8,128)S(1)}, u32[]{:S(2)}, u32[]{:S(2)}) collective-permute-start(f32[256,256]{1,0:T(8,128)S(1)} %fusion.13), channel_id=1, source_target_pairs={{0,62},{1,63},{2,0},{3,1},{4,2},{5,3},{6,4},{7,5},{8,6},{9,7},{10,... | collective-permute-start | bytes 786440 | tf_op jit(solution)/shard_map/ppermute | solution.py:22
  69.9 5.2 %collective-permute-start.8 = (f32[256,256]{1,0:T(8,128)S(1)}, f32[256,256]{1,0:T(8,128)S(1)}, u32[]{:S(2)}, u32[]{:S(2)}) collective-permute-start(f32[256,256]{1,0:T(8,128)S(1)} %fusion.13), channel_id=1, source_target_pairs={{0,1},{1,0},{2,3},{3,2},{4,5},{5,4},{6,7},{7,6},{8,9},{9,8},{10,11... | collective-permute-start | bytes 786440 | tf_op jit(solution)/shard_map/ppermute | solution.py:40
  71.9 9.8 %collective-permute-start.9 = (f32[256,256]{1,0:T(8,128)S(1)}, f32[256,256]{1,0:T(8,128)S(1)}, u32[]{:S(2)}, u32[]{:S(2)}) collective-permute-start(f32[256,256]{1,0:T(8,128)S(1)} %fusion.13), channel_id=1, source_target_pairs={{0,63},{1,2},{2,1},{3,4},{4,3},{5,6},{6,5},{7,8},{8,7},{9,10},{10,... | collective-permute-start | bytes 786440 | tf_op jit(solution)/shard_map/ppermute | solution.py:42
  82.1 12.5 %collective-permute-start.14 = (f32[256,256]{1,0:T(8,128)S(1)}, f32[256,256]{1,0:T(8,128)S(1)}, u32[]{:S(2)}, u32[]{:S(2)}) collective-permute-start(f32[256,256]{1,0:T(8,128)S(1)} %fusion.16), channel_id=1, source_target_pairs={{0,2},{1,3},{2,4},{3,5},{4,6},{5,7},{6,8},{7,9},{8,10},{9,11},{10,... | collective-permute-start | bytes 786440 | tf_op jit(solution)/shard_map/ppermute | solution.py:22
  84.0 11.0 %collective-permute-start.15 = (f32[256,256]{1,0:T(8,128)S(1)}, f32[256,256]{1,0:T(8,128)S(1)}, u32[]{:S(2)}, u32[]{:S(2)}) collective-permute-start(f32[256,256]{1,0:T(8,128)S(1)} %fusion.16), channel_id=1, source_target_pairs={{0,62},{1,63},{2,0},{3,1},{4,2},{5,3},{6,4},{7,5},{8,6},{9,7},{10,... | collective-permute-start | bytes 786440 | tf_op jit(solution)/shard_map/ppermute | solution.py:22
  90.4 4.9 %collective-permute-start.12 = (f32[256,256]{1,0:T(8,128)S(1)}, f32[256,256]{1,0:T(8,128)S(1)}, u32[]{:S(2)}, u32[]{:S(2)}) collective-permute-start(f32[256,256]{1,0:T(8,128)S(1)} %fusion.16), channel_id=1, source_target_pairs={{0,1},{1,0},{2,3},{3,2},{4,5},{5,4},{6,7},{7,6},{8,9},{9,8},{10,11... | collective-permute-start | bytes 786440 | tf_op jit(solution)/shard_map/ppermute | solution.py:40
  92.4 9.8 %collective-permute-start.13 = (f32[256,256]{1,0:T(8,128)S(1)}, f32[256,256]{1,0:T(8,128)S(1)}, u32[]{:S(2)}, u32[]{:S(2)}) collective-permute-start(f32[256,256]{1,0:T(8,128)S(1)} %fusion.16), channel_id=1, source_target_pairs={{0,63},{1,2},{2,1},{3,4},{4,3},{5,6},{6,5},{7,8},{8,7},{9,10},{10,... | collective-permute-start | bytes 786440 | tf_op jit(solution)/shard_map/ppermute | solution.py:42
  102.6 0.7 copy-start.1
  106.6 0.9 copy-start.2
Sparse Core Ops, SparseCore 0:
  106.7 47.1 reduce-scatter.1

commit v15 on v14

--- a/solution.py
+++ b/solution.py
@@ -35,12 +35,14 @@
     count = lax.axis_size("wide")
     swap_pairs = [(i, i ^ 1) for i in range(count)]
     cross_pairs = [(i, (i - 1) % count if i % 2 == 0 else (i + 1) % count) for i in range(count)]
+    near_pairs = [(i, (i + 2) % count if (i // 2) % 2 == 0 else (i - 2) % count) for i in range(count)]
+    wrap_pairs = [(i, (i - 2) % count if (i // 2) % 2 == 0 else (i + 2) % count) for i in range(count)]
     pieces = [
-        passed_along(field, "wide", 2),
+        lax.ppermute(field, "wide", near_pairs),
         lax.ppermute(field, "wide", swap_pairs),
         field,
         lax.ppermute(field, "wide", cross_pairs),
-        passed_along(field, "wide", -2),
+        lax.ppermute(field, "wide", wrap_pairs),
     ]
     total = None
     for idx in (2, 1, 3, 0, 4):
@@ -56,6 +58,7 @@
     owner = pattern // A_DEV
     relative = (owner - myself + HW + devcount) % devcount
     relative = jnp.where(myself % 2 == 0, jnp.where(relative == 1, 3, jnp.where(relative == 3, 1, relative)), relative)
+    relative = jnp.where((myself // 2) % 2 == 0, jnp.where(relative == 0, 4, jnp.where(relative == 4, 0, relative)), relative)
     slot_index = relative * A_DEV + pattern % A_DEV
     hdense = dense_hamiltonian(hblocks, slot_index)
     previous = subspace

time: 162 us -> 158 us (0.975)
  waiting for transfers between devices: 39.1 us -> 36.6 us
    ppermute x8, starting transfers between devices: 37 us -> 31.4 us  [the longest x4 19.9 us: apply_ham(): lax.ppermute(field, 'wide', wrap_pairs)]
    ppermute x4, waiting for transfers between devices: 15.3 us -> 10.5 us  [apply_ham(): lax.ppermute(field, 'wide', cross_pairs)]
    ppermute x4, starting transfers between devices: 10.2 us -> 13.2 us  [apply_ham(): lax.ppermute(field, 'wide', cross_pairs)]
    ppermute x4, starting transfers between devices: 7.82 us -> 10.1 us  [apply_ham(): lax.ppermute(field, 'wide', swap_pairs)]
  transfers between devices with their start and end apart: 17 -> 17, of which waited for: 5 -> 6; matrix products, arithmetic and copies ran while one was open for 12% -> 13% of each run, Pallas kernels for 0% -> 0%
where the time goes in v15:
time: 158 us; the launch traced here: 157 us
  starting transfers between devices  54.8 us (35%)
  waiting for transfers between devices  36.6 us (23%)
  blocking collectives  23.5 us (15%)
  matrix products  22.1 us (14%)
  between operations  14.5 us (9%)
  local copies, waits for them, and re-layouts  3.95 us (2%)
    all_to_all x1, blocking collectives, local(): gathered = lax.all_to_all(pieces, 'wide', 0, 0, tiled=True)  23.5 us
    reduce_scatter x1, waiting for transfers between devices, local(): rotated = lax.psum_scatter(rot_term, 'grp', scatter_dimension=1, tiled=True)  21.3 us
    ppermute x4, starting transfers between devices, apply_ham(): lax.ppermute(field, 'wide', wrap_pairs)  19.9 us
    ppermute x4, starting transfers between devices, apply_ham(): lax.ppermute(field, 'wide', cross_pairs)  13.2 us
    dot_general x20, matrix products, apply_ham(): jnp.dot(hdense[:, idx * rows:(idx + 1) * rows], pieces[idx], precision=HI...  12.5 us
    ppermute x4, starting transfers between devices, apply_ham(): lax.ppermute(field, 'wide', near_pairs)  11.6 us
    ppermute x4, waiting for transfers between devices, apply_ham(): lax.ppermute(field, 'wide', cross_pairs)  10.5 us
    ppermute x4, starting transfers between devices, apply_ham(): lax.ppermute(field, 'wide', swap_pairs)  10.1 us
  transfers between devices with their start and end apart: 17, of which 6 were waited for; matrix products, arithmetic and copies ran while one was open for 13% of the time, Pallas kernels for 0%

profile of v15, /device:TPU:6, one launch (start us, length us, event | category | flops | bytes accessed | tf_op | source)
XLA Modules:
  0.0 156.8 jit_solution(18224244027056247389)
XLA Ops:
  7.2 0.0 copy-start
  7.2 0.0 reduce-scatter.2.cloned.1.call-start
  7.2 2.1 %collective-permute-start = (f32[256,256]{1,0:T(8,128)}, f32[256,256]{1,0:T(8,128)}, u32[]{:S(2)}, u32[]{:S(2)}) collective-permute-start(f32[256,256]{1,0:T(8,128)} %param.4), channel_id=1, source_target_pairs={{0,1},{1,0},{2,3},{3,2},{4,5},{5,4},{6,7},{7,6},{8,9},{9,8},{10,11... | collective-permute-start | bytes 786440 | tf_op jit(solution)/shard_map/ppermute | solution.py:42
  9.3 4.3 %collective-permute-start.2 = (f32[256,256]{1,0:T(8,128)}, f32[256,256]{1,0:T(8,128)}, u32[]{:S(2)}, u32[]{:S(2)}) collective-permute-start(f32[256,256]{1,0:T(8,128)} %param.4), channel_id=1, source_target_pairs={{0,2},{1,3},{2,0},{3,1},{4,6},{5,7},{6,4},{7,5},{8,10},{9,11},{10,... | collective-permute-start | bytes 786440 | tf_op jit(solution)/shard_map/ppermute | solution.py:41
  13.6 9.4 %collective-permute-start.3 = (f32[256,256]{1,0:T(8,128)}, f32[256,256]{1,0:T(8,128)}, u32[]{:S(2)}, u32[]{:S(2)}) collective-permute-start(f32[256,256]{1,0:T(8,128)} %param.4), channel_id=1, source_target_pairs={{0,62},{1,63},{2,4},{3,5},{4,2},{5,3},{6,8},{7,9},{8,6},{9,7},{10,... | collective-permute-start | bytes 786440 | tf_op jit(solution)/shard_map/ppermute | solution.py:45
  23.0 1.9 %collective-permute-start.1 = (f32[256,256]{1,0:T(8,128)}, f32[256,256]{1,0:T(8,128)}, u32[]{:S(2)}, u32[]{:S(2)}) collective-permute-start(f32[256,256]{1,0:T(8,128)} %param.4), channel_id=1, source_target_pairs={{0,63},{1,2},{2,1},{3,4},{4,3},{5,6},{6,5},{7,8},{8,7},{9,10},{10,... | collective-permute-start | bytes 786440 | tf_op jit(solution)/shard_map/ppermute | solution.py:44
  25.0 0.7 fusion.58
  25.7 5.8 %fusion.2 = f32[4,64,20,64]{3,2,1,0:T(8,128)} fusion(f32[4,16,64,64]{3,2,1,0:T(8,128)} %param.5, s32[4,16]{1,0:T(4,128)S(1)} %fusion.58), kind=kOutput, calls=%fused_computation.2 | convolution fusion | flops 62915840 | bytes 2359552 | tf_op jit(solution)/shard_map/asp,asij->aipj/dot_general | solution.py:29
  31.4 2.2 %reshape.14 = f32[256,1280]{1,0:T(8,128)S(1)} reshape(f32[4,64,20,64]{3,2,1,0:T(8,128)} %fusion.2) | data formatting | bytes 2621440 | tf_op jit(solution)/shard_map/reshape | solution.py:30
  33.7 1.3 fusion.48
  35.0 0.0 copy-start.3
  35.0 0.0 collective-permute-done.2
  35.0 1.4 fusion.32
  36.4 0.0 collective-permute-done.3
  36.4 1.3 fusion.24
  37.8 1.3 convolution_add_fusion.7
  39.1 1.4 broadcast_multiply_fusion
  40.5 3.5 %collective-permute-start.6 = (f32[256,256]{1,0:T(8,128)S(1)}, f32[256,256]{1,0:T(8,128)S(1)}, u32[]{:S(2)}, u32[]{:S(2)}) collective-permute-start(f32[256,256]{1,0:T(8,128)S(1)} %get-tuple-element.2), channel_id=1, source_target_pairs={{0,2},{1,3},{2,0},{3,1},{4,6},{5,7},{6,4},{7,5},{8,10},{9,11},{10,... | collective-permute-start | bytes 786440 | tf_op jit(solution)/shard_map/ppermute | solution.py:41
  43.9 1.9 %collective-permute-start.4 = (f32[256,256]{1,0:T(8,128)S(1)}, f32[256,256]{1,0:T(8,128)S(1)}, u32[]{:S(2)}, u32[]{:S(2)}) collective-permute-start(f32[256,256]{1,0:T(8,128)S(1)} %get-tuple-element.2), channel_id=1, source_target_pairs={{0,1},{1,0},{2,3},{3,2},{4,5},{5,4},{6,7},{7,6},{8,9},{9,8},{10,11... | collective-permute-start | bytes 786440 | tf_op jit(solution)/shard_map/ppermute | solution.py:42
  45.9 4.6 %collective-permute-start.7 = (f32[256,256]{1,0:T(8,128)S(1)}, f32[256,256]{1,0:T(8,128)S(1)}, u32[]{:S(2)}, u32[]{:S(2)}) collective-permute-start(f32[256,256]{1,0:T(8,128)S(1)} %get-tuple-element.2), channel_id=1, source_target_pairs={{0,62},{1,63},{2,4},{3,5},{4,2},{5,3},{6,8},{7,9},{8,6},{9,7},{10,... | collective-permute-start | bytes 786440 | tf_op jit(solution)/shard_map/ppermute | solution.py:45
  50.5 3.2 %collective-permute-start.5 = (f32[256,256]{1,0:T(8,128)S(1)}, f32[256,256]{1,0:T(8,128)S(1)}, u32[]{:S(2)}, u32[]{:S(2)}) collective-permute-start(f32[256,256]{1,0:T(8,128)S(1)} %get-tuple-element.2), channel_id=1, source_target_pairs={{0,63},{1,2},{2,1},{3,4},{4,3},{5,6},{6,5},{7,8},{8,7},{9,10},{10,... | collective-permute-start | bytes 786440 | tf_op jit(solution)/shard_map/ppermute | solution.py:44
  53.7 0.4 fusion.46
  54.1 0.0 collective-permute-done.6
  54.1 0.4 fusion.30
  54.5 4.5 %collective-permute-done.7 = f32[256,256]{1,0:T(8,128)S(1)} collective-permute-done((f32[256,256]{1,0:T(8,128)S(1)}, f32[256,256]{1,0:T(8,128)S(1)}, u32[]{:S(2)}, u32[]{:S(2)}) %collective-permute-start.7) | collective-permute-done | bytes 262176 | tf_op jit(solution)/shard_map/ppermute | solution.py:45
  59.0 0.4 fusion.22
  59.4 0.0 collective-permute-done.4
  59.4 0.4 convolution_add_fusion.5
  59.8 1.6 %collective-permute-done.5 = f32[256,256]{1,0:T(8,128)S(1)} collective-permute-done((f32[256,256]{1,0:T(8,128)S(1)}, f32[256,256]{1,0:T(8,128)S(1)}, u32[]{:S(2)}, u32[]{:S(2)}) %collective-permute-start.5) | collective-permute-done | bytes 262176 | tf_op jit(solution)/shard_map/ppermute | solution.py:44
  61.4 0.4 fusion.13
  61.8 1.9 %collective-permute-start.10 = (f32[256,256]{1,0:T(8,128)S(1)}, f32[256,256]{1,0:T(8,128)S(1)}, u32[]{:S(2)}, u32[]{:S(2)}) collective-permute-start(f32[256,256]{1,0:T(8,128)S(1)} %fusion.13), channel_id=1, source_target_pairs={{0,2},{1,3},{2,0},{3,1},{4,6},{5,7},{6,4},{7,5},{8,10},{9,11},{10,... | collective-permute-start | bytes 786440 | tf_op jit(solution)/shard_map/ppermute | solution.py:41
  63.7 3.7 %collective-permute-start.11 = (f32[256,256]{1,0:T(8,128)S(1)}, f32[256,256]{1,0:T(8,128)S(1)}, u32[]{:S(2)}, u32[]{:S(2)}) collective-permute-start(f32[256,256]{1,0:T(8,128)S(1)} %fusion.13), channel_id=1, source_target_pairs={{0,62},{1,63},{2,4},{3,5},{4,2},{5,3},{6,8},{7,9},{8,6},{9,7},{10,... | collective-permute-start | bytes 786440 | tf_op jit(solution)/shard_map/ppermute | solution.py:45
  67.5 0.4 fusion.44
  67.9 1.9 %collective-permute-start.8 = (f32[256,256]{1,0:T(8,128)S(1)}, f32[256,256]{1,0:T(8,128)S(1)}, u32[]{:S(2)}, u32[]{:S(2)}) collective-permute-start(f32[256,256]{1,0:T(8,128)S(1)} %fusion.13), channel_id=1, source_target_pairs={{0,1},{1,0},{2,3},{3,2},{4,5},{5,4},{6,7},{7,6},{8,9},{9,8},{10,11... | collective-permute-start | bytes 786440 | tf_op jit(solution)/shard_map/ppermute | solution.py:42
  69.8 4.3 %collective-permute-start.9 = (f32[256,256]{1,0:T(8,128)S(1)}, f32[256,256]{1,0:T(8,128)S(1)}, u32[]{:S(2)}, u32[]{:S(2)}) collective-permute-start(f32[256,256]{1,0:T(8,128)S(1)} %fusion.13), channel_id=1, source_target_pairs={{0,63},{1,2},{2,1},{3,4},{4,3},{5,6},{6,5},{7,8},{8,7},{9,10},{10,... | collective-permute-start | bytes 786440 | tf_op jit(solution)/shard_map/ppermute | solution.py:44
  74.1 0.4 fusion.28
  74.5 0.0 collective-permute-done.11
  74.5 0.4 fusion.20
  74.9 0.0 collective-permute-done.8
  74.9 0.4 convolution_add_fusion.3
  75.3 4.3 %collective-permute-done.9 = f32[256,256]{1,0:T(8,128)S(1)} collective-permute-done((f32[256,256]{1,0:T(8,128)S(1)}, f32[256,256]{1,0:T(8,128)S(1)}, u32[]{:S(2)}, u32[]{:S(2)}) %collective-permute-start.9) | collective-permute-done | bytes 262176 | tf_op jit(solution)/shard_map/ppermute | solution.py:44
  79.6 0.4 fusion.16
  80.0 1.9 %collective-permute-start.14 = (f32[256,256]{1,0:T(8,128)S(1)}, f32[256,256]{1,0:T(8,128)S(1)}, u32[]{:S(2)}, u32[]{:S(2)}) collective-permute-start(f32[256,256]{1,0:T(8,128)S(1)} %fusion.16), channel_id=1, source_target_pairs={{0,2},{1,3},{2,0},{3,1},{4,6},{5,7},{6,4},{7,5},{8,10},{9,11},{10,... | collective-permute-start | bytes 786440 | tf_op jit(solution)/shard_map/ppermute | solution.py:41
  81.9 2.2 %collective-permute-start.15 = (f32[256,256]{1,0:T(8,128)S(1)}, f32[256,256]{1,0:T(8,128)S(1)}, u32[]{:S(2)}, u32[]{:S(2)}) collective-permute-start(f32[256,256]{1,0:T(8,128)S(1)} %fusion.16), channel_id=1, source_target_pairs={{0,62},{1,63},{2,4},{3,5},{4,2},{5,3},{6,8},{7,9},{8,6},{9,7},{10,... | collective-permute-start | bytes 786440 | tf_op jit(solution)/shard_map/ppermute | solution.py:45
  84.1 0.4 fusion.50
  84.5 4.2 %collective-permute-start.12 = (f32[256,256]{1,0:T(8,128)S(1)}, f32[256,256]{1,0:T(8,128)S(1)}, u32[]{:S(2)}, u32[]{:S(2)}) collective-permute-start(f32[256,256]{1,0:T(8,128)S(1)} %fusion.16), channel_id=1, source_target_pairs={{0,1},{1,0},{2,3},{3,2},{4,5},{5,4},{6,7},{7,6},{8,9},{9,8},{10,11... | collective-permute-start | bytes 786440 | tf_op jit(solution)/shard_map/ppermute | solution.py:42
  88.7 3.8 %collective-permute-start.13 = (f32[256,256]{1,0:T(8,128)S(1)}, f32[256,256]{1,0:T(8,128)S(1)}, u32[]{:S(2)}, u32[]{:S(2)}) collective-permute-start(f32[256,256]{1,0:T(8,128)S(1)} %fusion.16), channel_id=1, source_target_pairs={{0,63},{1,2},{2,1},{3,4},{4,3},{5,6},{6,5},{7,8},{8,7},{9,10},{10,... | collective-permute-start | bytes 786440 | tf_op jit(solution)/shard_map/ppermute | solution.py:44
  92.5 0.4 fusion.34
  92.9 0.2 collective-permute-done.15
  93.1 0.4 fusion.26
  93.5 0.0 collective-permute-done.12
  93.5 0.4 convolution_add_fusion.1
  93.9 4.6 %collective-permute-done.13 = f32[256,256]{1,0:T(8,128)S(1)} collective-permute-done((f32[256,256]{1,0:T(8,128)S(1)}, f32[256,256]{1,0:T(8,128)S(1)}, u32[]{:S(2)}, u32[]{:S(2)}) %collective-permute-start.13) | collective-permute-done | bytes 262176 | tf_op jit(solution)/shard_map/ppermute | solution.py:44
  98.5 0.4 fusion.19
  98.9 0.7 copy-done.1
  99.6 3.2 %fusion.65 = f32[256,2048]{1,0:T(8,128)} fusion(f32[256,256]{1,0:T(8,128)S(1)} %fusion.19, f32[256,2048]{1,0:T(8,128)S(1)} %copy-done), kind=kOutput, calls=%fused_computation.84 | convolution fusion | flops 1610612736 | bytes 4456448 | tf_op jit(solution)/shard_map/dot_general | solution.py:84
  102.9 0.0 reduce-scatter.2.cloned.1.call-update
  102.9 0.9 copy-done.2
  103.8 0.6 fusion.66
  104.4 0.1 reshape.12
  104.5 23.5 %all_to_all.5 = f32[64,4,256]{2,1,0:T(4,128)S(1)} all-to-all(f32[64,4,256]{2,1,0:T(4,128)S(1)} %reshape.12), channel_id=1, replica_groups=mesh['grp'=8,'wide'=64] {'wide'}, dimensions={0} | all-to-all | bytes 524288 | tf_op jit(solution)/shard_map/all_to_all | solution.py:82
  128.0 0.1 reduce_sum.9
  128.1 0.6 broadcast_multiply_fusion.1
  128.7 21.3 %reduce-scatter.2.cloned.1.call-done = f32[256,256]{1,0:T(8,128)} async-done(((f32[256,2048]{1,0:T(8,128)}), f32[256,256]{1,0:T(8,128)}) %reduce-scatter.2.cloned.1.call-update) | async-done | bytes 262160 | tf_op jit(solution)/shard_map/reduce_scatter | solution.py:87
  (8 shorter events, 0.0 us)
Async XLA Ops:
  7.2 92.5 %copy-start = (f32[256,2048]{1,0:T(8,128)S(1)}, f32[256,2048]{1,0:T(8,128)}, u32[]{:S(2)}) copy-start(f32[256,2048]{1,0:T(8,128)} %param.7) | copy-start | bytes 6291460
  7.2 142.8 %reduce-scatter.2.cloned.1.call-start = ((), (), s32[]{:S(2)}) async-start(), calls=%async_computation.2 | async-start | bytes 2359296 | tf_op jit(solution)/shard_map/reduce_scatter | solution.py:87
  7.2 30.5 %collective-permute-start = (f32[256,256]{1,0:T(8,128)}, f32[256,256]{1,0:T(8,128)}, u32[]{:S(2)}, u32[]{:S(2)}) collective-permute-start(f32[256,256]{1,0:T(8,128)} %param.4), channel_id=1, source_target_pairs={{0,1},{1,0},{2,3},{3,2},{4,5},{5,4},{6,7},{7,6},{8,9},{9,8},{10,11... | collective-permute-start | bytes 786440 | tf_op jit(solution)/shard_map/ppermute | solution.py:42
  9.3 25.7 %collective-permute-start.2 = (f32[256,256]{1,0:T(8,128)}, f32[256,256]{1,0:T(8,128)}, u32[]{:S(2)}, u32[]{:S(2)}) collective-permute-start(f32[256,256]{1,0:T(8,128)} %param.4), channel_id=1, source_target_pairs={{0,2},{1,3},{2,0},{3,1},{4,6},{5,7},{6,4},{7,5},{8,10},{9,11},{10,... | collective-permute-start | bytes 786440 | tf_op jit(solution)/shard_map/ppermute | solution.py:41
  13.6 22.8 %collective-permute-start.3 = (f32[256,256]{1,0:T(8,128)}, f32[256,256]{1,0:T(8,128)}, u32[]{:S(2)}, u32[]{:S(2)}) collective-permute-start(f32[256,256]{1,0:T(8,128)} %param.4), channel_id=1, source_target_pairs={{0,62},{1,63},{2,4},{3,5},{4,2},{5,3},{6,8},{7,9},{8,6},{9,7},{10,... | collective-permute-start | bytes 786440 | tf_op jit(solution)/shard_map/ppermute | solution.py:45
  23.0 16.1 %collective-permute-start.1 = (f32[256,256]{1,0:T(8,128)}, f32[256,256]{1,0:T(8,128)}, u32[]{:S(2)}, u32[]{:S(2)}) collective-permute-start(f32[256,256]{1,0:T(8,128)} %param.4), channel_id=1, source_target_pairs={{0,63},{1,2},{2,1},{3,4},{4,3},{5,6},{6,5},{7,8},{8,7},{9,10},{10,... | collective-permute-start | bytes 786440 | tf_op jit(solution)/shard_map/ppermute | solution.py:44
  35.0 4.1 %copy-start.3 = (f32[256,256]{1,0:T(8,128)S(1)}, f32[256,256]{1,0:T(8,128)}, u32[]{:S(2)}) copy-start(f32[256,256]{1,0:T(8,128)} %param.4) | copy-start | bytes 786436
  40.5 13.6 %collective-permute-start.6 = (f32[256,256]{1,0:T(8,128)S(1)}, f32[256,256]{1,0:T(8,128)S(1)}, u32[]{:S(2)}, u32[]{:S(2)}) collective-permute-start(f32[256,256]{1,0:T(8,128)S(1)} %get-tuple-element.2), channel_id=1, source_target_pairs={{0,2},{1,3},{2,0},{3,1},{4,6},{5,7},{6,4},{7,5},{8,10},{9,11},{10,... | collective-permute-start | bytes 786440 | tf_op jit(solution)/shard_map/ppermute | solution.py:41
  43.9 15.4 %collective-permute-start.4 = (f32[256,256]{1,0:T(8,128)S(1)}, f32[256,256]{1,0:T(8,128)S(1)}, u32[]{:S(2)}, u32[]{:S(2)}) collective-permute-start(f32[256,256]{1,0:T(8,128)S(1)} %get-tuple-element.2), channel_id=1, source_target_pairs={{0,1},{1,0},{2,3},{3,2},{4,5},{5,4},{6,7},{7,6},{8,9},{9,8},{10,11... | collective-permute-start | bytes 786440 | tf_op jit(solution)/shard_map/ppermute | solution.py:42
  45.9 13.1 %collective-permute-start.7 = (f32[256,256]{1,0:T(8,128)S(1)}, f32[256,256]{1,0:T(8,128)S(1)}, u32[]{:S(2)}, u32[]{:S(2)}) collective-permute-start(f32[256,256]{1,0:T(8,128)S(1)} %get-tuple-element.2), channel_id=1, source_target_pairs={{0,62},{1,63},{2,4},{3,5},{4,2},{5,3},{6,8},{7,9},{8,6},{9,7},{10,... | collective-permute-start | bytes 786440 | tf_op jit(solution)/shard_map/ppermute | solution.py:45
  50.5 10.9 %collective-permute-start.5 = (f32[256,256]{1,0:T(8,128)S(1)}, f32[256,256]{1,0:T(8,128)S(1)}, u32[]{:S(2)}, u32[]{:S(2)}) collective-permute-start(f32[256,256]{1,0:T(8,128)S(1)} %get-tuple-element.2), channel_id=1, source_target_pairs={{0,63},{1,2},{2,1},{3,4},{4,3},{5,6},{6,5},{7,8},{8,7},{9,10},{10,... | collective-permute-start | bytes 786440 | tf_op jit(solution)/shard_map/ppermute | solution.py:44
  61.8 12.3 %collective-permute-start.10 = (f32[256,256]{1,0:T(8,128)S(1)}, f32[256,256]{1,0:T(8,128)S(1)}, u32[]{:S(2)}, u32[]{:S(2)}) collective-permute-start(f32[256,256]{1,0:T(8,128)S(1)} %fusion.13), channel_id=1, source_target_pairs={{0,2},{1,3},{2,0},{3,1},{4,6},{5,7},{6,4},{7,5},{8,10},{9,11},{10,... | collective-permute-start | bytes 786440 | tf_op jit(solution)/shard_map/ppermute | solution.py:41
  63.7 10.8 %collective-permute-start.11 = (f32[256,256]{1,0:T(8,128)S(1)}, f32[256,256]{1,0:T(8,128)S(1)}, u32[]{:S(2)}, u32[]{:S(2)}) collective-permute-start(f32[256,256]{1,0:T(8,128)S(1)} %fusion.13), channel_id=1, source_target_pairs={{0,62},{1,63},{2,4},{3,5},{4,2},{5,3},{6,8},{7,9},{8,6},{9,7},{10,... | collective-permute-start | bytes 786440 | tf_op jit(solution)/shard_map/ppermute | solution.py:45
  67.9 7.1 %collective-permute-start.8 = (f32[256,256]{1,0:T(8,128)S(1)}, f32[256,256]{1,0:T(8,128)S(1)}, u32[]{:S(2)}, u32[]{:S(2)}) collective-permute-start(f32[256,256]{1,0:T(8,128)S(1)} %fusion.13), channel_id=1, source_target_pairs={{0,1},{1,0},{2,3},{3,2},{4,5},{5,4},{6,7},{7,6},{8,9},{9,8},{10,11... | collective-permute-start | bytes 786440 | tf_op jit(solution)/shard_map/ppermute | solution.py:42
  69.8 9.8 %collective-permute-start.9 = (f32[256,256]{1,0:T(8,128)S(1)}, f32[256,256]{1,0:T(8,128)S(1)}, u32[]{:S(2)}, u32[]{:S(2)}) collective-permute-start(f32[256,256]{1,0:T(8,128)S(1)} %fusion.13), channel_id=1, source_target_pairs={{0,63},{1,2},{2,1},{3,4},{4,3},{5,6},{6,5},{7,8},{8,7},{9,10},{10,... | collective-permute-start | bytes 786440 | tf_op jit(solution)/shard_map/ppermute | solution.py:44
  80.0 12.5 %collective-permute-start.14 = (f32[256,256]{1,0:T(8,128)S(1)}, f32[256,256]{1,0:T(8,128)S(1)}, u32[]{:S(2)}, u32[]{:S(2)}) collective-permute-start(f32[256,256]{1,0:T(8,128)S(1)} %fusion.16), channel_id=1, source_target_pairs={{0,2},{1,3},{2,0},{3,1},{4,6},{5,7},{6,4},{7,5},{8,10},{9,11},{10,... | collective-permute-start | bytes 786440 | tf_op jit(solution)/shard_map/ppermute | solution.py:41
  81.9 11.2 %collective-permute-start.15 = (f32[256,256]{1,0:T(8,128)S(1)}, f32[256,256]{1,0:T(8,128)S(1)}, u32[]{:S(2)}, u32[]{:S(2)}) collective-permute-start(f32[256,256]{1,0:T(8,128)S(1)} %fusion.16), channel_id=1, source_target_pairs={{0,62},{1,63},{2,4},{3,5},{4,2},{5,3},{6,8},{7,9},{8,6},{9,7},{10,... | collective-permute-start | bytes 786440 | tf_op jit(solution)/shard_map/ppermute | solution.py:45
  84.5 9.0 %collective-permute-start.12 = (f32[256,256]{1,0:T(8,128)S(1)}, f32[256,256]{1,0:T(8,128)S(1)}, u32[]{:S(2)}, u32[]{:S(2)}) collective-permute-start(f32[256,256]{1,0:T(8,128)S(1)} %fusion.16), channel_id=1, source_target_pairs={{0,1},{1,0},{2,3},{3,2},{4,5},{5,4},{6,7},{7,6},{8,9},{9,8},{10,11... | collective-permute-start | bytes 786440 | tf_op jit(solution)/shard_map/ppermute | solution.py:42
  88.7 9.8 %collective-permute-start.13 = (f32[256,256]{1,0:T(8,128)S(1)}, f32[256,256]{1,0:T(8,128)S(1)}, u32[]{:S(2)}, u32[]{:S(2)}) collective-permute-start(f32[256,256]{1,0:T(8,128)S(1)} %fusion.16), channel_id=1, source_target_pairs={{0,63},{1,2},{2,1},{3,4},{4,3},{5,6},{6,5},{7,8},{8,7},{9,10},{10,... | collective-permute-start | bytes 786440 | tf_op jit(solution)/shard_map/ppermute | solution.py:44
  98.9 0.7 copy-start.1
  102.9 0.9 copy-start.2
Sparse Core Ops, SparseCore 0:
  103.0 46.9 reduce-scatter.1

commit v16 on v15

--- a/solution.py
+++ b/solution.py
@@ -61,6 +61,8 @@
     relative = jnp.where((myself // 2) % 2 == 0, jnp.where(relative == 0, 4, jnp.where(relative == 4, 0, relative)), relative)
     slot_index = relative * A_DEV + pattern % A_DEV
     hdense = dense_hamiltonian(hblocks, slot_index)
+    subspace, probe_h = lax.optimization_barrier((subspace, hdense[:8, :128]))
+    subspace = subspace + 0.0 * probe_h[0, 0]
     previous = subspace
     current = (apply_ham(subspace, hdense) - cheb_center * subspace) / cheb_half
     for step in range(DEGREE - 1):

time: 158 us -> 155 us (0.981)
  matrix products: 22.1 us -> 17.3 us
  waiting for transfers between devices: 36.6 us -> 34.7 us
    ppermute x4, waiting for transfers between devices: 10.5 us -> 5.18 us  [apply_ham(): lax.ppermute(field, 'wide', cross_pairs)]
    dot_general x20, matrix products: 12.5 us -> 7.72 us  [apply_ham(): jnp.dot(hdense[:, idx * rows:(idx + 1) * rows], pieces[idx], precision=HI...]
    ppermute x4, starting transfers between devices: 19.9 us -> 23.9 us  [apply_ham(): lax.ppermute(field, 'wide', wrap_pairs)]
    ppermute x4, starting transfers between devices: 10.1 us -> 13.2 us  [apply_ham(): lax.ppermute(field, 'wide', swap_pairs)]
    ppermute x4, starting transfers between devices: 13.2 us -> 10.2 us  [apply_ham(): lax.ppermute(field, 'wide', cross_pairs)]
    ppermute x4, starting transfers between devices: 11.6 us -> 8.7 us  [apply_ham(): lax.ppermute(field, 'wide', near_pairs)]
    ppermute x4, waiting for transfers between devices: 4.76 us -> 6.92 us  [apply_ham(): lax.ppermute(field, 'wide', wrap_pairs)]
  transfers between devices with their start and end apart: 17 -> 17, of which waited for: 6 -> 8; matrix products, arithmetic and copies ran while one was open for 13% -> 5% of each run, Pallas kernels for 0% -> 0%
where the time goes in v16:
time: 155 us; the launch traced here: 154 us
  starting transfers between devices  56 us (36%)
  waiting for transfers between devices  34.7 us (22%)
  blocking collectives  23.5 us (15%)
  matrix products  17.3 us (11%)
  between operations  15.1 us (10%)
  local copies, waits for them, and re-layouts  4.56 us (3%)
  other arithmetic  2.5 us (2%)
    ppermute x4, starting transfers between devices, apply_ham(): lax.ppermute(field, 'wide', wrap_pairs)  23.9 us
    all_to_all x1, blocking collectives, local(): gathered = lax.all_to_all(pieces, 'wide', 0, 0, tiled=True)  23.5 us
    reduce_scatter x1, waiting for transfers between devices, local(): rotated = lax.psum_scatter(rot_term, 'grp', scatter_dimension=1, tiled=True)  21.3 us
    ppermute x4, starting transfers between devices, apply_ham(): lax.ppermute(field, 'wide', swap_pairs)  13.2 us
    ppermute x4, starting transfers between devices, apply_ham(): lax.ppermute(field, 'wide', cross_pairs)  10.2 us
    ppermute x4, starting transfers between devices, apply_ham(): lax.ppermute(field, 'wide', near_pairs)  8.7 us
    dot_general x20, matrix products, apply_ham(): jnp.dot(hdense[:, idx * rows:(idx + 1) * rows], pieces[idx], precision=HI...  7.72 us
    ppermute x4, waiting for transfers between devices, apply_ham(): lax.ppermute(field, 'wide', wrap_pairs)  6.92 us
  transfers between devices with their start and end apart: 17, of which 8 were waited for; matrix products, arithmetic and copies ran while one was open for 5% of the time, Pallas kernels for 0%

profile of v16, /device:TPU:6, one launch (start us, length us, event | category | flops | bytes accessed | tf_op | source)
XLA Modules:
  0.0 153.8 jit_solution(17420887781242805619)
XLA Ops:
  7.2 0.0 copy-start
  7.2 0.0 reduce-scatter.2.cloned.1.call-start
  7.3 0.8 fusion.58
  8.1 5.8 %fusion.2 = f32[4,64,20,64]{3,2,1,0:T(8,128)} fusion(f32[4,16,64,64]{3,2,1,0:T(8,128)} %param.5, s32[4,16]{1,0:T(4,128)S(1)} %fusion.58), kind=kOutput, calls=%fused_computation.2 | convolution fusion | flops 62915840 | bytes 2359552 | tf_op jit(solution)/shard_map/asp,asij->aipj/dot_general | solution.py:29
  13.9 2.2 %reshape.16 = f32[256,1280]{1,0:T(8,128)S(1)} reshape(f32[4,64,20,64]{3,2,1,0:T(8,128)} %fusion.2) | data formatting | bytes 2621440 | tf_op jit(solution)/shard_map/reshape | solution.py:30
  16.1 0.1 copy.12
  16.2 0.5 slice.16
  17.4 1.0 broadcast_add_fusion
  18.4 11.2 %collective-permute-start.3 = (f32[256,256]{1,0:T(8,128)S(1)}, f32[256,256]{1,0:T(8,128)S(1)}, u32[]{:S(2)}, u32[]{:S(2)}) collective-permute-start(f32[256,256]{1,0:T(8,128)S(1)} %broadcast_add_fusion), channel_id=1, source_target_pairs={{0,62},{1,63},{2,4},{3,5},{4,2},{5,3},{6,8},{7,9},{8,6},{9,7},{10,... | collective-permute-start | bytes 786440 | tf_op jit(solution)/shard_map/ppermute | solution.py:45
  29.6 1.9 %collective-permute-start.2 = (f32[256,256]{1,0:T(8,128)S(1)}, f32[256,256]{1,0:T(8,128)S(1)}, u32[]{:S(2)}, u32[]{:S(2)}) collective-permute-start(f32[256,256]{1,0:T(8,128)S(1)} %broadcast_add_fusion), channel_id=1, source_target_pairs={{0,2},{1,3},{2,0},{3,1},{4,6},{5,7},{6,4},{7,5},{8,10},{9,11},{10,... | collective-permute-start | bytes 786440 | tf_op jit(solution)/shard_map/ppermute | solution.py:41
  31.5 1.9 %collective-permute-start.1 = (f32[256,256]{1,0:T(8,128)S(1)}, f32[256,256]{1,0:T(8,128)S(1)}, u32[]{:S(2)}, u32[]{:S(2)}) collective-permute-start(f32[256,256]{1,0:T(8,128)S(1)} %broadcast_add_fusion), channel_id=1, source_target_pairs={{0,63},{1,2},{2,1},{3,4},{4,3},{5,6},{6,5},{7,8},{8,7},{9,10},{10,... | collective-permute-start | bytes 786440 | tf_op jit(solution)/shard_map/ppermute | solution.py:44
  33.4 4.0 %collective-permute-start = (f32[256,256]{1,0:T(8,128)S(1)}, f32[256,256]{1,0:T(8,128)S(1)}, u32[]{:S(2)}, u32[]{:S(2)}) collective-permute-start(f32[256,256]{1,0:T(8,128)S(1)} %broadcast_add_fusion), channel_id=1, source_target_pairs={{0,1},{1,0},{2,3},{3,2},{4,5},{5,4},{6,7},{7,6},{8,9},{9,8},{10,11... | collective-permute-start | bytes 786440 | tf_op jit(solution)/shard_map/ppermute | solution.py:42
  37.5 0.4 fusion.48
  37.9 0.0 collective-permute-done.3
  37.9 0.4 fusion.24
  38.2 1.0 collective-permute-done.2
  39.2 0.4 fusion.32
  39.6 0.0 collective-permute-done
  39.6 0.4 convolution_add_fusion.7
  40.0 1.3 collective-permute-done.1
  41.3 0.4 broadcast_multiply_fusion
  41.7 2.9 %collective-permute-start.6 = (f32[256,256]{1,0:T(8,128)S(1)}, f32[256,256]{1,0:T(8,128)S(1)}, u32[]{:S(2)}, u32[]{:S(2)}) collective-permute-start(f32[256,256]{1,0:T(8,128)S(1)} %get-tuple-element.6), channel_id=1, source_target_pairs={{0,2},{1,3},{2,0},{3,1},{4,6},{5,7},{6,4},{7,5},{8,10},{9,11},{10,... | collective-permute-start | bytes 786440 | tf_op jit(solution)/shard_map/ppermute | solution.py:41
  44.7 1.9 %collective-permute-start.5 = (f32[256,256]{1,0:T(8,128)S(1)}, f32[256,256]{1,0:T(8,128)S(1)}, u32[]{:S(2)}, u32[]{:S(2)}) collective-permute-start(f32[256,256]{1,0:T(8,128)S(1)} %get-tuple-element.6), channel_id=1, source_target_pairs={{0,63},{1,2},{2,1},{3,4},{4,3},{5,6},{6,5},{7,8},{8,7},{9,10},{10,... | collective-permute-start | bytes 786440 | tf_op jit(solution)/shard_map/ppermute | solution.py:44
  46.6 3.0 %collective-permute-start.4 = (f32[256,256]{1,0:T(8,128)S(1)}, f32[256,256]{1,0:T(8,128)S(1)}, u32[]{:S(2)}, u32[]{:S(2)}) collective-permute-start(f32[256,256]{1,0:T(8,128)S(1)} %get-tuple-element.6), channel_id=1, source_target_pairs={{0,1},{1,0},{2,3},{3,2},{4,5},{5,4},{6,7},{7,6},{8,9},{9,8},{10,11... | collective-permute-start | bytes 786440 | tf_op jit(solution)/shard_map/ppermute | solution.py:42
  49.6 5.0 %collective-permute-start.7 = (f32[256,256]{1,0:T(8,128)S(1)}, f32[256,256]{1,0:T(8,128)S(1)}, u32[]{:S(2)}, u32[]{:S(2)}) collective-permute-start(f32[256,256]{1,0:T(8,128)S(1)} %get-tuple-element.6), channel_id=1, source_target_pairs={{0,62},{1,63},{2,4},{3,5},{4,2},{5,3},{6,8},{7,9},{8,6},{9,7},{10,... | collective-permute-start | bytes 786440 | tf_op jit(solution)/shard_map/ppermute | solution.py:45
  54.7 0.4 fusion.46
  55.1 0.4 fusion.30
  55.5 6.4 %collective-permute-done.7 = f32[256,256]{1,0:T(8,128)S(1)} collective-permute-done((f32[256,256]{1,0:T(8,128)S(1)}, f32[256,256]{1,0:T(8,128)S(1)}, u32[]{:S(2)}, u32[]{:S(2)}) %collective-permute-start.7) | collective-permute-done | bytes 262176 | tf_op jit(solution)/shard_map/ppermute | solution.py:45
  61.8 0.4 fusion.22
  62.2 0.4 convolution_add_fusion.5
  62.6 0.4 fusion.13
  63.0 5.0 %collective-permute-start.11 = (f32[256,256]{1,0:T(8,128)S(1)}, f32[256,256]{1,0:T(8,128)S(1)}, u32[]{:S(2)}, u32[]{:S(2)}) collective-permute-start(f32[256,256]{1,0:T(8,128)S(1)} %fusion.13), channel_id=1, source_target_pairs={{0,62},{1,63},{2,4},{3,5},{4,2},{5,3},{6,8},{7,9},{8,6},{9,7},{10,... | collective-permute-start | bytes 786440 | tf_op jit(solution)/shard_map/ppermute | solution.py:45
  68.1 1.9 %collective-permute-start.10 = (f32[256,256]{1,0:T(8,128)S(1)}, f32[256,256]{1,0:T(8,128)S(1)}, u32[]{:S(2)}, u32[]{:S(2)}) collective-permute-start(f32[256,256]{1,0:T(8,128)S(1)} %fusion.13), channel_id=1, source_target_pairs={{0,2},{1,3},{2,0},{3,1},{4,6},{5,7},{6,4},{7,5},{8,10},{9,11},{10,... | collective-permute-start | bytes 786440 | tf_op jit(solution)/shard_map/ppermute | solution.py:41
  70.0 0.4 fusion.44
  70.4 1.9 %collective-permute-start.9 = (f32[256,256]{1,0:T(8,128)S(1)}, f32[256,256]{1,0:T(8,128)S(1)}, u32[]{:S(2)}, u32[]{:S(2)}) collective-permute-start(f32[256,256]{1,0:T(8,128)S(1)} %fusion.13), channel_id=1, source_target_pairs={{0,63},{1,2},{2,1},{3,4},{4,3},{5,6},{6,5},{7,8},{8,7},{9,10},{10,... | collective-permute-start | bytes 786440 | tf_op jit(solution)/shard_map/ppermute | solution.py:44
  72.3 4.0 %collective-permute-start.8 = (f32[256,256]{1,0:T(8,128)S(1)}, f32[256,256]{1,0:T(8,128)S(1)}, u32[]{:S(2)}, u32[]{:S(2)}) collective-permute-start(f32[256,256]{1,0:T(8,128)S(1)} %fusion.13), channel_id=1, source_target_pairs={{0,1},{1,0},{2,3},{3,2},{4,5},{5,4},{6,7},{7,6},{8,9},{9,8},{10,11... | collective-permute-start | bytes 786440 | tf_op jit(solution)/shard_map/ppermute | solution.py:42
  76.4 0.4 fusion.20
  76.8 0.3 collective-permute-done.10
  77.1 0.4 fusion.28
  77.5 0.0 collective-permute-done.8
  77.5 0.4 convolution_add_fusion.3
  77.9 2.3 %collective-permute-done.9 = f32[256,256]{1,0:T(8,128)S(1)} collective-permute-done((f32[256,256]{1,0:T(8,128)S(1)}, f32[256,256]{1,0:T(8,128)S(1)}, u32[]{:S(2)}, u32[]{:S(2)}) %collective-permute-start.9) | collective-permute-done | bytes 262176 | tf_op jit(solution)/shard_map/ppermute | solution.py:44
  80.2 0.4 fusion.16
  80.6 2.6 %collective-permute-start.15 = (f32[256,256]{1,0:T(8,128)S(1)}, f32[256,256]{1,0:T(8,128)S(1)}, u32[]{:S(2)}, u32[]{:S(2)}) collective-permute-start(f32[256,256]{1,0:T(8,128)S(1)} %fusion.16), channel_id=1, source_target_pairs={{0,62},{1,63},{2,4},{3,5},{4,2},{5,3},{6,8},{7,9},{8,6},{9,7},{10,... | collective-permute-start | bytes 786440 | tf_op jit(solution)/shard_map/ppermute | solution.py:45
  83.2 1.9 %collective-permute-start.14 = (f32[256,256]{1,0:T(8,128)S(1)}, f32[256,256]{1,0:T(8,128)S(1)}, u32[]{:S(2)}, u32[]{:S(2)}) collective-permute-start(f32[256,256]{1,0:T(8,128)S(1)} %fusion.16), channel_id=1, source_target_pairs={{0,2},{1,3},{2,0},{3,1},{4,6},{5,7},{6,4},{7,5},{8,10},{9,11},{10,... | collective-permute-start | bytes 786440 | tf_op jit(solution)/shard_map/ppermute | solution.py:41
  85.2 0.4 fusion.50
  85.6 4.5 %collective-permute-start.13 = (f32[256,256]{1,0:T(8,128)S(1)}, f32[256,256]{1,0:T(8,128)S(1)}, u32[]{:S(2)}, u32[]{:S(2)}) collective-permute-start(f32[256,256]{1,0:T(8,128)S(1)} %fusion.16), channel_id=1, source_target_pairs={{0,63},{1,2},{2,1},{3,4},{4,3},{5,6},{6,5},{7,8},{8,7},{9,10},{10,... | collective-permute-start | bytes 786440 | tf_op jit(solution)/shard_map/ppermute | solution.py:44
  90.0 2.1 %collective-permute-start.12 = (f32[256,256]{1,0:T(8,128)S(1)}, f32[256,256]{1,0:T(8,128)S(1)}, u32[]{:S(2)}, u32[]{:S(2)}) collective-permute-start(f32[256,256]{1,0:T(8,128)S(1)} %fusion.16), channel_id=1, source_target_pairs={{0,1},{1,0},{2,3},{3,2},{4,5},{5,4},{6,7},{7,6},{8,9},{9,8},{10,11... | collective-permute-start | bytes 786440 | tf_op jit(solution)/shard_map/ppermute | solution.py:42
  92.2 0.5 collective-permute-done.15
  92.7 0.4 fusion.26
  93.1 0.4 fusion.34
  93.5 0.4 convolution_add_fusion.1
  93.9 1.6 %collective-permute-done.13 = f32[256,256]{1,0:T(8,128)S(1)} collective-permute-done((f32[256,256]{1,0:T(8,128)S(1)}, f32[256,256]{1,0:T(8,128)S(1)}, u32[]{:S(2)}, u32[]{:S(2)}) %collective-permute-start.13) | collective-permute-done | bytes 262176 | tf_op jit(solution)/shard_map/ppermute | solution.py:44
  95.5 0.4 fusion.19
  95.9 0.7 copy-done.1
  96.6 3.3 %fusion.65 = f32[256,2048]{1,0:T(8,128)} fusion(f32[256,256]{1,0:T(8,128)S(1)} %fusion.19, f32[256,2048]{1,0:T(8,128)S(1)} %copy-done), kind=kOutput, calls=%fused_computation.85 | convolution fusion | flops 1610612736 | bytes 4456448 | tf_op jit(solution)/shard_map/dot_general | solution.py:86
  99.9 0.0 reduce-scatter.2.cloned.1.call-update
  99.9 0.9 copy-done.2
  100.8 0.6 fusion.66
  101.4 0.1 reshape.14
  101.5 23.5 %all_to_all.5 = f32[64,4,256]{2,1,0:T(4,128)S(1)} all-to-all(f32[64,4,256]{2,1,0:T(4,128)S(1)} %reshape.14), channel_id=1, replica_groups=mesh['grp'=8,'wide'=64] {'wide'}, dimensions={0} | all-to-all | bytes 524288 | tf_op jit(solution)/shard_map/all_to_all | solution.py:84
  125.0 0.1 reduce_sum.9
  125.1 0.6 broadcast_multiply_fusion.1
  125.7 21.3 %reduce-scatter.2.cloned.1.call-done = f32[256,256]{1,0:T(8,128)} async-done(((f32[256,2048]{1,0:T(8,128)}), f32[256,256]{1,0:T(8,128)}) %reduce-scatter.2.cloned.1.call-update) | async-done | bytes 262160 | tf_op jit(solution)/shard_map/reduce_scatter | solution.py:89
  (10 shorter events, 0.0 us)
Async XLA Ops:
  7.2 89.4 %copy-start = (f32[256,2048]{1,0:T(8,128)S(1)}, f32[256,2048]{1,0:T(8,128)}, u32[]{:S(2)}) copy-start(f32[256,2048]{1,0:T(8,128)} %param.7) | copy-start | bytes 6291460
  7.2 139.8 %reduce-scatter.2.cloned.1.call-start = ((), (), s32[]{:S(2)}) async-start(), calls=%async_computation.2 | async-start | bytes 2359296 | tf_op jit(solution)/shard_map/reduce_scatter | solution.py:89
  18.4 19.5 %collective-permute-start.3 = (f32[256,256]{1,0:T(8,128)S(1)}, f32[256,256]{1,0:T(8,128)S(1)}, u32[]{:S(2)}, u32[]{:S(2)}) collective-permute-start(f32[256,256]{1,0:T(8,128)S(1)} %broadcast_add_fusion), channel_id=1, source_target_pairs={{0,62},{1,63},{2,4},{3,5},{4,2},{5,3},{6,8},{7,9},{8,6},{9,7},{10,... | collective-permute-start | bytes 786440 | tf_op jit(solution)/shard_map/ppermute | solution.py:45
  29.6 9.7 %collective-permute-start.2 = (f32[256,256]{1,0:T(8,128)S(1)}, f32[256,256]{1,0:T(8,128)S(1)}, u32[]{:S(2)}, u32[]{:S(2)}) collective-permute-start(f32[256,256]{1,0:T(8,128)S(1)} %broadcast_add_fusion), channel_id=1, source_target_pairs={{0,2},{1,3},{2,0},{3,1},{4,6},{5,7},{6,4},{7,5},{8,10},{9,11},{10,... | collective-permute-start | bytes 786440 | tf_op jit(solution)/shard_map/ppermute | solution.py:41
  31.5 9.8 %collective-permute-start.1 = (f32[256,256]{1,0:T(8,128)S(1)}, f32[256,256]{1,0:T(8,128)S(1)}, u32[]{:S(2)}, u32[]{:S(2)}) collective-permute-start(f32[256,256]{1,0:T(8,128)S(1)} %broadcast_add_fusion), channel_id=1, source_target_pairs={{0,63},{1,2},{2,1},{3,4},{4,3},{5,6},{6,5},{7,8},{8,7},{9,10},{10,... | collective-permute-start | bytes 786440 | tf_op jit(solution)/shard_map/ppermute | solution.py:44
  33.4 6.2 %collective-permute-start = (f32[256,256]{1,0:T(8,128)S(1)}, f32[256,256]{1,0:T(8,128)S(1)}, u32[]{:S(2)}, u32[]{:S(2)}) collective-permute-start(f32[256,256]{1,0:T(8,128)S(1)} %broadcast_add_fusion), channel_id=1, source_target_pairs={{0,1},{1,0},{2,3},{3,2},{4,5},{5,4},{6,7},{7,6},{8,9},{9,8},{10,11... | collective-permute-start | bytes 786440 | tf_op jit(solution)/shard_map/ppermute | solution.py:42
  41.7 13.3 %collective-permute-start.6 = (f32[256,256]{1,0:T(8,128)S(1)}, f32[256,256]{1,0:T(8,128)S(1)}, u32[]{:S(2)}, u32[]{:S(2)}) collective-permute-start(f32[256,256]{1,0:T(8,128)S(1)} %get-tuple-element.6), channel_id=1, source_target_pairs={{0,2},{1,3},{2,0},{3,1},{4,6},{5,7},{6,4},{7,5},{8,10},{9,11},{10,... | collective-permute-start | bytes 786440 | tf_op jit(solution)/shard_map/ppermute | solution.py:41
  44.7 18.0 %collective-permute-start.5 = (f32[256,256]{1,0:T(8,128)S(1)}, f32[256,256]{1,0:T(8,128)S(1)}, u32[]{:S(2)}, u32[]{:S(2)}) collective-permute-start(f32[256,256]{1,0:T(8,128)S(1)} %get-tuple-element.6), channel_id=1, source_target_pairs={{0,63},{1,2},{2,1},{3,4},{4,3},{5,6},{6,5},{7,8},{8,7},{9,10},{10,... | collective-permute-start | bytes 786440 | tf_op jit(solution)/shard_map/ppermute | solution.py:44
  46.6 15.6 %collective-permute-start.4 = (f32[256,256]{1,0:T(8,128)S(1)}, f32[256,256]{1,0:T(8,128)S(1)}, u32[]{:S(2)}, u32[]{:S(2)}) collective-permute-start(f32[256,256]{1,0:T(8,128)S(1)} %get-tuple-element.6), channel_id=1, source_target_pairs={{0,1},{1,0},{2,3},{3,2},{4,5},{5,4},{6,7},{7,6},{8,9},{9,8},{10,11... | collective-permute-start | bytes 786440 | tf_op jit(solution)/shard_map/ppermute | solution.py:42
  49.6 12.2 %collective-permute-start.7 = (f32[256,256]{1,0:T(8,128)S(1)}, f32[256,256]{1,0:T(8,128)S(1)}, u32[]{:S(2)}, u32[]{:S(2)}) collective-permute-start(f32[256,256]{1,0:T(8,128)S(1)} %get-tuple-element.6), channel_id=1, source_target_pairs={{0,62},{1,63},{2,4},{3,5},{4,2},{5,3},{6,8},{7,9},{8,6},{9,7},{10,... | collective-permute-start | bytes 786440 | tf_op jit(solution)/shard_map/ppermute | solution.py:45
  63.0 13.3 %collective-permute-start.11 = (f32[256,256]{1,0:T(8,128)S(1)}, f32[256,256]{1,0:T(8,128)S(1)}, u32[]{:S(2)}, u32[]{:S(2)}) collective-permute-start(f32[256,256]{1,0:T(8,128)S(1)} %fusion.13), channel_id=1, source_target_pairs={{0,62},{1,63},{2,4},{3,5},{4,2},{5,3},{6,8},{7,9},{8,6},{9,7},{10,... | collective-permute-start | bytes 786440 | tf_op jit(solution)/shard_map/ppermute | solution.py:45
  68.1 9.0 %collective-permute-start.10 = (f32[256,256]{1,0:T(8,128)S(1)}, f32[256,256]{1,0:T(8,128)S(1)}, u32[]{:S(2)}, u32[]{:S(2)}) collective-permute-start(f32[256,256]{1,0:T(8,128)S(1)} %fusion.13), channel_id=1, source_target_pairs={{0,2},{1,3},{2,0},{3,1},{4,6},{5,7},{6,4},{7,5},{8,10},{9,11},{10,... | collective-permute-start | bytes 786440 | tf_op jit(solution)/shard_map/ppermute | solution.py:41
  70.4 9.8 %collective-permute-start.9 = (f32[256,256]{1,0:T(8,128)S(1)}, f32[256,256]{1,0:T(8,128)S(1)}, u32[]{:S(2)}, u32[]{:S(2)}) collective-permute-start(f32[256,256]{1,0:T(8,128)S(1)} %fusion.13), channel_id=1, source_target_pairs={{0,63},{1,2},{2,1},{3,4},{4,3},{5,6},{6,5},{7,8},{8,7},{9,10},{10,... | collective-permute-start | bytes 786440 | tf_op jit(solution)/shard_map/ppermute | solution.py:44
  72.3 5.2 %collective-permute-start.8 = (f32[256,256]{1,0:T(8,128)S(1)}, f32[256,256]{1,0:T(8,128)S(1)}, u32[]{:S(2)}, u32[]{:S(2)}) collective-permute-start(f32[256,256]{1,0:T(8,128)S(1)} %fusion.13), channel_id=1, source_target_pairs={{0,1},{1,0},{2,3},{3,2},{4,5},{5,4},{6,7},{7,6},{8,9},{9,8},{10,11... | collective-permute-start | bytes 786440 | tf_op jit(solution)/shard_map/ppermute | solution.py:42
  80.6 12.1 %collective-permute-start.15 = (f32[256,256]{1,0:T(8,128)S(1)}, f32[256,256]{1,0:T(8,128)S(1)}, u32[]{:S(2)}, u32[]{:S(2)}) collective-permute-start(f32[256,256]{1,0:T(8,128)S(1)} %fusion.16), channel_id=1, source_target_pairs={{0,62},{1,63},{2,4},{3,5},{4,2},{5,3},{6,8},{7,9},{8,6},{9,7},{10,... | collective-permute-start | bytes 786440 | tf_op jit(solution)/shard_map/ppermute | solution.py:45
  83.2 9.9 %collective-permute-start.14 = (f32[256,256]{1,0:T(8,128)S(1)}, f32[256,256]{1,0:T(8,128)S(1)}, u32[]{:S(2)}, u32[]{:S(2)}) collective-permute-start(f32[256,256]{1,0:T(8,128)S(1)} %fusion.16), channel_id=1, source_target_pairs={{0,2},{1,3},{2,0},{3,1},{4,6},{5,7},{6,4},{7,5},{8,10},{9,11},{10,... | collective-permute-start | bytes 786440 | tf_op jit(solution)/shard_map/ppermute | solution.py:41
  85.6 9.9 %collective-permute-start.13 = (f32[256,256]{1,0:T(8,128)S(1)}, f32[256,256]{1,0:T(8,128)S(1)}, u32[]{:S(2)}, u32[]{:S(2)}) collective-permute-start(f32[256,256]{1,0:T(8,128)S(1)} %fusion.16), channel_id=1, source_target_pairs={{0,63},{1,2},{2,1},{3,4},{4,3},{5,6},{6,5},{7,8},{8,7},{9,10},{10,... | collective-permute-start | bytes 786440 | tf_op jit(solution)/shard_map/ppermute | solution.py:44
  90.0 3.4 %collective-permute-start.12 = (f32[256,256]{1,0:T(8,128)S(1)}, f32[256,256]{1,0:T(8,128)S(1)}, u32[]{:S(2)}, u32[]{:S(2)}) collective-permute-start(f32[256,256]{1,0:T(8,128)S(1)} %fusion.16), channel_id=1, source_target_pairs={{0,1},{1,0},{2,3},{3,2},{4,5},{5,4},{6,7},{7,6},{8,9},{9,8},{10,11... | collective-permute-start | bytes 786440 | tf_op jit(solution)/shard_map/ppermute | solution.py:42
  95.9 0.7 copy-start.1
  99.9 0.9 copy-start.2
Sparse Core Ops, SparseCore 0:
  100.0 46.9 reduce-scatter.1

commit v17 on v16

--- a/solution.py
+++ b/solution.py
@@ -52,6 +52,22 @@
     return total
 
 
+def split3(x):
+    x1 = lax.reduce_precision(x, exponent_bits=8, mantissa_bits=7)
+    rest = x - x1
+    x2 = lax.reduce_precision(rest, exponent_bits=8, mantissa_bits=7)
+    return [p.astype(jnp.bfloat16) for p in (x1, x2, rest - x2)]
+
+
+def split_dot(a, b_parts):
+    a_parts = split3(a)
+    total = None
+    for i, j in ((1, 1), (2, 0), (0, 2), (1, 0), (0, 1), (0, 0)):
+        term = jnp.dot(a_parts[i], b_parts[j], preferred_element_type=jnp.float32)
+        total = term if total is None else total + term
+    return total
+
+
 def local(subspace, hblocks, pattern, rotation):
     devcount = lax.axis_size("wide")
     myself = lax.axis_index("wide")
@@ -83,9 +99,7 @@
     pieces = gram_term.reshape(devcount, -1, gram_term.shape[1])
     gathered = lax.all_to_all(pieces, "wide", 0, 0, tiled=True)
     correlation = jnp.sum(gathered, axis=0) / total_rows
-    rot_term = jnp.dot(
-        current, rotation, precision=HI, preferred_element_type=jnp.float32
-    )
+    rot_term = split_dot(current, split3(rotation))
     rotated = lax.psum_scatter(rot_term, "grp", scatter_dimension=1, tiled=True)
     return (rotated, correlation)
 

time: 155 us -> 154 us (level)
    dot_general x1 -> x6, matrix products: 3.25 us -> 4.23 us  [split_dot(): term = jnp.dot(a_parts[i], b_parts[j], preferred_element_type=jnp.float32)]
where the time goes in v17:
time: 154 us; the launch traced here: 153 us
  starting transfers between devices  56 us (36%)
  waiting for transfers between devices  34.7 us (23%)
  blocking collectives  23.5 us (15%)
  matrix products  16.8 us (11%)
  between operations  15.2 us (10%)
  local copies, waits for them, and re-layouts  4.54 us (3%)
  other arithmetic  2.5 us (2%)
    ppermute x4, starting transfers between devices, apply_ham(): lax.ppermute(field, 'wide', wrap_pairs)  23.9 us
    all_to_all x1, blocking collectives, local(): gathered = lax.all_to_all(pieces, 'wide', 0, 0, tiled=True)  23.5 us
    reduce_scatter x1, waiting for transfers between devices, local(): rotated = lax.psum_scatter(rot_term, 'grp', scatter_dimension=1, tiled=True)  21.3 us
    ppermute x4, starting transfers between devices, apply_ham(): lax.ppermute(field, 'wide', swap_pairs)  13.2 us
    ppermute x4, starting transfers between devices, apply_ham(): lax.ppermute(field, 'wide', cross_pairs)  10.2 us
    ppermute x4, starting transfers between devices, apply_ham(): lax.ppermute(field, 'wide', near_pairs)  8.7 us
    dot_general x20, matrix products, apply_ham(): jnp.dot(hdense[:, idx * rows:(idx + 1) * rows], pieces[idx], precision=HI...  7.73 us
    ppermute x4, waiting for transfers between devices, apply_ham(): lax.ppermute(field, 'wide', wrap_pairs)  6.92 us
  transfers between devices with their start and end apart: 17, of which 8 were waited for; matrix products, arithmetic and copies ran while one was open for 5% of the time, Pallas kernels for 0%

profile of v17, /device:TPU:6, one launch (start us, length us, event | category | flops | bytes accessed | tf_op | source)
XLA Modules:
  0.0 153.3 jit_solution(6787028101976528033)
XLA Ops:
  7.3 0.8 fusion.63
  8.1 0.7 copy-done
  8.8 4.3 %fusion.3 = f32[4,64,20,64]{3,2,1,0:T(8,128)} fusion(f32[4,16,64,64]{3,2,1,0:T(8,128)S(1)} %copy-done, s32[4,16]{1,0:T(4,128)S(1)} %fusion.63), kind=kOutput, calls=%fused_computation.12 | convolution fusion | flops 62915840 | bytes 2359552 | tf_op jit(solution)/shard_map/asp,asij->aipj/dot_general | solution.py:29
  13.0 2.2 %reshape.16 = f32[256,1280]{1,0:T(8,128)S(1)} reshape(f32[4,64,20,64]{3,2,1,0:T(8,128)} %fusion.3) | data formatting | bytes 2621440 | tf_op jit(solution)/shard_map/reshape | solution.py:30
  15.3 0.1 copy.12
  15.4 0.5 slice.16
  16.5 1.0 broadcast_add_fusion
  17.5 11.2 %collective-permute-start.3 = (f32[256,256]{1,0:T(8,128)S(1)}, f32[256,256]{1,0:T(8,128)S(1)}, u32[]{:S(2)}, u32[]{:S(2)}) collective-permute-start(f32[256,256]{1,0:T(8,128)S(1)} %broadcast_add_fusion), channel_id=1, source_target_pairs={{0,62},{1,63},{2,4},{3,5},{4,2},{5,3},{6,8},{7,9},{8,6},{9,7},{10,... | collective-permute-start | bytes 786440 | tf_op jit(solution)/shard_map/ppermute | solution.py:45
  28.7 1.9 %collective-permute-start.2 = (f32[256,256]{1,0:T(8,128)S(1)}, f32[256,256]{1,0:T(8,128)S(1)}, u32[]{:S(2)}, u32[]{:S(2)}) collective-permute-start(f32[256,256]{1,0:T(8,128)S(1)} %broadcast_add_fusion), channel_id=1, source_target_pairs={{0,2},{1,3},{2,0},{3,1},{4,6},{5,7},{6,4},{7,5},{8,10},{9,11},{10,... | collective-permute-start | bytes 786440 | tf_op jit(solution)/shard_map/ppermute | solution.py:41
  30.7 1.9 %collective-permute-start.1 = (f32[256,256]{1,0:T(8,128)S(1)}, f32[256,256]{1,0:T(8,128)S(1)}, u32[]{:S(2)}, u32[]{:S(2)}) collective-permute-start(f32[256,256]{1,0:T(8,128)S(1)} %broadcast_add_fusion), channel_id=1, source_target_pairs={{0,63},{1,2},{2,1},{3,4},{4,3},{5,6},{6,5},{7,8},{8,7},{9,10},{10,... | collective-permute-start | bytes 786440 | tf_op jit(solution)/shard_map/ppermute | solution.py:44
  32.6 4.0 %collective-permute-start = (f32[256,256]{1,0:T(8,128)S(1)}, f32[256,256]{1,0:T(8,128)S(1)}, u32[]{:S(2)}, u32[]{:S(2)}) collective-permute-start(f32[256,256]{1,0:T(8,128)S(1)} %broadcast_add_fusion), channel_id=1, source_target_pairs={{0,1},{1,0},{2,3},{3,2},{4,5},{5,4},{6,7},{7,6},{8,9},{9,8},{10,11... | collective-permute-start | bytes 786440 | tf_op jit(solution)/shard_map/ppermute | solution.py:42
  36.6 0.4 fusion.51
  37.0 0.4 fusion.27
  37.4 1.0 collective-permute-done.2
  38.4 0.4 fusion.35
  38.8 0.4 convolution_add_fusion.12
  39.2 1.3 collective-permute-done.1
  40.5 0.4 broadcast_multiply_fusion
  40.9 2.9 %collective-permute-start.6 = (f32[256,256]{1,0:T(8,128)S(1)}, f32[256,256]{1,0:T(8,128)S(1)}, u32[]{:S(2)}, u32[]{:S(2)}) collective-permute-start(f32[256,256]{1,0:T(8,128)S(1)} %get-tuple-element.6), channel_id=1, source_target_pairs={{0,2},{1,3},{2,0},{3,1},{4,6},{5,7},{6,4},{7,5},{8,10},{9,11},{10,... | collective-permute-start | bytes 786440 | tf_op jit(solution)/shard_map/ppermute | solution.py:41
  43.8 1.9 %collective-permute-start.5 = (f32[256,256]{1,0:T(8,128)S(1)}, f32[256,256]{1,0:T(8,128)S(1)}, u32[]{:S(2)}, u32[]{:S(2)}) collective-permute-start(f32[256,256]{1,0:T(8,128)S(1)} %get-tuple-element.6), channel_id=1, source_target_pairs={{0,63},{1,2},{2,1},{3,4},{4,3},{5,6},{6,5},{7,8},{8,7},{9,10},{10,... | collective-permute-start | bytes 786440 | tf_op jit(solution)/shard_map/ppermute | solution.py:44
  45.8 3.0 %collective-permute-start.4 = (f32[256,256]{1,0:T(8,128)S(1)}, f32[256,256]{1,0:T(8,128)S(1)}, u32[]{:S(2)}, u32[]{:S(2)}) collective-permute-start(f32[256,256]{1,0:T(8,128)S(1)} %get-tuple-element.6), channel_id=1, source_target_pairs={{0,1},{1,0},{2,3},{3,2},{4,5},{5,4},{6,7},{7,6},{8,9},{9,8},{10,11... | collective-permute-start | bytes 786440 | tf_op jit(solution)/shard_map/ppermute | solution.py:42
  48.8 5.0 %collective-permute-start.7 = (f32[256,256]{1,0:T(8,128)S(1)}, f32[256,256]{1,0:T(8,128)S(1)}, u32[]{:S(2)}, u32[]{:S(2)}) collective-permute-start(f32[256,256]{1,0:T(8,128)S(1)} %get-tuple-element.6), channel_id=1, source_target_pairs={{0,62},{1,63},{2,4},{3,5},{4,2},{5,3},{6,8},{7,9},{8,6},{9,7},{10,... | collective-permute-start | bytes 786440 | tf_op jit(solution)/shard_map/ppermute | solution.py:45
  53.8 0.4 fusion.49
  54.2 0.4 fusion.33
  54.6 6.4 %collective-permute-done.7 = f32[256,256]{1,0:T(8,128)S(1)} collective-permute-done((f32[256,256]{1,0:T(8,128)S(1)}, f32[256,256]{1,0:T(8,128)S(1)}, u32[]{:S(2)}, u32[]{:S(2)}) %collective-permute-start.7) | collective-permute-done | bytes 262176 | tf_op jit(solution)/shard_map/ppermute | solution.py:45
  61.0 0.4 fusion.25
  61.4 0.4 convolution_add_fusion.10
  61.8 0.4 fusion.14
  62.2 5.1 %collective-permute-start.11 = (f32[256,256]{1,0:T(8,128)S(1)}, f32[256,256]{1,0:T(8,128)S(1)}, u32[]{:S(2)}, u32[]{:S(2)}) collective-permute-start(f32[256,256]{1,0:T(8,128)S(1)} %fusion.14), channel_id=1, source_target_pairs={{0,62},{1,63},{2,4},{3,5},{4,2},{5,3},{6,8},{7,9},{8,6},{9,7},{10,... | collective-permute-start | bytes 786440 | tf_op jit(solution)/shard_map/ppermute | solution.py:45
  67.3 1.9 %collective-permute-start.10 = (f32[256,256]{1,0:T(8,128)S(1)}, f32[256,256]{1,0:T(8,128)S(1)}, u32[]{:S(2)}, u32[]{:S(2)}) collective-permute-start(f32[256,256]{1,0:T(8,128)S(1)} %fusion.14), channel_id=1, source_target_pairs={{0,2},{1,3},{2,0},{3,1},{4,6},{5,7},{6,4},{7,5},{8,10},{9,11},{10,... | collective-permute-start | bytes 786440 | tf_op jit(solution)/shard_map/ppermute | solution.py:41
  69.2 0.4 fusion.47
  69.6 1.9 %collective-permute-start.9 = (f32[256,256]{1,0:T(8,128)S(1)}, f32[256,256]{1,0:T(8,128)S(1)}, u32[]{:S(2)}, u32[]{:S(2)}) collective-permute-start(f32[256,256]{1,0:T(8,128)S(1)} %fusion.14), channel_id=1, source_target_pairs={{0,63},{1,2},{2,1},{3,4},{4,3},{5,6},{6,5},{7,8},{8,7},{9,10},{10,... | collective-permute-start | bytes 786440 | tf_op jit(solution)/shard_map/ppermute | solution.py:44
  71.5 4.0 %collective-permute-start.8 = (f32[256,256]{1,0:T(8,128)S(1)}, f32[256,256]{1,0:T(8,128)S(1)}, u32[]{:S(2)}, u32[]{:S(2)}) collective-permute-start(f32[256,256]{1,0:T(8,128)S(1)} %fusion.14), channel_id=1, source_target_pairs={{0,1},{1,0},{2,3},{3,2},{4,5},{5,4},{6,7},{7,6},{8,9},{9,8},{10,11... | collective-permute-start | bytes 786440 | tf_op jit(solution)/shard_map/ppermute | solution.py:42
  75.6 0.4 fusion.23
  75.9 0.3 collective-permute-done.10
  76.3 0.4 fusion.31
  76.6 0.0 collective-permute-done.8
  76.7 0.4 convolution_add_fusion.8
  77.1 2.3 %collective-permute-done.9 = f32[256,256]{1,0:T(8,128)S(1)} collective-permute-done((f32[256,256]{1,0:T(8,128)S(1)}, f32[256,256]{1,0:T(8,128)S(1)}, u32[]{:S(2)}, u32[]{:S(2)}) %collective-permute-start.9) | collective-permute-done | bytes 262176 | tf_op jit(solution)/shard_map/ppermute | solution.py:44
  79.4 0.4 fusion.17
  79.8 2.6 %collective-permute-start.15 = (f32[256,256]{1,0:T(8,128)S(1)}, f32[256,256]{1,0:T(8,128)S(1)}, u32[]{:S(2)}, u32[]{:S(2)}) collective-permute-start(f32[256,256]{1,0:T(8,128)S(1)} %fusion.17), channel_id=1, source_target_pairs={{0,62},{1,63},{2,4},{3,5},{4,2},{5,3},{6,8},{7,9},{8,6},{9,7},{10,... | collective-permute-start | bytes 786440 | tf_op jit(solution)/shard_map/ppermute | solution.py:45
  82.4 1.9 %collective-permute-start.14 = (f32[256,256]{1,0:T(8,128)S(1)}, f32[256,256]{1,0:T(8,128)S(1)}, u32[]{:S(2)}, u32[]{:S(2)}) collective-permute-start(f32[256,256]{1,0:T(8,128)S(1)} %fusion.17), channel_id=1, source_target_pairs={{0,2},{1,3},{2,0},{3,1},{4,6},{5,7},{6,4},{7,5},{8,10},{9,11},{10,... | collective-permute-start | bytes 786440 | tf_op jit(solution)/shard_map/ppermute | solution.py:41
  84.3 0.4 fusion.53
  84.7 4.5 %collective-permute-start.13 = (f32[256,256]{1,0:T(8,128)S(1)}, f32[256,256]{1,0:T(8,128)S(1)}, u32[]{:S(2)}, u32[]{:S(2)}) collective-permute-start(f32[256,256]{1,0:T(8,128)S(1)} %fusion.17), channel_id=1, source_target_pairs={{0,63},{1,2},{2,1},{3,4},{4,3},{5,6},{6,5},{7,8},{8,7},{9,10},{10,... | collective-permute-start | bytes 786440 | tf_op jit(solution)/shard_map/ppermute | solution.py:44
  89.2 2.1 %collective-permute-start.12 = (f32[256,256]{1,0:T(8,128)S(1)}, f32[256,256]{1,0:T(8,128)S(1)}, u32[]{:S(2)}, u32[]{:S(2)}) collective-permute-start(f32[256,256]{1,0:T(8,128)S(1)} %fusion.17), channel_id=1, source_target_pairs={{0,1},{1,0},{2,3},{3,2},{4,5},{5,4},{6,7},{7,6},{8,9},{9,8},{10,11... | collective-permute-start | bytes 786440 | tf_op jit(solution)/shard_map/ppermute | solution.py:42
  91.3 0.5 collective-permute-done.15
  91.9 0.4 fusion.29
  92.3 0.4 fusion.37
  92.7 0.4 convolution_add_fusion.6
  93.1 1.6 %collective-permute-done.13 = f32[256,256]{1,0:T(8,128)S(1)} collective-permute-done((f32[256,256]{1,0:T(8,128)S(1)}, f32[256,256]{1,0:T(8,128)S(1)}, u32[]{:S(2)}, u32[]{:S(2)}) %collective-permute-start.13) | collective-permute-done | bytes 262176 | tf_op jit(solution)/shard_map/ppermute | solution.py:44
  94.6 0.4 fusion.20
  95.1 0.5 fusion.55
  95.5 0.4 convolution_add_fusion.4
  96.0 0.6 convolution_add_fusion.3
  96.6 0.4 convolution_add_fusion.2
  97.1 0.5 convolution_add_fusion.1
  97.6 1.8 %convolution_add_fusion = f32[256,2048]{1,0:T(8,128)} fusion(f32[256,2048]{1,0:T(8,128)S(1)} %convolution_add_fusion.1, f32[256,256]{1,0:T(8,128)S(1)} %fusion.20, f32[256,2048]{1,0:T(8,128)S(1)} %copy-done.1), kind=kOutput, calls=%fused_computation.4 | convolution fusion | flops 270139392 | bytes 6553600 | tf_op jit(solution)/shard_map/dot_general | solution.py:66
  99.4 0.9 copy-done.3
  100.3 0.6 fusion.70
  100.9 0.1 reshape.14
  101.0 23.5 %all_to_all.5 = f32[64,4,256]{2,1,0:T(4,128)S(1)} all-to-all(f32[64,4,256]{2,1,0:T(4,128)S(1)} %reshape.14), channel_id=1, replica_groups=mesh['grp'=8,'wide'=64] {'wide'}, dimensions={0} | all-to-all | bytes 524288 | tf_op jit(solution)/shard_map/all_to_all | solution.py:100
  124.5 0.1 reduce_sum.9
  124.6 0.6 broadcast_multiply_fusion.1
  125.2 21.3 %reduce-scatter.2.cloned.1.call-done = f32[256,256]{1,0:T(8,128)} async-done(((f32[256,2048]{1,0:T(8,128)}), f32[256,256]{1,0:T(8,128)}) %reduce-scatter.2.cloned.1.call-update) | async-done | bytes 262160 | tf_op jit(solution)/shard_map/reduce_scatter | solution.py:103
  (17 shorter events, 0.1 us)
Async XLA Ops:
  7.2 1.6 %copy-start = (f32[4,16,64,64]{3,2,1,0:T(8,128)S(1)}, f32[4,16,64,64]{3,2,1,0:T(8,128)}, u32[]{:S(2)}) copy-start(f32[4,16,64,64]{3,2,1,0:T(8,128)} %param.5) | copy-start | bytes 3145732
  7.2 139.3 %reduce-scatter.2.cloned.1.call-start = ((), (), s32[]{:S(2)}) async-start(), calls=%async_computation.2 | async-start | bytes 2359296 | tf_op jit(solution)/shard_map/reduce_scatter | solution.py:103
  17.5 19.5 %collective-permute-start.3 = (f32[256,256]{1,0:T(8,128)S(1)}, f32[256,256]{1,0:T(8,128)S(1)}, u32[]{:S(2)}, u32[]{:S(2)}) collective-permute-start(f32[256,256]{1,0:T(8,128)S(1)} %broadcast_add_fusion), channel_id=1, source_target_pairs={{0,62},{1,63},{2,4},{3,5},{4,2},{5,3},{6,8},{7,9},{8,6},{9,7},{10,... | collective-permute-start | bytes 786440 | tf_op jit(solution)/shard_map/ppermute | solution.py:45
  28.7 9.7 %collective-permute-start.2 = (f32[256,256]{1,0:T(8,128)S(1)}, f32[256,256]{1,0:T(8,128)S(1)}, u32[]{:S(2)}, u32[]{:S(2)}) collective-permute-start(f32[256,256]{1,0:T(8,128)S(1)} %broadcast_add_fusion), channel_id=1, source_target_pairs={{0,2},{1,3},{2,0},{3,1},{4,6},{5,7},{6,4},{7,5},{8,10},{9,11},{10,... | collective-permute-start | bytes 786440 | tf_op jit(solution)/shard_map/ppermute | solution.py:41
  30.7 9.8 %collective-permute-start.1 = (f32[256,256]{1,0:T(8,128)S(1)}, f32[256,256]{1,0:T(8,128)S(1)}, u32[]{:S(2)}, u32[]{:S(2)}) collective-permute-start(f32[256,256]{1,0:T(8,128)S(1)} %broadcast_add_fusion), channel_id=1, source_target_pairs={{0,63},{1,2},{2,1},{3,4},{4,3},{5,6},{6,5},{7,8},{8,7},{9,10},{10,... | collective-permute-start | bytes 786440 | tf_op jit(solution)/shard_map/ppermute | solution.py:44
  32.6 6.2 %collective-permute-start = (f32[256,256]{1,0:T(8,128)S(1)}, f32[256,256]{1,0:T(8,128)S(1)}, u32[]{:S(2)}, u32[]{:S(2)}) collective-permute-start(f32[256,256]{1,0:T(8,128)S(1)} %broadcast_add_fusion), channel_id=1, source_target_pairs={{0,1},{1,0},{2,3},{3,2},{4,5},{5,4},{6,7},{7,6},{8,9},{9,8},{10,11... | collective-permute-start | bytes 786440 | tf_op jit(solution)/shard_map/ppermute | solution.py:42
  40.9 13.3 %collective-permute-start.6 = (f32[256,256]{1,0:T(8,128)S(1)}, f32[256,256]{1,0:T(8,128)S(1)}, u32[]{:S(2)}, u32[]{:S(2)}) collective-permute-start(f32[256,256]{1,0:T(8,128)S(1)} %get-tuple-element.6), channel_id=1, source_target_pairs={{0,2},{1,3},{2,0},{3,1},{4,6},{5,7},{6,4},{7,5},{8,10},{9,11},{10,... | collective-permute-start | bytes 786440 | tf_op jit(solution)/shard_map/ppermute | solution.py:41
  43.8 18.0 %collective-permute-start.5 = (f32[256,256]{1,0:T(8,128)S(1)}, f32[256,256]{1,0:T(8,128)S(1)}, u32[]{:S(2)}, u32[]{:S(2)}) collective-permute-start(f32[256,256]{1,0:T(8,128)S(1)} %get-tuple-element.6), channel_id=1, source_target_pairs={{0,63},{1,2},{2,1},{3,4},{4,3},{5,6},{6,5},{7,8},{8,7},{9,10},{10,... | collective-permute-start | bytes 786440 | tf_op jit(solution)/shard_map/ppermute | solution.py:44
  45.8 15.6 %collective-permute-start.4 = (f32[256,256]{1,0:T(8,128)S(1)}, f32[256,256]{1,0:T(8,128)S(1)}, u32[]{:S(2)}, u32[]{:S(2)}) collective-permute-start(f32[256,256]{1,0:T(8,128)S(1)} %get-tuple-element.6), channel_id=1, source_target_pairs={{0,1},{1,0},{2,3},{3,2},{4,5},{5,4},{6,7},{7,6},{8,9},{9,8},{10,11... | collective-permute-start | bytes 786440 | tf_op jit(solution)/shard_map/ppermute | solution.py:42
  48.8 12.2 %collective-permute-start.7 = (f32[256,256]{1,0:T(8,128)S(1)}, f32[256,256]{1,0:T(8,128)S(1)}, u32[]{:S(2)}, u32[]{:S(2)}) collective-permute-start(f32[256,256]{1,0:T(8,128)S(1)} %get-tuple-element.6), channel_id=1, source_target_pairs={{0,62},{1,63},{2,4},{3,5},{4,2},{5,3},{6,8},{7,9},{8,6},{9,7},{10,... | collective-permute-start | bytes 786440 | tf_op jit(solution)/shard_map/ppermute | solution.py:45
  62.2 13.3 %collective-permute-start.11 = (f32[256,256]{1,0:T(8,128)S(1)}, f32[256,256]{1,0:T(8,128)S(1)}, u32[]{:S(2)}, u32[]{:S(2)}) collective-permute-start(f32[256,256]{1,0:T(8,128)S(1)} %fusion.14), channel_id=1, source_target_pairs={{0,62},{1,63},{2,4},{3,5},{4,2},{5,3},{6,8},{7,9},{8,6},{9,7},{10,... | collective-permute-start | bytes 786440 | tf_op jit(solution)/shard_map/ppermute | solution.py:45
  67.3 9.0 %collective-permute-start.10 = (f32[256,256]{1,0:T(8,128)S(1)}, f32[256,256]{1,0:T(8,128)S(1)}, u32[]{:S(2)}, u32[]{:S(2)}) collective-permute-start(f32[256,256]{1,0:T(8,128)S(1)} %fusion.14), channel_id=1, source_target_pairs={{0,2},{1,3},{2,0},{3,1},{4,6},{5,7},{6,4},{7,5},{8,10},{9,11},{10,... | collective-permute-start | bytes 786440 | tf_op jit(solution)/shard_map/ppermute | solution.py:41
  69.6 9.8 %collective-permute-start.9 = (f32[256,256]{1,0:T(8,128)S(1)}, f32[256,256]{1,0:T(8,128)S(1)}, u32[]{:S(2)}, u32[]{:S(2)}) collective-permute-start(f32[256,256]{1,0:T(8,128)S(1)} %fusion.14), channel_id=1, source_target_pairs={{0,63},{1,2},{2,1},{3,4},{4,3},{5,6},{6,5},{7,8},{8,7},{9,10},{10,... | collective-permute-start | bytes 786440 | tf_op jit(solution)/shard_map/ppermute | solution.py:44
  71.5 5.2 %collective-permute-start.8 = (f32[256,256]{1,0:T(8,128)S(1)}, f32[256,256]{1,0:T(8,128)S(1)}, u32[]{:S(2)}, u32[]{:S(2)}) collective-permute-start(f32[256,256]{1,0:T(8,128)S(1)} %fusion.14), channel_id=1, source_target_pairs={{0,1},{1,0},{2,3},{3,2},{4,5},{5,4},{6,7},{7,6},{8,9},{9,8},{10,11... | collective-permute-start | bytes 786440 | tf_op jit(solution)/shard_map/ppermute | solution.py:42
  79.8 12.0 %collective-permute-start.15 = (f32[256,256]{1,0:T(8,128)S(1)}, f32[256,256]{1,0:T(8,128)S(1)}, u32[]{:S(2)}, u32[]{:S(2)}) collective-permute-start(f32[256,256]{1,0:T(8,128)S(1)} %fusion.17), channel_id=1, source_target_pairs={{0,62},{1,63},{2,4},{3,5},{4,2},{5,3},{6,8},{7,9},{8,6},{9,7},{10,... | collective-permute-start | bytes 786440 | tf_op jit(solution)/shard_map/ppermute | solution.py:45
  82.4 9.9 %collective-permute-start.14 = (f32[256,256]{1,0:T(8,128)S(1)}, f32[256,256]{1,0:T(8,128)S(1)}, u32[]{:S(2)}, u32[]{:S(2)}) collective-permute-start(f32[256,256]{1,0:T(8,128)S(1)} %fusion.17), channel_id=1, source_target_pairs={{0,2},{1,3},{2,0},{3,1},{4,6},{5,7},{6,4},{7,5},{8,10},{9,11},{10,... | collective-permute-start | bytes 786440 | tf_op jit(solution)/shard_map/ppermute | solution.py:41
  84.7 9.9 %collective-permute-start.13 = (f32[256,256]{1,0:T(8,128)S(1)}, f32[256,256]{1,0:T(8,128)S(1)}, u32[]{:S(2)}, u32[]{:S(2)}) collective-permute-start(f32[256,256]{1,0:T(8,128)S(1)} %fusion.17), channel_id=1, source_target_pairs={{0,63},{1,2},{2,1},{3,4},{4,3},{5,6},{6,5},{7,8},{8,7},{9,10},{10,... | collective-permute-start | bytes 786440 | tf_op jit(solution)/shard_map/ppermute | solution.py:44
  89.2 3.4 %collective-permute-start.12 = (f32[256,256]{1,0:T(8,128)S(1)}, f32[256,256]{1,0:T(8,128)S(1)}, u32[]{:S(2)}, u32[]{:S(2)}) collective-permute-start(f32[256,256]{1,0:T(8,128)S(1)} %fusion.17), channel_id=1, source_target_pairs={{0,1},{1,0},{2,3},{3,2},{4,5},{5,4},{6,7},{7,6},{8,9},{9,8},{10,11... | collective-permute-start | bytes 786440 | tf_op jit(solution)/shard_map/ppermute | solution.py:42
  92.2 2.8 %copy-start.1 = (f32[256,2048]{1,0:T(8,128)S(1)}, f32[256,2048]{1,0:T(8,128)}, u32[]{:S(2)}) copy-start(f32[256,2048]{1,0:T(8,128)} %param.7) | copy-start | bytes 6291460
  95.1 2.5 %copy-start.2 = (f32[256,256]{1,0:T(8,128)}, f32[256,256]{1,0:T(8,128)S(1)}, u32[]{:S(2)}) copy-start(f32[256,256]{1,0:T(8,128)S(1)} %fusion.20) | copy-start | bytes 786436
  99.4 0.9 copy-start.3
Sparse Core Ops, SparseCore 0:
  99.5 46.9 reduce-scatter.1

commit v18 on v16

--- a/solution.py
+++ b/solution.py
@@ -62,7 +62,6 @@
     slot_index = relative * A_DEV + pattern % A_DEV
     hdense = dense_hamiltonian(hblocks, slot_index)
     subspace, probe_h = lax.optimization_barrier((subspace, hdense[:8, :128]))
-    subspace = subspace + 0.0 * probe_h[0, 0]
     previous = subspace
     current = (apply_ham(subspace, hdense) - cheb_center * subspace) / cheb_half
     for step in range(DEGREE - 1):
@@ -82,7 +81,7 @@
     )
     pieces = gram_term.reshape(devcount, -1, gram_term.shape[1])
     gathered = lax.all_to_all(pieces, "wide", 0, 0, tiled=True)
-    correlation = jnp.sum(gathered, axis=0) / total_rows
+    correlation = jnp.sum(gathered, axis=0) / total_rows + 0.0 * probe_h[0, 0]
     rot_term = jnp.dot(
         current, rotation, precision=HI, preferred_element_type=jnp.float32
     )

time: 155 us -> 153 us (0.987)
  blocking collectives: 23.5 us -> 0 us
  starting transfers between devices: 56 us -> 68.2 us
  waiting for transfers between devices: 34.7 us -> 43.8 us
    all_to_all x1 -> x0, blocking collectives: 23.5 us -> none  [local(): gathered = lax.all_to_all(pieces, 'wide', 0, 0, tiled=True)]
    all_to_all x0 -> x1, starting transfers between devices: none -> 12.2 us  [local(): gathered = lax.all_to_all(pieces, 'wide', 0, 0, tiled=True)]
    all_to_all x0 -> x1, waiting for transfers between devices: none -> 10.4 us  [local(): gathered = lax.all_to_all(pieces, 'wide', 0, 0, tiled=True)]
  transfers between devices with their start and end apart: 17 -> 18, of which waited for: 8 -> 9; matrix products, arithmetic and copies ran while one was open for 5% -> 6% of each run, Pallas kernels for 0% -> 0%
where the time goes in v18:
time: 153 us; the launch traced here: 152 us
  starting transfers between devices  68.2 us (45%)
  waiting for transfers between devices  43.8 us (29%)
  matrix products  18.3 us (12%)
  between operations  15.1 us (10%)
  local copies, waits for them, and re-layouts  5.24 us (3%)
  other arithmetic  1.53 us (1%)
    ppermute x4, starting transfers between devices, apply_ham(): lax.ppermute(field, 'wide', wrap_pairs)  23.9 us
    reduce_scatter x1, waiting for transfers between devices, local(): rotated = lax.psum_scatter(rot_term, 'grp', scatter_dimension=1, tiled=True)  20.7 us
    ppermute x4, starting transfers between devices, apply_ham(): lax.ppermute(field, 'wide', swap_pairs)  13.2 us
    all_to_all x1, starting transfers between devices, local(): gathered = lax.all_to_all(pieces, 'wide', 0, 0, tiled=True)  12.2 us
    all_to_all x1, waiting for transfers between devices, local(): gathered = lax.all_to_all(pieces, 'wide', 0, 0, tiled=True)  10.4 us
    ppermute x4, starting transfers between devices, apply_ham(): lax.ppermute(field, 'wide', cross_pairs)  10.2 us
    ppermute x4, starting transfers between devices, apply_ham(): lax.ppermute(field, 'wide', near_pairs)  8.7 us
    dot_general x20, matrix products, apply_ham(): jnp.dot(hdense[:, idx * rows:(idx + 1) * rows], pieces[idx], precision=HI...  8.68 us
  transfers between devices with their start and end apart: 18, of which 9 were waited for; matrix products, arithmetic and copies ran while one was open for 6% of the time, Pallas kernels for 0%

profile of v18, /device:TPU:6, one launch (start us, length us, event | category | flops | bytes accessed | tf_op | source)
XLA Modules:
  0.0 152.2 jit_solution(4228930533220998160)
XLA Ops:
  7.2 0.0 copy-start
  7.2 0.0 reduce-scatter.2.cloned.1.call-start
  7.3 0.8 fusion.58
  8.1 5.8 %fusion.2 = f32[4,64,20,64]{3,2,1,0:T(8,128)} fusion(f32[4,16,64,64]{3,2,1,0:T(8,128)} %param.5, s32[4,16]{1,0:T(4,128)S(1)} %fusion.58), kind=kOutput, calls=%fused_computation.2 | convolution fusion | flops 62915840 | bytes 2359552 | tf_op jit(solution)/shard_map/asp,asij->aipj/dot_general | solution.py:29
  13.9 2.2 %reshape.16 = f32[256,1280]{1,0:T(8,128)S(1)} reshape(f32[4,64,20,64]{3,2,1,0:T(8,128)} %fusion.2) | data formatting | bytes 2621440 | tf_op jit(solution)/shard_map/reshape | solution.py:30
  16.1 0.1 copy.12
  16.2 11.2 %collective-permute-start.3 = (f32[256,256]{1,0:T(8,128)}, f32[256,256]{1,0:T(8,128)S(1)}, u32[]{:S(2)}, u32[]{:S(2)}) collective-permute-start(f32[256,256]{1,0:T(8,128)} %param.4), channel_id=1, source_target_pairs={{0,62},{1,63},{2,4},{3,5},{4,2},{5,3},{6,8},{7,9},{8,6},{9,7},{10,... | collective-permute-start | bytes 786440 | tf_op jit(solution)/shard_map/ppermute | solution.py:45
  27.4 1.9 %collective-permute-start.2 = (f32[256,256]{1,0:T(8,128)}, f32[256,256]{1,0:T(8,128)S(1)}, u32[]{:S(2)}, u32[]{:S(2)}) collective-permute-start(f32[256,256]{1,0:T(8,128)} %param.4), channel_id=1, source_target_pairs={{0,2},{1,3},{2,0},{3,1},{4,6},{5,7},{6,4},{7,5},{8,10},{9,11},{10,... | collective-permute-start | bytes 786440 | tf_op jit(solution)/shard_map/ppermute | solution.py:41
  29.4 1.9 %collective-permute-start.1 = (f32[256,256]{1,0:T(8,128)}, f32[256,256]{1,0:T(8,128)S(1)}, u32[]{:S(2)}, u32[]{:S(2)}) collective-permute-start(f32[256,256]{1,0:T(8,128)} %param.4), channel_id=1, source_target_pairs={{0,63},{1,2},{2,1},{3,4},{4,3},{5,6},{6,5},{7,8},{8,7},{9,10},{10,... | collective-permute-start | bytes 786440 | tf_op jit(solution)/shard_map/ppermute | solution.py:44
  31.3 4.0 %collective-permute-start = (f32[256,256]{1,0:T(8,128)}, f32[256,256]{1,0:T(8,128)S(1)}, u32[]{:S(2)}, u32[]{:S(2)}) collective-permute-start(f32[256,256]{1,0:T(8,128)} %param.4), channel_id=1, source_target_pairs={{0,1},{1,0},{2,3},{3,2},{4,5},{5,4},{6,7},{7,6},{8,9},{9,8},{10,11... | collective-permute-start | bytes 786440 | tf_op jit(solution)/shard_map/ppermute | solution.py:42
  35.3 1.3 fusion.48
  36.7 0.0 copy-start.3
  36.7 0.0 collective-permute-done.3
  36.7 0.4 fusion.24
  37.1 0.2 collective-permute-done.2
  37.3 0.4 fusion.32
  37.7 0.4 convolution_add_fusion.7
  38.1 1.3 collective-permute-done.1
  39.4 0.4 broadcast_multiply_fusion
  39.8 2.9 %collective-permute-start.6 = (f32[256,256]{1,0:T(8,128)S(1)}, f32[256,256]{1,0:T(8,128)S(1)}, u32[]{:S(2)}, u32[]{:S(2)}) collective-permute-start(f32[256,256]{1,0:T(8,128)S(1)} %get-tuple-element.6), channel_id=1, source_target_pairs={{0,2},{1,3},{2,0},{3,1},{4,6},{5,7},{6,4},{7,5},{8,10},{9,11},{10,... | collective-permute-start | bytes 786440 | tf_op jit(solution)/shard_map/ppermute | solution.py:41
  42.7 1.9 %collective-permute-start.5 = (f32[256,256]{1,0:T(8,128)S(1)}, f32[256,256]{1,0:T(8,128)S(1)}, u32[]{:S(2)}, u32[]{:S(2)}) collective-permute-start(f32[256,256]{1,0:T(8,128)S(1)} %get-tuple-element.6), channel_id=1, source_target_pairs={{0,63},{1,2},{2,1},{3,4},{4,3},{5,6},{6,5},{7,8},{8,7},{9,10},{10,... | collective-permute-start | bytes 786440 | tf_op jit(solution)/shard_map/ppermute | solution.py:44
  44.7 3.0 %collective-permute-start.4 = (f32[256,256]{1,0:T(8,128)S(1)}, f32[256,256]{1,0:T(8,128)S(1)}, u32[]{:S(2)}, u32[]{:S(2)}) collective-permute-start(f32[256,256]{1,0:T(8,128)S(1)} %get-tuple-element.6), channel_id=1, source_target_pairs={{0,1},{1,0},{2,3},{3,2},{4,5},{5,4},{6,7},{7,6},{8,9},{9,8},{10,11... | collective-permute-start | bytes 786440 | tf_op jit(solution)/shard_map/ppermute | solution.py:42
  47.7 5.0 %collective-permute-start.7 = (f32[256,256]{1,0:T(8,128)S(1)}, f32[256,256]{1,0:T(8,128)S(1)}, u32[]{:S(2)}, u32[]{:S(2)}) collective-permute-start(f32[256,256]{1,0:T(8,128)S(1)} %get-tuple-element.6), channel_id=1, source_target_pairs={{0,62},{1,63},{2,4},{3,5},{4,2},{5,3},{6,8},{7,9},{8,6},{9,7},{10,... | collective-permute-start | bytes 786440 | tf_op jit(solution)/shard_map/ppermute | solution.py:45
  52.7 0.4 fusion.46
  53.1 0.4 fusion.30
  53.5 6.4 %collective-permute-done.7 = f32[256,256]{1,0:T(8,128)S(1)} collective-permute-done((f32[256,256]{1,0:T(8,128)S(1)}, f32[256,256]{1,0:T(8,128)S(1)}, u32[]{:S(2)}, u32[]{:S(2)}) %collective-permute-start.7) | collective-permute-done | bytes 262176 | tf_op jit(solution)/shard_map/ppermute | solution.py:45
  59.9 0.4 fusion.22
  60.3 0.4 convolution_add_fusion.5
  60.7 0.4 fusion.13
  61.1 5.0 %collective-permute-start.11 = (f32[256,256]{1,0:T(8,128)S(1)}, f32[256,256]{1,0:T(8,128)S(1)}, u32[]{:S(2)}, u32[]{:S(2)}) collective-permute-start(f32[256,256]{1,0:T(8,128)S(1)} %fusion.13), channel_id=1, source_target_pairs={{0,62},{1,63},{2,4},{3,5},{4,2},{5,3},{6,8},{7,9},{8,6},{9,7},{10,... | collective-permute-start | bytes 786440 | tf_op jit(solution)/shard_map/ppermute | solution.py:45
  66.2 1.9 %collective-permute-start.10 = (f32[256,256]{1,0:T(8,128)S(1)}, f32[256,256]{1,0:T(8,128)S(1)}, u32[]{:S(2)}, u32[]{:S(2)}) collective-permute-start(f32[256,256]{1,0:T(8,128)S(1)} %fusion.13), channel_id=1, source_target_pairs={{0,2},{1,3},{2,0},{3,1},{4,6},{5,7},{6,4},{7,5},{8,10},{9,11},{10,... | collective-permute-start | bytes 786440 | tf_op jit(solution)/shard_map/ppermute | solution.py:41
  68.1 0.4 fusion.44
  68.5 1.9 %collective-permute-start.9 = (f32[256,256]{1,0:T(8,128)S(1)}, f32[256,256]{1,0:T(8,128)S(1)}, u32[]{:S(2)}, u32[]{:S(2)}) collective-permute-start(f32[256,256]{1,0:T(8,128)S(1)} %fusion.13), channel_id=1, source_target_pairs={{0,63},{1,2},{2,1},{3,4},{4,3},{5,6},{6,5},{7,8},{8,7},{9,10},{10,... | collective-permute-start | bytes 786440 | tf_op jit(solution)/shard_map/ppermute | solution.py:44
  70.4 4.0 %collective-permute-start.8 = (f32[256,256]{1,0:T(8,128)S(1)}, f32[256,256]{1,0:T(8,128)S(1)}, u32[]{:S(2)}, u32[]{:S(2)}) collective-permute-start(f32[256,256]{1,0:T(8,128)S(1)} %fusion.13), channel_id=1, source_target_pairs={{0,1},{1,0},{2,3},{3,2},{4,5},{5,4},{6,7},{7,6},{8,9},{9,8},{10,11... | collective-permute-start | bytes 786440 | tf_op jit(solution)/shard_map/ppermute | solution.py:42
  74.5 0.4 fusion.20
  74.9 0.3 collective-permute-done.10
  75.2 0.4 fusion.28
  75.6 0.0 collective-permute-done.8
  75.6 0.4 convolution_add_fusion.3
  76.0 2.3 %collective-permute-done.9 = f32[256,256]{1,0:T(8,128)S(1)} collective-permute-done((f32[256,256]{1,0:T(8,128)S(1)}, f32[256,256]{1,0:T(8,128)S(1)}, u32[]{:S(2)}, u32[]{:S(2)}) %collective-permute-start.9) | collective-permute-done | bytes 262176 | tf_op jit(solution)/shard_map/ppermute | solution.py:44
  78.3 0.4 fusion.16
  78.7 2.6 %collective-permute-start.15 = (f32[256,256]{1,0:T(8,128)S(1)}, f32[256,256]{1,0:T(8,128)S(1)}, u32[]{:S(2)}, u32[]{:S(2)}) collective-permute-start(f32[256,256]{1,0:T(8,128)S(1)} %fusion.16), channel_id=1, source_target_pairs={{0,62},{1,63},{2,4},{3,5},{4,2},{5,3},{6,8},{7,9},{8,6},{9,7},{10,... | collective-permute-start | bytes 786440 | tf_op jit(solution)/shard_map/ppermute | solution.py:45
  81.3 1.9 %collective-permute-start.14 = (f32[256,256]{1,0:T(8,128)S(1)}, f32[256,256]{1,0:T(8,128)S(1)}, u32[]{:S(2)}, u32[]{:S(2)}) collective-permute-start(f32[256,256]{1,0:T(8,128)S(1)} %fusion.16), channel_id=1, source_target_pairs={{0,2},{1,3},{2,0},{3,1},{4,6},{5,7},{6,4},{7,5},{8,10},{9,11},{10,... | collective-permute-start | bytes 786440 | tf_op jit(solution)/shard_map/ppermute | solution.py:41
  83.2 0.4 fusion.50
  83.6 4.5 %collective-permute-start.13 = (f32[256,256]{1,0:T(8,128)S(1)}, f32[256,256]{1,0:T(8,128)S(1)}, u32[]{:S(2)}, u32[]{:S(2)}) collective-permute-start(f32[256,256]{1,0:T(8,128)S(1)} %fusion.16), channel_id=1, source_target_pairs={{0,63},{1,2},{2,1},{3,4},{4,3},{5,6},{6,5},{7,8},{8,7},{9,10},{10,... | collective-permute-start | bytes 786440 | tf_op jit(solution)/shard_map/ppermute | solution.py:44
  88.1 2.1 %collective-permute-start.12 = (f32[256,256]{1,0:T(8,128)S(1)}, f32[256,256]{1,0:T(8,128)S(1)}, u32[]{:S(2)}, u32[]{:S(2)}) collective-permute-start(f32[256,256]{1,0:T(8,128)S(1)} %fusion.16), channel_id=1, source_target_pairs={{0,1},{1,0},{2,3},{3,2},{4,5},{5,4},{6,7},{7,6},{8,9},{9,8},{10,11... | collective-permute-start | bytes 786440 | tf_op jit(solution)/shard_map/ppermute | solution.py:42
  90.2 0.5 collective-permute-done.15
  90.8 0.4 fusion.26
  91.2 0.4 fusion.34
  91.6 0.4 convolution_add_fusion.1
  92.0 1.6 %collective-permute-done.13 = f32[256,256]{1,0:T(8,128)S(1)} collective-permute-done((f32[256,256]{1,0:T(8,128)S(1)}, f32[256,256]{1,0:T(8,128)S(1)}, u32[]{:S(2)}, u32[]{:S(2)}) %collective-permute-start.13) | collective-permute-done | bytes 262176 | tf_op jit(solution)/shard_map/ppermute | solution.py:44
  93.5 0.4 fusion.19
  94.0 0.7 copy-done.1
  94.7 3.2 %fusion.65 = f32[256,2048]{1,0:T(8,128)} fusion(f32[256,256]{1,0:T(8,128)S(1)} %fusion.19, f32[256,2048]{1,0:T(8,128)S(1)} %copy-done), kind=kOutput, calls=%fused_computation.84 | convolution fusion | flops 1610612736 | bytes 4456448 | tf_op jit(solution)/shard_map/dot_general | solution.py:85
  97.9 0.0 reduce-scatter.2.cloned.1.call-update
  97.9 0.9 copy-done.2
  98.9 0.6 fusion.66
  99.5 0.8 reshape.14
  100.2 12.2 %all-to-all-start = ((f32[64,4,256]{2,1,0:T(4,128)}), f32[64,4,256]{2,1,0:T(4,128)S(1)}, u32[]{:S(2)}, u32[]{:S(2)}) async-start(f32[64,4,256]{2,1,0:T(4,128)} %reshape.14), calls=%async_computation.1 | async-start | bytes 524288 | tf_op jit(solution)/shard_map/all_to_all | solution.py:83
  112.4 0.5 slice.20
  113.6 10.4 %all-to-all-done = f32[64,4,256]{2,1,0:T(4,128)S(1)} async-done(((f32[64,4,256]{2,1,0:T(4,128)}), f32[64,4,256]{2,1,0:T(4,128)S(1)}, u32[]{:S(2)}, u32[]{:S(2)}) %all-to-all-start) | async-done | bytes 262176 | tf_op jit(solution)/shard_map/all_to_all | solution.py:83
  124.0 0.1 reduce_sum.9
  124.1 0.6 multiply_add_fusion
  124.7 20.7 %reduce-scatter.2.cloned.1.call-done = f32[256,256]{1,0:T(8,128)} async-done(((f32[256,2048]{1,0:T(8,128)}), f32[256,256]{1,0:T(8,128)}) %reduce-scatter.2.cloned.1.call-update) | async-done | bytes 262160 | tf_op jit(solution)/shard_map/reduce_scatter | solution.py:88
  (12 shorter events, 0.0 us)
Async XLA Ops:
  7.2 87.5 %copy-start = (f32[256,2048]{1,0:T(8,128)S(1)}, f32[256,2048]{1,0:T(8,128)}, u32[]{:S(2)}) copy-start(f32[256,2048]{1,0:T(8,128)} %param.7) | copy-start | bytes 6291460
  7.2 138.1 %reduce-scatter.2.cloned.1.call-start = ((), (), s32[]{:S(2)}) async-start(), calls=%async_computation.2 | async-start | bytes 2359296 | tf_op jit(solution)/shard_map/reduce_scatter | solution.py:88
  16.2 20.5 %collective-permute-start.3 = (f32[256,256]{1,0:T(8,128)}, f32[256,256]{1,0:T(8,128)S(1)}, u32[]{:S(2)}, u32[]{:S(2)}) collective-permute-start(f32[256,256]{1,0:T(8,128)} %param.4), channel_id=1, source_target_pairs={{0,62},{1,63},{2,4},{3,5},{4,2},{5,3},{6,8},{7,9},{8,6},{9,7},{10,... | collective-permute-start | bytes 786440 | tf_op jit(solution)/shard_map/ppermute | solution.py:45
  27.4 9.9 %collective-permute-start.2 = (f32[256,256]{1,0:T(8,128)}, f32[256,256]{1,0:T(8,128)S(1)}, u32[]{:S(2)}, u32[]{:S(2)}) collective-permute-start(f32[256,256]{1,0:T(8,128)} %param.4), channel_id=1, source_target_pairs={{0,2},{1,3},{2,0},{3,1},{4,6},{5,7},{6,4},{7,5},{8,10},{9,11},{10,... | collective-permute-start | bytes 786440 | tf_op jit(solution)/shard_map/ppermute | solution.py:41
  29.4 10.0 %collective-permute-start.1 = (f32[256,256]{1,0:T(8,128)}, f32[256,256]{1,0:T(8,128)S(1)}, u32[]{:S(2)}, u32[]{:S(2)}) collective-permute-start(f32[256,256]{1,0:T(8,128)} %param.4), channel_id=1, source_target_pairs={{0,63},{1,2},{2,1},{3,4},{4,3},{5,6},{6,5},{7,8},{8,7},{9,10},{10,... | collective-permute-start | bytes 786440 | tf_op jit(solution)/shard_map/ppermute | solution.py:44
  31.3 6.4 %collective-permute-start = (f32[256,256]{1,0:T(8,128)}, f32[256,256]{1,0:T(8,128)S(1)}, u32[]{:S(2)}, u32[]{:S(2)}) collective-permute-start(f32[256,256]{1,0:T(8,128)} %param.4), channel_id=1, source_target_pairs={{0,1},{1,0},{2,3},{3,2},{4,5},{5,4},{6,7},{7,6},{8,9},{9,8},{10,11... | collective-permute-start | bytes 786440 | tf_op jit(solution)/shard_map/ppermute | solution.py:42
  36.7 2.7 %copy-start.3 = (f32[256,256]{1,0:T(8,128)S(1)}, f32[256,256]{1,0:T(8,128)}, u32[]{:S(2)}) copy-start(f32[256,256]{1,0:T(8,128)} %param.4) | copy-start | bytes 786436
  39.8 13.3 %collective-permute-start.6 = (f32[256,256]{1,0:T(8,128)S(1)}, f32[256,256]{1,0:T(8,128)S(1)}, u32[]{:S(2)}, u32[]{:S(2)}) collective-permute-start(f32[256,256]{1,0:T(8,128)S(1)} %get-tuple-element.6), channel_id=1, source_target_pairs={{0,2},{1,3},{2,0},{3,1},{4,6},{5,7},{6,4},{7,5},{8,10},{9,11},{10,... | collective-permute-start | bytes 786440 | tf_op jit(solution)/shard_map/ppermute | solution.py:41
  42.7 18.0 %collective-permute-start.5 = (f32[256,256]{1,0:T(8,128)S(1)}, f32[256,256]{1,0:T(8,128)S(1)}, u32[]{:S(2)}, u32[]{:S(2)}) collective-permute-start(f32[256,256]{1,0:T(8,128)S(1)} %get-tuple-element.6), channel_id=1, source_target_pairs={{0,63},{1,2},{2,1},{3,4},{4,3},{5,6},{6,5},{7,8},{8,7},{9,10},{10,... | collective-permute-start | bytes 786440 | tf_op jit(solution)/shard_map/ppermute | solution.py:44
  44.7 15.6 %collective-permute-start.4 = (f32[256,256]{1,0:T(8,128)S(1)}, f32[256,256]{1,0:T(8,128)S(1)}, u32[]{:S(2)}, u32[]{:S(2)}) collective-permute-start(f32[256,256]{1,0:T(8,128)S(1)} %get-tuple-element.6), channel_id=1, source_target_pairs={{0,1},{1,0},{2,3},{3,2},{4,5},{5,4},{6,7},{7,6},{8,9},{9,8},{10,11... | collective-permute-start | bytes 786440 | tf_op jit(solution)/shard_map/ppermute | solution.py:42
  47.7 12.2 %collective-permute-start.7 = (f32[256,256]{1,0:T(8,128)S(1)}, f32[256,256]{1,0:T(8,128)S(1)}, u32[]{:S(2)}, u32[]{:S(2)}) collective-permute-start(f32[256,256]{1,0:T(8,128)S(1)} %get-tuple-element.6), channel_id=1, source_target_pairs={{0,62},{1,63},{2,4},{3,5},{4,2},{5,3},{6,8},{7,9},{8,6},{9,7},{10,... | collective-permute-start | bytes 786440 | tf_op jit(solution)/shard_map/ppermute | solution.py:45
  61.1 13.3 %collective-permute-start.11 = (f32[256,256]{1,0:T(8,128)S(1)}, f32[256,256]{1,0:T(8,128)S(1)}, u32[]{:S(2)}, u32[]{:S(2)}) collective-permute-start(f32[256,256]{1,0:T(8,128)S(1)} %fusion.13), channel_id=1, source_target_pairs={{0,62},{1,63},{2,4},{3,5},{4,2},{5,3},{6,8},{7,9},{8,6},{9,7},{10,... | collective-permute-start | bytes 786440 | tf_op jit(solution)/shard_map/ppermute | solution.py:45
  66.2 9.0 %collective-permute-start.10 = (f32[256,256]{1,0:T(8,128)S(1)}, f32[256,256]{1,0:T(8,128)S(1)}, u32[]{:S(2)}, u32[]{:S(2)}) collective-permute-start(f32[256,256]{1,0:T(8,128)S(1)} %fusion.13), channel_id=1, source_target_pairs={{0,2},{1,3},{2,0},{3,1},{4,6},{5,7},{6,4},{7,5},{8,10},{9,11},{10,... | collective-permute-start | bytes 786440 | tf_op jit(solution)/shard_map/ppermute | solution.py:41
  68.5 9.8 %collective-permute-start.9 = (f32[256,256]{1,0:T(8,128)S(1)}, f32[256,256]{1,0:T(8,128)S(1)}, u32[]{:S(2)}, u32[]{:S(2)}) collective-permute-start(f32[256,256]{1,0:T(8,128)S(1)} %fusion.13), channel_id=1, source_target_pairs={{0,63},{1,2},{2,1},{3,4},{4,3},{5,6},{6,5},{7,8},{8,7},{9,10},{10,... | collective-permute-start | bytes 786440 | tf_op jit(solution)/shard_map/ppermute | solution.py:44
  70.4 5.2 %collective-permute-start.8 = (f32[256,256]{1,0:T(8,128)S(1)}, f32[256,256]{1,0:T(8,128)S(1)}, u32[]{:S(2)}, u32[]{:S(2)}) collective-permute-start(f32[256,256]{1,0:T(8,128)S(1)} %fusion.13), channel_id=1, source_target_pairs={{0,1},{1,0},{2,3},{3,2},{4,5},{5,4},{6,7},{7,6},{8,9},{9,8},{10,11... | collective-permute-start | bytes 786440 | tf_op jit(solution)/shard_map/ppermute | solution.py:42
  78.7 12.0 %collective-permute-start.15 = (f32[256,256]{1,0:T(8,128)S(1)}, f32[256,256]{1,0:T(8,128)S(1)}, u32[]{:S(2)}, u32[]{:S(2)}) collective-permute-start(f32[256,256]{1,0:T(8,128)S(1)} %fusion.16), channel_id=1, source_target_pairs={{0,62},{1,63},{2,4},{3,5},{4,2},{5,3},{6,8},{7,9},{8,6},{9,7},{10,... | collective-permute-start | bytes 786440 | tf_op jit(solution)/shard_map/ppermute | solution.py:45
  81.3 9.8 %collective-permute-start.14 = (f32[256,256]{1,0:T(8,128)S(1)}, f32[256,256]{1,0:T(8,128)S(1)}, u32[]{:S(2)}, u32[]{:S(2)}) collective-permute-start(f32[256,256]{1,0:T(8,128)S(1)} %fusion.16), channel_id=1, source_target_pairs={{0,2},{1,3},{2,0},{3,1},{4,6},{5,7},{6,4},{7,5},{8,10},{9,11},{10,... | collective-permute-start | bytes 786440 | tf_op jit(solution)/shard_map/ppermute | solution.py:41
  83.6 9.9 %collective-permute-start.13 = (f32[256,256]{1,0:T(8,128)S(1)}, f32[256,256]{1,0:T(8,128)S(1)}, u32[]{:S(2)}, u32[]{:S(2)}) collective-permute-start(f32[256,256]{1,0:T(8,128)S(1)} %fusion.16), channel_id=1, source_target_pairs={{0,63},{1,2},{2,1},{3,4},{4,3},{5,6},{6,5},{7,8},{8,7},{9,10},{10,... | collective-permute-start | bytes 786440 | tf_op jit(solution)/shard_map/ppermute | solution.py:44
  88.1 3.4 %collective-permute-start.12 = (f32[256,256]{1,0:T(8,128)S(1)}, f32[256,256]{1,0:T(8,128)S(1)}, u32[]{:S(2)}, u32[]{:S(2)}) collective-permute-start(f32[256,256]{1,0:T(8,128)S(1)} %fusion.16), channel_id=1, source_target_pairs={{0,1},{1,0},{2,3},{3,2},{4,5},{5,4},{6,7},{7,6},{8,9},{9,8},{10,11... | collective-permute-start | bytes 786440 | tf_op jit(solution)/shard_map/ppermute | solution.py:42
  94.0 0.7 copy-start.1
  97.9 0.9 copy-start.2
  100.2 23.7 %all-to-all-start = ((f32[64,4,256]{2,1,0:T(4,128)}), f32[64,4,256]{2,1,0:T(4,128)S(1)}, u32[]{:S(2)}, u32[]{:S(2)}) async-start(f32[64,4,256]{2,1,0:T(4,128)} %reshape.14), calls=%async_computation.1 | async-start | bytes 524288 | tf_op jit(solution)/shard_map/all_to_all | solution.py:83
Sparse Core Ops, SparseCore 0:
  98.1 47.2 reduce-scatter.1

commit v19 on v18

--- a/solution.py
+++ b/solution.py
@@ -27,7 +27,7 @@
     window_blocks = (2 * HW + 1) * A_DEV
     onehot = (slot_index[:, :, None] == jnp.arange(window_blocks)[None, None, :]).astype(jnp.float32)
     hd = jnp.einsum("asp,asij->aipj", onehot, hblocks, precision=HI)
-    return hd.reshape(local_blocks * B, window_blocks * B)
+    return hd.reshape(local_blocks * B, window_blocks * B), hd[0, :8, 0, :]
 
 
 def apply_ham(field, hdense):
@@ -60,8 +60,8 @@
     relative = jnp.where(myself % 2 == 0, jnp.where(relative == 1, 3, jnp.where(relative == 3, 1, relative)), relative)
     relative = jnp.where((myself // 2) % 2 == 0, jnp.where(relative == 0, 4, jnp.where(relative == 4, 0, relative)), relative)
     slot_index = relative * A_DEV + pattern % A_DEV
-    hdense = dense_hamiltonian(hblocks, slot_index)
-    subspace, probe_h = lax.optimization_barrier((subspace, hdense[:8, :128]))
+    hdense, probe_h = dense_hamiltonian(hblocks, slot_index)
+    subspace, probe_h = lax.optimization_barrier((subspace, probe_h))
     previous = subspace
     current = (apply_ham(subspace, hdense) - cheb_center * subspace) / cheb_half
     for step in range(DEGREE - 1):

time: 153 us -> 153 us (level)
  matrix products: 18.3 us -> 21.5 us
    dot_general x20, matrix products: 8.68 us -> 13.5 us  [apply_ham(): jnp.dot(hdense[:, idx * rows:(idx + 1) * rows], pieces[idx], precision=HI...]
    dot_general x1, matrix products: 5.78 us -> 4.14 us  [dense_hamiltonian(): hd = jnp.einsum('asp,asij->aipj', onehot, hblocks, precision=HI)]
  transfers between devices with their start and end apart: 18 -> 18, of which waited for: 9 -> 7; matrix products, arithmetic and copies ran while one was open for 6% -> 10% of each run, Pallas kernels for 0% -> 0%
where the time goes in v19:
time: 153 us; the launch traced here: 152 us
  starting transfers between devices  66.7 us (44%)
  waiting for transfers between devices  42.4 us (28%)
  matrix products  21.5 us (14%)
  between operations  15.2 us (10%)
  local copies, waits for them, and re-layouts  5.15 us (3%)
  other arithmetic  1.53 us (1%)
    ppermute x4, starting transfers between devices, apply_ham(): lax.ppermute(field, 'wide', wrap_pairs)  23 us
    reduce_scatter x1, waiting for transfers between devices, local(): rotated = lax.psum_scatter(rot_term, 'grp', scatter_dimension=1, tiled=True)  19.3 us
    dot_general x20, matrix products, apply_ham(): jnp.dot(hdense[:, idx * rows:(idx + 1) * rows], pieces[idx], precision=HI...  13.5 us
    ppermute x4, starting transfers between devices, apply_ham(): lax.ppermute(field, 'wide', swap_pairs)  12.5 us
    all_to_all x1, starting transfers between devices, local(): gathered = lax.all_to_all(pieces, 'wide', 0, 0, tiled=True)  12.1 us
    ppermute x4, starting transfers between devices, apply_ham(): lax.ppermute(field, 'wide', cross_pairs)  11.4 us
    all_to_all x1, waiting for transfers between devices, local(): gathered = lax.all_to_all(pieces, 'wide', 0, 0, tiled=True)  10.4 us
    ppermute x4, starting transfers between devices, apply_ham(): lax.ppermute(field, 'wide', near_pairs)  7.69 us
  transfers between devices with their start and end apart: 18, of which 7 were waited for; matrix products, arithmetic and copies ran while one was open for 10% of the time, Pallas kernels for 0%

profile of v19, /device:TPU:6, one launch (start us, length us, event | category | flops | bytes accessed | tf_op | source)
XLA Modules:
  0.0 152.4 jit_solution(1059688406116696519)
XLA Ops:
  7.2 0.0 copy-start
  7.2 0.0 reduce-scatter.2.cloned.1.call-start
  7.3 0.8 fusion.58
  8.1 4.1 %fusion.2 = f32[4,64,20,64]{3,2,1,0:T(8,128)S(1)} fusion(f32[4,16,64,64]{3,2,1,0:T(8,128)} %param.5, s32[4,16]{1,0:T(4,128)S(1)} %fusion.58), kind=kOutput, calls=%fused_computation.2 | convolution fusion | flops 62915840 | bytes 2359552 | tf_op jit(solution)/shard_map/asp,asij->aipj/dot_general | solution.py:29
  12.3 11.2 %collective-permute-start.3 = (f32[256,256]{1,0:T(8,128)}, f32[256,256]{1,0:T(8,128)}, u32[]{:S(2)}, u32[]{:S(2)}) collective-permute-start(f32[256,256]{1,0:T(8,128)} %param.4), channel_id=1, source_target_pairs={{0,62},{1,63},{2,4},{3,5},{4,2},{5,3},{6,8},{7,9},{8,6},{9,7},{10,... | collective-permute-start | bytes 786440 | tf_op jit(solution)/shard_map/ppermute | solution.py:45
  23.5 1.9 %collective-permute-start.2 = (f32[256,256]{1,0:T(8,128)}, f32[256,256]{1,0:T(8,128)}, u32[]{:S(2)}, u32[]{:S(2)}) collective-permute-start(f32[256,256]{1,0:T(8,128)} %param.4), channel_id=1, source_target_pairs={{0,2},{1,3},{2,0},{3,1},{4,6},{5,7},{6,4},{7,5},{8,10},{9,11},{10,... | collective-permute-start | bytes 786440 | tf_op jit(solution)/shard_map/ppermute | solution.py:41
  25.4 1.9 %collective-permute-start.1 = (f32[256,256]{1,0:T(8,128)}, f32[256,256]{1,0:T(8,128)}, u32[]{:S(2)}, u32[]{:S(2)}) collective-permute-start(f32[256,256]{1,0:T(8,128)} %param.4), channel_id=1, source_target_pairs={{0,63},{1,2},{2,1},{3,4},{4,3},{5,6},{6,5},{7,8},{8,7},{9,10},{10,... | collective-permute-start | bytes 786440 | tf_op jit(solution)/shard_map/ppermute | solution.py:44
  27.4 4.0 %collective-permute-start = (f32[256,256]{1,0:T(8,128)}, f32[256,256]{1,0:T(8,128)}, u32[]{:S(2)}, u32[]{:S(2)}) collective-permute-start(f32[256,256]{1,0:T(8,128)} %param.4), channel_id=1, source_target_pairs={{0,1},{1,0},{2,3},{3,2},{4,5},{5,4},{6,7},{7,6},{8,9},{9,8},{10,11... | collective-permute-start | bytes 786440 | tf_op jit(solution)/shard_map/ppermute | solution.py:42
  31.4 2.2 %reshape.16 = f32[256,1280]{1,0:T(8,128)S(1)} reshape(f32[4,64,20,64]{3,2,1,0:T(8,128)} %copy-done.1) | data formatting | bytes 2621440 | tf_op jit(solution)/shard_map/reshape | solution.py:30
  33.6 1.3 fusion.48
  35.0 0.0 collective-permute-done.3
  35.0 1.3 fusion.24
  36.3 1.3 fusion.32
  37.7 0.0 collective-permute-done
  37.7 1.3 convolution_add_fusion.7
  39.0 0.0 collective-permute-done.1
  39.0 1.4 broadcast_multiply_fusion
  40.5 1.9 %collective-permute-start.6 = (f32[256,256]{1,0:T(8,128)S(1)}, f32[256,256]{1,0:T(8,128)S(1)}, u32[]{:S(2)}, u32[]{:S(2)}) collective-permute-start(f32[256,256]{1,0:T(8,128)S(1)} %get-tuple-element.6), channel_id=1, source_target_pairs={{0,2},{1,3},{2,0},{3,1},{4,6},{5,7},{6,4},{7,5},{8,10},{9,11},{10,... | collective-permute-start | bytes 786440 | tf_op jit(solution)/shard_map/ppermute | solution.py:41
  42.4 3.6 %collective-permute-start.5 = (f32[256,256]{1,0:T(8,128)S(1)}, f32[256,256]{1,0:T(8,128)S(1)}, u32[]{:S(2)}, u32[]{:S(2)}) collective-permute-start(f32[256,256]{1,0:T(8,128)S(1)} %get-tuple-element.6), channel_id=1, source_target_pairs={{0,63},{1,2},{2,1},{3,4},{4,3},{5,6},{6,5},{7,8},{8,7},{9,10},{10,... | collective-permute-start | bytes 786440 | tf_op jit(solution)/shard_map/ppermute | solution.py:44
  46.1 2.3 %collective-permute-start.4 = (f32[256,256]{1,0:T(8,128)S(1)}, f32[256,256]{1,0:T(8,128)S(1)}, u32[]{:S(2)}, u32[]{:S(2)}) collective-permute-start(f32[256,256]{1,0:T(8,128)S(1)} %get-tuple-element.6), channel_id=1, source_target_pairs={{0,1},{1,0},{2,3},{3,2},{4,5},{5,4},{6,7},{7,6},{8,9},{9,8},{10,11... | collective-permute-start | bytes 786440 | tf_op jit(solution)/shard_map/ppermute | solution.py:42
  48.4 4.0 %collective-permute-start.7 = (f32[256,256]{1,0:T(8,128)S(1)}, f32[256,256]{1,0:T(8,128)S(1)}, u32[]{:S(2)}, u32[]{:S(2)}) collective-permute-start(f32[256,256]{1,0:T(8,128)S(1)} %get-tuple-element.6), channel_id=1, source_target_pairs={{0,62},{1,63},{2,4},{3,5},{4,2},{5,3},{6,8},{7,9},{8,6},{9,7},{10,... | collective-permute-start | bytes 786440 | tf_op jit(solution)/shard_map/ppermute | solution.py:45
  52.4 0.4 fusion.46
  52.8 0.4 fusion.30
  53.2 7.5 %collective-permute-done.7 = f32[256,256]{1,0:T(8,128)S(1)} collective-permute-done((f32[256,256]{1,0:T(8,128)S(1)}, f32[256,256]{1,0:T(8,128)S(1)}, u32[]{:S(2)}, u32[]{:S(2)}) %collective-permute-start.7) | collective-permute-done | bytes 262176 | tf_op jit(solution)/shard_map/ppermute | solution.py:45
  60.7 0.4 fusion.22
  61.1 0.0 collective-permute-done.4
  61.1 0.4 convolution_add_fusion.5
  61.5 0.0 collective-permute-done.5
  61.5 1.4 fusion.13
  62.9 3.9 %collective-permute-start.11 = (f32[256,256]{1,0:T(8,128)S(1)}, f32[256,256]{1,0:T(8,128)S(1)}, u32[]{:S(2)}, u32[]{:S(2)}) collective-permute-start(f32[256,256]{1,0:T(8,128)S(1)} %fusion.13), channel_id=1, source_target_pairs={{0,62},{1,63},{2,4},{3,5},{4,2},{5,3},{6,8},{7,9},{8,6},{9,7},{10,... | collective-permute-start | bytes 786440 | tf_op jit(solution)/shard_map/ppermute | solution.py:45
  66.8 1.9 %collective-permute-start.10 = (f32[256,256]{1,0:T(8,128)S(1)}, f32[256,256]{1,0:T(8,128)S(1)}, u32[]{:S(2)}, u32[]{:S(2)}) collective-permute-start(f32[256,256]{1,0:T(8,128)S(1)} %fusion.13), channel_id=1, source_target_pairs={{0,2},{1,3},{2,0},{3,1},{4,6},{5,7},{6,4},{7,5},{8,10},{9,11},{10,... | collective-permute-start | bytes 786440 | tf_op jit(solution)/shard_map/ppermute | solution.py:41
  68.7 0.4 fusion.44
  69.1 2.6 %collective-permute-start.9 = (f32[256,256]{1,0:T(8,128)S(1)}, f32[256,256]{1,0:T(8,128)S(1)}, u32[]{:S(2)}, u32[]{:S(2)}) collective-permute-start(f32[256,256]{1,0:T(8,128)S(1)} %fusion.13), channel_id=1, source_target_pairs={{0,63},{1,2},{2,1},{3,4},{4,3},{5,6},{6,5},{7,8},{8,7},{9,10},{10,... | collective-permute-start | bytes 786440 | tf_op jit(solution)/shard_map/ppermute | solution.py:44
  71.8 3.3 %collective-permute-start.8 = (f32[256,256]{1,0:T(8,128)S(1)}, f32[256,256]{1,0:T(8,128)S(1)}, u32[]{:S(2)}, u32[]{:S(2)}) collective-permute-start(f32[256,256]{1,0:T(8,128)S(1)} %fusion.13), channel_id=1, source_target_pairs={{0,1},{1,0},{2,3},{3,2},{4,5},{5,4},{6,7},{7,6},{8,9},{9,8},{10,11... | collective-permute-start | bytes 786440 | tf_op jit(solution)/shard_map/ppermute | solution.py:42
  75.1 0.4 fusion.20
  75.5 0.3 collective-permute-done.10
  75.8 0.4 fusion.28
  76.2 0.0 collective-permute-done.8
  76.2 0.4 convolution_add_fusion.3
  76.6 2.3 %collective-permute-done.9 = f32[256,256]{1,0:T(8,128)S(1)} collective-permute-done((f32[256,256]{1,0:T(8,128)S(1)}, f32[256,256]{1,0:T(8,128)S(1)}, u32[]{:S(2)}, u32[]{:S(2)}) %collective-permute-start.9) | collective-permute-done | bytes 262176 | tf_op jit(solution)/shard_map/ppermute | solution.py:44
  78.9 0.4 fusion.16
  79.4 3.8 %collective-permute-start.15 = (f32[256,256]{1,0:T(8,128)S(1)}, f32[256,256]{1,0:T(8,128)S(1)}, u32[]{:S(2)}, u32[]{:S(2)}) collective-permute-start(f32[256,256]{1,0:T(8,128)S(1)} %fusion.16), channel_id=1, source_target_pairs={{0,62},{1,63},{2,4},{3,5},{4,2},{5,3},{6,8},{7,9},{8,6},{9,7},{10,... | collective-permute-start | bytes 786440 | tf_op jit(solution)/shard_map/ppermute | solution.py:45
  83.2 1.9 %collective-permute-start.14 = (f32[256,256]{1,0:T(8,128)S(1)}, f32[256,256]{1,0:T(8,128)S(1)}, u32[]{:S(2)}, u32[]{:S(2)}) collective-permute-start(f32[256,256]{1,0:T(8,128)S(1)} %fusion.16), channel_id=1, source_target_pairs={{0,2},{1,3},{2,0},{3,1},{4,6},{5,7},{6,4},{7,5},{8,10},{9,11},{10,... | collective-permute-start | bytes 786440 | tf_op jit(solution)/shard_map/ppermute | solution.py:41
  85.1 0.4 fusion.50
  85.5 3.2 %collective-permute-start.13 = (f32[256,256]{1,0:T(8,128)S(1)}, f32[256,256]{1,0:T(8,128)S(1)}, u32[]{:S(2)}, u32[]{:S(2)}) collective-permute-start(f32[256,256]{1,0:T(8,128)S(1)} %fusion.16), channel_id=1, source_target_pairs={{0,63},{1,2},{2,1},{3,4},{4,3},{5,6},{6,5},{7,8},{8,7},{9,10},{10,... | collective-permute-start | bytes 786440 | tf_op jit(solution)/shard_map/ppermute | solution.py:44
  88.8 2.9 %collective-permute-start.12 = (f32[256,256]{1,0:T(8,128)S(1)}, f32[256,256]{1,0:T(8,128)S(1)}, u32[]{:S(2)}, u32[]{:S(2)}) collective-permute-start(f32[256,256]{1,0:T(8,128)S(1)} %fusion.16), channel_id=1, source_target_pairs={{0,1},{1,0},{2,3},{3,2},{4,5},{5,4},{6,7},{7,6},{8,9},{9,8},{10,11... | collective-permute-start | bytes 786440 | tf_op jit(solution)/shard_map/ppermute | solution.py:42
  91.7 0.4 fusion.26
  92.0 0.2 collective-permute-done.14
  92.2 0.4 fusion.34
  92.6 0.4 convolution_add_fusion.1
  93.0 2.3 %collective-permute-done.13 = f32[256,256]{1,0:T(8,128)S(1)} collective-permute-done((f32[256,256]{1,0:T(8,128)S(1)}, f32[256,256]{1,0:T(8,128)S(1)}, u32[]{:S(2)}, u32[]{:S(2)}) %collective-permute-start.13) | collective-permute-done | bytes 262176 | tf_op jit(solution)/shard_map/ppermute | solution.py:44
  95.3 0.4 fusion.19
  95.7 0.7 copy-done.2
  96.4 3.2 %fusion.65 = f32[256,2048]{1,0:T(8,128)} fusion(f32[256,256]{1,0:T(8,128)S(1)} %fusion.19, f32[256,2048]{1,0:T(8,128)S(1)} %copy-done), kind=kOutput, calls=%fused_computation.84 | convolution fusion | flops 1610612736 | bytes 4456448 | tf_op jit(solution)/shard_map/dot_general | solution.py:85
  99.7 0.0 reduce-scatter.2.cloned.1.call-update
  99.7 0.9 copy-done.3
  100.6 0.6 fusion.66
  101.2 0.8 reshape.14
  102.0 12.1 %all-to-all-start = ((f32[64,4,256]{2,1,0:T(4,128)}), f32[64,4,256]{2,1,0:T(4,128)S(1)}, u32[]{:S(2)}, u32[]{:S(2)}) async-start(f32[64,4,256]{2,1,0:T(4,128)} %reshape.14), calls=%async_computation.1 | async-start | bytes 524288 | tf_op jit(solution)/shard_map/all_to_all | solution.py:83
  114.1 0.5 slice.20
  115.2 10.4 %all-to-all-done = f32[64,4,256]{2,1,0:T(4,128)S(1)} async-done(((f32[64,4,256]{2,1,0:T(4,128)}), f32[64,4,256]{2,1,0:T(4,128)S(1)}, u32[]{:S(2)}, u32[]{:S(2)}) %all-to-all-start) | async-done | bytes 262176 | tf_op jit(solution)/shard_map/all_to_all | solution.py:83
  125.6 0.1 reduce_sum.9
  125.7 0.6 multiply_add_fusion
  126.3 19.3 %reduce-scatter.2.cloned.1.call-done = f32[256,256]{1,0:T(8,128)} async-done(((f32[256,2048]{1,0:T(8,128)}), f32[256,256]{1,0:T(8,128)}) %reduce-scatter.2.cloned.1.call-update) | async-done | bytes 262160 | tf_op jit(solution)/shard_map/reduce_scatter | solution.py:88
  (11 shorter events, 0.0 us)
Async XLA Ops:
  7.2 89.3 %copy-start = (f32[256,2048]{1,0:T(8,128)S(1)}, f32[256,2048]{1,0:T(8,128)}, u32[]{:S(2)}) copy-start(f32[256,2048]{1,0:T(8,128)} %param.7) | copy-start | bytes 6291460
  7.2 138.4 %reduce-scatter.2.cloned.1.call-start = ((), (), s32[]{:S(2)}) async-start(), calls=%async_computation.2 | async-start | bytes 2359296 | tf_op jit(solution)/shard_map/reduce_scatter | solution.py:88
  12.2 15.1 %copy-start.1 = (f32[4,64,20,64]{3,2,1,0:T(8,128)}, f32[4,64,20,64]{3,2,1,0:T(8,128)S(1)}, u32[]{:S(2)}) copy-start(f32[4,64,20,64]{3,2,1,0:T(8,128)S(1)} %fusion.2) | copy-start | bytes 3932164
  12.3 22.7 %collective-permute-start.3 = (f32[256,256]{1,0:T(8,128)}, f32[256,256]{1,0:T(8,128)}, u32[]{:S(2)}, u32[]{:S(2)}) collective-permute-start(f32[256,256]{1,0:T(8,128)} %param.4), channel_id=1, source_target_pairs={{0,62},{1,63},{2,4},{3,5},{4,2},{5,3},{6,8},{7,9},{8,6},{9,7},{10,... | collective-permute-start | bytes 786440 | tf_op jit(solution)/shard_map/ppermute | solution.py:45
  23.5 12.8 %collective-permute-start.2 = (f32[256,256]{1,0:T(8,128)}, f32[256,256]{1,0:T(8,128)}, u32[]{:S(2)}, u32[]{:S(2)}) collective-permute-start(f32[256,256]{1,0:T(8,128)} %param.4), channel_id=1, source_target_pairs={{0,2},{1,3},{2,0},{3,1},{4,6},{5,7},{6,4},{7,5},{8,10},{9,11},{10,... | collective-permute-start | bytes 786440 | tf_op jit(solution)/shard_map/ppermute | solution.py:41
  25.4 13.6 %collective-permute-start.1 = (f32[256,256]{1,0:T(8,128)}, f32[256,256]{1,0:T(8,128)}, u32[]{:S(2)}, u32[]{:S(2)}) collective-permute-start(f32[256,256]{1,0:T(8,128)} %param.4), channel_id=1, source_target_pairs={{0,63},{1,2},{2,1},{3,4},{4,3},{5,6},{6,5},{7,8},{8,7},{9,10},{10,... | collective-permute-start | bytes 786440 | tf_op jit(solution)/shard_map/ppermute | solution.py:44
  27.4 10.3 %collective-permute-start = (f32[256,256]{1,0:T(8,128)}, f32[256,256]{1,0:T(8,128)}, u32[]{:S(2)}, u32[]{:S(2)}) collective-permute-start(f32[256,256]{1,0:T(8,128)} %param.4), channel_id=1, source_target_pairs={{0,1},{1,0},{2,3},{3,2},{4,5},{5,4},{6,7},{7,6},{8,9},{9,8},{10,11... | collective-permute-start | bytes 786440 | tf_op jit(solution)/shard_map/ppermute | solution.py:42
  40.5 12.3 %collective-permute-start.6 = (f32[256,256]{1,0:T(8,128)S(1)}, f32[256,256]{1,0:T(8,128)S(1)}, u32[]{:S(2)}, u32[]{:S(2)}) collective-permute-start(f32[256,256]{1,0:T(8,128)S(1)} %get-tuple-element.6), channel_id=1, source_target_pairs={{0,2},{1,3},{2,0},{3,1},{4,6},{5,7},{6,4},{7,5},{8,10},{9,11},{10,... | collective-permute-start | bytes 786440 | tf_op jit(solution)/shard_map/ppermute | solution.py:41
  42.4 19.1 %collective-permute-start.5 = (f32[256,256]{1,0:T(8,128)S(1)}, f32[256,256]{1,0:T(8,128)S(1)}, u32[]{:S(2)}, u32[]{:S(2)}) collective-permute-start(f32[256,256]{1,0:T(8,128)S(1)} %get-tuple-element.6), channel_id=1, source_target_pairs={{0,63},{1,2},{2,1},{3,4},{4,3},{5,6},{6,5},{7,8},{8,7},{9,10},{10,... | collective-permute-start | bytes 786440 | tf_op jit(solution)/shard_map/ppermute | solution.py:44
  46.1 15.0 %collective-permute-start.4 = (f32[256,256]{1,0:T(8,128)S(1)}, f32[256,256]{1,0:T(8,128)S(1)}, u32[]{:S(2)}, u32[]{:S(2)}) collective-permute-start(f32[256,256]{1,0:T(8,128)S(1)} %get-tuple-element.6), channel_id=1, source_target_pairs={{0,1},{1,0},{2,3},{3,2},{4,5},{5,4},{6,7},{7,6},{8,9},{9,8},{10,11... | collective-permute-start | bytes 786440 | tf_op jit(solution)/shard_map/ppermute | solution.py:42
  48.4 12.3 %collective-permute-start.7 = (f32[256,256]{1,0:T(8,128)S(1)}, f32[256,256]{1,0:T(8,128)S(1)}, u32[]{:S(2)}, u32[]{:S(2)}) collective-permute-start(f32[256,256]{1,0:T(8,128)S(1)} %get-tuple-element.6), channel_id=1, source_target_pairs={{0,62},{1,63},{2,4},{3,5},{4,2},{5,3},{6,8},{7,9},{8,6},{9,7},{10,... | collective-permute-start | bytes 786440 | tf_op jit(solution)/shard_map/ppermute | solution.py:45
  62.9 12.2 %collective-permute-start.11 = (f32[256,256]{1,0:T(8,128)S(1)}, f32[256,256]{1,0:T(8,128)S(1)}, u32[]{:S(2)}, u32[]{:S(2)}) collective-permute-start(f32[256,256]{1,0:T(8,128)S(1)} %fusion.13), channel_id=1, source_target_pairs={{0,62},{1,63},{2,4},{3,5},{4,2},{5,3},{6,8},{7,9},{8,6},{9,7},{10,... | collective-permute-start | bytes 786440 | tf_op jit(solution)/shard_map/ppermute | solution.py:45
  66.8 9.0 %collective-permute-start.10 = (f32[256,256]{1,0:T(8,128)S(1)}, f32[256,256]{1,0:T(8,128)S(1)}, u32[]{:S(2)}, u32[]{:S(2)}) collective-permute-start(f32[256,256]{1,0:T(8,128)S(1)} %fusion.13), channel_id=1, source_target_pairs={{0,2},{1,3},{2,0},{3,1},{4,6},{5,7},{6,4},{7,5},{8,10},{9,11},{10,... | collective-permute-start | bytes 786440 | tf_op jit(solution)/shard_map/ppermute | solution.py:41
  69.1 9.8 %collective-permute-start.9 = (f32[256,256]{1,0:T(8,128)S(1)}, f32[256,256]{1,0:T(8,128)S(1)}, u32[]{:S(2)}, u32[]{:S(2)}) collective-permute-start(f32[256,256]{1,0:T(8,128)S(1)} %fusion.13), channel_id=1, source_target_pairs={{0,63},{1,2},{2,1},{3,4},{4,3},{5,6},{6,5},{7,8},{8,7},{9,10},{10,... | collective-permute-start | bytes 786440 | tf_op jit(solution)/shard_map/ppermute | solution.py:44
  71.8 4.5 %collective-permute-start.8 = (f32[256,256]{1,0:T(8,128)S(1)}, f32[256,256]{1,0:T(8,128)S(1)}, u32[]{:S(2)}, u32[]{:S(2)}) collective-permute-start(f32[256,256]{1,0:T(8,128)S(1)} %fusion.13), channel_id=1, source_target_pairs={{0,1},{1,0},{2,3},{3,2},{4,5},{5,4},{6,7},{7,6},{8,9},{9,8},{10,11... | collective-permute-start | bytes 786440 | tf_op jit(solution)/shard_map/ppermute | solution.py:42
  79.4 12.3 %collective-permute-start.15 = (f32[256,256]{1,0:T(8,128)S(1)}, f32[256,256]{1,0:T(8,128)S(1)}, u32[]{:S(2)}, u32[]{:S(2)}) collective-permute-start(f32[256,256]{1,0:T(8,128)S(1)} %fusion.16), channel_id=1, source_target_pairs={{0,62},{1,63},{2,4},{3,5},{4,2},{5,3},{6,8},{7,9},{8,6},{9,7},{10,... | collective-permute-start | bytes 786440 | tf_op jit(solution)/shard_map/ppermute | solution.py:45
  83.2 9.0 %collective-permute-start.14 = (f32[256,256]{1,0:T(8,128)S(1)}, f32[256,256]{1,0:T(8,128)S(1)}, u32[]{:S(2)}, u32[]{:S(2)}) collective-permute-start(f32[256,256]{1,0:T(8,128)S(1)} %fusion.16), channel_id=1, source_target_pairs={{0,2},{1,3},{2,0},{3,1},{4,6},{5,7},{6,4},{7,5},{8,10},{9,11},{10,... | collective-permute-start | bytes 786440 | tf_op jit(solution)/shard_map/ppermute | solution.py:41
  85.5 9.8 %collective-permute-start.13 = (f32[256,256]{1,0:T(8,128)S(1)}, f32[256,256]{1,0:T(8,128)S(1)}, u32[]{:S(2)}, u32[]{:S(2)}) collective-permute-start(f32[256,256]{1,0:T(8,128)S(1)} %fusion.16), channel_id=1, source_target_pairs={{0,63},{1,2},{2,1},{3,4},{4,3},{5,6},{6,5},{7,8},{8,7},{9,10},{10,... | collective-permute-start | bytes 786440 | tf_op jit(solution)/shard_map/ppermute | solution.py:44
  88.8 3.8 %collective-permute-start.12 = (f32[256,256]{1,0:T(8,128)S(1)}, f32[256,256]{1,0:T(8,128)S(1)}, u32[]{:S(2)}, u32[]{:S(2)}) collective-permute-start(f32[256,256]{1,0:T(8,128)S(1)} %fusion.16), channel_id=1, source_target_pairs={{0,1},{1,0},{2,3},{3,2},{4,5},{5,4},{6,7},{7,6},{8,9},{9,8},{10,11... | collective-permute-start | bytes 786440 | tf_op jit(solution)/shard_map/ppermute | solution.py:42
  95.7 0.7 copy-start.2
  99.7 0.9 copy-start.3
  102.0 23.6 %all-to-all-start = ((f32[64,4,256]{2,1,0:T(4,128)}), f32[64,4,256]{2,1,0:T(4,128)S(1)}, u32[]{:S(2)}, u32[]{:S(2)}) async-start(f32[64,4,256]{2,1,0:T(4,128)} %reshape.14), calls=%async_computation.1 | async-start | bytes 524288 | tf_op jit(solution)/shard_map/all_to_all | solution.py:83
Sparse Core Ops, SparseCore 0:
  99.8 45.7 reduce-scatter.1

commit v20 on v18

--- a/solution.py
+++ b/solution.py
@@ -45,7 +45,7 @@
         lax.ppermute(field, "wide", wrap_pairs),
     ]
     total = None
-    for idx in (2, 1, 3, 0, 4):
+    for idx in (2, 1, 0, 3, 4):
         term = jnp.dot(hdense[:, idx * rows:(idx + 1) * rows], pieces[idx], precision=HI,
                        preferred_element_type=jnp.float32)
         total = term if total is None else total + term

time: 153 us -> 154 us (level)
  waiting for transfers between devices: 43.8 us -> 49.7 us
  starting transfers between devices: 68.2 us -> 63.1 us
    ppermute x4, waiting for transfers between devices: 0.54 us -> 6.09 us  [apply_ham(): lax.ppermute(field, 'wide', near_pairs)]
    ppermute x4, starting transfers between devices: 13.2 us -> 7.86 us  [apply_ham(): lax.ppermute(field, 'wide', swap_pairs)]
  transfers between devices with their start and end apart: 18 -> 18, of which waited for: 9 -> 10; matrix products, arithmetic and copies ran while one was open for 6% -> 6% of each run, Pallas kernels for 0% -> 0%
where the time goes in v20:
time: 154 us; the launch traced here: 153 us
  starting transfers between devices  63.1 us (41%)
  waiting for transfers between devices  49.7 us (32%)
  matrix products  18.3 us (12%)
  between operations  15.1 us (10%)
  local copies, waits for them, and re-layouts  5.24 us (3%)
    ppermute x4, starting transfers between devices, apply_ham(): lax.ppermute(field, 'wide', wrap_pairs)  24.3 us
    reduce_scatter x1, waiting for transfers between devices, local(): rotated = lax.psum_scatter(rot_term, 'grp', scatter_dimension=1, tiled=True)  20.5 us
    all_to_all x1, starting transfers between devices, local(): gathered = lax.all_to_all(pieces, 'wide', 0, 0, tiled=True)  10.8 us
    all_to_all x1, waiting for transfers between devices, local(): gathered = lax.all_to_all(pieces, 'wide', 0, 0, tiled=True)  10.4 us
    ppermute x4, starting transfers between devices, apply_ham(): lax.ppermute(field, 'wide', cross_pairs)  10.3 us
    ppermute x4, starting transfers between devices, apply_ham(): lax.ppermute(field, 'wide', near_pairs)  9.95 us
    dot_general x20, matrix products, apply_ham(): jnp.dot(hdense[:, idx * rows:(idx + 1) * rows], pieces[idx], precision=HI...  8.67 us
    ppermute x4, waiting for transfers between devices, apply_ham(): lax.ppermute(field, 'wide', wrap_pairs)  8.2 us
  transfers between devices with their start and end apart: 18, of which 10 were waited for; matrix products, arithmetic and copies ran while one was open for 6% of the time, Pallas kernels for 0%

profile of v20, /device:TPU:6, one launch (start us, length us, event | category | flops | bytes accessed | tf_op | source)
XLA Modules:
  0.0 153.0 jit_solution(14161870454161252195)
XLA Ops:
  7.2 0.0 copy-start
  7.2 0.0 reduce-scatter.2.cloned.1.call-start
  7.3 0.8 fusion.58
  8.1 5.8 %fusion.2 = f32[4,64,20,64]{3,2,1,0:T(8,128)} fusion(f32[4,16,64,64]{3,2,1,0:T(8,128)} %param.5, s32[4,16]{1,0:T(4,128)S(1)} %fusion.58), kind=kOutput, calls=%fused_computation.2 | convolution fusion | flops 62915840 | bytes 2359552 | tf_op jit(solution)/shard_map/asp,asij->aipj/dot_general | solution.py:29
  13.9 2.2 %reshape.16 = f32[256,1280]{1,0:T(8,128)S(1)} reshape(f32[4,64,20,64]{3,2,1,0:T(8,128)} %fusion.2) | data formatting | bytes 2621440 | tf_op jit(solution)/shard_map/reshape | solution.py:30
  16.1 0.1 copy.12
  16.2 11.2 %collective-permute-start.3 = (f32[256,256]{1,0:T(8,128)}, f32[256,256]{1,0:T(8,128)S(1)}, u32[]{:S(2)}, u32[]{:S(2)}) collective-permute-start(f32[256,256]{1,0:T(8,128)} %param.4), channel_id=1, source_target_pairs={{0,62},{1,63},{2,4},{3,5},{4,2},{5,3},{6,8},{7,9},{8,6},{9,7},{10,... | collective-permute-start | bytes 786440 | tf_op jit(solution)/shard_map/ppermute | solution.py:45
  27.4 1.9 %collective-permute-start.2 = (f32[256,256]{1,0:T(8,128)}, f32[256,256]{1,0:T(8,128)S(1)}, u32[]{:S(2)}, u32[]{:S(2)}) collective-permute-start(f32[256,256]{1,0:T(8,128)} %param.4), channel_id=1, source_target_pairs={{0,63},{1,2},{2,1},{3,4},{4,3},{5,6},{6,5},{7,8},{8,7},{9,10},{10,... | collective-permute-start | bytes 786440 | tf_op jit(solution)/shard_map/ppermute | solution.py:44
  29.4 3.1 %collective-permute-start.1 = (f32[256,256]{1,0:T(8,128)}, f32[256,256]{1,0:T(8,128)S(1)}, u32[]{:S(2)}, u32[]{:S(2)}) collective-permute-start(f32[256,256]{1,0:T(8,128)} %param.4), channel_id=1, source_target_pairs={{0,2},{1,3},{2,0},{3,1},{4,6},{5,7},{6,4},{7,5},{8,10},{9,11},{10,... | collective-permute-start | bytes 786440 | tf_op jit(solution)/shard_map/ppermute | solution.py:41
  32.5 1.9 %collective-permute-start = (f32[256,256]{1,0:T(8,128)}, f32[256,256]{1,0:T(8,128)S(1)}, u32[]{:S(2)}, u32[]{:S(2)}) collective-permute-start(f32[256,256]{1,0:T(8,128)} %param.4), channel_id=1, source_target_pairs={{0,1},{1,0},{2,3},{3,2},{4,5},{5,4},{6,7},{7,6},{8,9},{9,8},{10,11... | collective-permute-start | bytes 786440 | tf_op jit(solution)/shard_map/ppermute | solution.py:42
  34.4 1.3 fusion.48
  35.7 0.0 copy-start.3
  35.7 0.0 collective-permute-done.3
  35.7 0.4 fusion.24
  36.1 1.3 collective-permute-done.2
  37.5 0.4 fusion.32
  37.8 0.4 convolution_add_fusion.7
  38.2 2.5 %collective-permute-done.1 = f32[256,256]{1,0:T(8,128)S(1)} collective-permute-done((f32[256,256]{1,0:T(8,128)}, f32[256,256]{1,0:T(8,128)S(1)}, u32[]{:S(2)}, u32[]{:S(2)}) %collective-permute-start.1) | collective-permute-done | bytes 262176 | tf_op jit(solution)/shard_map/ppermute | solution.py:41
  40.7 0.4 broadcast_multiply_fusion
  41.1 2.0 %collective-permute-start.6 = (f32[256,256]{1,0:T(8,128)S(1)}, f32[256,256]{1,0:T(8,128)S(1)}, u32[]{:S(2)}, u32[]{:S(2)}) collective-permute-start(f32[256,256]{1,0:T(8,128)S(1)} %get-tuple-element.6), channel_id=1, source_target_pairs={{0,63},{1,2},{2,1},{3,4},{4,3},{5,6},{6,5},{7,8},{8,7},{9,10},{10,... | collective-permute-start | bytes 786440 | tf_op jit(solution)/shard_map/ppermute | solution.py:44
  43.1 2.1 %collective-permute-start.5 = (f32[256,256]{1,0:T(8,128)S(1)}, f32[256,256]{1,0:T(8,128)S(1)}, u32[]{:S(2)}, u32[]{:S(2)}) collective-permute-start(f32[256,256]{1,0:T(8,128)S(1)} %get-tuple-element.6), channel_id=1, source_target_pairs={{0,2},{1,3},{2,0},{3,1},{4,6},{5,7},{6,4},{7,5},{8,10},{9,11},{10,... | collective-permute-start | bytes 786440 | tf_op jit(solution)/shard_map/ppermute | solution.py:41
  45.3 1.9 %collective-permute-start.4 = (f32[256,256]{1,0:T(8,128)S(1)}, f32[256,256]{1,0:T(8,128)S(1)}, u32[]{:S(2)}, u32[]{:S(2)}) collective-permute-start(f32[256,256]{1,0:T(8,128)S(1)} %get-tuple-element.6), channel_id=1, source_target_pairs={{0,1},{1,0},{2,3},{3,2},{4,5},{5,4},{6,7},{7,6},{8,9},{9,8},{10,11... | collective-permute-start | bytes 786440 | tf_op jit(solution)/shard_map/ppermute | solution.py:42
  47.2 5.8 %collective-permute-start.7 = (f32[256,256]{1,0:T(8,128)S(1)}, f32[256,256]{1,0:T(8,128)S(1)}, u32[]{:S(2)}, u32[]{:S(2)}) collective-permute-start(f32[256,256]{1,0:T(8,128)S(1)} %get-tuple-element.6), channel_id=1, source_target_pairs={{0,62},{1,63},{2,4},{3,5},{4,2},{5,3},{6,8},{7,9},{8,6},{9,7},{10,... | collective-permute-start | bytes 786440 | tf_op jit(solution)/shard_map/ppermute | solution.py:45
  53.0 0.4 fusion.46
  53.4 0.4 fusion.30
  53.8 6.1 %collective-permute-done.7 = f32[256,256]{1,0:T(8,128)S(1)} collective-permute-done((f32[256,256]{1,0:T(8,128)S(1)}, f32[256,256]{1,0:T(8,128)S(1)}, u32[]{:S(2)}, u32[]{:S(2)}) %collective-permute-start.7) | collective-permute-done | bytes 262176 | tf_op jit(solution)/shard_map/ppermute | solution.py:45
  59.9 0.4 fusion.22
  60.3 0.4 convolution_add_fusion.5
  60.7 0.4 fusion.13
  61.1 5.3 %collective-permute-start.11 = (f32[256,256]{1,0:T(8,128)S(1)}, f32[256,256]{1,0:T(8,128)S(1)}, u32[]{:S(2)}, u32[]{:S(2)}) collective-permute-start(f32[256,256]{1,0:T(8,128)S(1)} %fusion.13), channel_id=1, source_target_pairs={{0,62},{1,63},{2,4},{3,5},{4,2},{5,3},{6,8},{7,9},{8,6},{9,7},{10,... | collective-permute-start | bytes 786440 | tf_op jit(solution)/shard_map/ppermute | solution.py:45
  66.5 1.9 %collective-permute-start.10 = (f32[256,256]{1,0:T(8,128)S(1)}, f32[256,256]{1,0:T(8,128)S(1)}, u32[]{:S(2)}, u32[]{:S(2)}) collective-permute-start(f32[256,256]{1,0:T(8,128)S(1)} %fusion.13), channel_id=1, source_target_pairs={{0,63},{1,2},{2,1},{3,4},{4,3},{5,6},{6,5},{7,8},{8,7},{9,10},{10,... | collective-permute-start | bytes 786440 | tf_op jit(solution)/shard_map/ppermute | solution.py:44
  68.4 0.4 fusion.44
  68.8 2.4 %collective-permute-start.9 = (f32[256,256]{1,0:T(8,128)S(1)}, f32[256,256]{1,0:T(8,128)S(1)}, u32[]{:S(2)}, u32[]{:S(2)}) collective-permute-start(f32[256,256]{1,0:T(8,128)S(1)} %fusion.13), channel_id=1, source_target_pairs={{0,2},{1,3},{2,0},{3,1},{4,6},{5,7},{6,4},{7,5},{8,10},{9,11},{10,... | collective-permute-start | bytes 786440 | tf_op jit(solution)/shard_map/ppermute | solution.py:41
  71.2 1.9 %collective-permute-start.8 = (f32[256,256]{1,0:T(8,128)S(1)}, f32[256,256]{1,0:T(8,128)S(1)}, u32[]{:S(2)}, u32[]{:S(2)}) collective-permute-start(f32[256,256]{1,0:T(8,128)S(1)} %fusion.13), channel_id=1, source_target_pairs={{0,1},{1,0},{2,3},{3,2},{4,5},{5,4},{6,7},{7,6},{8,9},{9,8},{10,11... | collective-permute-start | bytes 786440 | tf_op jit(solution)/shard_map/ppermute | solution.py:42
  73.1 0.4 fusion.20
  73.5 2.7 %collective-permute-done.10 = f32[256,256]{1,0:T(8,128)S(1)} collective-permute-done((f32[256,256]{1,0:T(8,128)S(1)}, f32[256,256]{1,0:T(8,128)S(1)}, u32[]{:S(2)}, u32[]{:S(2)}) %collective-permute-start.10) | collective-permute-done | bytes 262176 | tf_op jit(solution)/shard_map/ppermute | solution.py:44
  76.3 0.4 fusion.28
  76.7 0.4 convolution_add_fusion.3
  77.1 1.8 %collective-permute-done.9 = f32[256,256]{1,0:T(8,128)S(1)} collective-permute-done((f32[256,256]{1,0:T(8,128)S(1)}, f32[256,256]{1,0:T(8,128)S(1)}, u32[]{:S(2)}, u32[]{:S(2)}) %collective-permute-start.9) | collective-permute-done | bytes 262176 | tf_op jit(solution)/shard_map/ppermute | solution.py:41
  78.8 0.4 fusion.16
  79.3 1.9 %collective-permute-start.15 = (f32[256,256]{1,0:T(8,128)S(1)}, f32[256,256]{1,0:T(8,128)S(1)}, u32[]{:S(2)}, u32[]{:S(2)}) collective-permute-start(f32[256,256]{1,0:T(8,128)S(1)} %fusion.16), channel_id=1, source_target_pairs={{0,62},{1,63},{2,4},{3,5},{4,2},{5,3},{6,8},{7,9},{8,6},{9,7},{10,... | collective-permute-start | bytes 786440 | tf_op jit(solution)/shard_map/ppermute | solution.py:45
  81.2 4.4 %collective-permute-start.14 = (f32[256,256]{1,0:T(8,128)S(1)}, f32[256,256]{1,0:T(8,128)S(1)}, u32[]{:S(2)}, u32[]{:S(2)}) collective-permute-start(f32[256,256]{1,0:T(8,128)S(1)} %fusion.16), channel_id=1, source_target_pairs={{0,63},{1,2},{2,1},{3,4},{4,3},{5,6},{6,5},{7,8},{8,7},{9,10},{10,... | collective-permute-start | bytes 786440 | tf_op jit(solution)/shard_map/ppermute | solution.py:44
  85.6 0.4 fusion.50
  86.0 2.3 %collective-permute-start.13 = (f32[256,256]{1,0:T(8,128)S(1)}, f32[256,256]{1,0:T(8,128)S(1)}, u32[]{:S(2)}, u32[]{:S(2)}) collective-permute-start(f32[256,256]{1,0:T(8,128)S(1)} %fusion.16), channel_id=1, source_target_pairs={{0,2},{1,3},{2,0},{3,1},{4,6},{5,7},{6,4},{7,5},{8,10},{9,11},{10,... | collective-permute-start | bytes 786440 | tf_op jit(solution)/shard_map/ppermute | solution.py:41
  88.3 2.1 %collective-permute-start.12 = (f32[256,256]{1,0:T(8,128)S(1)}, f32[256,256]{1,0:T(8,128)S(1)}, u32[]{:S(2)}, u32[]{:S(2)}) collective-permute-start(f32[256,256]{1,0:T(8,128)S(1)} %fusion.16), channel_id=1, source_target_pairs={{0,1},{1,0},{2,3},{3,2},{4,5},{5,4},{6,7},{7,6},{8,9},{9,8},{10,11... | collective-permute-start | bytes 786440 | tf_op jit(solution)/shard_map/ppermute | solution.py:42
  90.4 2.1 %collective-permute-done.15 = f32[256,256]{1,0:T(8,128)S(1)} collective-permute-done((f32[256,256]{1,0:T(8,128)S(1)}, f32[256,256]{1,0:T(8,128)S(1)}, u32[]{:S(2)}, u32[]{:S(2)}) %collective-permute-start.15) | collective-permute-done | bytes 262176 | tf_op jit(solution)/shard_map/ppermute | solution.py:45
  92.5 0.4 fusion.26
  92.9 0.4 collective-permute-done.14
  93.3 0.4 fusion.34
  93.7 0.4 convolution_add_fusion.1
  94.1 1.8 %collective-permute-done.13 = f32[256,256]{1,0:T(8,128)S(1)} collective-permute-done((f32[256,256]{1,0:T(8,128)S(1)}, f32[256,256]{1,0:T(8,128)S(1)}, u32[]{:S(2)}, u32[]{:S(2)}) %collective-permute-start.13) | collective-permute-done | bytes 262176 | tf_op jit(solution)/shard_map/ppermute | solution.py:41
  96.0 0.4 fusion.19
  96.4 0.7 copy-done.1
  97.1 3.2 %fusion.65 = f32[256,2048]{1,0:T(8,128)} fusion(f32[256,256]{1,0:T(8,128)S(1)} %fusion.19, f32[256,2048]{1,0:T(8,128)S(1)} %copy-done), kind=kOutput, calls=%fused_computation.84 | convolution fusion | flops 1610612736 | bytes 4456448 | tf_op jit(solution)/shard_map/dot_general | solution.py:85
  100.3 0.0 reduce-scatter.2.cloned.1.call-update
  100.4 0.9 copy-done.2
  101.3 0.6 fusion.66
  101.9 0.8 reshape.14
  102.6 10.8 %all-to-all-start = ((f32[64,4,256]{2,1,0:T(4,128)}), f32[64,4,256]{2,1,0:T(4,128)S(1)}, u32[]{:S(2)}, u32[]{:S(2)}) async-start(f32[64,4,256]{2,1,0:T(4,128)} %reshape.14), calls=%async_computation.1 | async-start | bytes 524288 | tf_op jit(solution)/shard_map/all_to_all | solution.py:83
  113.4 0.5 slice.20
  114.6 10.4 %all-to-all-done = f32[64,4,256]{2,1,0:T(4,128)S(1)} async-done(((f32[64,4,256]{2,1,0:T(4,128)}), f32[64,4,256]{2,1,0:T(4,128)S(1)}, u32[]{:S(2)}, u32[]{:S(2)}) %all-to-all-start) | async-done | bytes 262176 | tf_op jit(solution)/shard_map/all_to_all | solution.py:83
  125.0 0.1 reduce_sum.9
  125.1 0.6 multiply_add_fusion
  125.7 20.5 %reduce-scatter.2.cloned.1.call-done = f32[256,256]{1,0:T(8,128)} async-done(((f32[256,2048]{1,0:T(8,128)}), f32[256,256]{1,0:T(8,128)}) %reduce-scatter.2.cloned.1.call-update) | async-done | bytes 262160 | tf_op jit(solution)/shard_map/reduce_scatter | solution.py:88
  (12 shorter events, 0.0 us)
Async XLA Ops:
  7.2 89.9 %copy-start = (f32[256,2048]{1,0:T(8,128)S(1)}, f32[256,2048]{1,0:T(8,128)}, u32[]{:S(2)}) copy-start(f32[256,2048]{1,0:T(8,128)} %param.7) | copy-start | bytes 6291460
  7.2 139.0 %reduce-scatter.2.cloned.1.call-start = ((), (), s32[]{:S(2)}) async-start(), calls=%async_computation.2 | async-start | bytes 2359296 | tf_op jit(solution)/shard_map/reduce_scatter | solution.py:88
  16.2 19.5 %collective-permute-start.3 = (f32[256,256]{1,0:T(8,128)}, f32[256,256]{1,0:T(8,128)S(1)}, u32[]{:S(2)}, u32[]{:S(2)}) collective-permute-start(f32[256,256]{1,0:T(8,128)} %param.4), channel_id=1, source_target_pairs={{0,62},{1,63},{2,4},{3,5},{4,2},{5,3},{6,8},{7,9},{8,6},{9,7},{10,... | collective-permute-start | bytes 786440 | tf_op jit(solution)/shard_map/ppermute | solution.py:45
  27.4 10.0 %collective-permute-start.2 = (f32[256,256]{1,0:T(8,128)}, f32[256,256]{1,0:T(8,128)S(1)}, u32[]{:S(2)}, u32[]{:S(2)}) collective-permute-start(f32[256,256]{1,0:T(8,128)} %param.4), channel_id=1, source_target_pairs={{0,63},{1,2},{2,1},{3,4},{4,3},{5,6},{6,5},{7,8},{8,7},{9,10},{10,... | collective-permute-start | bytes 786440 | tf_op jit(solution)/shard_map/ppermute | solution.py:44
  29.4 11.3 %collective-permute-start.1 = (f32[256,256]{1,0:T(8,128)}, f32[256,256]{1,0:T(8,128)S(1)}, u32[]{:S(2)}, u32[]{:S(2)}) collective-permute-start(f32[256,256]{1,0:T(8,128)} %param.4), channel_id=1, source_target_pairs={{0,2},{1,3},{2,0},{3,1},{4,6},{5,7},{6,4},{7,5},{8,10},{9,11},{10,... | collective-permute-start | bytes 786440 | tf_op jit(solution)/shard_map/ppermute | solution.py:41
  32.5 5.4 %collective-permute-start = (f32[256,256]{1,0:T(8,128)}, f32[256,256]{1,0:T(8,128)S(1)}, u32[]{:S(2)}, u32[]{:S(2)}) collective-permute-start(f32[256,256]{1,0:T(8,128)} %param.4), channel_id=1, source_target_pairs={{0,1},{1,0},{2,3},{3,2},{4,5},{5,4},{6,7},{7,6},{8,9},{9,8},{10,11... | collective-permute-start | bytes 786440 | tf_op jit(solution)/shard_map/ppermute | solution.py:42
  35.7 5.0 %copy-start.3 = (f32[256,256]{1,0:T(8,128)S(1)}, f32[256,256]{1,0:T(8,128)}, u32[]{:S(2)}) copy-start(f32[256,256]{1,0:T(8,128)} %param.4) | copy-start | bytes 786436
  41.1 12.3 %collective-permute-start.6 = (f32[256,256]{1,0:T(8,128)S(1)}, f32[256,256]{1,0:T(8,128)S(1)}, u32[]{:S(2)}, u32[]{:S(2)}) collective-permute-start(f32[256,256]{1,0:T(8,128)S(1)} %get-tuple-element.6), channel_id=1, source_target_pairs={{0,63},{1,2},{2,1},{3,4},{4,3},{5,6},{6,5},{7,8},{8,7},{9,10},{10,... | collective-permute-start | bytes 786440 | tf_op jit(solution)/shard_map/ppermute | solution.py:44
  43.1 17.6 %collective-permute-start.5 = (f32[256,256]{1,0:T(8,128)S(1)}, f32[256,256]{1,0:T(8,128)S(1)}, u32[]{:S(2)}, u32[]{:S(2)}) collective-permute-start(f32[256,256]{1,0:T(8,128)S(1)} %get-tuple-element.6), channel_id=1, source_target_pairs={{0,2},{1,3},{2,0},{3,1},{4,6},{5,7},{6,4},{7,5},{8,10},{9,11},{10,... | collective-permute-start | bytes 786440 | tf_op jit(solution)/shard_map/ppermute | solution.py:41
  45.3 15.0 %collective-permute-start.4 = (f32[256,256]{1,0:T(8,128)S(1)}, f32[256,256]{1,0:T(8,128)S(1)}, u32[]{:S(2)}, u32[]{:S(2)}) collective-permute-start(f32[256,256]{1,0:T(8,128)S(1)} %get-tuple-element.6), channel_id=1, source_target_pairs={{0,1},{1,0},{2,3},{3,2},{4,5},{5,4},{6,7},{7,6},{8,9},{9,8},{10,11... | collective-permute-start | bytes 786440 | tf_op jit(solution)/shard_map/ppermute | solution.py:42
  47.2 12.7 %collective-permute-start.7 = (f32[256,256]{1,0:T(8,128)S(1)}, f32[256,256]{1,0:T(8,128)S(1)}, u32[]{:S(2)}, u32[]{:S(2)}) collective-permute-start(f32[256,256]{1,0:T(8,128)S(1)} %get-tuple-element.6), channel_id=1, source_target_pairs={{0,62},{1,63},{2,4},{3,5},{4,2},{5,3},{6,8},{7,9},{8,6},{9,7},{10,... | collective-permute-start | bytes 786440 | tf_op jit(solution)/shard_map/ppermute | solution.py:45
  61.1 12.0 %collective-permute-start.11 = (f32[256,256]{1,0:T(8,128)S(1)}, f32[256,256]{1,0:T(8,128)S(1)}, u32[]{:S(2)}, u32[]{:S(2)}) collective-permute-start(f32[256,256]{1,0:T(8,128)S(1)} %fusion.13), channel_id=1, source_target_pairs={{0,62},{1,63},{2,4},{3,5},{4,2},{5,3},{6,8},{7,9},{8,6},{9,7},{10,... | collective-permute-start | bytes 786440 | tf_op jit(solution)/shard_map/ppermute | solution.py:45
  66.5 9.8 %collective-permute-start.10 = (f32[256,256]{1,0:T(8,128)S(1)}, f32[256,256]{1,0:T(8,128)S(1)}, u32[]{:S(2)}, u32[]{:S(2)}) collective-permute-start(f32[256,256]{1,0:T(8,128)S(1)} %fusion.13), channel_id=1, source_target_pairs={{0,63},{1,2},{2,1},{3,4},{4,3},{5,6},{6,5},{7,8},{8,7},{9,10},{10,... | collective-permute-start | bytes 786440 | tf_op jit(solution)/shard_map/ppermute | solution.py:44
  68.8 10.1 %collective-permute-start.9 = (f32[256,256]{1,0:T(8,128)S(1)}, f32[256,256]{1,0:T(8,128)S(1)}, u32[]{:S(2)}, u32[]{:S(2)}) collective-permute-start(f32[256,256]{1,0:T(8,128)S(1)} %fusion.13), channel_id=1, source_target_pairs={{0,2},{1,3},{2,0},{3,1},{4,6},{5,7},{6,4},{7,5},{8,10},{9,11},{10,... | collective-permute-start | bytes 786440 | tf_op jit(solution)/shard_map/ppermute | solution.py:41
  71.2 5.5 %collective-permute-start.8 = (f32[256,256]{1,0:T(8,128)S(1)}, f32[256,256]{1,0:T(8,128)S(1)}, u32[]{:S(2)}, u32[]{:S(2)}) collective-permute-start(f32[256,256]{1,0:T(8,128)S(1)} %fusion.13), channel_id=1, source_target_pairs={{0,1},{1,0},{2,3},{3,2},{4,5},{5,4},{6,7},{7,6},{8,9},{9,8},{10,11... | collective-permute-start | bytes 786440 | tf_op jit(solution)/shard_map/ppermute | solution.py:42
  79.3 13.2 %collective-permute-start.15 = (f32[256,256]{1,0:T(8,128)S(1)}, f32[256,256]{1,0:T(8,128)S(1)}, u32[]{:S(2)}, u32[]{:S(2)}) collective-permute-start(f32[256,256]{1,0:T(8,128)S(1)} %fusion.16), channel_id=1, source_target_pairs={{0,62},{1,63},{2,4},{3,5},{4,2},{5,3},{6,8},{7,9},{8,6},{9,7},{10,... | collective-permute-start | bytes 786440 | tf_op jit(solution)/shard_map/ppermute | solution.py:45
  81.2 12.1 %collective-permute-start.14 = (f32[256,256]{1,0:T(8,128)S(1)}, f32[256,256]{1,0:T(8,128)S(1)}, u32[]{:S(2)}, u32[]{:S(2)}) collective-permute-start(f32[256,256]{1,0:T(8,128)S(1)} %fusion.16), channel_id=1, source_target_pairs={{0,63},{1,2},{2,1},{3,4},{4,3},{5,6},{6,5},{7,8},{8,7},{9,10},{10,... | collective-permute-start | bytes 786440 | tf_op jit(solution)/shard_map/ppermute | solution.py:44
  86.0 10.0 %collective-permute-start.13 = (f32[256,256]{1,0:T(8,128)S(1)}, f32[256,256]{1,0:T(8,128)S(1)}, u32[]{:S(2)}, u32[]{:S(2)}) collective-permute-start(f32[256,256]{1,0:T(8,128)S(1)} %fusion.16), channel_id=1, source_target_pairs={{0,2},{1,3},{2,0},{3,1},{4,6},{5,7},{6,4},{7,5},{8,10},{9,11},{10,... | collective-permute-start | bytes 786440 | tf_op jit(solution)/shard_map/ppermute | solution.py:41
  88.3 5.4 %collective-permute-start.12 = (f32[256,256]{1,0:T(8,128)S(1)}, f32[256,256]{1,0:T(8,128)S(1)}, u32[]{:S(2)}, u32[]{:S(2)}) collective-permute-start(f32[256,256]{1,0:T(8,128)S(1)} %fusion.16), channel_id=1, source_target_pairs={{0,1},{1,0},{2,3},{3,2},{4,5},{5,4},{6,7},{7,6},{8,9},{9,8},{10,11... | collective-permute-start | bytes 786440 | tf_op jit(solution)/shard_map/ppermute | solution.py:42
  96.4 0.7 copy-start.1
  100.3 0.9 copy-start.2
  102.6 22.3 %all-to-all-start = ((f32[64,4,256]{2,1,0:T(4,128)}), f32[64,4,256]{2,1,0:T(4,128)S(1)}, u32[]{:S(2)}, u32[]{:S(2)}) async-start(f32[64,4,256]{2,1,0:T(4,128)} %reshape.14), calls=%async_computation.1 | async-start | bytes 524288 | tf_op jit(solution)/shard_map/all_to_all | solution.py:83
Sparse Core Ops, SparseCore 0:
  100.5 45.6 reduce-scatter.1

commit v21 on v18

--- a/solution.py
+++ b/solution.py
@@ -83,7 +83,7 @@
     gathered = lax.all_to_all(pieces, "wide", 0, 0, tiled=True)
     correlation = jnp.sum(gathered, axis=0) / total_rows + 0.0 * probe_h[0, 0]
     rot_term = jnp.dot(
-        current, rotation, precision=HI, preferred_element_type=jnp.float32
+        current, rotation, precision=lax.Precision.HIGH, preferred_element_type=jnp.float32
     )
     rotated = lax.psum_scatter(rot_term, "grp", scatter_dimension=1, tiled=True)
     return (rotated, correlation)

time: 153 us -> 152 us (level)
  no operation moved by 1% of the time
where the time goes in v21:
time: 152 us; the launch traced here: 151 us
  starting transfers between devices  68.2 us (45%)
  waiting for transfers between devices  43.7 us (29%)
  matrix products  17.5 us (12%)
  between operations  15.1 us (10%)
  local copies, waits for them, and re-layouts  5.24 us (3%)
  other arithmetic  1.53 us (1%)
    ppermute x4, starting transfers between devices, apply_ham(): lax.ppermute(field, 'wide', wrap_pairs)  23.9 us
    reduce_scatter x1, waiting for transfers between devices, local(): rotated = lax.psum_scatter(rot_term, 'grp', scatter_dimension=1, tiled=True)  20.6 us
    ppermute x4, starting transfers between devices, apply_ham(): lax.ppermute(field, 'wide', swap_pairs)  13.2 us
    all_to_all x1, starting transfers between devices, local(): gathered = lax.all_to_all(pieces, 'wide', 0, 0, tiled=True)  12.2 us
    all_to_all x1, waiting for transfers between devices, local(): gathered = lax.all_to_all(pieces, 'wide', 0, 0, tiled=True)  10.4 us
    ppermute x4, starting transfers between devices, apply_ham(): lax.ppermute(field, 'wide', cross_pairs)  10.2 us
    ppermute x4, starting transfers between devices, apply_ham(): lax.ppermute(field, 'wide', near_pairs)  8.7 us
    dot_general x20, matrix products, apply_ham(): jnp.dot(hdense[:, idx * rows:(idx + 1) * rows], pieces[idx], precision=HI...  8.68 us
  transfers between devices with their start and end apart: 18, of which 9 were waited for; matrix products, arithmetic and copies ran while one was open for 6% of the time, Pallas kernels for 0%

profile of v21, /device:TPU:6, one launch (start us, length us, event | category | flops | bytes accessed | tf_op | source)
XLA Modules:
  0.0 151.3 jit_solution(10245876030148027864)
XLA Ops:
  7.2 0.0 copy-start
  7.2 0.0 reduce-scatter.2.cloned.1.call-start
  7.3 0.8 fusion.58
  8.1 5.8 %fusion.2 = f32[4,64,20,64]{3,2,1,0:T(8,128)} fusion(f32[4,16,64,64]{3,2,1,0:T(8,128)} %param.5, s32[4,16]{1,0:T(4,128)S(1)} %fusion.58), kind=kOutput, calls=%fused_computation.2 | convolution fusion | flops 62915840 | bytes 2359552 | tf_op jit(solution)/shard_map/asp,asij->aipj/dot_general | solution.py:29
  13.9 2.2 %reshape.16 = f32[256,1280]{1,0:T(8,128)S(1)} reshape(f32[4,64,20,64]{3,2,1,0:T(8,128)} %fusion.2) | data formatting | bytes 2621440 | tf_op jit(solution)/shard_map/reshape | solution.py:30
  16.1 0.1 copy.12
  16.2 11.2 %collective-permute-start.3 = (f32[256,256]{1,0:T(8,128)}, f32[256,256]{1,0:T(8,128)S(1)}, u32[]{:S(2)}, u32[]{:S(2)}) collective-permute-start(f32[256,256]{1,0:T(8,128)} %param.4), channel_id=1, source_target_pairs={{0,62},{1,63},{2,4},{3,5},{4,2},{5,3},{6,8},{7,9},{8,6},{9,7},{10,... | collective-permute-start | bytes 786440 | tf_op jit(solution)/shard_map/ppermute | solution.py:45
  27.4 1.9 %collective-permute-start.2 = (f32[256,256]{1,0:T(8,128)}, f32[256,256]{1,0:T(8,128)S(1)}, u32[]{:S(2)}, u32[]{:S(2)}) collective-permute-start(f32[256,256]{1,0:T(8,128)} %param.4), channel_id=1, source_target_pairs={{0,2},{1,3},{2,0},{3,1},{4,6},{5,7},{6,4},{7,5},{8,10},{9,11},{10,... | collective-permute-start | bytes 786440 | tf_op jit(solution)/shard_map/ppermute | solution.py:41
  29.4 1.9 %collective-permute-start.1 = (f32[256,256]{1,0:T(8,128)}, f32[256,256]{1,0:T(8,128)S(1)}, u32[]{:S(2)}, u32[]{:S(2)}) collective-permute-start(f32[256,256]{1,0:T(8,128)} %param.4), channel_id=1, source_target_pairs={{0,63},{1,2},{2,1},{3,4},{4,3},{5,6},{6,5},{7,8},{8,7},{9,10},{10,... | collective-permute-start | bytes 786440 | tf_op jit(solution)/shard_map/ppermute | solution.py:44
  31.3 4.0 %collective-permute-start = (f32[256,256]{1,0:T(8,128)}, f32[256,256]{1,0:T(8,128)S(1)}, u32[]{:S(2)}, u32[]{:S(2)}) collective-permute-start(f32[256,256]{1,0:T(8,128)} %param.4), channel_id=1, source_target_pairs={{0,1},{1,0},{2,3},{3,2},{4,5},{5,4},{6,7},{7,6},{8,9},{9,8},{10,11... | collective-permute-start | bytes 786440 | tf_op jit(solution)/shard_map/ppermute | solution.py:42
  35.3 1.3 fusion.48
  36.7 0.0 copy-start.3
  36.7 0.0 collective-permute-done.3
  36.7 0.4 fusion.24
  37.1 0.2 collective-permute-done.2
  37.3 0.4 fusion.32
  37.7 0.4 convolution_add_fusion.7
  38.1 1.3 collective-permute-done.1
  39.4 0.4 broadcast_multiply_fusion
  39.8 2.9 %collective-permute-start.6 = (f32[256,256]{1,0:T(8,128)S(1)}, f32[256,256]{1,0:T(8,128)S(1)}, u32[]{:S(2)}, u32[]{:S(2)}) collective-permute-start(f32[256,256]{1,0:T(8,128)S(1)} %get-tuple-element.6), channel_id=1, source_target_pairs={{0,2},{1,3},{2,0},{3,1},{4,6},{5,7},{6,4},{7,5},{8,10},{9,11},{10,... | collective-permute-start | bytes 786440 | tf_op jit(solution)/shard_map/ppermute | solution.py:41
  42.7 1.9 %collective-permute-start.5 = (f32[256,256]{1,0:T(8,128)S(1)}, f32[256,256]{1,0:T(8,128)S(1)}, u32[]{:S(2)}, u32[]{:S(2)}) collective-permute-start(f32[256,256]{1,0:T(8,128)S(1)} %get-tuple-element.6), channel_id=1, source_target_pairs={{0,63},{1,2},{2,1},{3,4},{4,3},{5,6},{6,5},{7,8},{8,7},{9,10},{10,... | collective-permute-start | bytes 786440 | tf_op jit(solution)/shard_map/ppermute | solution.py:44
  44.7 3.0 %collective-permute-start.4 = (f32[256,256]{1,0:T(8,128)S(1)}, f32[256,256]{1,0:T(8,128)S(1)}, u32[]{:S(2)}, u32[]{:S(2)}) collective-permute-start(f32[256,256]{1,0:T(8,128)S(1)} %get-tuple-element.6), channel_id=1, source_target_pairs={{0,1},{1,0},{2,3},{3,2},{4,5},{5,4},{6,7},{7,6},{8,9},{9,8},{10,11... | collective-permute-start | bytes 786440 | tf_op jit(solution)/shard_map/ppermute | solution.py:42
  47.7 5.0 %collective-permute-start.7 = (f32[256,256]{1,0:T(8,128)S(1)}, f32[256,256]{1,0:T(8,128)S(1)}, u32[]{:S(2)}, u32[]{:S(2)}) collective-permute-start(f32[256,256]{1,0:T(8,128)S(1)} %get-tuple-element.6), channel_id=1, source_target_pairs={{0,62},{1,63},{2,4},{3,5},{4,2},{5,3},{6,8},{7,9},{8,6},{9,7},{10,... | collective-permute-start | bytes 786440 | tf_op jit(solution)/shard_map/ppermute | solution.py:45
  52.7 0.4 fusion.46
  53.1 0.4 fusion.30
  53.5 6.4 %collective-permute-done.7 = f32[256,256]{1,0:T(8,128)S(1)} collective-permute-done((f32[256,256]{1,0:T(8,128)S(1)}, f32[256,256]{1,0:T(8,128)S(1)}, u32[]{:S(2)}, u32[]{:S(2)}) %collective-permute-start.7) | collective-permute-done | bytes 262176 | tf_op jit(solution)/shard_map/ppermute | solution.py:45
  59.9 0.4 fusion.22
  60.3 0.4 convolution_add_fusion.5
  60.7 0.4 fusion.13
  61.1 5.0 %collective-permute-start.11 = (f32[256,256]{1,0:T(8,128)S(1)}, f32[256,256]{1,0:T(8,128)S(1)}, u32[]{:S(2)}, u32[]{:S(2)}) collective-permute-start(f32[256,256]{1,0:T(8,128)S(1)} %fusion.13), channel_id=1, source_target_pairs={{0,62},{1,63},{2,4},{3,5},{4,2},{5,3},{6,8},{7,9},{8,6},{9,7},{10,... | collective-permute-start | bytes 786440 | tf_op jit(solution)/shard_map/ppermute | solution.py:45
  66.2 1.9 %collective-permute-start.10 = (f32[256,256]{1,0:T(8,128)S(1)}, f32[256,256]{1,0:T(8,128)S(1)}, u32[]{:S(2)}, u32[]{:S(2)}) collective-permute-start(f32[256,256]{1,0:T(8,128)S(1)} %fusion.13), channel_id=1, source_target_pairs={{0,2},{1,3},{2,0},{3,1},{4,6},{5,7},{6,4},{7,5},{8,10},{9,11},{10,... | collective-permute-start | bytes 786440 | tf_op jit(solution)/shard_map/ppermute | solution.py:41
  68.1 0.4 fusion.44
  68.5 1.9 %collective-permute-start.9 = (f32[256,256]{1,0:T(8,128)S(1)}, f32[256,256]{1,0:T(8,128)S(1)}, u32[]{:S(2)}, u32[]{:S(2)}) collective-permute-start(f32[256,256]{1,0:T(8,128)S(1)} %fusion.13), channel_id=1, source_target_pairs={{0,63},{1,2},{2,1},{3,4},{4,3},{5,6},{6,5},{7,8},{8,7},{9,10},{10,... | collective-permute-start | bytes 786440 | tf_op jit(solution)/shard_map/ppermute | solution.py:44
  70.4 4.0 %collective-permute-start.8 = (f32[256,256]{1,0:T(8,128)S(1)}, f32[256,256]{1,0:T(8,128)S(1)}, u32[]{:S(2)}, u32[]{:S(2)}) collective-permute-start(f32[256,256]{1,0:T(8,128)S(1)} %fusion.13), channel_id=1, source_target_pairs={{0,1},{1,0},{2,3},{3,2},{4,5},{5,4},{6,7},{7,6},{8,9},{9,8},{10,11... | collective-permute-start | bytes 786440 | tf_op jit(solution)/shard_map/ppermute | solution.py:42
  74.5 0.4 fusion.20
  74.9 0.3 collective-permute-done.10
  75.2 0.4 fusion.28
  75.6 0.0 collective-permute-done.8
  75.6 0.4 convolution_add_fusion.3
  76.0 2.3 %collective-permute-done.9 = f32[256,256]{1,0:T(8,128)S(1)} collective-permute-done((f32[256,256]{1,0:T(8,128)S(1)}, f32[256,256]{1,0:T(8,128)S(1)}, u32[]{:S(2)}, u32[]{:S(2)}) %collective-permute-start.9) | collective-permute-done | bytes 262176 | tf_op jit(solution)/shard_map/ppermute | solution.py:44
  78.3 0.4 fusion.16
  78.7 2.6 %collective-permute-start.15 = (f32[256,256]{1,0:T(8,128)S(1)}, f32[256,256]{1,0:T(8,128)S(1)}, u32[]{:S(2)}, u32[]{:S(2)}) collective-permute-start(f32[256,256]{1,0:T(8,128)S(1)} %fusion.16), channel_id=1, source_target_pairs={{0,62},{1,63},{2,4},{3,5},{4,2},{5,3},{6,8},{7,9},{8,6},{9,7},{10,... | collective-permute-start | bytes 786440 | tf_op jit(solution)/shard_map/ppermute | solution.py:45
  81.3 1.9 %collective-permute-start.14 = (f32[256,256]{1,0:T(8,128)S(1)}, f32[256,256]{1,0:T(8,128)S(1)}, u32[]{:S(2)}, u32[]{:S(2)}) collective-permute-start(f32[256,256]{1,0:T(8,128)S(1)} %fusion.16), channel_id=1, source_target_pairs={{0,2},{1,3},{2,0},{3,1},{4,6},{5,7},{6,4},{7,5},{8,10},{9,11},{10,... | collective-permute-start | bytes 786440 | tf_op jit(solution)/shard_map/ppermute | solution.py:41
  83.2 0.4 fusion.50
  83.6 4.5 %collective-permute-start.13 = (f32[256,256]{1,0:T(8,128)S(1)}, f32[256,256]{1,0:T(8,128)S(1)}, u32[]{:S(2)}, u32[]{:S(2)}) collective-permute-start(f32[256,256]{1,0:T(8,128)S(1)} %fusion.16), channel_id=1, source_target_pairs={{0,63},{1,2},{2,1},{3,4},{4,3},{5,6},{6,5},{7,8},{8,7},{9,10},{10,... | collective-permute-start | bytes 786440 | tf_op jit(solution)/shard_map/ppermute | solution.py:44
  88.1 2.1 %collective-permute-start.12 = (f32[256,256]{1,0:T(8,128)S(1)}, f32[256,256]{1,0:T(8,128)S(1)}, u32[]{:S(2)}, u32[]{:S(2)}) collective-permute-start(f32[256,256]{1,0:T(8,128)S(1)} %fusion.16), channel_id=1, source_target_pairs={{0,1},{1,0},{2,3},{3,2},{4,5},{5,4},{6,7},{7,6},{8,9},{9,8},{10,11... | collective-permute-start | bytes 786440 | tf_op jit(solution)/shard_map/ppermute | solution.py:42
  90.2 0.5 collective-permute-done.15
  90.8 0.4 fusion.26
  91.2 0.4 fusion.34
  91.6 0.4 convolution_add_fusion.1
  92.0 1.6 %collective-permute-done.13 = f32[256,256]{1,0:T(8,128)S(1)} collective-permute-done((f32[256,256]{1,0:T(8,128)S(1)}, f32[256,256]{1,0:T(8,128)S(1)}, u32[]{:S(2)}, u32[]{:S(2)}) %collective-permute-start.13) | collective-permute-done | bytes 262176 | tf_op jit(solution)/shard_map/ppermute | solution.py:44
  93.5 0.4 fusion.19
  94.0 0.7 copy-done.1
  94.7 2.4 %fusion.65 = f32[256,2048]{1,0:T(8,128)} fusion(f32[256,256]{1,0:T(8,128)S(1)} %fusion.19, f32[256,2048]{1,0:T(8,128)S(1)} %copy-done), kind=kOutput, calls=%fused_computation.84 | convolution fusion | flops 805306368 | bytes 4456448 | tf_op jit(solution)/shard_map/dot_general | solution.py:85
  97.1 0.0 reduce-scatter.2.cloned.1.call-update
  97.1 0.9 copy-done.2
  98.1 0.6 fusion.66
  98.7 0.8 reshape.14
  99.4 12.2 %all-to-all-start = ((f32[64,4,256]{2,1,0:T(4,128)}), f32[64,4,256]{2,1,0:T(4,128)S(1)}, u32[]{:S(2)}, u32[]{:S(2)}) async-start(f32[64,4,256]{2,1,0:T(4,128)} %reshape.14), calls=%async_computation.1 | async-start | bytes 524288 | tf_op jit(solution)/shard_map/all_to_all | solution.py:83
  111.6 0.5 slice.20
  112.8 10.4 %all-to-all-done = f32[64,4,256]{2,1,0:T(4,128)S(1)} async-done(((f32[64,4,256]{2,1,0:T(4,128)}), f32[64,4,256]{2,1,0:T(4,128)S(1)}, u32[]{:S(2)}, u32[]{:S(2)}) %all-to-all-start) | async-done | bytes 262176 | tf_op jit(solution)/shard_map/all_to_all | solution.py:83
  123.2 0.1 reduce_sum.9
  123.3 0.6 multiply_add_fusion
  123.9 20.6 %reduce-scatter.2.cloned.1.call-done = f32[256,256]{1,0:T(8,128)} async-done(((f32[256,2048]{1,0:T(8,128)}), f32[256,256]{1,0:T(8,128)}) %reduce-scatter.2.cloned.1.call-update) | async-done | bytes 262160 | tf_op jit(solution)/shard_map/reduce_scatter | solution.py:88
  (12 shorter events, 0.0 us)
Async XLA Ops:
  7.2 87.5 %copy-start = (f32[256,2048]{1,0:T(8,128)S(1)}, f32[256,2048]{1,0:T(8,128)}, u32[]{:S(2)}) copy-start(f32[256,2048]{1,0:T(8,128)} %param.7) | copy-start | bytes 6291460
  7.2 137.3 %reduce-scatter.2.cloned.1.call-start = ((), (), s32[]{:S(2)}) async-start(), calls=%async_computation.2 | async-start | bytes 2359296 | tf_op jit(solution)/shard_map/reduce_scatter | solution.py:88
  16.2 20.5 %collective-permute-start.3 = (f32[256,256]{1,0:T(8,128)}, f32[256,256]{1,0:T(8,128)S(1)}, u32[]{:S(2)}, u32[]{:S(2)}) collective-permute-start(f32[256,256]{1,0:T(8,128)} %param.4), channel_id=1, source_target_pairs={{0,62},{1,63},{2,4},{3,5},{4,2},{5,3},{6,8},{7,9},{8,6},{9,7},{10,... | collective-permute-start | bytes 786440 | tf_op jit(solution)/shard_map/ppermute | solution.py:45
  27.4 9.9 %collective-permute-start.2 = (f32[256,256]{1,0:T(8,128)}, f32[256,256]{1,0:T(8,128)S(1)}, u32[]{:S(2)}, u32[]{:S(2)}) collective-permute-start(f32[256,256]{1,0:T(8,128)} %param.4), channel_id=1, source_target_pairs={{0,2},{1,3},{2,0},{3,1},{4,6},{5,7},{6,4},{7,5},{8,10},{9,11},{10,... | collective-permute-start | bytes 786440 | tf_op jit(solution)/shard_map/ppermute | solution.py:41
  29.4 10.0 %collective-permute-start.1 = (f32[256,256]{1,0:T(8,128)}, f32[256,256]{1,0:T(8,128)S(1)}, u32[]{:S(2)}, u32[]{:S(2)}) collective-permute-start(f32[256,256]{1,0:T(8,128)} %param.4), channel_id=1, source_target_pairs={{0,63},{1,2},{2,1},{3,4},{4,3},{5,6},{6,5},{7,8},{8,7},{9,10},{10,... | collective-permute-start | bytes 786440 | tf_op jit(solution)/shard_map/ppermute | solution.py:44
  31.3 6.4 %collective-permute-start = (f32[256,256]{1,0:T(8,128)}, f32[256,256]{1,0:T(8,128)S(1)}, u32[]{:S(2)}, u32[]{:S(2)}) collective-permute-start(f32[256,256]{1,0:T(8,128)} %param.4), channel_id=1, source_target_pairs={{0,1},{1,0},{2,3},{3,2},{4,5},{5,4},{6,7},{7,6},{8,9},{9,8},{10,11... | collective-permute-start | bytes 786440 | tf_op jit(solution)/shard_map/ppermute | solution.py:42
  36.7 2.7 %copy-start.3 = (f32[256,256]{1,0:T(8,128)S(1)}, f32[256,256]{1,0:T(8,128)}, u32[]{:S(2)}) copy-start(f32[256,256]{1,0:T(8,128)} %param.4) | copy-start | bytes 786436
  39.8 13.3 %collective-permute-start.6 = (f32[256,256]{1,0:T(8,128)S(1)}, f32[256,256]{1,0:T(8,128)S(1)}, u32[]{:S(2)}, u32[]{:S(2)}) collective-permute-start(f32[256,256]{1,0:T(8,128)S(1)} %get-tuple-element.6), channel_id=1, source_target_pairs={{0,2},{1,3},{2,0},{3,1},{4,6},{5,7},{6,4},{7,5},{8,10},{9,11},{10,... | collective-permute-start | bytes 786440 | tf_op jit(solution)/shard_map/ppermute | solution.py:41
  42.7 18.0 %collective-permute-start.5 = (f32[256,256]{1,0:T(8,128)S(1)}, f32[256,256]{1,0:T(8,128)S(1)}, u32[]{:S(2)}, u32[]{:S(2)}) collective-permute-start(f32[256,256]{1,0:T(8,128)S(1)} %get-tuple-element.6), channel_id=1, source_target_pairs={{0,63},{1,2},{2,1},{3,4},{4,3},{5,6},{6,5},{7,8},{8,7},{9,10},{10,... | collective-permute-start | bytes 786440 | tf_op jit(solution)/shard_map/ppermute | solution.py:44
  44.7 15.6 %collective-permute-start.4 = (f32[256,256]{1,0:T(8,128)S(1)}, f32[256,256]{1,0:T(8,128)S(1)}, u32[]{:S(2)}, u32[]{:S(2)}) collective-permute-start(f32[256,256]{1,0:T(8,128)S(1)} %get-tuple-element.6), channel_id=1, source_target_pairs={{0,1},{1,0},{2,3},{3,2},{4,5},{5,4},{6,7},{7,6},{8,9},{9,8},{10,11... | collective-permute-start | bytes 786440 | tf_op jit(solution)/shard_map/ppermute | solution.py:42
  47.7 12.2 %collective-permute-start.7 = (f32[256,256]{1,0:T(8,128)S(1)}, f32[256,256]{1,0:T(8,128)S(1)}, u32[]{:S(2)}, u32[]{:S(2)}) collective-permute-start(f32[256,256]{1,0:T(8,128)S(1)} %get-tuple-element.6), channel_id=1, source_target_pairs={{0,62},{1,63},{2,4},{3,5},{4,2},{5,3},{6,8},{7,9},{8,6},{9,7},{10,... | collective-permute-start | bytes 786440 | tf_op jit(solution)/shard_map/ppermute | solution.py:45
  61.1 13.3 %collective-permute-start.11 = (f32[256,256]{1,0:T(8,128)S(1)}, f32[256,256]{1,0:T(8,128)S(1)}, u32[]{:S(2)}, u32[]{:S(2)}) collective-permute-start(f32[256,256]{1,0:T(8,128)S(1)} %fusion.13), channel_id=1, source_target_pairs={{0,62},{1,63},{2,4},{3,5},{4,2},{5,3},{6,8},{7,9},{8,6},{9,7},{10,... | collective-permute-start | bytes 786440 | tf_op jit(solution)/shard_map/ppermute | solution.py:45
  66.2 9.0 %collective-permute-start.10 = (f32[256,256]{1,0:T(8,128)S(1)}, f32[256,256]{1,0:T(8,128)S(1)}, u32[]{:S(2)}, u32[]{:S(2)}) collective-permute-start(f32[256,256]{1,0:T(8,128)S(1)} %fusion.13), channel_id=1, source_target_pairs={{0,2},{1,3},{2,0},{3,1},{4,6},{5,7},{6,4},{7,5},{8,10},{9,11},{10,... | collective-permute-start | bytes 786440 | tf_op jit(solution)/shard_map/ppermute | solution.py:41
  68.5 9.8 %collective-permute-start.9 = (f32[256,256]{1,0:T(8,128)S(1)}, f32[256,256]{1,0:T(8,128)S(1)}, u32[]{:S(2)}, u32[]{:S(2)}) collective-permute-start(f32[256,256]{1,0:T(8,128)S(1)} %fusion.13), channel_id=1, source_target_pairs={{0,63},{1,2},{2,1},{3,4},{4,3},{5,6},{6,5},{7,8},{8,7},{9,10},{10,... | collective-permute-start | bytes 786440 | tf_op jit(solution)/shard_map/ppermute | solution.py:44
  70.4 5.2 %collective-permute-start.8 = (f32[256,256]{1,0:T(8,128)S(1)}, f32[256,256]{1,0:T(8,128)S(1)}, u32[]{:S(2)}, u32[]{:S(2)}) collective-permute-start(f32[256,256]{1,0:T(8,128)S(1)} %fusion.13), channel_id=1, source_target_pairs={{0,1},{1,0},{2,3},{3,2},{4,5},{5,4},{6,7},{7,6},{8,9},{9,8},{10,11... | collective-permute-start | bytes 786440 | tf_op jit(solution)/shard_map/ppermute | solution.py:42
  78.7 12.0 %collective-permute-start.15 = (f32[256,256]{1,0:T(8,128)S(1)}, f32[256,256]{1,0:T(8,128)S(1)}, u32[]{:S(2)}, u32[]{:S(2)}) collective-permute-start(f32[256,256]{1,0:T(8,128)S(1)} %fusion.16), channel_id=1, source_target_pairs={{0,62},{1,63},{2,4},{3,5},{4,2},{5,3},{6,8},{7,9},{8,6},{9,7},{10,... | collective-permute-start | bytes 786440 | tf_op jit(solution)/shard_map/ppermute | solution.py:45
  81.3 9.8 %collective-permute-start.14 = (f32[256,256]{1,0:T(8,128)S(1)}, f32[256,256]{1,0:T(8,128)S(1)}, u32[]{:S(2)}, u32[]{:S(2)}) collective-permute-start(f32[256,256]{1,0:T(8,128)S(1)} %fusion.16), channel_id=1, source_target_pairs={{0,2},{1,3},{2,0},{3,1},{4,6},{5,7},{6,4},{7,5},{8,10},{9,11},{10,... | collective-permute-start | bytes 786440 | tf_op jit(solution)/shard_map/ppermute | solution.py:41
  83.6 9.9 %collective-permute-start.13 = (f32[256,256]{1,0:T(8,128)S(1)}, f32[256,256]{1,0:T(8,128)S(1)}, u32[]{:S(2)}, u32[]{:S(2)}) collective-permute-start(f32[256,256]{1,0:T(8,128)S(1)} %fusion.16), channel_id=1, source_target_pairs={{0,63},{1,2},{2,1},{3,4},{4,3},{5,6},{6,5},{7,8},{8,7},{9,10},{10,... | collective-permute-start | bytes 786440 | tf_op jit(solution)/shard_map/ppermute | solution.py:44
  88.1 3.4 %collective-permute-start.12 = (f32[256,256]{1,0:T(8,128)S(1)}, f32[256,256]{1,0:T(8,128)S(1)}, u32[]{:S(2)}, u32[]{:S(2)}) collective-permute-start(f32[256,256]{1,0:T(8,128)S(1)} %fusion.16), channel_id=1, source_target_pairs={{0,1},{1,0},{2,3},{3,2},{4,5},{5,4},{6,7},{7,6},{8,9},{9,8},{10,11... | collective-permute-start | bytes 786440 | tf_op jit(solution)/shard_map/ppermute | solution.py:42
  94.0 0.7 copy-start.1
  97.1 0.9 copy-start.2
  99.4 23.7 %all-to-all-start = ((f32[64,4,256]{2,1,0:T(4,128)}), f32[64,4,256]{2,1,0:T(4,128)S(1)}, u32[]{:S(2)}, u32[]{:S(2)}) async-start(f32[64,4,256]{2,1,0:T(4,128)} %reshape.14), calls=%async_computation.1 | async-start | bytes 524288 | tf_op jit(solution)/shard_map/all_to_all | solution.py:83
Sparse Core Ops, SparseCore 0:
  97.3 47.1 reduce-scatter.1
